TPU v7x, 32 devices: a whole 2x2x4 slice. The times are simulated.
32 devices in a mesh: groups: 2 (over x), tok: 16 (over z, y, core).
Axes of the slice: x: 2, y: 2, z: 4, core: 2. Of those that a mesh axis runs over, the one named last changes fastest.
Arguments:
- queries: bfloat16 [4096, 2048], P(('groups', 'tok')), parts along dimension 0, may hold values from -6 to 6
- key_matrix: bfloat16 [4096, 512], P(('groups', 'tok')), parts along dimension 0, may hold values from -6 to 6
- value_matrix: bfloat16 [4096, 512], P(('groups', 'tok')), parts along dimension 0, may hold values from -6 to 6
- attention_output: bfloat16 [4096, 2048], P(('groups', 'tok')), parts along dimension 0, may hold values from -3 to 3
- output_gradient: bfloat16 [4096, 2048], P(('groups', 'tok')), parts along dimension 0, may hold values from -48 to 48
- log_sum_norm: float32 [16, 4096], P(None, ('groups', 'tok')), parts along dimension 1, may hold values from 6 to 8
- doc_ids: int32 [4096], P(('groups', 'tok')), parts along dimension 0, may hold values from 0 to 7, never falling along the last dimension, each value on 1 to 1024 neighbouring positions
Outputs:
- query_grad: bfloat16 [4096, 2048], P(('groups', 'tok')), parts along dimension 0
- key_grad: bfloat16 [4096, 512], P(('groups', 'tok')), parts along dimension 0
- value_grad: bfloat16 [4096, 512], P(('groups', 'tok')), parts along dimension 0
There are 2 independent parts, one for each index of `groups`. A program takes and returns all parts, laid end to end along the dimension named above; each array names one. Nothing has to cross between parts.
Inputs may be any that keep to these rules, and one draw needn't show every extreme that they name: `doc_ids`: document ids never fall along the slab; each document has 1 to 1024 tokens and one has exactly 1024.
All inputs are finite; a program needn't handle non-finite values.
Results may differ from a plain program's by a relative error of at most 0.0051.
Values may be sent and summed in bfloat16 or wider, within the bound.
No kernel may reach another device: no remote copies, remote signals or barrier semaphores. Data moves between devices by JAX's collectives and lax.ppermute only.
A program may use at most 128 MiB of HBM per device.

v0:
```python
import functools
import math

import jax
import jax.numpy as jnp
from jax import lax
from jax.experimental import pallas as pl
from jax.experimental.pallas import tpu as pltpu
from jax.sharding import PartitionSpec as P

WINDOW = 4096
QUERY_HEADS = 16
KEY_VALUE_HEADS = 4
HEAD_SIZE = 128
GROUP = QUERY_HEADS // KEY_VALUE_HEADS
SCALE = HEAD_SIZE ** (-0.5)
LOG2E = math.log2(math.e)
EXTRA = 8
F32 = jnp.float32
BF16 = jnp.bfloat16

VMEM = pl.BlockSpec(memory_space=pltpu.VMEM)
SMEM = pl.BlockSpec(memory_space=pltpu.SMEM)


def dot(a, b, dims):
    return lax.dot_general(a, b, (dims, ((), ())), preferred_element_type=F32)


HBM = pl.BlockSpec(memory_space=pltpu.MemorySpace.HBM)
TOKEN = jax.ShapeDtypeStruct((8, 128), F32)


def call(kernel, ins, outs, scratch=(), flops=0, name=None, specs=None, out_specs=None):
    specs = specs or [VMEM] * (len(ins) - 1)
    ins = [ins[0]] + [
        pltpu.with_memory_space_constraint(x, pltpu.MemorySpace.HBM) if spec is HBM else x
        for x, spec in zip(ins[1:], specs)
    ]
    size = sum(math.prod(o.shape) * o.dtype.itemsize for o in outs)
    size += sum(math.prod(x.shape) * x.dtype.itemsize for x in ins)
    return pl.pallas_call(
        kernel,
        out_shape=outs,
        in_specs=[SMEM] + specs,
        out_specs=out_specs or [VMEM] * len(outs),
        scratch_shapes=list(scratch),
        cost_estimate=pl.CostEstimate(flops=flops, bytes_accessed=size, transcendentals=0),
        compiler_params=pltpu.CompilerParams(vmem_limit_bytes=48 << 20),
        name=name,
    )(*ins)


def head_columns(g):
    return pl.ds(pl.multiple_of(g * HEAD_SIZE, HEAD_SIZE), HEAD_SIZE)


def pack_keys(rows, place, key_ref, value_ref, doc_ref, *rest):
    outs, (ids, doc_sem, sems) = rest[:-3], rest[-3:]
    first = pltpu.make_async_copy(doc_ref, ids, doc_sem)
    first.start()
    copies = []
    for s, out in enumerate(outs):
        cut = head_columns(place[1] ^ s)
        for k, source in enumerate((key_ref, value_ref)):
            target = out.at[k * rows : (k + 1) * rows, :]
            copies.append(pltpu.make_async_copy(source.at[:, cut], target, sems.at[s, k]))
    for copy in copies:
        copy.start()
    first.wait()
    docs = jnp.broadcast_to((ids[...] + 1).astype(F32), (EXTRA, rows)).astype(BF16)
    for out in outs:
        out[2 * rows :, 0:rows] = docs
    for copy in copies:
        copy.wait()


def pack_queries(rows, place, query_ref, grad_ref, output_ref, norm_ref, *rest):
    outs, (token, grads, outputs, stats, sems, more_sems) = rest[:-6], rest[-6:]
    first = pltpu.make_async_copy(grad_ref, grads, more_sems.at[0])
    second = pltpu.make_async_copy(output_ref, outputs, more_sems.at[1])
    first.start()
    second.start()
    copies = []
    for s, out in enumerate(outs):
        for h in range(GROUP):
            cut = head_columns((place[1] ^ s) * GROUP + h)
            for k, source in enumerate((query_ref, grad_ref)):
                at = (k * GROUP + h) * rows
                target = out.at[at : at + rows, :]
                copies.append(pltpu.make_async_copy(source.at[:, cut], target, sems.at[s, k, h]))
    for copy in copies:
        copy.start()
    first.wait()
    second.wait()
    lane = lax.broadcasted_iota(jnp.int32, (rows, HEAD_SIZE), 1)
    columns = jnp.zeros((rows, HEAD_SIZE), F32)
    for h in range(QUERY_HEADS):
        cut = slice(h * HEAD_SIZE, (h + 1) * HEAD_SIZE)
        product = grads[:, cut].astype(F32) * outputs[:, cut].astype(F32)
        columns = jnp.where(lane == h, jnp.sum(product, 1, keepdims=True), columns)
    delta = columns.T
    for g in range(KEY_VALUE_HEADS):
        stats[g, 0:GROUP, :] = norm_ref[g * GROUP : (g + 1) * GROUP, :]
        stats[g, GROUP : 2 * GROUP, :] = delta[g * GROUP : (g + 1) * GROUP, :]
    for s, out in enumerate(outs):
        left = stats[place[1] ^ s]
        for part in range(3):
            term = left.astype(BF16)
            at = 2 * GROUP * rows + part * EXTRA
            out[at : at + EXTRA, 0:rows] = term
            left = left - term.astype(F32)
    for copy in copies:
        copy.wait()
    token[...] = jnp.zeros_like(token)


def join(rows, place, *refs):
    parts = KEY_VALUE_HEADS
    pieces, out = refs[:parts], refs[-1]
    span = parts * rows
    for s, piece in enumerate(pieces):
        a = place[1] ^ s
        for k in range(2):
            at = pl.multiple_of(k * span + a * rows, rows)
            out[pl.ds(at, rows), :] = piece[k * rows : (k + 1) * rows, :]
        at = pl.multiple_of(2 * span + a * EXTRA, EXTRA)
        out[pl.ds(at, EXTRA), :] = piece[2 * rows :, :]


def attend_scratch(rows):
    parts = KEY_VALUE_HEADS
    return [
        pltpu.VMEM((parts, HEAD_SIZE, GROUP * rows), F32),
        pltpu.VMEM((2 * parts * rows, HEAD_SIZE), F32),
        pltpu.VMEM((HEAD_SIZE, parts * rows), BF16),
        pltpu.VMEM((parts * rows, rows), F32),
        pltpu.SMEM((2 * parts,), F32),
    ]


def attend(rows, offsets, reach, first, last, place, *refs):
    parts = KEY_VALUE_HEADS
    queries, refs = refs[:parts], refs[parts:]
    own, refs = refs[0], refs[1:]
    keys, refs = refs[: len(offsets)], refs[len(offsets) :]
    if not first:
        dq_in, refs = refs[0], refs[1:]
    if last:
        dq_out, refs = refs[:parts], refs[parts:]
    else:
        dq_out, refs = refs[0], refs[1:]
    kv_out, refs = refs[: len(offsets)], refs[len(offsets) :]
    dq, dkv, key_t, docs_t, docs_s = refs
    row, me = place[0], place[1]
    width = GROUP * rows
    span = parts * rows
    for a in range(parts):
        docs = own[2 * span + a * EXTRA : 2 * span + a * EXTRA + 1, 0:rows].astype(F32)
        docs_s[a] = jnp.min(docs)
    dq[...] = jnp.zeros_like(dq)
    for at, offset in enumerate(offsets):
        dkv[...] = jnp.zeros_like(dkv)
        key_ref = keys[at]
        for b in range(parts):
            cut = slice(b * rows, (b + 1) * rows)
            key_t[:, cut] = key_ref[cut, :].T
            docs = key_ref[2 * span + b * EXTRA : 2 * span + b * EXTRA + 1, 0:rows].astype(F32)
            docs_t[cut, :] = jnp.broadcast_to(docs, (rows, rows)).T
            if b == parts - 1:
                docs_s[parts] = jnp.max(docs)
        for s in range(parts):
            a = me ^ s
            near = offset * span + a * rows
            live = (near - span + 1 < reach) & (row >= offset) & (docs_s[a] <= docs_s[parts])

            @pl.when(live)
            def _(s=s, a=a, near=near, key_ref=key_ref, offset=offset):
                docs = own[pl.ds(pl.multiple_of(2 * span + a * EXTRA, EXTRA), EXTRA), :]
                docs = docs.astype(F32)[0:1, 0:rows]
                query = queries[s][0:width, :]
                grad = queries[s][width : 2 * width, :]
                stats = queries[s][2 * width :, :].astype(F32)
                stats = stats[0:EXTRA] + stats[EXTRA : 2 * EXTRA] + stats[2 * EXTRA :]
                gap = (
                    near
                    + lax.broadcasted_iota(jnp.int32, (span, rows), 1)
                    - lax.broadcasted_iota(jnp.int32, (span, rows), 0)
                )
                mask = docs_t[...] == docs
                if offset == 0:
                    mask = mask & (gap >= 0)
                if (offset + 1) * span > WINDOW:
                    mask = mask & (gap < WINDOW)
                scores = dot(key_ref[0:span, :], query, ((1,), (1,)))
                dprob = dot(key_ref[span : 2 * span, :], grad, ((1,), (1,)))
                probs, dscores = [], []
                for h in range(GROUP):
                    cut = slice(h * rows, (h + 1) * rows)
                    norm = stats[h : h + 1, :] * LOG2E
                    delta = stats[GROUP + h : GROUP + h + 1, :]
                    prob = jnp.exp2(scores[:, cut] * (SCALE * LOG2E) - norm)
                    prob = jnp.where(mask, prob, 0.0)
                    probs.append(prob.astype(BF16))
                    dscores.append((prob * (dprob[:, cut] - delta) * SCALE).astype(BF16))
                prob = jnp.concatenate(probs, 1)
                dscore = jnp.concatenate(dscores, 1)
                dkv[0:span, :] += dot(dscore, query, ((1,), (0,)))
                dkv[span:, :] += dot(prob, grad, ((1,), (0,)))
                dq[s] += dot(key_t[...], dscore, ((1,), (0,)))

        kv_out[at][...] = dkv[...].astype(kv_out[at].dtype)
    for s in range(parts):
        total = dq[s] if first else dq[s] + dq_in[s]
        if last:
            dq_out[s][...] = total.astype(BF16)
        else:
            dq_out[s] = total


def add_terms(rows, count, place, *refs):
    parts = KEY_VALUE_HEADS
    terms, outs = refs[:count], refs[-parts:]
    for s, out in enumerate(outs):
        for k in range(2):
            at = pl.multiple_of((k * parts + (place[1] ^ s)) * rows, rows)
            total = terms[0][pl.ds(at, rows), :]
            for term in terms[1:]:
                total = total + term[pl.ds(at, rows), :].astype(F32)
            out[k * rows : (k + 1) * rows, :] = total.astype(BF16)


def spread_queries(rows, place, *refs):
    pieces, (out, token, turned, sems) = refs[:-4], refs[-4:]
    width = GROUP * HEAD_SIZE
    copies = []
    for s, piece in enumerate(pieces):
        for h in range(GROUP):
            cut = slice(h * HEAD_SIZE, (h + 1) * HEAD_SIZE)
            turned[s, :, cut] = piece[:, h * rows : (h + 1) * rows].T
        cut = pl.ds(pl.multiple_of((place[1] ^ s) * width, width), width)
        copies.append(pltpu.make_async_copy(turned.at[s], out.at[:, cut], sems.at[s]))
        copies[-1].start()
    token[...] = jnp.zeros_like(token)
    for copy in copies:
        copy.wait()


def spread_keys(rows, place, *refs):
    pieces, outs, sems = refs[:-3], refs[-3:-1], refs[-1]
    copies = []
    for s, piece in enumerate(pieces):
        for k, out in enumerate(outs):
            source = piece.at[k * rows : (k + 1) * rows, :]
            target = out.at[:, head_columns(place[1] ^ s)]
            copies.append(pltpu.make_async_copy(source, target, sems.at[s, k]))
            copies[-1].start()
    for copy in copies:
        copy.wait()


def local(
    queries, key_matrix, value_matrix, attention_output, output_gradient, log_sum_norm, doc_ids
):
    parts = KEY_VALUE_HEADS
    rows = queries.shape[0]
    count = lax.axis_size("tok")
    span = parts * rows
    reach = min(WINDOW, count * rows // 2)
    behind = min(-(-(reach - 1) // span), count // parts - 1)
    device = lax.axis_index("tok")
    place = jnp.stack([device // parts, device % parts]).astype(jnp.int32)
    width = GROUP * rows
    shape = jax.ShapeDtypeStruct

    def across(value, s):
        return lax.ppermute(value, "tok", [(t, t ^ s) for t in range(count)])

    def along(value, steps):
        return lax.ppermute(
            value, "tok", [(t, (t + steps * parts) % count) for t in range(count)]
        )

    def exchange(pieces):
        return [pieces[0]] + [across(pieces[s], s) for s in range(1, parts)]

    pieces = call(
        functools.partial(pack_keys, rows),
        (place, key_matrix, value_matrix, doc_ids.reshape(1, rows)),
        [shape((2 * rows + EXTRA, HEAD_SIZE), BF16)] * parts,
        scratch=[
            pltpu.VMEM((1, rows), jnp.int32),
            pltpu.SemaphoreType.DMA(()),
            pltpu.SemaphoreType.DMA((parts, 2)),
        ],
        specs=[HBM, HBM, HBM],
        name="pack_keys",
    )
    pieces = exchange(pieces)
    *query_pieces, token = call(
        functools.partial(pack_queries, rows),
        (place, queries, output_gradient, attention_output, log_sum_norm),
        [shape((2 * width + 3 * EXTRA, HEAD_SIZE), BF16)] * parts + [TOKEN],
        scratch=[
            pltpu.VMEM(queries.shape, BF16),
            pltpu.VMEM(queries.shape, BF16),
            pltpu.VMEM((parts, 2 * GROUP, rows), F32),
            pltpu.SemaphoreType.DMA((parts, 2, GROUP)),
            pltpu.SemaphoreType.DMA((2,)),
        ],
        specs=[HBM, HBM, HBM, VMEM],
        name="pack_queries",
    )
    (own,) = call(
        functools.partial(join, rows),
        (place, *pieces, token),
        [shape((parts * (2 * rows + EXTRA), HEAD_SIZE), BF16)],
        name="join",
    )
    query_pieces = exchange(query_pieces)
    windows = [own]
    for _ in range(behind):
        windows.append(along(windows[-1], 1))

    kv_shape = (2 * span, HEAD_SIZE)
    stages = [tuple(range(min(2, behind + 1)))] + [(d,) for d in range(2, behind + 1)]
    dq, terms = None, []
    for k, offsets in enumerate(stages):
        first, last = k == 0, k == len(stages) - 1
        ins = [place, *query_pieces, own, *[windows[d] for d in offsets]]
        if not first:
            ins.append(dq)
        if last:
            outs = [shape((HEAD_SIZE, width), BF16)] * parts
        else:
            outs = [shape((parts, HEAD_SIZE, width), F32)]
        outs = outs + [shape(kv_shape, F32 if d == 0 else BF16) for d in offsets]
        got = call(
            functools.partial(attend, rows, offsets, reach, first, last),
            ins,
            outs,
            scratch=attend_scratch(rows),
            flops=10 * len(offsets) * span * span * GROUP * HEAD_SIZE,
            name="attend_" + "_".join(map(str, offsets)),
        )
        dq = got[:parts] if last else got[0]
        for d, term in zip(offsets, got[-len(offsets) :]):
            terms.append(term if d == 0 else along(term, -d))

    query_grad, token = call(
        functools.partial(spread_queries, rows),
        (place, *exchange(dq)),
        [shape((rows, parts * GROUP * HEAD_SIZE), BF16), TOKEN],
        scratch=[
            pltpu.VMEM((parts, rows, GROUP * HEAD_SIZE), BF16),
            pltpu.SemaphoreType.DMA((parts,)),
        ],
        out_specs=[HBM, VMEM],
        name="spread_queries",
    )
    pieces = call(
        functools.partial(add_terms, rows, len(terms)),
        (place, *terms, token),
        [shape((2 * rows, HEAD_SIZE), BF16)] * parts,
        name="add_terms",
    )
    key_grad, value_grad = call(
        functools.partial(spread_keys, rows),
        (place, *exchange(pieces)),
        [shape((rows, parts * HEAD_SIZE), BF16)] * 2,
        scratch=[pltpu.SemaphoreType.DMA((parts, 2))],
        out_specs=[HBM, HBM],
        name="spread_keys",
    )
    return query_grad, key_grad, value_grad


def solution(mesh):
    axes = ("groups", "tok")
    return jax.shard_map(
        local,
        mesh=mesh,
        in_specs=(
            P(axes, None),
            P(axes, None),
            P(axes, None),
            P(axes, None),
            P(axes, None),
            P(None, axes),
            P(axes),
        ),
        out_specs=(P(axes, None), P(axes, None), P(axes, None)),
        check_vma=False,
    )
```

profile of v0, /device:TPU:0, one launch (start us, length us, event | category | flops | bytes accessed | tf_op | source)
XLA Modules:
  0.0 62.3 jit_solution(10682737607930368592)
XLA Ops:
  0.6 0.1 pad_add_fusion.place
  0.7 1.5 %pack_keys.1 = (bf16[264,128]{1,0:T(8,128)(2,1)S(1)}, bf16[264,128]{1,0:T(8,128)(2,1)S(1)}, bf16[264,128]{1,0:T(8,128)(2,1)S(1)}, bf16[264,128]{1,0:T(8,128)(2,1)S(1)}) custom-call(s32[2]{0:T(128)S(1)} %pad_add_fusion.place, bf16[128,512]{1,0:T(8,128)(2,1)} %key_ref.1, bf16[128,512]{1,0:T(8,128)(2,1)} %value_ref.1, s32[1,128]{1,0:T(1,128)} %bitcast.3), custom_call_target="tpu_custom_call" | custom-call | bytes 533000 | tf_op jit(solution)/shard_map/pack_keys/pallas_call | solution.py:42
  2.2 0.6 collective-permute-start.3
  2.8 2.6 %collective-permute-start.4 = (bf16[264,128]{1,0:T(8,128)(2,1)S(1)}, bf16[264,128]{1,0:T(8,128)(2,1)S(1)}, u32[]{:S(2)}, u32[]{:S(2)}) collective-permute-start(bf16[264,128]{1,0:T(8,128)(2,1)S(1)} %get-tuple-element.34), channel_id=1, source_target_pairs={{0,2},{1,3},{2,0},{3,1},{4,6},{5,7},{6,4},{7,5},{8,10},{9,11},{10,... | collective-permute-start | bytes 202760 | tf_op jit(solution)/shard_map/ppermute | solution.py:277
  5.4 0.0 collective-permute-start.5
  5.4 3.0 %pack_queries.1 = (bf16[1048,128]{1,0:T(8,128)(2,1)S(1)}, bf16[1048,128]{1,0:T(8,128)(2,1)S(1)}, bf16[1048,128]{1,0:T(8,128)(2,1)S(1)}, bf16[1048,128]{1,0:T(8,128)(2,1)S(1)}, f32[8,128]{1,0:T(8,128)S(1)}) custom-call(s32[2]{0:T(128)S(1)} %pad_add_fusion.place, bf16[128,2048]{1,0:T(8,128)(2,1)} %query_ref.1, bf16[128,2048]{1,0:T(8,128)(2,1)} %grad_ref.1, ...), custom_call_target="tpu_custom_call" | custom-call | bytes 2658312 | tf_op jit(solution)/shard_map/pack_queries/pallas_call | solution.py:42
  8.4 1.1 %collective-permute-done.5.refs_3_ = bf16[264,128]{1,0:T(8,128)(2,1)S(1)} collective-permute-done((bf16[264,128]{1,0:T(8,128)(2,1)S(1)}, bf16[264,128]{1,0:T(8,128)(2,1)S(1)}, u32[]{:S(2)}, u32[]{:S(2)}) %collective-permute-start.5) | collective-permute-done | bytes 67616 | tf_op jit(solution)/shard_map/ppermute | solution.py:277
  9.5 0.6 join.1.refs_4_.refs_5_
  10.1 1.6 %collective-permute-start.6 = (bf16[1056,128]{1,0:T(8,128)(2,1)S(1)}, bf16[1056,128]{1,0:T(8,128)(2,1)S(1)}, u32[]{:S(2)}, u32[]{:S(2)}) collective-permute-start(bf16[1056,128]{1,0:T(8,128)(2,1)S(1)} %join.1.refs_4_.refs_5_), channel_id=1, source_target_pairs={{0,4},{1,5},{2,6},{3,7},{4,8},{5,9},{6,10},{7,11},{8,12},{9,13},{1... | collective-permute-start | bytes 811016 | tf_op jit(solution)/shard_map/ppermute | solution.py:280
  11.7 1.4 %collective-permute-start.1 = (bf16[1048,128]{1,0:T(8,128)(2,1)S(1)}, bf16[1048,128]{1,0:T(8,128)(2,1)S(1)}, u32[]{:S(2)}, u32[]{:S(2)}) collective-permute-start(bf16[1048,128]{1,0:T(8,128)(2,1)S(1)} %get-tuple-element.30), channel_id=1, source_target_pairs={{0,2},{1,3},{2,0},{3,1},{4,6},{5,7},{6,4},{7,5},{8,10},{9,11},{10,... | collective-permute-start | bytes 804872 | tf_op jit(solution)/shard_map/ppermute | solution.py:277
  13.1 0.5 collective-permute-start.2
  13.6 7.0 %collective-permute-done.6.refs_6_ = bf16[1056,128]{1,0:T(8,128)(2,1)S(1)} collective-permute-done((bf16[1056,128]{1,0:T(8,128)(2,1)S(1)}, bf16[1056,128]{1,0:T(8,128)(2,1)S(1)}, u32[]{:S(2)}, u32[]{:S(2)}) %collective-permute-start.6) | collective-permute-done | bytes 270368 | tf_op jit(solution)/shard_map/ppermute | solution.py:280
  20.5 0.5 collective-permute-done.1.refs_2_
  21.0 4.8 %collective-permute-done.2.refs_3_ = bf16[1048,128]{1,0:T(8,128)(2,1)S(1)} collective-permute-done((bf16[1048,128]{1,0:T(8,128)(2,1)S(1)}, bf16[1048,128]{1,0:T(8,128)(2,1)S(1)}, u32[]{:S(2)}, u32[]{:S(2)}) %collective-permute-start.2) | collective-permute-done | bytes 268320 | tf_op jit(solution)/shard_map/ppermute | solution.py:277
  25.8 4.5 %attend_0_1.1 = (f32[4,128,512]{2,1,0:T(8,128)S(1)}, f32[1024,128]{1,0:T(8,128)S(1)}, bf16[1024,128]{1,0:T(8,128)(2,1)S(1)}) custom-call(s32[2]{0:T(128)S(1)} %pad_add_fusion.place, bf16[1048,128]{1,0:T(8,128)(2,1)S(1)} %get-tuple-element.28.refs_0_, bf16[1048,128]{1,0:T(8,128)(2,1)S(1)} %collective-permute-done.refs_1_, ...), custom_call_target="tpu_custom_call" | custom-call | flops 2684354560 | bytes 3719176 | tf_op jit(solution)/shard_map/attend_0_1/pallas_call | solution.py:42
  30.3 4.8 %collective-permute-start.11 = (bf16[1024,128]{1,0:T(8,128)(2,1)S(1)}, bf16[1024,128]{1,0:T(8,128)(2,1)S(1)}, u32[]{:S(2)}, u32[]{:S(2)}) collective-permute-start(bf16[1024,128]{1,0:T(8,128)(2,1)S(1)} %get-tuple-element.44), channel_id=1, source_target_pairs={{0,12},{1,13},{2,14},{3,15},{4,0},{5,1},{6,2},{7,3},{8,4},{9,5},{1... | collective-permute-start | bytes 786440 | tf_op jit(solution)/shard_map/ppermute | solution.py:280
  35.1 1.0 %attend_2.1 = (bf16[128,512]{1,0:T(8,128)(2,1)S(1)}, bf16[128,512]{1,0:T(8,128)(2,1)S(1)}, bf16[128,512]{1,0:T(8,128)(2,1)S(1)}, bf16[128,512]{1,0:T(8,128)(2,1)S(1)}, bf16[1024,128]{1,0:T(8,128)(2,1)S(1)}) custom-call(s32[2]{0:T(128)S(1)} %pad_add_fusion.place, bf16[1048,128]{1,0:T(8,128)(2,1)S(1)} %get-tuple-element.28.refs_0_, ...), custom_call_target="tpu_custom_call" | custom-call | flops 1342177280 | bytes 3448840 | tf_op jit(solution)/shard_map/attend_2/pallas_call | solution.py:42
  36.1 1.2 %collective-permute-start.12 = (bf16[1024,128]{1,0:T(8,128)(2,1)S(1)}, bf16[1024,128]{1,0:T(8,128)(2,1)S(1)}, u32[]{:S(2)}, u32[]{:S(2)}) collective-permute-start(bf16[1024,128]{1,0:T(8,128)(2,1)S(1)} %get-tuple-element.45), channel_id=1, source_target_pairs={{0,8},{1,9},{2,10},{3,11},{4,12},{5,13},{6,14},{7,15},{8,0},{9,1},... | collective-permute-start | bytes 786440 | tf_op jit(solution)/shard_map/ppermute | solution.py:280
  37.4 0.3 collective-permute-start.8
  37.7 1.3 %collective-permute-start.9 = (bf16[128,512]{1,0:T(8,128)(2,1)S(1)}, bf16[128,512]{1,0:T(8,128)(2,1)S(1)}, u32[]{:S(2)}, u32[]{:S(2)}) collective-permute-start(bf16[128,512]{1,0:T(8,128)(2,1)S(1)} %get-tuple-element.40), channel_id=1, source_target_pairs={{0,2},{1,3},{2,0},{3,1},{4,6},{5,7},{6,4},{7,5},{8,10},{9,11},{10,... | collective-permute-start | bytes 393224 | tf_op jit(solution)/shard_map/ppermute | solution.py:277
  39.0 0.3 collective-permute-start.10
  39.2 4.8 %collective-permute-done.9.refs_2_ = bf16[128,512]{1,0:T(8,128)(2,1)S(1)} collective-permute-done((bf16[128,512]{1,0:T(8,128)(2,1)S(1)}, bf16[128,512]{1,0:T(8,128)(2,1)S(1)}, u32[]{:S(2)}, u32[]{:S(2)}) %collective-permute-start.9) | collective-permute-done | bytes 131104 | tf_op jit(solution)/shard_map/ppermute | solution.py:277
  44.1 1.2 %collective-permute-done.10.refs_3_ = bf16[128,512]{1,0:T(8,128)(2,1)S(1)} collective-permute-done((bf16[128,512]{1,0:T(8,128)(2,1)S(1)}, bf16[128,512]{1,0:T(8,128)(2,1)S(1)}, u32[]{:S(2)}, u32[]{:S(2)}) %collective-permute-start.10) | collective-permute-done | bytes 131104 | tf_op jit(solution)/shard_map/ppermute | solution.py:277
  45.3 1.4 %spread_queries.1 = (bf16[128,2048]{1,0:T(8,128)(2,1)}, f32[8,128]{1,0:T(8,128)S(1)}) custom-call(s32[2]{0:T(128)S(1)} %pad_add_fusion.place, bf16[128,512]{1,0:T(8,128)(2,1)S(1)} %get-tuple-element.38.refs_0_, bf16[128,512]{1,0:T(8,128)(2,1)S(1)} %collective-permute-done.8.refs_1_, bf16[128,512]{1,0:T(8,128)(2,1)S(1)} %collective-permute-done.9.refs_2_, ...), custom_call_target="tpu_custom_call" | custom-call | bytes 1052680 | tf_op jit(solution)/shard_map/spread_queries/pallas_call | solution.py:42
  46.8 7.8 %collective-permute-done.12.refs_2_ = bf16[1024,128]{1,0:T(8,128)(2,1)S(1)} collective-permute-done((bf16[1024,128]{1,0:T(8,128)(2,1)S(1)}, bf16[1024,128]{1,0:T(8,128)(2,1)S(1)}, u32[]{:S(2)}, u32[]{:S(2)}) %collective-permute-start.12) | collective-permute-done | bytes 262176 | tf_op jit(solution)/shard_map/ppermute | solution.py:280
  54.6 0.6 %add_terms.1 = (bf16[256,128]{1,0:T(8,128)(2,1)S(1)}, bf16[256,128]{1,0:T(8,128)(2,1)S(1)}, bf16[256,128]{1,0:T(8,128)(2,1)S(1)}, bf16[256,128]{1,0:T(8,128)(2,1)S(1)}) custom-call(s32[2]{0:T(128)S(1)} %pad_add_fusion.place, f32[1024,128]{1,0:T(8,128)S(1)} %get-tuple-element.43.refs_0_, bf16[1024,128]{1,0:T(8,128)(2,1)S(1)} %collective-permute-done.11.refs_1_, ...), custom_call_target="tpu_custom_call" | custom-call | bytes 1314824 | tf_op jit(solution)/shard_map/add_terms/pallas_call | solution.py:42
  55.2 0.1 collective-permute-start.13
  55.3 1.3 %collective-permute-start.14 = (bf16[256,128]{1,0:T(8,128)(2,1)S(1)}, bf16[256,128]{1,0:T(8,128)(2,1)S(1)}, u32[]{:S(2)}, u32[]{:S(2)}) collective-permute-start(bf16[256,128]{1,0:T(8,128)(2,1)S(1)} %get-tuple-element.49), channel_id=1, source_target_pairs={{0,2},{1,3},{2,0},{3,1},{4,6},{5,7},{6,4},{7,5},{8,10},{9,11},{10,... | collective-permute-start | bytes 196616 | tf_op jit(solution)/shard_map/ppermute | solution.py:277
  56.6 0.5 collective-permute-start.15
  57.1 2.8 %collective-permute-done.14.refs_2_ = bf16[256,128]{1,0:T(8,128)(2,1)S(1)} collective-permute-done((bf16[256,128]{1,0:T(8,128)(2,1)S(1)}, bf16[256,128]{1,0:T(8,128)(2,1)S(1)}, u32[]{:S(2)}, u32[]{:S(2)}) %collective-permute-start.14) | collective-permute-done | bytes 65568 | tf_op jit(solution)/shard_map/ppermute | solution.py:277
  60.0 1.1 %collective-permute-done.15.refs_3_ = bf16[256,128]{1,0:T(8,128)(2,1)S(1)} collective-permute-done((bf16[256,128]{1,0:T(8,128)(2,1)S(1)}, bf16[256,128]{1,0:T(8,128)(2,1)S(1)}, u32[]{:S(2)}, u32[]{:S(2)}) %collective-permute-start.15) | collective-permute-done | bytes 65568 | tf_op jit(solution)/shard_map/ppermute | solution.py:277
  61.0 1.3 %spread_keys.1 = (bf16[128,512]{1,0:T(8,128)(2,1)}, bf16[128,512]{1,0:T(8,128)(2,1)}) custom-call(s32[2]{0:T(128)S(1)} %pad_add_fusion.place, bf16[256,128]{1,0:T(8,128)(2,1)S(1)} %get-tuple-element.47.refs_0_, bf16[256,128]{1,0:T(8,128)(2,1)S(1)} %collective-permute-done.13.refs_1_, bf16[256,128]{1,0:T(8,128)(2,1)S(1)} %collective-permute-done.14.refs_2_, ...), custom_call_target="tpu_custom_call" | custom-call | bytes 524296 | tf_op jit(solution)/shard_map/spread_keys/pallas_call | solution.py:42
  (11 shorter events, 0.0 us)
Async XLA Ops:
  0.7 4.7 %copy-start = (f32[16,128]{1,0:T(8,128)S(1)}, f32[16,128]{1,0:T(8,128)}, u32[]{:S(2)}) copy-start(f32[16,128]{1,0:T(8,128)} %norm_ref.1) | copy-start | bytes 24580
  2.2 6.2 %collective-permute-start.3 = (bf16[264,128]{1,0:T(8,128)(2,1)S(1)}, bf16[264,128]{1,0:T(8,128)(2,1)S(1)}, u32[]{:S(2)}, u32[]{:S(2)}) collective-permute-start(bf16[264,128]{1,0:T(8,128)(2,1)S(1)} %get-tuple-element.33), channel_id=1, source_target_pairs={{0,1},{1,0},{2,3},{3,2},{4,5},{5,4},{6,7},{7,6},{8,9},{9,8},{10,11... | collective-permute-start | bytes 202760 | tf_op jit(solution)/shard_map/ppermute | solution.py:277
  2.8 5.6 %collective-permute-start.4 = (bf16[264,128]{1,0:T(8,128)(2,1)S(1)}, bf16[264,128]{1,0:T(8,128)(2,1)S(1)}, u32[]{:S(2)}, u32[]{:S(2)}) collective-permute-start(bf16[264,128]{1,0:T(8,128)(2,1)S(1)} %get-tuple-element.34), channel_id=1, source_target_pairs={{0,2},{1,3},{2,0},{3,1},{4,6},{5,7},{6,4},{7,5},{8,10},{9,11},{10,... | collective-permute-start | bytes 202760 | tf_op jit(solution)/shard_map/ppermute | solution.py:277
  5.4 4.1 %collective-permute-start.5 = (bf16[264,128]{1,0:T(8,128)(2,1)S(1)}, bf16[264,128]{1,0:T(8,128)(2,1)S(1)}, u32[]{:S(2)}, u32[]{:S(2)}) collective-permute-start(bf16[264,128]{1,0:T(8,128)(2,1)S(1)} %get-tuple-element.35), channel_id=1, source_target_pairs={{0,3},{1,2},{2,1},{3,0},{4,7},{5,6},{6,5},{7,4},{8,11},{9,10},{10,... | collective-permute-start | bytes 202760 | tf_op jit(solution)/shard_map/ppermute | solution.py:277
  10.1 10.5 %collective-permute-start.6 = (bf16[1056,128]{1,0:T(8,128)(2,1)S(1)}, bf16[1056,128]{1,0:T(8,128)(2,1)S(1)}, u32[]{:S(2)}, u32[]{:S(2)}) collective-permute-start(bf16[1056,128]{1,0:T(8,128)(2,1)S(1)} %join.1.refs_4_.refs_5_), channel_id=1, source_target_pairs={{0,4},{1,5},{2,6},{3,7},{4,8},{5,9},{6,10},{7,11},{8,12},{9,13},{1... | collective-permute-start | bytes 811016 | tf_op jit(solution)/shard_map/ppermute | solution.py:280
  11.7 8.8 %collective-permute-start = (bf16[1048,128]{1,0:T(8,128)(2,1)S(1)}, bf16[1048,128]{1,0:T(8,128)(2,1)S(1)}, u32[]{:S(2)}, u32[]{:S(2)}) collective-permute-start(bf16[1048,128]{1,0:T(8,128)(2,1)S(1)} %get-tuple-element.29), channel_id=1, source_target_pairs={{0,1},{1,0},{2,3},{3,2},{4,5},{5,4},{6,7},{7,6},{8,9},{9,8},{10,11... | collective-permute-start | bytes 804872 | tf_op jit(solution)/shard_map/ppermute | solution.py:277
  11.7 9.3 %collective-permute-start.1 = (bf16[1048,128]{1,0:T(8,128)(2,1)S(1)}, bf16[1048,128]{1,0:T(8,128)(2,1)S(1)}, u32[]{:S(2)}, u32[]{:S(2)}) collective-permute-start(bf16[1048,128]{1,0:T(8,128)(2,1)S(1)} %get-tuple-element.30), channel_id=1, source_target_pairs={{0,2},{1,3},{2,0},{3,1},{4,6},{5,7},{6,4},{7,5},{8,10},{9,11},{10,... | collective-permute-start | bytes 804872 | tf_op jit(solution)/shard_map/ppermute | solution.py:277
  13.1 12.8 %collective-permute-start.2 = (bf16[1048,128]{1,0:T(8,128)(2,1)S(1)}, bf16[1048,128]{1,0:T(8,128)(2,1)S(1)}, u32[]{:S(2)}, u32[]{:S(2)}) collective-permute-start(bf16[1048,128]{1,0:T(8,128)(2,1)S(1)} %get-tuple-element.31), channel_id=1, source_target_pairs={{0,3},{1,2},{2,1},{3,0},{4,7},{5,6},{6,5},{7,4},{8,11},{9,10},{10,... | collective-permute-start | bytes 804872 | tf_op jit(solution)/shard_map/ppermute | solution.py:277
  20.5 14.6 %collective-permute-start.7 = (bf16[1056,128]{1,0:T(8,128)(2,1)S(1)}, bf16[1056,128]{1,0:T(8,128)(2,1)S(1)}, u32[]{:S(2)}, u32[]{:S(2)}) collective-permute-start(bf16[1056,128]{1,0:T(8,128)(2,1)S(1)} %collective-permute-done.6.refs_6_), channel_id=1, source_target_pairs={{0,4},{1,5},{2,6},{3,7},{4,8},{5,9},{6,10},{7,11},{8,12},{9,13},{1... | collective-permute-start | bytes 811016 | tf_op jit(solution)/shard_map/ppermute | solution.py:280
  30.3 16.5 %collective-permute-start.11 = (bf16[1024,128]{1,0:T(8,128)(2,1)S(1)}, bf16[1024,128]{1,0:T(8,128)(2,1)S(1)}, u32[]{:S(2)}, u32[]{:S(2)}) collective-permute-start(bf16[1024,128]{1,0:T(8,128)(2,1)S(1)} %get-tuple-element.44), channel_id=1, source_target_pairs={{0,12},{1,13},{2,14},{3,15},{4,0},{5,1},{6,2},{7,3},{8,4},{9,5},{1... | collective-permute-start | bytes 786440 | tf_op jit(solution)/shard_map/ppermute | solution.py:280
  36.1 18.5 %collective-permute-start.12 = (bf16[1024,128]{1,0:T(8,128)(2,1)S(1)}, bf16[1024,128]{1,0:T(8,128)(2,1)S(1)}, u32[]{:S(2)}, u32[]{:S(2)}) collective-permute-start(bf16[1024,128]{1,0:T(8,128)(2,1)S(1)} %get-tuple-element.45), channel_id=1, source_target_pairs={{0,8},{1,9},{2,10},{3,11},{4,12},{5,13},{6,14},{7,15},{8,0},{9,1},... | collective-permute-start | bytes 786440 | tf_op jit(solution)/shard_map/ppermute | solution.py:280
  37.4 1.9 %collective-permute-start.8 = (bf16[128,512]{1,0:T(8,128)(2,1)S(1)}, bf16[128,512]{1,0:T(8,128)(2,1)S(1)}, u32[]{:S(2)}, u32[]{:S(2)}) collective-permute-start(bf16[128,512]{1,0:T(8,128)(2,1)S(1)} %get-tuple-element.39), channel_id=1, source_target_pairs={{0,1},{1,0},{2,3},{3,2},{4,5},{5,4},{6,7},{7,6},{8,9},{9,8},{10,11... | collective-permute-start | bytes 393224 | tf_op jit(solution)/shard_map/ppermute | solution.py:277
  37.7 6.4 %collective-permute-start.9 = (bf16[128,512]{1,0:T(8,128)(2,1)S(1)}, bf16[128,512]{1,0:T(8,128)(2,1)S(1)}, u32[]{:S(2)}, u32[]{:S(2)}) collective-permute-start(bf16[128,512]{1,0:T(8,128)(2,1)S(1)} %get-tuple-element.40), channel_id=1, source_target_pairs={{0,2},{1,3},{2,0},{3,1},{4,6},{5,7},{6,4},{7,5},{8,10},{9,11},{10,... | collective-permute-start | bytes 393224 | tf_op jit(solution)/shard_map/ppermute | solution.py:277
  39.0 6.3 %collective-permute-start.10 = (bf16[128,512]{1,0:T(8,128)(2,1)S(1)}, bf16[128,512]{1,0:T(8,128)(2,1)S(1)}, u32[]{:S(2)}, u32[]{:S(2)}) collective-permute-start(bf16[128,512]{1,0:T(8,128)(2,1)S(1)} %get-tuple-element.41), channel_id=1, source_target_pairs={{0,3},{1,2},{2,1},{3,0},{4,7},{5,6},{6,5},{7,4},{8,11},{9,10},{10,... | collective-permute-start | bytes 393224 | tf_op jit(solution)/shard_map/ppermute | solution.py:277
  55.2 1.9 %collective-permute-start.13 = (bf16[256,128]{1,0:T(8,128)(2,1)S(1)}, bf16[256,128]{1,0:T(8,128)(2,1)S(1)}, u32[]{:S(2)}, u32[]{:S(2)}) collective-permute-start(bf16[256,128]{1,0:T(8,128)(2,1)S(1)} %get-tuple-element.48), channel_id=1, source_target_pairs={{0,1},{1,0},{2,3},{3,2},{4,5},{5,4},{6,7},{7,6},{8,9},{9,8},{10,11... | collective-permute-start | bytes 196616 | tf_op jit(solution)/shard_map/ppermute | solution.py:277
  55.3 4.6 %collective-permute-start.14 = (bf16[256,128]{1,0:T(8,128)(2,1)S(1)}, bf16[256,128]{1,0:T(8,128)(2,1)S(1)}, u32[]{:S(2)}, u32[]{:S(2)}) collective-permute-start(bf16[256,128]{1,0:T(8,128)(2,1)S(1)} %get-tuple-element.49), channel_id=1, source_target_pairs={{0,2},{1,3},{2,0},{3,1},{4,6},{5,7},{6,4},{7,5},{8,10},{9,11},{10,... | collective-permute-start | bytes 196616 | tf_op jit(solution)/shard_map/ppermute | solution.py:277
  56.6 4.4 %collective-permute-start.15 = (bf16[256,128]{1,0:T(8,128)(2,1)S(1)}, bf16[256,128]{1,0:T(8,128)(2,1)S(1)}, u32[]{:S(2)}, u32[]{:S(2)}) collective-permute-start(bf16[256,128]{1,0:T(8,128)(2,1)S(1)} %get-tuple-element.50), channel_id=1, source_target_pairs={{0,3},{1,2},{2,1},{3,0},{4,7},{5,6},{6,5},{7,4},{8,11},{9,10},{10,... | collective-permute-start | bytes 196616 | tf_op jit(solution)/shard_map/ppermute | solution.py:277
where the time goes:
time: 62.6 us; the launch traced here: 62.3 us
  waiting for transfers between devices  31.1 us (50%)
  starting transfers between devices  16.5 us (26%)
  Pallas kernels  13.9 us (22%)
  between operations  0.73 us (1%)
    ppermute x12, waiting for transfers between devices, across(): return lax.ppermute(value, 'tok', [(t, t ^ s) for t in range(count)])  16.3 us
    ppermute x4, waiting for transfers between devices, along(): lax.ppermute(value, 'tok', [(t, (t + steps * parts) % count) for t in ran...  14.8 us
    pallas_call x8, Pallas kernels, call(): pl.pallas_call(kernel, out_shape=outs, in_specs=[SMEM] + specs, out_specs...  13.9 us
    ppermute x12, starting transfers between devices, across(): return lax.ppermute(value, 'tok', [(t, t ^ s) for t in range(count)])  8.82 us
    ppermute x4, starting transfers between devices, along(): lax.ppermute(value, 'tok', [(t, (t + steps * parts) % count) for t in ran...  7.68 us
  transfers between devices with their start and end apart: 16, of which 9 were waited for; matrix products, arithmetic and copies ran while one was open for 0% of the time, Pallas kernels for 16%

commit v1 on v0

--- a/solution.py
+++ b/solution.py
@@ -31,7 +31,7 @@
 TOKEN = jax.ShapeDtypeStruct((8, 128), F32)
 
 
-def call(kernel, ins, outs, scratch=(), flops=0, name=None, specs=None, out_specs=None):
+def call(kernel, ins, outs, scratch=(), flops=0, specs=None, out_specs=None):
     specs = specs or [VMEM] * (len(ins) - 1)
     ins = [ins[0]] + [
         pltpu.with_memory_space_constraint(x, pltpu.MemorySpace.HBM) if spec is HBM else x
@@ -47,7 +47,6 @@
         scratch_shapes=list(scratch),
         cost_estimate=pl.CostEstimate(flops=flops, bytes_accessed=size, transcendentals=0),
         compiler_params=pltpu.CompilerParams(vmem_limit_bytes=48 << 20),
-        name=name,
     )(*ins)
 
 
@@ -139,19 +138,17 @@
     ]
 
 
-def attend(rows, offsets, reach, first, last, place, *refs):
+def attend(rows, offset, reach, first, last, place, *refs):
     parts = KEY_VALUE_HEADS
     queries, refs = refs[:parts], refs[parts:]
-    own, refs = refs[0], refs[1:]
-    keys, refs = refs[: len(offsets)], refs[len(offsets) :]
+    own, key_ref, refs = refs[0], refs[1], refs[2:]
     if not first:
         dq_in, refs = refs[0], refs[1:]
     if last:
         dq_out, refs = refs[:parts], refs[parts:]
     else:
         dq_out, refs = refs[0], refs[1:]
-    kv_out, refs = refs[: len(offsets)], refs[len(offsets) :]
-    dq, dkv, key_t, docs_t, docs_s = refs
+    kv_out, dq, dkv, key_t, docs_t, docs_s = refs
     row, me = place[0], place[1]
     width = GROUP * rows
     span = parts * rows
@@ -159,57 +156,55 @@
         docs = own[2 * span + a * EXTRA : 2 * span + a * EXTRA + 1, 0:rows].astype(F32)
         docs_s[a] = jnp.min(docs)
     dq[...] = jnp.zeros_like(dq)
-    for at, offset in enumerate(offsets):
-        dkv[...] = jnp.zeros_like(dkv)
-        key_ref = keys[at]
-        for b in range(parts):
-            cut = slice(b * rows, (b + 1) * rows)
-            key_t[:, cut] = key_ref[cut, :].T
-            docs = key_ref[2 * span + b * EXTRA : 2 * span + b * EXTRA + 1, 0:rows].astype(F32)
-            docs_t[cut, :] = jnp.broadcast_to(docs, (rows, rows)).T
-            if b == parts - 1:
-                docs_s[parts] = jnp.max(docs)
-        for s in range(parts):
-            a = me ^ s
-            near = offset * span + a * rows
-            live = (near - span + 1 < reach) & (row >= offset) & (docs_s[a] <= docs_s[parts])
-
-            @pl.when(live)
-            def _(s=s, a=a, near=near, key_ref=key_ref, offset=offset):
-                docs = own[pl.ds(pl.multiple_of(2 * span + a * EXTRA, EXTRA), EXTRA), :]
-                docs = docs.astype(F32)[0:1, 0:rows]
-                query = queries[s][0:width, :]
-                grad = queries[s][width : 2 * width, :]
-                stats = queries[s][2 * width :, :].astype(F32)
-                stats = stats[0:EXTRA] + stats[EXTRA : 2 * EXTRA] + stats[2 * EXTRA :]
-                gap = (
-                    near
-                    + lax.broadcasted_iota(jnp.int32, (span, rows), 1)
-                    - lax.broadcasted_iota(jnp.int32, (span, rows), 0)
-                )
-                mask = docs_t[...] == docs
-                if offset == 0:
-                    mask = mask & (gap >= 0)
-                if (offset + 1) * span > WINDOW:
-                    mask = mask & (gap < WINDOW)
-                scores = dot(key_ref[0:span, :], query, ((1,), (1,)))
-                dprob = dot(key_ref[span : 2 * span, :], grad, ((1,), (1,)))
-                probs, dscores = [], []
-                for h in range(GROUP):
-                    cut = slice(h * rows, (h + 1) * rows)
-                    norm = stats[h : h + 1, :] * LOG2E
-                    delta = stats[GROUP + h : GROUP + h + 1, :]
-                    prob = jnp.exp2(scores[:, cut] * (SCALE * LOG2E) - norm)
-                    prob = jnp.where(mask, prob, 0.0)
-                    probs.append(prob.astype(BF16))
-                    dscores.append((prob * (dprob[:, cut] - delta) * SCALE).astype(BF16))
-                prob = jnp.concatenate(probs, 1)
-                dscore = jnp.concatenate(dscores, 1)
-                dkv[0:span, :] += dot(dscore, query, ((1,), (0,)))
-                dkv[span:, :] += dot(prob, grad, ((1,), (0,)))
-                dq[s] += dot(key_t[...], dscore, ((1,), (0,)))
-
-        kv_out[at][...] = dkv[...].astype(kv_out[at].dtype)
+    dkv[...] = jnp.zeros_like(dkv)
+    for b in range(parts):
+        cut = slice(b * rows, (b + 1) * rows)
+        key_t[:, cut] = key_ref[cut, :].T
+        docs = key_ref[2 * span + b * EXTRA : 2 * span + b * EXTRA + 1, 0:rows].astype(F32)
+        docs_t[cut, :] = jnp.broadcast_to(docs, (rows, rows)).T
+        if b == parts - 1:
+            docs_s[parts] = jnp.max(docs)
+    for s in range(parts):
+        a = me ^ s
+        near = offset * span + a * rows
+        live = (near - span + 1 < reach) & (row >= offset) & (docs_s[a] <= docs_s[parts])
+
+        @pl.when(live)
+        def _(s=s, a=a, near=near):
+            docs = own[pl.ds(pl.multiple_of(2 * span + a * EXTRA, EXTRA), EXTRA), :]
+            docs = docs.astype(F32)[0:1, 0:rows]
+            query = queries[s][0:width, :]
+            grad = queries[s][width : 2 * width, :]
+            stats = queries[s][2 * width :, :].astype(F32)
+            stats = stats[0:EXTRA] + stats[EXTRA : 2 * EXTRA] + stats[2 * EXTRA :]
+            gap = (
+                near
+                + lax.broadcasted_iota(jnp.int32, (span, rows), 1)
+                - lax.broadcasted_iota(jnp.int32, (span, rows), 0)
+            )
+            mask = docs_t[...] == docs
+            if offset == 0:
+                mask = mask & (gap >= 0)
+            if (offset + 1) * span > WINDOW:
+                mask = mask & (gap < WINDOW)
+            scores = dot(key_ref[0:span, :], query, ((1,), (1,)))
+            dprob = dot(key_ref[span : 2 * span, :], grad, ((1,), (1,)))
+            probs, dscores = [], []
+            for h in range(GROUP):
+                cut = slice(h * rows, (h + 1) * rows)
+                norm = stats[h : h + 1, :] * LOG2E
+                delta = stats[GROUP + h : GROUP + h + 1, :]
+                prob = jnp.exp2(scores[:, cut] * (SCALE * LOG2E) - norm)
+                prob = jnp.where(mask, prob, 0.0)
+                probs.append(prob.astype(BF16))
+                dscores.append((prob * (dprob[:, cut] - delta) * SCALE).astype(BF16))
+            prob = jnp.concatenate(probs, 1)
+            dscore = jnp.concatenate(dscores, 1)
+            dkv[0:span, :] += dot(dscore, query, ((1,), (0,)))
+            dkv[span:, :] += dot(prob, grad, ((1,), (0,)))
+            dq[s] += dot(key_t[...], dscore, ((1,), (0,)))
+
+    kv_out[...] = dkv[...].astype(kv_out.dtype)
     for s in range(parts):
         total = dq[s] if first else dq[s] + dq_in[s]
         if last:
@@ -218,15 +213,17 @@
             dq_out[s] = total
 
 
-def add_terms(rows, count, place, *refs):
+def add_terms(place, arrived, term, out):
+    out[...] = (arrived[...].astype(F32) + term[...]).astype(BF16)
+
+
+def cut_terms(rows, count, place, *refs):
     parts = KEY_VALUE_HEADS
     terms, outs = refs[:count], refs[-parts:]
     for s, out in enumerate(outs):
         for k in range(2):
             at = pl.multiple_of((k * parts + (place[1] ^ s)) * rows, rows)
-            total = terms[0][pl.ds(at, rows), :]
-            for term in terms[1:]:
-                total = total + term[pl.ds(at, rows), :].astype(F32)
+            total = sum(term[pl.ds(at, rows), :].astype(F32) for term in terms)
             out[k * rows : (k + 1) * rows, :] = total.astype(BF16)
 
 
@@ -246,12 +243,17 @@
         copy.wait()
 
 
-def spread_keys(rows, place, *refs):
-    pieces, outs, sems = refs[:-3], refs[-3:-1], refs[-1]
+def spread_keys(rows, sources, place, *refs):
+    parts = KEY_VALUE_HEADS
+    pieces, (key_out, value_out, total, sems) = refs[:-5], refs[-4:]
     copies = []
-    for s, piece in enumerate(pieces):
-        for k, out in enumerate(outs):
-            source = piece.at[k * rows : (k + 1) * rows, :]
+    for s in range(parts):
+        term = pieces[s][...].astype(F32)
+        for k in range(1, sources):
+            term = term + pieces[k * parts + s][...].astype(F32)
+        total[s] = term.astype(BF16)
+        for k, out in enumerate((key_out, value_out)):
+            source = total.at[s, k * rows : (k + 1) * rows, :]
             target = out.at[:, head_columns(place[1] ^ s)]
             copies.append(pltpu.make_async_copy(source, target, sems.at[s, k]))
             copies[-1].start()
@@ -273,16 +275,12 @@
     width = GROUP * rows
     shape = jax.ShapeDtypeStruct
 
-    def across(value, s):
-        return lax.ppermute(value, "tok", [(t, t ^ s) for t in range(count)])
-
-    def along(value, steps):
-        return lax.ppermute(
-            value, "tok", [(t, (t + steps * parts) % count) for t in range(count)]
-        )
+    def move(value, steps, s=0):
+        pairs = [(t, ((t + steps * parts) % count) ^ s) for t in range(count)]
+        return lax.ppermute(value, "tok", pairs)
 
     def exchange(pieces):
-        return [pieces[0]] + [across(pieces[s], s) for s in range(1, parts)]
+        return [pieces[0]] + [move(pieces[s], 0, s) for s in range(1, parts)]
 
     pieces = call(
         functools.partial(pack_keys, rows),
@@ -294,7 +292,6 @@
             pltpu.SemaphoreType.DMA((parts, 2)),
         ],
         specs=[HBM, HBM, HBM],
-        name="pack_keys",
     )
     pieces = exchange(pieces)
     *query_pieces, token = call(
@@ -309,68 +306,80 @@
             pltpu.SemaphoreType.DMA((2,)),
         ],
         specs=[HBM, HBM, HBM, VMEM],
-        name="pack_queries",
     )
     (own,) = call(
         functools.partial(join, rows),
         (place, *pieces, token),
         [shape((parts * (2 * rows + EXTRA), HEAD_SIZE), BF16)],
-        name="join",
     )
     query_pieces = exchange(query_pieces)
     windows = [own]
     for _ in range(behind):
-        windows.append(along(windows[-1], 1))
+        windows.append(move(windows[-1], 1))
 
     kv_shape = (2 * span, HEAD_SIZE)
-    stages = [tuple(range(min(2, behind + 1)))] + [(d,) for d in range(2, behind + 1)]
-    dq, terms = None, []
-    for k, offsets in enumerate(stages):
+    stages = [0] + list(range(behind, 0, -1))
+    dq, own_term, sent = None, None, None
+    for k, offset in enumerate(stages):
         first, last = k == 0, k == len(stages) - 1
-        ins = [place, *query_pieces, own, *[windows[d] for d in offsets]]
+        ins = [place, *query_pieces, own, windows[offset]]
         if not first:
             ins.append(dq)
         if last:
             outs = [shape((HEAD_SIZE, width), BF16)] * parts
         else:
             outs = [shape((parts, HEAD_SIZE, width), F32)]
-        outs = outs + [shape(kv_shape, F32 if d == 0 else BF16) for d in offsets]
+        outs = outs + [shape(kv_shape, BF16 if offset == behind > 0 else F32)]
         got = call(
-            functools.partial(attend, rows, offsets, reach, first, last),
+            functools.partial(attend, rows, offset, reach, first, last),
             ins,
             outs,
             scratch=attend_scratch(rows),
-            flops=10 * len(offsets) * span * span * GROUP * HEAD_SIZE,
-            name="attend_" + "_".join(map(str, offsets)),
+            flops=10 * span * span * GROUP * HEAD_SIZE,
         )
-        dq = got[:parts] if last else got[0]
-        for d, term in zip(offsets, got[-len(offsets) :]):
-            terms.append(term if d == 0 else along(term, -d))
-
+        dq, term = (got[:parts] if last else got[0]), got[-1]
+        piece_shapes = [shape((2 * rows, HEAD_SIZE), BF16)] * parts
+        if offset == 0:
+            own_term = term
+        elif offset == 1:
+            terms = (term,) if sent is None else (sent, term)
+            got = call(
+                functools.partial(cut_terms, rows, len(terms)), (place, *terms), piece_shapes
+            )
+            sent = [move(piece, -1, s) for s, piece in enumerate(got)]
+        elif sent is None:
+            sent = move(term, -1)
+        else:
+            (term,) = call(add_terms, (place, sent, term), [shape(kv_shape, BF16)])
+            sent = move(term, -1)
+
+    dq_pieces = exchange(dq)
+    own_pieces = call(
+        functools.partial(cut_terms, rows, 1),
+        (place, own_term, *([] if sent is None else got[:1])),
+        piece_shapes,
+    )
+    own_pieces = exchange(own_pieces)
     query_grad, token = call(
         functools.partial(spread_queries, rows),
-        (place, *exchange(dq)),
+        (place, *dq_pieces),
         [shape((rows, parts * GROUP * HEAD_SIZE), BF16), TOKEN],
         scratch=[
             pltpu.VMEM((parts, rows, GROUP * HEAD_SIZE), BF16),
             pltpu.SemaphoreType.DMA((parts,)),
         ],
         out_specs=[HBM, VMEM],
-        name="spread_queries",
-    )
-    pieces = call(
-        functools.partial(add_terms, rows, len(terms)),
-        (place, *terms, token),
-        [shape((2 * rows, HEAD_SIZE), BF16)] * parts,
-        name="add_terms",
-    )
+    )
+    pieces = own_pieces + (sent or [])
     key_grad, value_grad = call(
-        functools.partial(spread_keys, rows),
-        (place, *exchange(pieces)),
+        functools.partial(spread_keys, rows, len(pieces) // parts),
+        (place, *pieces, token),
         [shape((rows, parts * HEAD_SIZE), BF16)] * 2,
-        scratch=[pltpu.SemaphoreType.DMA((parts, 2))],
+        scratch=[
+            pltpu.VMEM((parts, 2 * rows, HEAD_SIZE), BF16),
+            pltpu.SemaphoreType.DMA((parts, 2)),
+        ],
         out_specs=[HBM, HBM],
-        name="spread_keys",
     )
     return query_grad, key_grad, value_grad
 

time: 62.6 us -> 57.4 us (0.917)
  waiting for transfers between devices: 31.1 us -> 18.9 us
  starting transfers between devices: 16.5 us -> 22.3 us
  Pallas kernels: 13.9 us -> 15.1 us
    ppermute x16 -> x19, waiting for transfers between devices: 31.1 us -> 18.9 us  [move(): return lax.ppermute(value, 'tok', pairs)]
    ppermute x16 -> x19, starting transfers between devices: 16.5 us -> 22.3 us  [move(): return lax.ppermute(value, 'tok', pairs)]
    pallas_call x8 -> x10, Pallas kernels: 13.9 us -> 15.1 us  [call(): pl.pallas_call(kernel, out_shape=outs, in_specs=[SMEM] + specs, out_specs...]
  transfers between devices with their start and end apart: 16 -> 19, of which waited for: 9 -> 7; matrix products, arithmetic and copies ran while one was open for 0% -> 0% of each run, Pallas kernels for 16% -> 19%
where the time goes in v1:
time: 57.4 us; the launch traced here: 57.1 us
  starting transfers between devices  22.3 us (39%)
  waiting for transfers between devices  18.9 us (33%)
  Pallas kernels  15.1 us (26%)
  between operations  0.81 us (1%)
    ppermute x19, starting transfers between devices, move(): return lax.ppermute(value, 'tok', pairs)  22.3 us
    ppermute x19, waiting for transfers between devices, move(): return lax.ppermute(value, 'tok', pairs)  18.9 us
    pallas_call x10, Pallas kernels, call(): pl.pallas_call(kernel, out_shape=outs, in_specs=[SMEM] + specs, out_specs...  15.1 us
  transfers between devices with their start and end apart: 19, of which 7 were waited for; matrix products, arithmetic and copies ran while one was open for 0% of the time, Pallas kernels for 19%

profile of v1, /device:TPU:0, one launch (start us, length us, event | category | flops | bytes accessed | tf_op | source)
XLA Modules:
  0.0 57.1 jit_solution(1636835802793825491)
XLA Ops:
  0.7 1.5 %shard_map.95 = (bf16[264,128]{1,0:T(8,128)(2,1)S(1)}, bf16[264,128]{1,0:T(8,128)(2,1)S(1)}, bf16[264,128]{1,0:T(8,128)(2,1)S(1)}, bf16[264,128]{1,0:T(8,128)(2,1)S(1)}) custom-call(s32[2]{0:T(128)S(1)} %pad_add_fusion.place, bf16[128,512]{1,0:T(8,128)(2,1)} %key_ref.1, bf16[128,512]{1,0:T(8,128)(2,1)} %value_ref.1, s32[1,128]{1,0:T(1,128)} %bitcast.3), custom_call_target="tpu_custom_call" | custom-call | bytes 533000 | tf_op jit(solution)/shard_map/pallas_call | solution.py:42
  2.2 0.6 collective-permute-start.3
  2.8 2.6 %collective-permute-start.4 = (bf16[264,128]{1,0:T(8,128)(2,1)S(1)}, bf16[264,128]{1,0:T(8,128)(2,1)S(1)}, u32[]{:S(2)}, u32[]{:S(2)}) collective-permute-start(bf16[264,128]{1,0:T(8,128)(2,1)S(1)} %get-tuple-element.39), channel_id=1, source_target_pairs={{0,2},{1,3},{2,0},{3,1},{4,6},{5,7},{6,4},{7,5},{8,10},{9,11},{10,... | collective-permute-start | bytes 202760 | tf_op jit(solution)/shard_map/ppermute | solution.py:280
  5.4 3.0 %shard_map.94 = (bf16[1048,128]{1,0:T(8,128)(2,1)S(1)}, bf16[1048,128]{1,0:T(8,128)(2,1)S(1)}, bf16[1048,128]{1,0:T(8,128)(2,1)S(1)}, bf16[1048,128]{1,0:T(8,128)(2,1)S(1)}, f32[8,128]{1,0:T(8,128)S(1)}) custom-call(s32[2]{0:T(128)S(1)} %pad_add_fusion.place, bf16[128,2048]{1,0:T(8,128)(2,1)} %query_ref.1, bf16[128,2048]{1,0:T(8,128)(2,1)} %grad_ref.1, ...), custom_call_target="tpu_custom_call" | custom-call | bytes 2658312 | tf_op jit(solution)/shard_map/pallas_call | solution.py:42
  8.4 1.1 %collective-permute-done.5.refs_3_ = bf16[264,128]{1,0:T(8,128)(2,1)S(1)} collective-permute-done((bf16[264,128]{1,0:T(8,128)(2,1)S(1)}, bf16[264,128]{1,0:T(8,128)(2,1)S(1)}, u32[]{:S(2)}, u32[]{:S(2)}) %collective-permute-start.5) | collective-permute-done | bytes 67616 | tf_op jit(solution)/shard_map/ppermute | solution.py:280
  9.5 0.6 shard_map.96.refs_4_.refs_5_
  10.1 1.6 %collective-permute-start.6 = (bf16[1056,128]{1,0:T(8,128)(2,1)S(1)}, bf16[1056,128]{1,0:T(8,128)(2,1)S(1)}, u32[]{:S(2)}, u32[]{:S(2)}) collective-permute-start(bf16[1056,128]{1,0:T(8,128)(2,1)S(1)} %shard_map.96.refs_4_.refs_5_), channel_id=1, source_target_pairs={{0,4},{1,5},{2,6},{3,7},{4,8},{5,9},{6,10},{7,11},{8,12},{9,13},{1... | collective-permute-start | bytes 811016 | tf_op jit(solution)/shard_map/ppermute | solution.py:280
  11.7 1.4 %collective-permute-start.1 = (bf16[1048,128]{1,0:T(8,128)(2,1)S(1)}, bf16[1048,128]{1,0:T(8,128)(2,1)S(1)}, u32[]{:S(2)}, u32[]{:S(2)}) collective-permute-start(bf16[1048,128]{1,0:T(8,128)(2,1)S(1)} %get-tuple-element.35), channel_id=1, source_target_pairs={{0,2},{1,3},{2,0},{3,1},{4,6},{5,7},{6,4},{7,5},{8,10},{9,11},{10,... | collective-permute-start | bytes 804872 | tf_op jit(solution)/shard_map/ppermute | solution.py:280
  13.1 0.5 collective-permute-start.2
  13.6 7.0 %collective-permute-done.6.refs_5_ = bf16[1056,128]{1,0:T(8,128)(2,1)S(1)} collective-permute-done((bf16[1056,128]{1,0:T(8,128)(2,1)S(1)}, bf16[1056,128]{1,0:T(8,128)(2,1)S(1)}, u32[]{:S(2)}, u32[]{:S(2)}) %collective-permute-start.6) | collective-permute-done | bytes 270368 | tf_op jit(solution)/shard_map/ppermute | solution.py:280
  20.5 0.5 collective-permute-done.1.refs_2_
  21.0 4.8 %collective-permute-done.2.refs_3_ = bf16[1048,128]{1,0:T(8,128)(2,1)S(1)} collective-permute-done((bf16[1048,128]{1,0:T(8,128)(2,1)S(1)}, bf16[1048,128]{1,0:T(8,128)(2,1)S(1)}, u32[]{:S(2)}, u32[]{:S(2)}) %collective-permute-start.2) | collective-permute-done | bytes 268320 | tf_op jit(solution)/shard_map/ppermute | solution.py:280
  25.8 4.3 %shard_map.97 = (f32[4,128,512]{2,1,0:T(8,128)S(1)}, f32[1024,128]{1,0:T(8,128)S(1)}) custom-call(s32[2]{0:T(128)S(1)} %pad_add_fusion.place, bf16[1048,128]{1,0:T(8,128)(2,1)S(1)} %get-tuple-element.33.refs_0_, bf16[1048,128]{1,0:T(8,128)(2,1)S(1)} %collective-permute-done.refs_1_, bf16[1048,128]{1,0:T(8,128)(2,1)S(1)} %collective-permute-done.1.refs_2_, ...), custom_call_target="tpu_custom_call" | custom-call | flops 1342177280 | bytes 3186696 | tf_op jit(solution)/shard_map/pallas_call | solution.py:42
  30.1 1.0 %shard_map.98 = (f32[4,128,512]{2,1,0:T(8,128)S(1)}, bf16[1024,128]{1,0:T(8,128)(2,1)S(1)}) custom-call(s32[2]{0:T(128)S(1)} %pad_add_fusion.place, bf16[1048,128]{1,0:T(8,128)(2,1)S(1)} %get-tuple-element.33.refs_0_, bf16[1048,128]{1,0:T(8,128)(2,1)S(1)} %collective-permute-done.refs_1_, bf16[1048,128]{1,0:T(8,128)(2,1)S(1)} %collective-permute-done.1.refs_2_, ...), custom_call_target="tpu_custom_call" | custom-call | flops 1342177280 | bytes 3973128 | tf_op jit(solution)/shard_map/pallas_call | solution.py:42
  31.1 3.1 %collective-permute-start.11 = (bf16[1024,128]{1,0:T(8,128)(2,1)S(1)}, bf16[1024,128]{1,0:T(8,128)(2,1)S(1)}, u32[]{:S(2)}, u32[]{:S(2)}) collective-permute-start(bf16[1024,128]{1,0:T(8,128)(2,1)S(1)} %get-tuple-element.50), channel_id=1, source_target_pairs={{0,12},{1,13},{2,14},{3,15},{4,0},{5,1},{6,2},{7,3},{8,4},{9,5},{1... | collective-permute-start | bytes 786440 | tf_op jit(solution)/shard_map/ppermute | solution.py:280
  34.2 0.9 %shard_map.99 = (bf16[128,512]{1,0:T(8,128)(2,1)S(1)}, bf16[128,512]{1,0:T(8,128)(2,1)S(1)}, bf16[128,512]{1,0:T(8,128)(2,1)S(1)}, bf16[128,512]{1,0:T(8,128)(2,1)S(1)}, f32[1024,128]{1,0:T(8,128)S(1)}) custom-call(s32[2]{0:T(128)S(1)} %pad_add_fusion.place, bf16[1048,128]{1,0:T(8,128)(2,1)S(1)} %get-tuple-element.33.refs_0_, ...), custom_call_target="tpu_custom_call" | custom-call | flops 1342177280 | bytes 3710984 | tf_op jit(solution)/shard_map/pallas_call | solution.py:42
  35.2 0.3 collective-permute-start.8
  35.5 1.3 %collective-permute-start.9 = (bf16[128,512]{1,0:T(8,128)(2,1)S(1)}, bf16[128,512]{1,0:T(8,128)(2,1)S(1)}, u32[]{:S(2)}, u32[]{:S(2)}) collective-permute-start(bf16[128,512]{1,0:T(8,128)(2,1)S(1)} %get-tuple-element.46), channel_id=1, source_target_pairs={{0,2},{1,3},{2,0},{3,1},{4,6},{5,7},{6,4},{7,5},{8,10},{9,11},{10,... | collective-permute-start | bytes 393224 | tf_op jit(solution)/shard_map/ppermute | solution.py:280
  36.8 0.3 collective-permute-start.10
  37.1 3.4 %collective-permute-done.11.refs_0_ = bf16[1024,128]{1,0:T(8,128)(2,1)S(1)} collective-permute-done((bf16[1024,128]{1,0:T(8,128)(2,1)S(1)}, bf16[1024,128]{1,0:T(8,128)(2,1)S(1)}, u32[]{:S(2)}, u32[]{:S(2)}) %collective-permute-start.11) | collective-permute-done | bytes 262176 | tf_op jit(solution)/shard_map/ppermute | solution.py:280
  40.5 0.6 %shard_map.101 = (bf16[256,128]{1,0:T(8,128)(2,1)S(1)}, bf16[256,128]{1,0:T(8,128)(2,1)S(1)}, bf16[256,128]{1,0:T(8,128)(2,1)S(1)}, bf16[256,128]{1,0:T(8,128)(2,1)S(1)}) custom-call(s32[2]{0:T(128)S(1)} %pad_add_fusion.place, bf16[1024,128]{1,0:T(8,128)(2,1)S(1)} %collective-permute-done.11.refs_0_, f32[1024,128]{1,0:T(8,128)S(1)} %get-tuple-element.51.refs_1_), custom_call_target="tpu_custom_call" | custom-call | bytes 1048584 | tf_op jit(solution)/shard_map/pallas_call | solution.py:42
  41.1 3.6 %collective-permute-start.16 = (bf16[256,128]{1,0:T(8,128)(2,1)S(1)}, bf16[256,128]{1,0:T(8,128)(2,1)S(1)}, u32[]{:S(2)}, u32[]{:S(2)}) collective-permute-start(bf16[256,128]{1,0:T(8,128)(2,1)S(1)} %get-tuple-element.57), channel_id=1, source_target_pairs={{0,13},{1,12},{2,15},{3,14},{4,1},{5,0},{6,3},{7,2},{8,5},{9,4},{1... | collective-permute-start | bytes 196616 | tf_op jit(solution)/shard_map/ppermute | solution.py:280
  44.8 1.5 %collective-permute-start.17 = (bf16[256,128]{1,0:T(8,128)(2,1)S(1)}, bf16[256,128]{1,0:T(8,128)(2,1)S(1)}, u32[]{:S(2)}, u32[]{:S(2)}) collective-permute-start(bf16[256,128]{1,0:T(8,128)(2,1)S(1)} %get-tuple-element.58), channel_id=1, source_target_pairs={{0,14},{1,15},{2,12},{3,13},{4,2},{5,3},{6,0},{7,1},{8,6},{9,7},{1... | collective-permute-start | bytes 196616 | tf_op jit(solution)/shard_map/ppermute | solution.py:280
  46.3 0.6 shard_map.102
  46.9 0.1 collective-permute-start.12
  47.0 0.8 %collective-permute-start.13 = (bf16[256,128]{1,0:T(8,128)(2,1)S(1)}, bf16[256,128]{1,0:T(8,128)(2,1)S(1)}, u32[]{:S(2)}, u32[]{:S(2)}) collective-permute-start(bf16[256,128]{1,0:T(8,128)(2,1)S(1)} %get-tuple-element.55), channel_id=1, source_target_pairs={{0,2},{1,3},{2,0},{3,1},{4,6},{5,7},{6,4},{7,5},{8,10},{9,11},{10,... | collective-permute-start | bytes 196616 | tf_op jit(solution)/shard_map/ppermute | solution.py:280
  47.8 1.1 %collective-permute-start.14 = (bf16[256,128]{1,0:T(8,128)(2,1)S(1)}, bf16[256,128]{1,0:T(8,128)(2,1)S(1)}, u32[]{:S(2)}, u32[]{:S(2)}) collective-permute-start(bf16[256,128]{1,0:T(8,128)(2,1)S(1)} %get-tuple-element.56), channel_id=1, source_target_pairs={{0,3},{1,2},{2,1},{3,0},{4,7},{5,6},{6,5},{7,4},{8,11},{9,10},{10,... | collective-permute-start | bytes 196616 | tf_op jit(solution)/shard_map/ppermute | solution.py:280
  48.9 1.6 %collective-permute-done.17.refs_6_ = bf16[256,128]{1,0:T(8,128)(2,1)S(1)} collective-permute-done((bf16[256,128]{1,0:T(8,128)(2,1)S(1)}, bf16[256,128]{1,0:T(8,128)(2,1)S(1)}, u32[]{:S(2)}, u32[]{:S(2)}) %collective-permute-start.17) | collective-permute-done | bytes 65568 | tf_op jit(solution)/shard_map/ppermute | solution.py:280
  50.5 3.4 %collective-permute-start.15 = (bf16[256,128]{1,0:T(8,128)(2,1)S(1)}, bf16[256,128]{1,0:T(8,128)(2,1)S(1)}, u32[]{:S(2)}, u32[]{:S(2)}) collective-permute-start(bf16[256,128]{1,0:T(8,128)(2,1)S(1)} %get-tuple-element.52.refs_1_), channel_id=1, source_target_pairs={{0,12},{1,13},{2,14},{3,15},{4,0},{5,1},{6,2},{7,3},{8,4},{9,5},{1... | collective-permute-start | bytes 196616 | tf_op jit(solution)/shard_map/ppermute | solution.py:280
  53.9 1.4 %shard_map.100 = (bf16[128,2048]{1,0:T(8,128)(2,1)}, f32[8,128]{1,0:T(8,128)S(1)}) custom-call(s32[2]{0:T(128)S(1)} %pad_add_fusion.place, bf16[128,512]{1,0:T(8,128)(2,1)S(1)} %get-tuple-element.44.refs_0_, bf16[128,512]{1,0:T(8,128)(2,1)S(1)} %collective-permute-done.8.refs_1_, bf16[128,512]{1,0:T(8,128)(2,1)S(1)} %collective-permute-done.9.refs_2_, ...), custom_call_target="tpu_custom_call" | custom-call | bytes 1052680 | tf_op jit(solution)/shard_map/pallas_call | solution.py:42
  55.4 0.4 collective-permute-done.15.refs_4_
  55.8 1.3 %shard_map.103 = (bf16[128,512]{1,0:T(8,128)(2,1)}, bf16[128,512]{1,0:T(8,128)(2,1)}) custom-call(s32[2]{0:T(128)S(1)} %pad_add_fusion.place, bf16[256,128]{1,0:T(8,128)(2,1)S(1)} %get-tuple-element.53.refs_0_, bf16[256,128]{1,0:T(8,128)(2,1)S(1)} %collective-permute-done.12.refs_1_, bf16[256,128]{1,0:T(8,128)(2,1)S(1)} %collective-permute-done.13.refs_2_, ...), custom_call_target="tpu_custom_call" | custom-call | bytes 790536 | tf_op jit(solution)/shard_map/pallas_call | solution.py:42
  (19 shorter events, 0.2 us)
Async XLA Ops:
  0.7 4.7 %copy-start = (f32[16,128]{1,0:T(8,128)S(1)}, f32[16,128]{1,0:T(8,128)}, u32[]{:S(2)}) copy-start(f32[16,128]{1,0:T(8,128)} %norm_ref.1) | copy-start | bytes 24580
  2.2 6.2 %collective-permute-start.3 = (bf16[264,128]{1,0:T(8,128)(2,1)S(1)}, bf16[264,128]{1,0:T(8,128)(2,1)S(1)}, u32[]{:S(2)}, u32[]{:S(2)}) collective-permute-start(bf16[264,128]{1,0:T(8,128)(2,1)S(1)} %get-tuple-element.38), channel_id=1, source_target_pairs={{0,1},{1,0},{2,3},{3,2},{4,5},{5,4},{6,7},{7,6},{8,9},{9,8},{10,11... | collective-permute-start | bytes 202760 | tf_op jit(solution)/shard_map/ppermute | solution.py:280
  2.8 5.6 %collective-permute-start.4 = (bf16[264,128]{1,0:T(8,128)(2,1)S(1)}, bf16[264,128]{1,0:T(8,128)(2,1)S(1)}, u32[]{:S(2)}, u32[]{:S(2)}) collective-permute-start(bf16[264,128]{1,0:T(8,128)(2,1)S(1)} %get-tuple-element.39), channel_id=1, source_target_pairs={{0,2},{1,3},{2,0},{3,1},{4,6},{5,7},{6,4},{7,5},{8,10},{9,11},{10,... | collective-permute-start | bytes 202760 | tf_op jit(solution)/shard_map/ppermute | solution.py:280
  5.4 4.1 %collective-permute-start.5 = (bf16[264,128]{1,0:T(8,128)(2,1)S(1)}, bf16[264,128]{1,0:T(8,128)(2,1)S(1)}, u32[]{:S(2)}, u32[]{:S(2)}) collective-permute-start(bf16[264,128]{1,0:T(8,128)(2,1)S(1)} %get-tuple-element.40), channel_id=1, source_target_pairs={{0,3},{1,2},{2,1},{3,0},{4,7},{5,6},{6,5},{7,4},{8,11},{9,10},{10,... | collective-permute-start | bytes 202760 | tf_op jit(solution)/shard_map/ppermute | solution.py:280
  10.1 10.5 %collective-permute-start.6 = (bf16[1056,128]{1,0:T(8,128)(2,1)S(1)}, bf16[1056,128]{1,0:T(8,128)(2,1)S(1)}, u32[]{:S(2)}, u32[]{:S(2)}) collective-permute-start(bf16[1056,128]{1,0:T(8,128)(2,1)S(1)} %shard_map.96.refs_4_.refs_5_), channel_id=1, source_target_pairs={{0,4},{1,5},{2,6},{3,7},{4,8},{5,9},{6,10},{7,11},{8,12},{9,13},{1... | collective-permute-start | bytes 811016 | tf_op jit(solution)/shard_map/ppermute | solution.py:280
  11.7 8.8 %collective-permute-start = (bf16[1048,128]{1,0:T(8,128)(2,1)S(1)}, bf16[1048,128]{1,0:T(8,128)(2,1)S(1)}, u32[]{:S(2)}, u32[]{:S(2)}) collective-permute-start(bf16[1048,128]{1,0:T(8,128)(2,1)S(1)} %get-tuple-element.34), channel_id=1, source_target_pairs={{0,1},{1,0},{2,3},{3,2},{4,5},{5,4},{6,7},{7,6},{8,9},{9,8},{10,11... | collective-permute-start | bytes 804872 | tf_op jit(solution)/shard_map/ppermute | solution.py:280
  11.7 9.3 %collective-permute-start.1 = (bf16[1048,128]{1,0:T(8,128)(2,1)S(1)}, bf16[1048,128]{1,0:T(8,128)(2,1)S(1)}, u32[]{:S(2)}, u32[]{:S(2)}) collective-permute-start(bf16[1048,128]{1,0:T(8,128)(2,1)S(1)} %get-tuple-element.35), channel_id=1, source_target_pairs={{0,2},{1,3},{2,0},{3,1},{4,6},{5,7},{6,4},{7,5},{8,10},{9,11},{10,... | collective-permute-start | bytes 804872 | tf_op jit(solution)/shard_map/ppermute | solution.py:280
  13.1 12.8 %collective-permute-start.2 = (bf16[1048,128]{1,0:T(8,128)(2,1)S(1)}, bf16[1048,128]{1,0:T(8,128)(2,1)S(1)}, u32[]{:S(2)}, u32[]{:S(2)}) collective-permute-start(bf16[1048,128]{1,0:T(8,128)(2,1)S(1)} %get-tuple-element.36), channel_id=1, source_target_pairs={{0,3},{1,2},{2,1},{3,0},{4,7},{5,6},{6,5},{7,4},{8,11},{9,10},{10,... | collective-permute-start | bytes 804872 | tf_op jit(solution)/shard_map/ppermute | solution.py:280
  20.5 9.6 %collective-permute-start.7 = (bf16[1056,128]{1,0:T(8,128)(2,1)S(1)}, bf16[1056,128]{1,0:T(8,128)(2,1)S(1)}, u32[]{:S(2)}, u32[]{:S(2)}) collective-permute-start(bf16[1056,128]{1,0:T(8,128)(2,1)S(1)} %collective-permute-done.6.refs_5_), channel_id=1, source_target_pairs={{0,4},{1,5},{2,6},{3,7},{4,8},{5,9},{6,10},{7,11},{8,12},{9,13},{1... | collective-permute-start | bytes 811016 | tf_op jit(solution)/shard_map/ppermute | solution.py:280
  31.1 9.4 %collective-permute-start.11 = (bf16[1024,128]{1,0:T(8,128)(2,1)S(1)}, bf16[1024,128]{1,0:T(8,128)(2,1)S(1)}, u32[]{:S(2)}, u32[]{:S(2)}) collective-permute-start(bf16[1024,128]{1,0:T(8,128)(2,1)S(1)} %get-tuple-element.50), channel_id=1, source_target_pairs={{0,12},{1,13},{2,14},{3,15},{4,0},{5,1},{6,2},{7,3},{8,4},{9,5},{1... | collective-permute-start | bytes 786440 | tf_op jit(solution)/shard_map/ppermute | solution.py:280
  35.2 11.7 %collective-permute-start.8 = (bf16[128,512]{1,0:T(8,128)(2,1)S(1)}, bf16[128,512]{1,0:T(8,128)(2,1)S(1)}, u32[]{:S(2)}, u32[]{:S(2)}) collective-permute-start(bf16[128,512]{1,0:T(8,128)(2,1)S(1)} %get-tuple-element.45), channel_id=1, source_target_pairs={{0,1},{1,0},{2,3},{3,2},{4,5},{5,4},{6,7},{7,6},{8,9},{9,8},{10,11... | collective-permute-start | bytes 393224 | tf_op jit(solution)/shard_map/ppermute | solution.py:280
  35.5 11.4 %collective-permute-start.9 = (bf16[128,512]{1,0:T(8,128)(2,1)S(1)}, bf16[128,512]{1,0:T(8,128)(2,1)S(1)}, u32[]{:S(2)}, u32[]{:S(2)}) collective-permute-start(bf16[128,512]{1,0:T(8,128)(2,1)S(1)} %get-tuple-element.46), channel_id=1, source_target_pairs={{0,2},{1,3},{2,0},{3,1},{4,6},{5,7},{6,4},{7,5},{8,10},{9,11},{10,... | collective-permute-start | bytes 393224 | tf_op jit(solution)/shard_map/ppermute | solution.py:280
  36.8 10.2 %collective-permute-start.10 = (bf16[128,512]{1,0:T(8,128)(2,1)S(1)}, bf16[128,512]{1,0:T(8,128)(2,1)S(1)}, u32[]{:S(2)}, u32[]{:S(2)}) collective-permute-start(bf16[128,512]{1,0:T(8,128)(2,1)S(1)} %get-tuple-element.47), channel_id=1, source_target_pairs={{0,3},{1,2},{2,1},{3,0},{4,7},{5,6},{6,5},{7,4},{8,11},{9,10},{10,... | collective-permute-start | bytes 393224 | tf_op jit(solution)/shard_map/ppermute | solution.py:280
  41.1 6.7 %collective-permute-start.16 = (bf16[256,128]{1,0:T(8,128)(2,1)S(1)}, bf16[256,128]{1,0:T(8,128)(2,1)S(1)}, u32[]{:S(2)}, u32[]{:S(2)}) collective-permute-start(bf16[256,128]{1,0:T(8,128)(2,1)S(1)} %get-tuple-element.57), channel_id=1, source_target_pairs={{0,13},{1,12},{2,15},{3,14},{4,1},{5,0},{6,3},{7,2},{8,5},{9,4},{1... | collective-permute-start | bytes 196616 | tf_op jit(solution)/shard_map/ppermute | solution.py:280
  44.8 5.7 %collective-permute-start.17 = (bf16[256,128]{1,0:T(8,128)(2,1)S(1)}, bf16[256,128]{1,0:T(8,128)(2,1)S(1)}, u32[]{:S(2)}, u32[]{:S(2)}) collective-permute-start(bf16[256,128]{1,0:T(8,128)(2,1)S(1)} %get-tuple-element.58), channel_id=1, source_target_pairs={{0,14},{1,15},{2,12},{3,13},{4,2},{5,3},{6,0},{7,1},{8,6},{9,7},{1... | collective-permute-start | bytes 196616 | tf_op jit(solution)/shard_map/ppermute | solution.py:280
  46.8 8.5 %collective-permute-start.18 = (bf16[256,128]{1,0:T(8,128)(2,1)S(1)}, bf16[256,128]{1,0:T(8,128)(2,1)S(1)}, u32[]{:S(2)}, u32[]{:S(2)}) collective-permute-start(bf16[256,128]{1,0:T(8,128)(2,1)S(1)} %get-tuple-element.59), channel_id=1, source_target_pairs={{0,15},{1,14},{2,13},{3,12},{4,3},{5,2},{6,1},{7,0},{8,7},{9,6},{1... | collective-permute-start | bytes 196616 | tf_op jit(solution)/shard_map/ppermute | solution.py:280
  46.9 8.5 %collective-permute-start.12 = (bf16[256,128]{1,0:T(8,128)(2,1)S(1)}, bf16[256,128]{1,0:T(8,128)(2,1)S(1)}, u32[]{:S(2)}, u32[]{:S(2)}) collective-permute-start(bf16[256,128]{1,0:T(8,128)(2,1)S(1)} %get-tuple-element.54), channel_id=1, source_target_pairs={{0,1},{1,0},{2,3},{3,2},{4,5},{5,4},{6,7},{7,6},{8,9},{9,8},{10,11... | collective-permute-start | bytes 196616 | tf_op jit(solution)/shard_map/ppermute | solution.py:280
  47.0 8.3 %collective-permute-start.13 = (bf16[256,128]{1,0:T(8,128)(2,1)S(1)}, bf16[256,128]{1,0:T(8,128)(2,1)S(1)}, u32[]{:S(2)}, u32[]{:S(2)}) collective-permute-start(bf16[256,128]{1,0:T(8,128)(2,1)S(1)} %get-tuple-element.55), channel_id=1, source_target_pairs={{0,2},{1,3},{2,0},{3,1},{4,6},{5,7},{6,4},{7,5},{8,10},{9,11},{10,... | collective-permute-start | bytes 196616 | tf_op jit(solution)/shard_map/ppermute | solution.py:280
  47.8 7.6 %collective-permute-start.14 = (bf16[256,128]{1,0:T(8,128)(2,1)S(1)}, bf16[256,128]{1,0:T(8,128)(2,1)S(1)}, u32[]{:S(2)}, u32[]{:S(2)}) collective-permute-start(bf16[256,128]{1,0:T(8,128)(2,1)S(1)} %get-tuple-element.56), channel_id=1, source_target_pairs={{0,3},{1,2},{2,1},{3,0},{4,7},{5,6},{6,5},{7,4},{8,11},{9,10},{10,... | collective-permute-start | bytes 196616 | tf_op jit(solution)/shard_map/ppermute | solution.py:280
  50.5 5.3 %collective-permute-start.15 = (bf16[256,128]{1,0:T(8,128)(2,1)S(1)}, bf16[256,128]{1,0:T(8,128)(2,1)S(1)}, u32[]{:S(2)}, u32[]{:S(2)}) collective-permute-start(bf16[256,128]{1,0:T(8,128)(2,1)S(1)} %get-tuple-element.52.refs_1_), channel_id=1, source_target_pairs={{0,12},{1,13},{2,14},{3,15},{4,0},{5,1},{6,2},{7,3},{8,4},{9,5},{1... | collective-permute-start | bytes 196616 | tf_op jit(solution)/shard_map/ppermute | solution.py:280

commit v2 on v1

--- a/solution.py
+++ b/solution.py
@@ -162,15 +162,18 @@
         key_t[:, cut] = key_ref[cut, :].T
         docs = key_ref[2 * span + b * EXTRA : 2 * span + b * EXTRA + 1, 0:rows].astype(F32)
         docs_t[cut, :] = jnp.broadcast_to(docs, (rows, rows)).T
-        if b == parts - 1:
-            docs_s[parts] = jnp.max(docs)
+        if (b + 1) % (parts // 2) == 0:
+            docs_s[parts + b // (parts // 2)] = jnp.max(docs)
+    half = span // 2
     for s in range(parts):
         a = me ^ s
         near = offset * span + a * rows
-        live = (near - span + 1 < reach) & (row >= offset) & (docs_s[a] <= docs_s[parts])
-
-        @pl.when(live)
-        def _(s=s, a=a, near=near):
+        low = (near - half + 1 < reach) & (row >= offset) & (docs_s[a] <= docs_s[parts])
+        high = (near - span + 1 < reach) & (row >= offset) & (docs_s[a] <= docs_s[parts + 1])
+        if offset == 0:
+            high = high & (a * rows + rows > half)
+
+        def block(start, stop, s=s, a=a, near=near):
             docs = own[pl.ds(pl.multiple_of(2 * span + a * EXTRA, EXTRA), EXTRA), :]
             docs = docs.astype(F32)[0:1, 0:rows]
             query = queries[s][0:width, :]
@@ -179,16 +182,17 @@
             stats = stats[0:EXTRA] + stats[EXTRA : 2 * EXTRA] + stats[2 * EXTRA :]
             gap = (
                 near
-                + lax.broadcasted_iota(jnp.int32, (span, rows), 1)
-                - lax.broadcasted_iota(jnp.int32, (span, rows), 0)
+                - start
+                + lax.broadcasted_iota(jnp.int32, (stop - start, rows), 1)
+                - lax.broadcasted_iota(jnp.int32, (stop - start, rows), 0)
             )
-            mask = docs_t[...] == docs
+            mask = docs_t[start:stop, :] == docs
             if offset == 0:
                 mask = mask & (gap >= 0)
             if (offset + 1) * span > WINDOW:
                 mask = mask & (gap < WINDOW)
-            scores = dot(key_ref[0:span, :], query, ((1,), (1,)))
-            dprob = dot(key_ref[span : 2 * span, :], grad, ((1,), (1,)))
+            scores = dot(key_ref[start:stop, :], query, ((1,), (1,)))
+            dprob = dot(key_ref[span + start : span + stop, :], grad, ((1,), (1,)))
             probs, dscores = [], []
             for h in range(GROUP):
                 cut = slice(h * rows, (h + 1) * rows)
@@ -200,9 +204,14 @@
                 dscores.append((prob * (dprob[:, cut] - delta) * SCALE).astype(BF16))
             prob = jnp.concatenate(probs, 1)
             dscore = jnp.concatenate(dscores, 1)
-            dkv[0:span, :] += dot(dscore, query, ((1,), (0,)))
-            dkv[span:, :] += dot(prob, grad, ((1,), (0,)))
-            dq[s] += dot(key_t[...], dscore, ((1,), (0,)))
+            dkv[start:stop, :] += dot(dscore, query, ((1,), (0,)))
+            dkv[span + start : span + stop, :] += dot(prob, grad, ((1,), (0,)))
+            dq[s] += dot(key_t[:, start:stop], dscore, ((1,), (0,)))
+
+        pl.when(low & high)(functools.partial(block, 0, span))
+        pl.when(high & ~low)(functools.partial(block, half, span))
+        if offset == 0:
+            pl.when(low & ~high)(functools.partial(block, 0, half))
 
     kv_out[...] = dkv[...].astype(kv_out.dtype)
     for s in range(parts):
@@ -275,9 +284,14 @@
     width = GROUP * rows
     shape = jax.ShapeDtypeStruct
 
-    def move(value, steps, s=0):
-        pairs = [(t, ((t + steps * parts) % count) ^ s) for t in range(count)]
-        return lax.ppermute(value, "tok", pairs)
+    def move(value, steps, s=0, low=0):
+        def target(t):
+            row, me = divmod(t, parts)
+            if row >= low:
+                row = low + (row - low + steps) % (count // parts - low)
+            return (row * parts + me) ^ s
+
+        return lax.ppermute(value, "tok", [(t, target(t)) for t in range(count)])
 
     def exchange(pieces):
         return [pieces[0]] + [move(pieces[s], 0, s) for s in range(1, parts)]
@@ -314,12 +328,12 @@
     )
     query_pieces = exchange(query_pieces)
     windows = [own]
-    for _ in range(behind):
-        windows.append(move(windows[-1], 1))
+    for k in range(behind):
+        windows.append(move(windows[-1], 1, low=k))
 
     kv_shape = (2 * span, HEAD_SIZE)
     stages = [0] + list(range(behind, 0, -1))
-    dq, own_term, sent = None, None, None
+    dq, own_pieces, sent = None, None, None
     for k, offset in enumerate(stages):
         first, last = k == 0, k == len(stages) - 1
         ins = [place, *query_pieces, own, windows[offset]]
@@ -340,7 +354,8 @@
         dq, term = (got[:parts] if last else got[0]), got[-1]
         piece_shapes = [shape((2 * rows, HEAD_SIZE), BF16)] * parts
         if offset == 0:
-            own_term = term
+            own_pieces = call(functools.partial(cut_terms, rows, 1), (place, term), piece_shapes)
+            own_pieces = exchange(own_pieces)
         elif offset == 1:
             terms = (term,) if sent is None else (sent, term)
             got = call(
@@ -348,18 +363,12 @@
             )
             sent = [move(piece, -1, s) for s, piece in enumerate(got)]
         elif sent is None:
-            sent = move(term, -1)
+            sent = move(term, -1, low=offset - 1)
         else:
             (term,) = call(add_terms, (place, sent, term), [shape(kv_shape, BF16)])
-            sent = move(term, -1)
+            sent = move(term, -1, low=offset - 1)
 
     dq_pieces = exchange(dq)
-    own_pieces = call(
-        functools.partial(cut_terms, rows, 1),
-        (place, own_term, *([] if sent is None else got[:1])),
-        piece_shapes,
-    )
-    own_pieces = exchange(own_pieces)
     query_grad, token = call(
         functools.partial(spread_queries, rows),
         (place, *dq_pieces),

time: 57.4 us -> 60.1 us (1.047)
  waiting for transfers between devices: 18.9 us -> 22.1 us
    ppermute x19, waiting for transfers between devices: 18.9 us -> 22.1 us  [move(): return lax.ppermute(value, 'tok', [(t, target(t)) for t in range(count)])]
    pallas_call x10, Pallas kernels: 15.1 us -> 14.5 us  [call(): pl.pallas_call(kernel, out_shape=outs, in_specs=[SMEM] + specs, out_specs...]
  transfers between devices with their start and end apart: 19 -> 19, of which waited for: 7 -> 6; matrix products, arithmetic and copies ran while one was open for 0% -> 0% of each run, Pallas kernels for 19% -> 17%
where the time goes in v2:
time: 60.1 us; the launch traced here: 59.8 us
  starting transfers between devices  22.2 us (37%)
  waiting for transfers between devices  22.1 us (37%)
  Pallas kernels  14.5 us (24%)
  between operations  0.98 us (2%)
    ppermute x19, starting transfers between devices, move(): return lax.ppermute(value, 'tok', [(t, target(t)) for t in range(count)])  22.2 us
    ppermute x19, waiting for transfers between devices, move(): return lax.ppermute(value, 'tok', [(t, target(t)) for t in range(count)])  22.1 us
    pallas_call x10, Pallas kernels, call(): pl.pallas_call(kernel, out_shape=outs, in_specs=[SMEM] + specs, out_specs...  14.5 us
  transfers between devices with their start and end apart: 19, of which 6 were waited for; matrix products, arithmetic and copies ran while one was open for 0% of the time, Pallas kernels for 17%

profile of v2, /device:TPU:0, one launch (start us, length us, event | category | flops | bytes accessed | tf_op | source)
XLA Modules:
  0.0 59.8 jit_solution(11984016596915790099)
XLA Ops:
  0.7 1.5 %shard_map.95 = (bf16[264,128]{1,0:T(8,128)(2,1)S(1)}, bf16[264,128]{1,0:T(8,128)(2,1)S(1)}, bf16[264,128]{1,0:T(8,128)(2,1)S(1)}, bf16[264,128]{1,0:T(8,128)(2,1)S(1)}) custom-call(s32[2]{0:T(128)S(1)} %pad_add_fusion.place, bf16[128,512]{1,0:T(8,128)(2,1)} %key_ref.1, bf16[128,512]{1,0:T(8,128)(2,1)} %value_ref.1, s32[1,128]{1,0:T(1,128)} %bitcast.3), custom_call_target="tpu_custom_call" | custom-call | bytes 533000 | tf_op jit(solution)/shard_map/pallas_call | solution.py:42
  2.2 0.6 collective-permute-start.3
  2.8 2.6 %collective-permute-start.4 = (bf16[264,128]{1,0:T(8,128)(2,1)S(1)}, bf16[264,128]{1,0:T(8,128)(2,1)S(1)}, u32[]{:S(2)}, u32[]{:S(2)}) collective-permute-start(bf16[264,128]{1,0:T(8,128)(2,1)S(1)} %get-tuple-element.39), channel_id=1, source_target_pairs={{0,2},{1,3},{2,0},{3,1},{4,6},{5,7},{6,4},{7,5},{8,10},{9,11},{10,... | collective-permute-start | bytes 202760 | tf_op jit(solution)/shard_map/ppermute | solution.py:294
  5.4 3.0 %shard_map.94 = (bf16[1048,128]{1,0:T(8,128)(2,1)S(1)}, bf16[1048,128]{1,0:T(8,128)(2,1)S(1)}, bf16[1048,128]{1,0:T(8,128)(2,1)S(1)}, bf16[1048,128]{1,0:T(8,128)(2,1)S(1)}, f32[8,128]{1,0:T(8,128)S(1)}) custom-call(s32[2]{0:T(128)S(1)} %pad_add_fusion.place, bf16[128,2048]{1,0:T(8,128)(2,1)} %query_ref.1, bf16[128,2048]{1,0:T(8,128)(2,1)} %grad_ref.1, ...), custom_call_target="tpu_custom_call" | custom-call | bytes 2658312 | tf_op jit(solution)/shard_map/pallas_call | solution.py:42
  8.4 1.1 %collective-permute-done.5.refs_3_ = bf16[264,128]{1,0:T(8,128)(2,1)S(1)} collective-permute-done((bf16[264,128]{1,0:T(8,128)(2,1)S(1)}, bf16[264,128]{1,0:T(8,128)(2,1)S(1)}, u32[]{:S(2)}, u32[]{:S(2)}) %collective-permute-start.5) | collective-permute-done | bytes 67616 | tf_op jit(solution)/shard_map/ppermute | solution.py:294
  9.5 0.6 shard_map.96.refs_4_.refs_5_
  10.1 1.6 %collective-permute-start.6 = (bf16[1056,128]{1,0:T(8,128)(2,1)S(1)}, bf16[1056,128]{1,0:T(8,128)(2,1)S(1)}, u32[]{:S(2)}, u32[]{:S(2)}) collective-permute-start(bf16[1056,128]{1,0:T(8,128)(2,1)S(1)} %shard_map.96.refs_4_.refs_5_), channel_id=1, source_target_pairs={{0,4},{1,5},{2,6},{3,7},{4,8},{5,9},{6,10},{7,11},{8,12},{9,13},{1... | collective-permute-start | bytes 811016 | tf_op jit(solution)/shard_map/ppermute | solution.py:294
  11.7 1.4 %collective-permute-start.1 = (bf16[1048,128]{1,0:T(8,128)(2,1)S(1)}, bf16[1048,128]{1,0:T(8,128)(2,1)S(1)}, u32[]{:S(2)}, u32[]{:S(2)}) collective-permute-start(bf16[1048,128]{1,0:T(8,128)(2,1)S(1)} %get-tuple-element.35), channel_id=1, source_target_pairs={{0,2},{1,3},{2,0},{3,1},{4,6},{5,7},{6,4},{7,5},{8,10},{9,11},{10,... | collective-permute-start | bytes 804872 | tf_op jit(solution)/shard_map/ppermute | solution.py:294
  13.1 0.5 collective-permute-start.2
  13.6 7.0 %collective-permute-done.6.refs_5_ = bf16[1056,128]{1,0:T(8,128)(2,1)S(1)} collective-permute-done((bf16[1056,128]{1,0:T(8,128)(2,1)S(1)}, bf16[1056,128]{1,0:T(8,128)(2,1)S(1)}, u32[]{:S(2)}, u32[]{:S(2)}) %collective-permute-start.6) | collective-permute-done | bytes 270368 | tf_op jit(solution)/shard_map/ppermute | solution.py:294
  20.5 0.7 %collective-permute-start.7 = (bf16[1056,128]{1,0:T(8,128)(2,1)S(1)}, bf16[1056,128]{1,0:T(8,128)(2,1)S(1)}, u32[]{:S(2)}, u32[]{:S(2)}) collective-permute-start(bf16[1056,128]{1,0:T(8,128)(2,1)S(1)} %collective-permute-done.6.refs_5_), channel_id=1, source_target_pairs={{0,0},{1,1},{2,2},{3,3},{4,8},{5,9},{6,10},{7,11},{8,12},{9,13},{1... | collective-permute-start | bytes 811016 | tf_op jit(solution)/shard_map/ppermute | solution.py:294
  21.2 4.6 %collective-permute-done.2.refs_3_ = bf16[1048,128]{1,0:T(8,128)(2,1)S(1)} collective-permute-done((bf16[1048,128]{1,0:T(8,128)(2,1)S(1)}, bf16[1048,128]{1,0:T(8,128)(2,1)S(1)}, u32[]{:S(2)}, u32[]{:S(2)}) %collective-permute-start.2) | collective-permute-done | bytes 268320 | tf_op jit(solution)/shard_map/ppermute | solution.py:294
  25.8 3.4 %shard_map.97 = (f32[4,128,512]{2,1,0:T(8,128)S(1)}, f32[1024,128]{1,0:T(8,128)S(1)}) custom-call(s32[2]{0:T(128)S(1)} %pad_add_fusion.place, bf16[1048,128]{1,0:T(8,128)(2,1)S(1)} %get-tuple-element.33.refs_0_, bf16[1048,128]{1,0:T(8,128)(2,1)S(1)} %collective-permute-done.refs_1_, bf16[1048,128]{1,0:T(8,128)(2,1)S(1)} %collective-permute-done.1.refs_2_, ...), custom_call_target="tpu_custom_call" | custom-call | flops 1342177280 | bytes 3186696 | tf_op jit(solution)/shard_map/pallas_call | solution.py:42
  29.3 1.2 %shard_map.98 = (f32[4,128,512]{2,1,0:T(8,128)S(1)}, bf16[1024,128]{1,0:T(8,128)(2,1)S(1)}) custom-call(s32[2]{0:T(128)S(1)} %pad_add_fusion.place, bf16[1048,128]{1,0:T(8,128)(2,1)S(1)} %get-tuple-element.33.refs_0_, bf16[1048,128]{1,0:T(8,128)(2,1)S(1)} %collective-permute-done.refs_1_, bf16[1048,128]{1,0:T(8,128)(2,1)S(1)} %collective-permute-done.1.refs_2_, ...), custom_call_target="tpu_custom_call" | custom-call | flops 1342177280 | bytes 3973128 | tf_op jit(solution)/shard_map/pallas_call | solution.py:42
  30.5 0.7 %collective-permute-start.14 = (bf16[1024,128]{1,0:T(8,128)(2,1)S(1)}, bf16[1024,128]{1,0:T(8,128)(2,1)S(1)}, u32[]{:S(2)}, u32[]{:S(2)}) collective-permute-start(bf16[1024,128]{1,0:T(8,128)(2,1)S(1)} %get-tuple-element.54), channel_id=1, source_target_pairs={{0,0},{1,1},{2,2},{3,3},{4,12},{5,13},{6,14},{7,15},{8,4},{9,5},{1... | collective-permute-start | bytes 786440 | tf_op jit(solution)/shard_map/ppermute | solution.py:294
  31.1 0.9 %shard_map.99 = (bf16[128,512]{1,0:T(8,128)(2,1)S(1)}, bf16[128,512]{1,0:T(8,128)(2,1)S(1)}, bf16[128,512]{1,0:T(8,128)(2,1)S(1)}, bf16[128,512]{1,0:T(8,128)(2,1)S(1)}, f32[1024,128]{1,0:T(8,128)S(1)}) custom-call(s32[2]{0:T(128)S(1)} %pad_add_fusion.place, bf16[1048,128]{1,0:T(8,128)(2,1)S(1)} %get-tuple-element.33.refs_0_, ...), custom_call_target="tpu_custom_call" | custom-call | flops 1342177280 | bytes 3710984 | tf_op jit(solution)/shard_map/pallas_call | solution.py:42
  32.1 0.4 collective-permute-start.8
  32.4 1.3 %collective-permute-start.9 = (bf16[128,512]{1,0:T(8,128)(2,1)S(1)}, bf16[128,512]{1,0:T(8,128)(2,1)S(1)}, u32[]{:S(2)}, u32[]{:S(2)}) collective-permute-start(bf16[128,512]{1,0:T(8,128)(2,1)S(1)} %get-tuple-element.46), channel_id=1, source_target_pairs={{0,2},{1,3},{2,0},{3,1},{4,6},{5,7},{6,4},{7,5},{8,10},{9,11},{10,... | collective-permute-start | bytes 393224 | tf_op jit(solution)/shard_map/ppermute | solution.py:294
  33.7 0.3 collective-permute-start.10
  34.0 0.6 shard_map.101
  34.6 0.6 %collective-permute-start.11 = (bf16[256,128]{1,0:T(8,128)(2,1)S(1)}, bf16[256,128]{1,0:T(8,128)(2,1)S(1)}, u32[]{:S(2)}, u32[]{:S(2)}) collective-permute-start(bf16[256,128]{1,0:T(8,128)(2,1)S(1)} %get-tuple-element.51), channel_id=1, source_target_pairs={{0,1},{1,0},{2,3},{3,2},{4,5},{5,4},{6,7},{7,6},{8,9},{9,8},{10,11... | collective-permute-start | bytes 196616 | tf_op jit(solution)/shard_map/ppermute | solution.py:294
  35.2 1.3 %collective-permute-start.12 = (bf16[256,128]{1,0:T(8,128)(2,1)S(1)}, bf16[256,128]{1,0:T(8,128)(2,1)S(1)}, u32[]{:S(2)}, u32[]{:S(2)}) collective-permute-start(bf16[256,128]{1,0:T(8,128)(2,1)S(1)} %get-tuple-element.52), channel_id=1, source_target_pairs={{0,2},{1,3},{2,0},{3,1},{4,6},{5,7},{6,4},{7,5},{8,10},{9,11},{10,... | collective-permute-start | bytes 196616 | tf_op jit(solution)/shard_map/ppermute | solution.py:294
  36.5 0.6 shard_map.102
  37.1 0.2 collective-permute-start.13
  37.4 5.6 %collective-permute-done.12.refs_2_ = bf16[256,128]{1,0:T(8,128)(2,1)S(1)} collective-permute-done((bf16[256,128]{1,0:T(8,128)(2,1)S(1)}, bf16[256,128]{1,0:T(8,128)(2,1)S(1)}, u32[]{:S(2)}, u32[]{:S(2)}) %collective-permute-start.12) | collective-permute-done | bytes 65568 | tf_op jit(solution)/shard_map/ppermute | solution.py:294
  43.0 6.7 %collective-permute-start.15 = (bf16[256,128]{1,0:T(8,128)(2,1)S(1)}, bf16[256,128]{1,0:T(8,128)(2,1)S(1)}, u32[]{:S(2)}, u32[]{:S(2)}) collective-permute-start(bf16[256,128]{1,0:T(8,128)(2,1)S(1)} %get-tuple-element.56), channel_id=1, source_target_pairs={{0,12},{1,13},{2,14},{3,15},{4,0},{5,1},{6,2},{7,3},{8,4},{9,5},{1... | collective-permute-start | bytes 196616 | tf_op jit(solution)/shard_map/ppermute | solution.py:294
  49.7 0.4 collective-permute-start.16
  50.0 3.1 %collective-permute-start.17 = (bf16[256,128]{1,0:T(8,128)(2,1)S(1)}, bf16[256,128]{1,0:T(8,128)(2,1)S(1)}, u32[]{:S(2)}, u32[]{:S(2)}) collective-permute-start(bf16[256,128]{1,0:T(8,128)(2,1)S(1)} %get-tuple-element.58), channel_id=1, source_target_pairs={{0,14},{1,15},{2,12},{3,13},{4,2},{5,3},{6,0},{7,1},{8,6},{9,7},{1... | collective-permute-start | bytes 196616 | tf_op jit(solution)/shard_map/ppermute | solution.py:294
  53.1 1.4 %shard_map.100 = (bf16[128,2048]{1,0:T(8,128)(2,1)}, f32[8,128]{1,0:T(8,128)S(1)}) custom-call(s32[2]{0:T(128)S(1)} %pad_add_fusion.place, bf16[128,512]{1,0:T(8,128)(2,1)S(1)} %get-tuple-element.44.refs_0_, bf16[128,512]{1,0:T(8,128)(2,1)S(1)} %collective-permute-done.8.refs_1_, bf16[128,512]{1,0:T(8,128)(2,1)S(1)} %collective-permute-done.9.refs_2_, ...), custom_call_target="tpu_custom_call" | custom-call | bytes 1052680 | tf_op jit(solution)/shard_map/pallas_call | solution.py:42
  54.6 1.0 %collective-permute-done.17.refs_6_ = bf16[256,128]{1,0:T(8,128)(2,1)S(1)} collective-permute-done((bf16[256,128]{1,0:T(8,128)(2,1)S(1)}, bf16[256,128]{1,0:T(8,128)(2,1)S(1)}, u32[]{:S(2)}, u32[]{:S(2)}) %collective-permute-start.17) | collective-permute-done | bytes 65568 | tf_op jit(solution)/shard_map/ppermute | solution.py:294
  55.6 2.8 %collective-permute-done.18.refs_7_ = bf16[256,128]{1,0:T(8,128)(2,1)S(1)} collective-permute-done((bf16[256,128]{1,0:T(8,128)(2,1)S(1)}, bf16[256,128]{1,0:T(8,128)(2,1)S(1)}, u32[]{:S(2)}, u32[]{:S(2)}) %collective-permute-start.18) | collective-permute-done | bytes 65568 | tf_op jit(solution)/shard_map/ppermute | solution.py:294
  58.3 1.3 %shard_map.103 = (bf16[128,512]{1,0:T(8,128)(2,1)}, bf16[128,512]{1,0:T(8,128)(2,1)}) custom-call(s32[2]{0:T(128)S(1)} %pad_add_fusion.place, bf16[256,128]{1,0:T(8,128)(2,1)S(1)} %get-tuple-element.50.refs_0_, bf16[256,128]{1,0:T(8,128)(2,1)S(1)} %collective-permute-done.11.refs_1_, bf16[256,128]{1,0:T(8,128)(2,1)S(1)} %collective-permute-done.12.refs_2_, ...), custom_call_target="tpu_custom_call" | custom-call | bytes 790536 | tf_op jit(solution)/shard_map/pallas_call | solution.py:42
  (19 shorter events, 0.2 us)
Async XLA Ops:
  0.7 4.7 %copy-start = (f32[16,128]{1,0:T(8,128)S(1)}, f32[16,128]{1,0:T(8,128)}, u32[]{:S(2)}) copy-start(f32[16,128]{1,0:T(8,128)} %norm_ref.1) | copy-start | bytes 24580
  2.2 6.2 %collective-permute-start.3 = (bf16[264,128]{1,0:T(8,128)(2,1)S(1)}, bf16[264,128]{1,0:T(8,128)(2,1)S(1)}, u32[]{:S(2)}, u32[]{:S(2)}) collective-permute-start(bf16[264,128]{1,0:T(8,128)(2,1)S(1)} %get-tuple-element.38), channel_id=1, source_target_pairs={{0,1},{1,0},{2,3},{3,2},{4,5},{5,4},{6,7},{7,6},{8,9},{9,8},{10,11... | collective-permute-start | bytes 202760 | tf_op jit(solution)/shard_map/ppermute | solution.py:294
  2.8 5.6 %collective-permute-start.4 = (bf16[264,128]{1,0:T(8,128)(2,1)S(1)}, bf16[264,128]{1,0:T(8,128)(2,1)S(1)}, u32[]{:S(2)}, u32[]{:S(2)}) collective-permute-start(bf16[264,128]{1,0:T(8,128)(2,1)S(1)} %get-tuple-element.39), channel_id=1, source_target_pairs={{0,2},{1,3},{2,0},{3,1},{4,6},{5,7},{6,4},{7,5},{8,10},{9,11},{10,... | collective-permute-start | bytes 202760 | tf_op jit(solution)/shard_map/ppermute | solution.py:294
  5.4 4.1 %collective-permute-start.5 = (bf16[264,128]{1,0:T(8,128)(2,1)S(1)}, bf16[264,128]{1,0:T(8,128)(2,1)S(1)}, u32[]{:S(2)}, u32[]{:S(2)}) collective-permute-start(bf16[264,128]{1,0:T(8,128)(2,1)S(1)} %get-tuple-element.40), channel_id=1, source_target_pairs={{0,3},{1,2},{2,1},{3,0},{4,7},{5,6},{6,5},{7,4},{8,11},{9,10},{10,... | collective-permute-start | bytes 202760 | tf_op jit(solution)/shard_map/ppermute | solution.py:294
  10.1 10.5 %collective-permute-start.6 = (bf16[1056,128]{1,0:T(8,128)(2,1)S(1)}, bf16[1056,128]{1,0:T(8,128)(2,1)S(1)}, u32[]{:S(2)}, u32[]{:S(2)}) collective-permute-start(bf16[1056,128]{1,0:T(8,128)(2,1)S(1)} %shard_map.96.refs_4_.refs_5_), channel_id=1, source_target_pairs={{0,4},{1,5},{2,6},{3,7},{4,8},{5,9},{6,10},{7,11},{8,12},{9,13},{1... | collective-permute-start | bytes 811016 | tf_op jit(solution)/shard_map/ppermute | solution.py:294
  11.7 9.5 %collective-permute-start = (bf16[1048,128]{1,0:T(8,128)(2,1)S(1)}, bf16[1048,128]{1,0:T(8,128)(2,1)S(1)}, u32[]{:S(2)}, u32[]{:S(2)}) collective-permute-start(bf16[1048,128]{1,0:T(8,128)(2,1)S(1)} %get-tuple-element.34), channel_id=1, source_target_pairs={{0,1},{1,0},{2,3},{3,2},{4,5},{5,4},{6,7},{7,6},{8,9},{9,8},{10,11... | collective-permute-start | bytes 804872 | tf_op jit(solution)/shard_map/ppermute | solution.py:294
  11.7 9.5 %collective-permute-start.1 = (bf16[1048,128]{1,0:T(8,128)(2,1)S(1)}, bf16[1048,128]{1,0:T(8,128)(2,1)S(1)}, u32[]{:S(2)}, u32[]{:S(2)}) collective-permute-start(bf16[1048,128]{1,0:T(8,128)(2,1)S(1)} %get-tuple-element.35), channel_id=1, source_target_pairs={{0,2},{1,3},{2,0},{3,1},{4,6},{5,7},{6,4},{7,5},{8,10},{9,11},{10,... | collective-permute-start | bytes 804872 | tf_op jit(solution)/shard_map/ppermute | solution.py:294
  13.1 12.8 %collective-permute-start.2 = (bf16[1048,128]{1,0:T(8,128)(2,1)S(1)}, bf16[1048,128]{1,0:T(8,128)(2,1)S(1)}, u32[]{:S(2)}, u32[]{:S(2)}) collective-permute-start(bf16[1048,128]{1,0:T(8,128)(2,1)S(1)} %get-tuple-element.36), channel_id=1, source_target_pairs={{0,3},{1,2},{2,1},{3,0},{4,7},{5,6},{6,5},{7,4},{8,11},{9,10},{10,... | collective-permute-start | bytes 804872 | tf_op jit(solution)/shard_map/ppermute | solution.py:294
  20.5 8.8 %collective-permute-start.7 = (bf16[1056,128]{1,0:T(8,128)(2,1)S(1)}, bf16[1056,128]{1,0:T(8,128)(2,1)S(1)}, u32[]{:S(2)}, u32[]{:S(2)}) collective-permute-start(bf16[1056,128]{1,0:T(8,128)(2,1)S(1)} %collective-permute-done.6.refs_5_), channel_id=1, source_target_pairs={{0,0},{1,1},{2,2},{3,3},{4,8},{5,9},{6,10},{7,11},{8,12},{9,13},{1... | collective-permute-start | bytes 811016 | tf_op jit(solution)/shard_map/ppermute | solution.py:294
  30.5 4.8 %collective-permute-start.14 = (bf16[1024,128]{1,0:T(8,128)(2,1)S(1)}, bf16[1024,128]{1,0:T(8,128)(2,1)S(1)}, u32[]{:S(2)}, u32[]{:S(2)}) collective-permute-start(bf16[1024,128]{1,0:T(8,128)(2,1)S(1)} %get-tuple-element.54), channel_id=1, source_target_pairs={{0,0},{1,1},{2,2},{3,3},{4,12},{5,13},{6,14},{7,15},{8,4},{9,5},{1... | collective-permute-start | bytes 786440 | tf_op jit(solution)/shard_map/ppermute | solution.py:294
  32.1 17.6 %collective-permute-start.8 = (bf16[128,512]{1,0:T(8,128)(2,1)S(1)}, bf16[128,512]{1,0:T(8,128)(2,1)S(1)}, u32[]{:S(2)}, u32[]{:S(2)}) collective-permute-start(bf16[128,512]{1,0:T(8,128)(2,1)S(1)} %get-tuple-element.45), channel_id=1, source_target_pairs={{0,1},{1,0},{2,3},{3,2},{4,5},{5,4},{6,7},{7,6},{8,9},{9,8},{10,11... | collective-permute-start | bytes 393224 | tf_op jit(solution)/shard_map/ppermute | solution.py:294
  32.4 17.6 %collective-permute-start.9 = (bf16[128,512]{1,0:T(8,128)(2,1)S(1)}, bf16[128,512]{1,0:T(8,128)(2,1)S(1)}, u32[]{:S(2)}, u32[]{:S(2)}) collective-permute-start(bf16[128,512]{1,0:T(8,128)(2,1)S(1)} %get-tuple-element.46), channel_id=1, source_target_pairs={{0,2},{1,3},{2,0},{3,1},{4,6},{5,7},{6,4},{7,5},{8,10},{9,11},{10,... | collective-permute-start | bytes 393224 | tf_op jit(solution)/shard_map/ppermute | solution.py:294
  33.7 19.4 %collective-permute-start.10 = (bf16[128,512]{1,0:T(8,128)(2,1)S(1)}, bf16[128,512]{1,0:T(8,128)(2,1)S(1)}, u32[]{:S(2)}, u32[]{:S(2)}) collective-permute-start(bf16[128,512]{1,0:T(8,128)(2,1)S(1)} %get-tuple-element.47), channel_id=1, source_target_pairs={{0,3},{1,2},{2,1},{3,0},{4,7},{5,6},{6,5},{7,4},{8,11},{9,10},{10,... | collective-permute-start | bytes 393224 | tf_op jit(solution)/shard_map/ppermute | solution.py:294
  34.6 2.5 %collective-permute-start.11 = (bf16[256,128]{1,0:T(8,128)(2,1)S(1)}, bf16[256,128]{1,0:T(8,128)(2,1)S(1)}, u32[]{:S(2)}, u32[]{:S(2)}) collective-permute-start(bf16[256,128]{1,0:T(8,128)(2,1)S(1)} %get-tuple-element.51), channel_id=1, source_target_pairs={{0,1},{1,0},{2,3},{3,2},{4,5},{5,4},{6,7},{7,6},{8,9},{9,8},{10,11... | collective-permute-start | bytes 196616 | tf_op jit(solution)/shard_map/ppermute | solution.py:294
  35.2 7.7 %collective-permute-start.12 = (bf16[256,128]{1,0:T(8,128)(2,1)S(1)}, bf16[256,128]{1,0:T(8,128)(2,1)S(1)}, u32[]{:S(2)}, u32[]{:S(2)}) collective-permute-start(bf16[256,128]{1,0:T(8,128)(2,1)S(1)} %get-tuple-element.52), channel_id=1, source_target_pairs={{0,2},{1,3},{2,0},{3,1},{4,6},{5,7},{6,4},{7,5},{8,10},{9,11},{10,... | collective-permute-start | bytes 196616 | tf_op jit(solution)/shard_map/ppermute | solution.py:294
  37.1 17.4 %collective-permute-start.13 = (bf16[256,128]{1,0:T(8,128)(2,1)S(1)}, bf16[256,128]{1,0:T(8,128)(2,1)S(1)}, u32[]{:S(2)}, u32[]{:S(2)}) collective-permute-start(bf16[256,128]{1,0:T(8,128)(2,1)S(1)} %get-tuple-element.53), channel_id=1, source_target_pairs={{0,3},{1,2},{2,1},{3,0},{4,7},{5,6},{6,5},{7,4},{8,11},{9,10},{10,... | collective-permute-start | bytes 196616 | tf_op jit(solution)/shard_map/ppermute | solution.py:294
  43.0 11.6 %collective-permute-start.15 = (bf16[256,128]{1,0:T(8,128)(2,1)S(1)}, bf16[256,128]{1,0:T(8,128)(2,1)S(1)}, u32[]{:S(2)}, u32[]{:S(2)}) collective-permute-start(bf16[256,128]{1,0:T(8,128)(2,1)S(1)} %get-tuple-element.56), channel_id=1, source_target_pairs={{0,12},{1,13},{2,14},{3,15},{4,0},{5,1},{6,2},{7,3},{8,4},{9,5},{1... | collective-permute-start | bytes 196616 | tf_op jit(solution)/shard_map/ppermute | solution.py:294
  49.7 4.9 %collective-permute-start.16 = (bf16[256,128]{1,0:T(8,128)(2,1)S(1)}, bf16[256,128]{1,0:T(8,128)(2,1)S(1)}, u32[]{:S(2)}, u32[]{:S(2)}) collective-permute-start(bf16[256,128]{1,0:T(8,128)(2,1)S(1)} %get-tuple-element.57), channel_id=1, source_target_pairs={{0,13},{1,12},{2,15},{3,14},{4,1},{5,0},{6,3},{7,2},{8,5},{9,4},{1... | collective-permute-start | bytes 196616 | tf_op jit(solution)/shard_map/ppermute | solution.py:294
  50.0 5.5 %collective-permute-start.17 = (bf16[256,128]{1,0:T(8,128)(2,1)S(1)}, bf16[256,128]{1,0:T(8,128)(2,1)S(1)}, u32[]{:S(2)}, u32[]{:S(2)}) collective-permute-start(bf16[256,128]{1,0:T(8,128)(2,1)S(1)} %get-tuple-element.58), channel_id=1, source_target_pairs={{0,14},{1,15},{2,12},{3,13},{4,2},{5,3},{6,0},{7,1},{8,6},{9,7},{1... | collective-permute-start | bytes 196616 | tf_op jit(solution)/shard_map/ppermute | solution.py:294
  53.1 5.3 %collective-permute-start.18 = (bf16[256,128]{1,0:T(8,128)(2,1)S(1)}, bf16[256,128]{1,0:T(8,128)(2,1)S(1)}, u32[]{:S(2)}, u32[]{:S(2)}) collective-permute-start(bf16[256,128]{1,0:T(8,128)(2,1)S(1)} %get-tuple-element.59), channel_id=1, source_target_pairs={{0,15},{1,14},{2,13},{3,12},{4,3},{5,2},{6,1},{7,0},{8,7},{9,6},{1... | collective-permute-start | bytes 196616 | tf_op jit(solution)/shard_map/ppermute | solution.py:294

commit v3 on v2

--- a/solution.py
+++ b/solution.py
@@ -284,14 +284,9 @@
     width = GROUP * rows
     shape = jax.ShapeDtypeStruct
 
-    def move(value, steps, s=0, low=0):
-        def target(t):
-            row, me = divmod(t, parts)
-            if row >= low:
-                row = low + (row - low + steps) % (count // parts - low)
-            return (row * parts + me) ^ s
-
-        return lax.ppermute(value, "tok", [(t, target(t)) for t in range(count)])
+    def move(value, steps, s=0):
+        pairs = [(t, ((t + steps * parts) % count) ^ s) for t in range(count)]
+        return lax.ppermute(value, "tok", pairs)
 
     def exchange(pieces):
         return [pieces[0]] + [move(pieces[s], 0, s) for s in range(1, parts)]
@@ -328,8 +323,8 @@
     )
     query_pieces = exchange(query_pieces)
     windows = [own]
-    for k in range(behind):
-        windows.append(move(windows[-1], 1, low=k))
+    for _ in range(behind):
+        windows.append(move(windows[-1], 1))
 
     kv_shape = (2 * span, HEAD_SIZE)
     stages = [0] + list(range(behind, 0, -1))
@@ -363,10 +358,10 @@
             )
             sent = [move(piece, -1, s) for s, piece in enumerate(got)]
         elif sent is None:
-            sent = move(term, -1, low=offset - 1)
+            sent = move(term, -1)
         else:
             (term,) = call(add_terms, (place, sent, term), [shape(kv_shape, BF16)])
-            sent = move(term, -1, low=offset - 1)
+            sent = move(term, -1)
 
     dq_pieces = exchange(dq)
     query_grad, token = call(

time: 60.1 us -> 58.1 us (0.967)
  starting transfers between devices: 22.2 us -> 19.4 us
  waiting for transfers between devices: 22.1 us -> 23 us
    ppermute x19, starting transfers between devices: 22.2 us -> 19.4 us  [move(): return lax.ppermute(value, 'tok', pairs)]
    ppermute x19, waiting for transfers between devices: 22.1 us -> 23 us  [move(): return lax.ppermute(value, 'tok', pairs)]
  transfers between devices with their start and end apart: 19 -> 19, of which waited for: 6 -> 9; matrix products, arithmetic and copies ran while one was open for 0% -> 0% of each run, Pallas kernels for 17% -> 17%
where the time goes in v3:
time: 58.1 us; the launch traced here: 57.9 us
  waiting for transfers between devices  23 us (40%)
  starting transfers between devices  19.4 us (33%)
  Pallas kernels  14.5 us (25%)
  between operations  0.95 us (2%)
    ppermute x19, waiting for transfers between devices, move(): return lax.ppermute(value, 'tok', pairs)  23 us
    ppermute x19, starting transfers between devices, move(): return lax.ppermute(value, 'tok', pairs)  19.4 us
    pallas_call x10, Pallas kernels, call(): pl.pallas_call(kernel, out_shape=outs, in_specs=[SMEM] + specs, out_specs...  14.5 us
  transfers between devices with their start and end apart: 19, of which 9 were waited for; matrix products, arithmetic and copies ran while one was open for 0% of the time, Pallas kernels for 17%

profile of v3, /device:TPU:0, one launch (start us, length us, event | category | flops | bytes accessed | tf_op | source)
XLA Modules:
  0.0 57.9 jit_solution(17786653377428238978)
XLA Ops:
  0.7 1.5 %shard_map.95 = (bf16[264,128]{1,0:T(8,128)(2,1)S(1)}, bf16[264,128]{1,0:T(8,128)(2,1)S(1)}, bf16[264,128]{1,0:T(8,128)(2,1)S(1)}, bf16[264,128]{1,0:T(8,128)(2,1)S(1)}) custom-call(s32[2]{0:T(128)S(1)} %pad_add_fusion.place, bf16[128,512]{1,0:T(8,128)(2,1)} %key_ref.1, bf16[128,512]{1,0:T(8,128)(2,1)} %value_ref.1, s32[1,128]{1,0:T(1,128)} %bitcast.3), custom_call_target="tpu_custom_call" | custom-call | bytes 533000 | tf_op jit(solution)/shard_map/pallas_call | solution.py:42
  2.2 0.6 collective-permute-start.3
  2.8 2.6 %collective-permute-start.4 = (bf16[264,128]{1,0:T(8,128)(2,1)S(1)}, bf16[264,128]{1,0:T(8,128)(2,1)S(1)}, u32[]{:S(2)}, u32[]{:S(2)}) collective-permute-start(bf16[264,128]{1,0:T(8,128)(2,1)S(1)} %get-tuple-element.39), channel_id=1, source_target_pairs={{0,2},{1,3},{2,0},{3,1},{4,6},{5,7},{6,4},{7,5},{8,10},{9,11},{10,... | collective-permute-start | bytes 202760 | tf_op jit(solution)/shard_map/ppermute | solution.py:289
  5.4 3.0 %shard_map.94 = (bf16[1048,128]{1,0:T(8,128)(2,1)S(1)}, bf16[1048,128]{1,0:T(8,128)(2,1)S(1)}, bf16[1048,128]{1,0:T(8,128)(2,1)S(1)}, bf16[1048,128]{1,0:T(8,128)(2,1)S(1)}, f32[8,128]{1,0:T(8,128)S(1)}) custom-call(s32[2]{0:T(128)S(1)} %pad_add_fusion.place, bf16[128,2048]{1,0:T(8,128)(2,1)} %query_ref.1, bf16[128,2048]{1,0:T(8,128)(2,1)} %grad_ref.1, ...), custom_call_target="tpu_custom_call" | custom-call | bytes 2658312 | tf_op jit(solution)/shard_map/pallas_call | solution.py:42
  8.4 1.1 %collective-permute-done.5.refs_3_ = bf16[264,128]{1,0:T(8,128)(2,1)S(1)} collective-permute-done((bf16[264,128]{1,0:T(8,128)(2,1)S(1)}, bf16[264,128]{1,0:T(8,128)(2,1)S(1)}, u32[]{:S(2)}, u32[]{:S(2)}) %collective-permute-start.5) | collective-permute-done | bytes 67616 | tf_op jit(solution)/shard_map/ppermute | solution.py:289
  9.5 0.6 shard_map.96.refs_4_.refs_5_
  10.1 1.6 %collective-permute-start.6 = (bf16[1056,128]{1,0:T(8,128)(2,1)S(1)}, bf16[1056,128]{1,0:T(8,128)(2,1)S(1)}, u32[]{:S(2)}, u32[]{:S(2)}) collective-permute-start(bf16[1056,128]{1,0:T(8,128)(2,1)S(1)} %shard_map.96.refs_4_.refs_5_), channel_id=1, source_target_pairs={{0,4},{1,5},{2,6},{3,7},{4,8},{5,9},{6,10},{7,11},{8,12},{9,13},{1... | collective-permute-start | bytes 811016 | tf_op jit(solution)/shard_map/ppermute | solution.py:289
  11.7 1.4 %collective-permute-start.1 = (bf16[1048,128]{1,0:T(8,128)(2,1)S(1)}, bf16[1048,128]{1,0:T(8,128)(2,1)S(1)}, u32[]{:S(2)}, u32[]{:S(2)}) collective-permute-start(bf16[1048,128]{1,0:T(8,128)(2,1)S(1)} %get-tuple-element.35), channel_id=1, source_target_pairs={{0,2},{1,3},{2,0},{3,1},{4,6},{5,7},{6,4},{7,5},{8,10},{9,11},{10,... | collective-permute-start | bytes 804872 | tf_op jit(solution)/shard_map/ppermute | solution.py:289
  13.1 0.5 collective-permute-start.2
  13.6 7.0 %collective-permute-done.6.refs_5_ = bf16[1056,128]{1,0:T(8,128)(2,1)S(1)} collective-permute-done((bf16[1056,128]{1,0:T(8,128)(2,1)S(1)}, bf16[1056,128]{1,0:T(8,128)(2,1)S(1)}, u32[]{:S(2)}, u32[]{:S(2)}) %collective-permute-start.6) | collective-permute-done | bytes 270368 | tf_op jit(solution)/shard_map/ppermute | solution.py:289
  20.5 0.5 collective-permute-done.1.refs_2_
  21.0 4.8 %collective-permute-done.2.refs_3_ = bf16[1048,128]{1,0:T(8,128)(2,1)S(1)} collective-permute-done((bf16[1048,128]{1,0:T(8,128)(2,1)S(1)}, bf16[1048,128]{1,0:T(8,128)(2,1)S(1)}, u32[]{:S(2)}, u32[]{:S(2)}) %collective-permute-start.2) | collective-permute-done | bytes 268320 | tf_op jit(solution)/shard_map/ppermute | solution.py:289
  25.8 3.4 %shard_map.97 = (f32[4,128,512]{2,1,0:T(8,128)S(1)}, f32[1024,128]{1,0:T(8,128)S(1)}) custom-call(s32[2]{0:T(128)S(1)} %pad_add_fusion.place, bf16[1048,128]{1,0:T(8,128)(2,1)S(1)} %get-tuple-element.33.refs_0_, bf16[1048,128]{1,0:T(8,128)(2,1)S(1)} %collective-permute-done.refs_1_, bf16[1048,128]{1,0:T(8,128)(2,1)S(1)} %collective-permute-done.1.refs_2_, ...), custom_call_target="tpu_custom_call" | custom-call | flops 1342177280 | bytes 3186696 | tf_op jit(solution)/shard_map/pallas_call | solution.py:42
  29.3 0.8 %collective-permute-done.7.refs_5_ = bf16[1056,128]{1,0:T(8,128)(2,1)S(1)} collective-permute-done((bf16[1056,128]{1,0:T(8,128)(2,1)S(1)}, bf16[1056,128]{1,0:T(8,128)(2,1)S(1)}, u32[]{:S(2)}, u32[]{:S(2)}) %collective-permute-start.7) | collective-permute-done | bytes 270368 | tf_op jit(solution)/shard_map/ppermute | solution.py:289
  30.1 1.2 %shard_map.98 = (f32[4,128,512]{2,1,0:T(8,128)S(1)}, bf16[1024,128]{1,0:T(8,128)(2,1)S(1)}) custom-call(s32[2]{0:T(128)S(1)} %pad_add_fusion.place, bf16[1048,128]{1,0:T(8,128)(2,1)S(1)} %get-tuple-element.33.refs_0_, bf16[1048,128]{1,0:T(8,128)(2,1)S(1)} %collective-permute-done.refs_1_, bf16[1048,128]{1,0:T(8,128)(2,1)S(1)} %collective-permute-done.1.refs_2_, ...), custom_call_target="tpu_custom_call" | custom-call | flops 1342177280 | bytes 3973128 | tf_op jit(solution)/shard_map/pallas_call | solution.py:42
  31.2 2.6 %collective-permute-start.14 = (bf16[1024,128]{1,0:T(8,128)(2,1)S(1)}, bf16[1024,128]{1,0:T(8,128)(2,1)S(1)}, u32[]{:S(2)}, u32[]{:S(2)}) collective-permute-start(bf16[1024,128]{1,0:T(8,128)(2,1)S(1)} %get-tuple-element.54), channel_id=1, source_target_pairs={{0,12},{1,13},{2,14},{3,15},{4,0},{5,1},{6,2},{7,3},{8,4},{9,5},{1... | collective-permute-start | bytes 786440 | tf_op jit(solution)/shard_map/ppermute | solution.py:289
  33.9 0.9 %shard_map.99 = (bf16[128,512]{1,0:T(8,128)(2,1)S(1)}, bf16[128,512]{1,0:T(8,128)(2,1)S(1)}, bf16[128,512]{1,0:T(8,128)(2,1)S(1)}, bf16[128,512]{1,0:T(8,128)(2,1)S(1)}, f32[1024,128]{1,0:T(8,128)S(1)}) custom-call(s32[2]{0:T(128)S(1)} %pad_add_fusion.place, bf16[1048,128]{1,0:T(8,128)(2,1)S(1)} %get-tuple-element.33.refs_0_, ...), custom_call_target="tpu_custom_call" | custom-call | flops 1342177280 | bytes 3710984 | tf_op jit(solution)/shard_map/pallas_call | solution.py:42
  34.8 0.4 collective-permute-start.8
  35.2 1.3 %collective-permute-start.9 = (bf16[128,512]{1,0:T(8,128)(2,1)S(1)}, bf16[128,512]{1,0:T(8,128)(2,1)S(1)}, u32[]{:S(2)}, u32[]{:S(2)}) collective-permute-start(bf16[128,512]{1,0:T(8,128)(2,1)S(1)} %get-tuple-element.46), channel_id=1, source_target_pairs={{0,2},{1,3},{2,0},{3,1},{4,6},{5,7},{6,4},{7,5},{8,10},{9,11},{10,... | collective-permute-start | bytes 393224 | tf_op jit(solution)/shard_map/ppermute | solution.py:289
  36.5 0.3 collective-permute-start.10
  36.8 0.6 shard_map.101
  37.3 0.6 %collective-permute-start.11 = (bf16[256,128]{1,0:T(8,128)(2,1)S(1)}, bf16[256,128]{1,0:T(8,128)(2,1)S(1)}, u32[]{:S(2)}, u32[]{:S(2)}) collective-permute-start(bf16[256,128]{1,0:T(8,128)(2,1)S(1)} %get-tuple-element.51), channel_id=1, source_target_pairs={{0,1},{1,0},{2,3},{3,2},{4,5},{5,4},{6,7},{7,6},{8,9},{9,8},{10,11... | collective-permute-start | bytes 196616 | tf_op jit(solution)/shard_map/ppermute | solution.py:289
  38.0 2.2 %collective-permute-done.14.refs_0_ = bf16[1024,128]{1,0:T(8,128)(2,1)S(1)} collective-permute-done((bf16[1024,128]{1,0:T(8,128)(2,1)S(1)}, bf16[1024,128]{1,0:T(8,128)(2,1)S(1)}, u32[]{:S(2)}, u32[]{:S(2)}) %collective-permute-start.14) | collective-permute-done | bytes 262176 | tf_op jit(solution)/shard_map/ppermute | solution.py:289
  40.2 1.3 %collective-permute-start.12 = (bf16[256,128]{1,0:T(8,128)(2,1)S(1)}, bf16[256,128]{1,0:T(8,128)(2,1)S(1)}, u32[]{:S(2)}, u32[]{:S(2)}) collective-permute-start(bf16[256,128]{1,0:T(8,128)(2,1)S(1)} %get-tuple-element.52), channel_id=1, source_target_pairs={{0,2},{1,3},{2,0},{3,1},{4,6},{5,7},{6,4},{7,5},{8,10},{9,11},{10,... | collective-permute-start | bytes 196616 | tf_op jit(solution)/shard_map/ppermute | solution.py:289
  41.5 0.6 %shard_map.102 = (bf16[256,128]{1,0:T(8,128)(2,1)S(1)}, bf16[256,128]{1,0:T(8,128)(2,1)S(1)}, bf16[256,128]{1,0:T(8,128)(2,1)S(1)}, bf16[256,128]{1,0:T(8,128)(2,1)S(1)}) custom-call(s32[2]{0:T(128)S(1)} %pad_add_fusion.place, bf16[1024,128]{1,0:T(8,128)(2,1)S(1)} %collective-permute-done.14.refs_0_, f32[1024,128]{1,0:T(8,128)S(1)} %get-tuple-element.55.refs_1_), custom_call_target="tpu_custom_call" | custom-call | bytes 1048584 | tf_op jit(solution)/shard_map/pallas_call | solution.py:42
  42.2 2.9 %collective-permute-done.12.refs_2_ = bf16[256,128]{1,0:T(8,128)(2,1)S(1)} collective-permute-done((bf16[256,128]{1,0:T(8,128)(2,1)S(1)}, bf16[256,128]{1,0:T(8,128)(2,1)S(1)}, u32[]{:S(2)}, u32[]{:S(2)}) %collective-permute-start.12) | collective-permute-done | bytes 65568 | tf_op jit(solution)/shard_map/ppermute | solution.py:289
  45.0 3.7 %collective-permute-start.15 = (bf16[256,128]{1,0:T(8,128)(2,1)S(1)}, bf16[256,128]{1,0:T(8,128)(2,1)S(1)}, u32[]{:S(2)}, u32[]{:S(2)}) collective-permute-start(bf16[256,128]{1,0:T(8,128)(2,1)S(1)} %get-tuple-element.56), channel_id=1, source_target_pairs={{0,12},{1,13},{2,14},{3,15},{4,0},{5,1},{6,2},{7,3},{8,4},{9,5},{1... | collective-permute-start | bytes 196616 | tf_op jit(solution)/shard_map/ppermute | solution.py:289
  48.7 2.4 %collective-permute-start.17 = (bf16[256,128]{1,0:T(8,128)(2,1)S(1)}, bf16[256,128]{1,0:T(8,128)(2,1)S(1)}, u32[]{:S(2)}, u32[]{:S(2)}) collective-permute-start(bf16[256,128]{1,0:T(8,128)(2,1)S(1)} %get-tuple-element.58), channel_id=1, source_target_pairs={{0,14},{1,15},{2,12},{3,13},{4,2},{5,3},{6,0},{7,1},{8,6},{9,7},{1... | collective-permute-start | bytes 196616 | tf_op jit(solution)/shard_map/ppermute | solution.py:289
  51.2 1.4 %shard_map.100 = (bf16[128,2048]{1,0:T(8,128)(2,1)}, f32[8,128]{1,0:T(8,128)S(1)}) custom-call(s32[2]{0:T(128)S(1)} %pad_add_fusion.place, bf16[128,512]{1,0:T(8,128)(2,1)S(1)} %get-tuple-element.44.refs_0_, bf16[128,512]{1,0:T(8,128)(2,1)S(1)} %collective-permute-done.8.refs_1_, bf16[128,512]{1,0:T(8,128)(2,1)S(1)} %collective-permute-done.9.refs_2_, ...), custom_call_target="tpu_custom_call" | custom-call | bytes 1052680 | tf_op jit(solution)/shard_map/pallas_call | solution.py:42
  52.7 1.3 %collective-permute-done.17.refs_6_ = bf16[256,128]{1,0:T(8,128)(2,1)S(1)} collective-permute-done((bf16[256,128]{1,0:T(8,128)(2,1)S(1)}, bf16[256,128]{1,0:T(8,128)(2,1)S(1)}, u32[]{:S(2)}, u32[]{:S(2)}) %collective-permute-start.17) | collective-permute-done | bytes 65568 | tf_op jit(solution)/shard_map/ppermute | solution.py:289
  54.0 2.5 %collective-permute-done.18.refs_7_ = bf16[256,128]{1,0:T(8,128)(2,1)S(1)} collective-permute-done((bf16[256,128]{1,0:T(8,128)(2,1)S(1)}, bf16[256,128]{1,0:T(8,128)(2,1)S(1)}, u32[]{:S(2)}, u32[]{:S(2)}) %collective-permute-start.18) | collective-permute-done | bytes 65568 | tf_op jit(solution)/shard_map/ppermute | solution.py:289
  56.4 1.3 %shard_map.103 = (bf16[128,512]{1,0:T(8,128)(2,1)}, bf16[128,512]{1,0:T(8,128)(2,1)}) custom-call(s32[2]{0:T(128)S(1)} %pad_add_fusion.place, bf16[256,128]{1,0:T(8,128)(2,1)S(1)} %get-tuple-element.50.refs_0_, bf16[256,128]{1,0:T(8,128)(2,1)S(1)} %collective-permute-done.11.refs_1_, bf16[256,128]{1,0:T(8,128)(2,1)S(1)} %collective-permute-done.12.refs_2_, ...), custom_call_target="tpu_custom_call" | custom-call | bytes 790536 | tf_op jit(solution)/shard_map/pallas_call | solution.py:42
  (19 shorter events, 0.2 us)
Async XLA Ops:
  0.7 4.7 %copy-start = (f32[16,128]{1,0:T(8,128)S(1)}, f32[16,128]{1,0:T(8,128)}, u32[]{:S(2)}) copy-start(f32[16,128]{1,0:T(8,128)} %norm_ref.1) | copy-start | bytes 24580
  2.2 6.2 %collective-permute-start.3 = (bf16[264,128]{1,0:T(8,128)(2,1)S(1)}, bf16[264,128]{1,0:T(8,128)(2,1)S(1)}, u32[]{:S(2)}, u32[]{:S(2)}) collective-permute-start(bf16[264,128]{1,0:T(8,128)(2,1)S(1)} %get-tuple-element.38), channel_id=1, source_target_pairs={{0,1},{1,0},{2,3},{3,2},{4,5},{5,4},{6,7},{7,6},{8,9},{9,8},{10,11... | collective-permute-start | bytes 202760 | tf_op jit(solution)/shard_map/ppermute | solution.py:289
  2.8 5.6 %collective-permute-start.4 = (bf16[264,128]{1,0:T(8,128)(2,1)S(1)}, bf16[264,128]{1,0:T(8,128)(2,1)S(1)}, u32[]{:S(2)}, u32[]{:S(2)}) collective-permute-start(bf16[264,128]{1,0:T(8,128)(2,1)S(1)} %get-tuple-element.39), channel_id=1, source_target_pairs={{0,2},{1,3},{2,0},{3,1},{4,6},{5,7},{6,4},{7,5},{8,10},{9,11},{10,... | collective-permute-start | bytes 202760 | tf_op jit(solution)/shard_map/ppermute | solution.py:289
  5.4 4.1 %collective-permute-start.5 = (bf16[264,128]{1,0:T(8,128)(2,1)S(1)}, bf16[264,128]{1,0:T(8,128)(2,1)S(1)}, u32[]{:S(2)}, u32[]{:S(2)}) collective-permute-start(bf16[264,128]{1,0:T(8,128)(2,1)S(1)} %get-tuple-element.40), channel_id=1, source_target_pairs={{0,3},{1,2},{2,1},{3,0},{4,7},{5,6},{6,5},{7,4},{8,11},{9,10},{10,... | collective-permute-start | bytes 202760 | tf_op jit(solution)/shard_map/ppermute | solution.py:289
  10.1 10.5 %collective-permute-start.6 = (bf16[1056,128]{1,0:T(8,128)(2,1)S(1)}, bf16[1056,128]{1,0:T(8,128)(2,1)S(1)}, u32[]{:S(2)}, u32[]{:S(2)}) collective-permute-start(bf16[1056,128]{1,0:T(8,128)(2,1)S(1)} %shard_map.96.refs_4_.refs_5_), channel_id=1, source_target_pairs={{0,4},{1,5},{2,6},{3,7},{4,8},{5,9},{6,10},{7,11},{8,12},{9,13},{1... | collective-permute-start | bytes 811016 | tf_op jit(solution)/shard_map/ppermute | solution.py:289
  11.7 8.8 %collective-permute-start = (bf16[1048,128]{1,0:T(8,128)(2,1)S(1)}, bf16[1048,128]{1,0:T(8,128)(2,1)S(1)}, u32[]{:S(2)}, u32[]{:S(2)}) collective-permute-start(bf16[1048,128]{1,0:T(8,128)(2,1)S(1)} %get-tuple-element.34), channel_id=1, source_target_pairs={{0,1},{1,0},{2,3},{3,2},{4,5},{5,4},{6,7},{7,6},{8,9},{9,8},{10,11... | collective-permute-start | bytes 804872 | tf_op jit(solution)/shard_map/ppermute | solution.py:289
  11.7 9.3 %collective-permute-start.1 = (bf16[1048,128]{1,0:T(8,128)(2,1)S(1)}, bf16[1048,128]{1,0:T(8,128)(2,1)S(1)}, u32[]{:S(2)}, u32[]{:S(2)}) collective-permute-start(bf16[1048,128]{1,0:T(8,128)(2,1)S(1)} %get-tuple-element.35), channel_id=1, source_target_pairs={{0,2},{1,3},{2,0},{3,1},{4,6},{5,7},{6,4},{7,5},{8,10},{9,11},{10,... | collective-permute-start | bytes 804872 | tf_op jit(solution)/shard_map/ppermute | solution.py:289
  13.1 12.8 %collective-permute-start.2 = (bf16[1048,128]{1,0:T(8,128)(2,1)S(1)}, bf16[1048,128]{1,0:T(8,128)(2,1)S(1)}, u32[]{:S(2)}, u32[]{:S(2)}) collective-permute-start(bf16[1048,128]{1,0:T(8,128)(2,1)S(1)} %get-tuple-element.36), channel_id=1, source_target_pairs={{0,3},{1,2},{2,1},{3,0},{4,7},{5,6},{6,5},{7,4},{8,11},{9,10},{10,... | collective-permute-start | bytes 804872 | tf_op jit(solution)/shard_map/ppermute | solution.py:289
  20.5 9.5 %collective-permute-start.7 = (bf16[1056,128]{1,0:T(8,128)(2,1)S(1)}, bf16[1056,128]{1,0:T(8,128)(2,1)S(1)}, u32[]{:S(2)}, u32[]{:S(2)}) collective-permute-start(bf16[1056,128]{1,0:T(8,128)(2,1)S(1)} %collective-permute-done.6.refs_5_), channel_id=1, source_target_pairs={{0,4},{1,5},{2,6},{3,7},{4,8},{5,9},{6,10},{7,11},{8,12},{9,13},{1... | collective-permute-start | bytes 811016 | tf_op jit(solution)/shard_map/ppermute | solution.py:289
  31.2 8.9 %collective-permute-start.14 = (bf16[1024,128]{1,0:T(8,128)(2,1)S(1)}, bf16[1024,128]{1,0:T(8,128)(2,1)S(1)}, u32[]{:S(2)}, u32[]{:S(2)}) collective-permute-start(bf16[1024,128]{1,0:T(8,128)(2,1)S(1)} %get-tuple-element.54), channel_id=1, source_target_pairs={{0,12},{1,13},{2,14},{3,15},{4,0},{5,1},{6,2},{7,3},{8,4},{9,5},{1... | collective-permute-start | bytes 786440 | tf_op jit(solution)/shard_map/ppermute | solution.py:289
  34.8 13.9 %collective-permute-start.8 = (bf16[128,512]{1,0:T(8,128)(2,1)S(1)}, bf16[128,512]{1,0:T(8,128)(2,1)S(1)}, u32[]{:S(2)}, u32[]{:S(2)}) collective-permute-start(bf16[128,512]{1,0:T(8,128)(2,1)S(1)} %get-tuple-element.45), channel_id=1, source_target_pairs={{0,1},{1,0},{2,3},{3,2},{4,5},{5,4},{6,7},{7,6},{8,9},{9,8},{10,11... | collective-permute-start | bytes 393224 | tf_op jit(solution)/shard_map/ppermute | solution.py:289
  35.2 13.6 %collective-permute-start.9 = (bf16[128,512]{1,0:T(8,128)(2,1)S(1)}, bf16[128,512]{1,0:T(8,128)(2,1)S(1)}, u32[]{:S(2)}, u32[]{:S(2)}) collective-permute-start(bf16[128,512]{1,0:T(8,128)(2,1)S(1)} %get-tuple-element.46), channel_id=1, source_target_pairs={{0,2},{1,3},{2,0},{3,1},{4,6},{5,7},{6,4},{7,5},{8,10},{9,11},{10,... | collective-permute-start | bytes 393224 | tf_op jit(solution)/shard_map/ppermute | solution.py:289
  36.5 14.7 %collective-permute-start.10 = (bf16[128,512]{1,0:T(8,128)(2,1)S(1)}, bf16[128,512]{1,0:T(8,128)(2,1)S(1)}, u32[]{:S(2)}, u32[]{:S(2)}) collective-permute-start(bf16[128,512]{1,0:T(8,128)(2,1)S(1)} %get-tuple-element.47), channel_id=1, source_target_pairs={{0,3},{1,2},{2,1},{3,0},{4,7},{5,6},{6,5},{7,4},{8,11},{9,10},{10,... | collective-permute-start | bytes 393224 | tf_op jit(solution)/shard_map/ppermute | solution.py:289
  37.3 4.7 %collective-permute-start.11 = (bf16[256,128]{1,0:T(8,128)(2,1)S(1)}, bf16[256,128]{1,0:T(8,128)(2,1)S(1)}, u32[]{:S(2)}, u32[]{:S(2)}) collective-permute-start(bf16[256,128]{1,0:T(8,128)(2,1)S(1)} %get-tuple-element.51), channel_id=1, source_target_pairs={{0,1},{1,0},{2,3},{3,2},{4,5},{5,4},{6,7},{7,6},{8,9},{9,8},{10,11... | collective-permute-start | bytes 196616 | tf_op jit(solution)/shard_map/ppermute | solution.py:289
  40.2 4.8 %collective-permute-start.12 = (bf16[256,128]{1,0:T(8,128)(2,1)S(1)}, bf16[256,128]{1,0:T(8,128)(2,1)S(1)}, u32[]{:S(2)}, u32[]{:S(2)}) collective-permute-start(bf16[256,128]{1,0:T(8,128)(2,1)S(1)} %get-tuple-element.52), channel_id=1, source_target_pairs={{0,2},{1,3},{2,0},{3,1},{4,6},{5,7},{6,4},{7,5},{8,10},{9,11},{10,... | collective-permute-start | bytes 196616 | tf_op jit(solution)/shard_map/ppermute | solution.py:289
  42.1 10.6 %collective-permute-start.13 = (bf16[256,128]{1,0:T(8,128)(2,1)S(1)}, bf16[256,128]{1,0:T(8,128)(2,1)S(1)}, u32[]{:S(2)}, u32[]{:S(2)}) collective-permute-start(bf16[256,128]{1,0:T(8,128)(2,1)S(1)} %get-tuple-element.53), channel_id=1, source_target_pairs={{0,3},{1,2},{2,1},{3,0},{4,7},{5,6},{6,5},{7,4},{8,11},{9,10},{10,... | collective-permute-start | bytes 196616 | tf_op jit(solution)/shard_map/ppermute | solution.py:289
  45.0 7.6 %collective-permute-start.15 = (bf16[256,128]{1,0:T(8,128)(2,1)S(1)}, bf16[256,128]{1,0:T(8,128)(2,1)S(1)}, u32[]{:S(2)}, u32[]{:S(2)}) collective-permute-start(bf16[256,128]{1,0:T(8,128)(2,1)S(1)} %get-tuple-element.56), channel_id=1, source_target_pairs={{0,12},{1,13},{2,14},{3,15},{4,0},{5,1},{6,2},{7,3},{8,4},{9,5},{1... | collective-permute-start | bytes 196616 | tf_op jit(solution)/shard_map/ppermute | solution.py:289
  48.7 3.9 %collective-permute-start.16 = (bf16[256,128]{1,0:T(8,128)(2,1)S(1)}, bf16[256,128]{1,0:T(8,128)(2,1)S(1)}, u32[]{:S(2)}, u32[]{:S(2)}) collective-permute-start(bf16[256,128]{1,0:T(8,128)(2,1)S(1)} %get-tuple-element.57), channel_id=1, source_target_pairs={{0,13},{1,12},{2,15},{3,14},{4,1},{5,0},{6,3},{7,2},{8,5},{9,4},{1... | collective-permute-start | bytes 196616 | tf_op jit(solution)/shard_map/ppermute | solution.py:289
  48.7 5.2 %collective-permute-start.17 = (bf16[256,128]{1,0:T(8,128)(2,1)S(1)}, bf16[256,128]{1,0:T(8,128)(2,1)S(1)}, u32[]{:S(2)}, u32[]{:S(2)}) collective-permute-start(bf16[256,128]{1,0:T(8,128)(2,1)S(1)} %get-tuple-element.58), channel_id=1, source_target_pairs={{0,14},{1,15},{2,12},{3,13},{4,2},{5,3},{6,0},{7,1},{8,6},{9,7},{1... | collective-permute-start | bytes 196616 | tf_op jit(solution)/shard_map/ppermute | solution.py:289
  51.2 5.3 %collective-permute-start.18 = (bf16[256,128]{1,0:T(8,128)(2,1)S(1)}, bf16[256,128]{1,0:T(8,128)(2,1)S(1)}, u32[]{:S(2)}, u32[]{:S(2)}) collective-permute-start(bf16[256,128]{1,0:T(8,128)(2,1)S(1)} %get-tuple-element.59), channel_id=1, source_target_pairs={{0,15},{1,14},{2,13},{3,12},{4,3},{5,2},{6,1},{7,0},{8,7},{9,6},{1... | collective-permute-start | bytes 196616 | tf_op jit(solution)/shard_map/ppermute | solution.py:289

commit v4 on v3

--- a/solution.py
+++ b/solution.py
@@ -74,7 +74,7 @@
         copy.wait()
 
 
-def pack_queries(rows, place, query_ref, grad_ref, output_ref, norm_ref, *rest):
+def pack_queries(rows, place, query_ref, grad_ref, output_ref, norm_ref, doc_ref, *rest):
     outs, (token, grads, outputs, stats, sems, more_sems) = rest[:-6], rest[-6:]
     first = pltpu.make_async_copy(grad_ref, grads, more_sems.at[0])
     second = pltpu.make_async_copy(output_ref, outputs, more_sems.at[1])
@@ -102,7 +102,9 @@
     for g in range(KEY_VALUE_HEADS):
         stats[g, 0:GROUP, :] = norm_ref[g * GROUP : (g + 1) * GROUP, :]
         stats[g, GROUP : 2 * GROUP, :] = delta[g * GROUP : (g + 1) * GROUP, :]
+    docs = jnp.broadcast_to((doc_ref[...] + 1).astype(F32), (EXTRA, rows)).astype(BF16)
     for s, out in enumerate(outs):
+        out[2 * GROUP * rows + 3 * EXTRA :, 0:rows] = docs
         left = stats[place[1] ^ s]
         for part in range(3):
             term = left.astype(BF16)
@@ -130,55 +132,64 @@
 def attend_scratch(rows):
     parts = KEY_VALUE_HEADS
     return [
-        pltpu.VMEM((parts, HEAD_SIZE, GROUP * rows), F32),
         pltpu.VMEM((2 * parts * rows, HEAD_SIZE), F32),
         pltpu.VMEM((HEAD_SIZE, parts * rows), BF16),
         pltpu.VMEM((parts * rows, rows), F32),
-        pltpu.SMEM((2 * parts,), F32),
     ]
 
 
 def attend(rows, offset, reach, first, last, place, *refs):
     parts = KEY_VALUE_HEADS
     queries, refs = refs[:parts], refs[parts:]
-    own, key_ref, refs = refs[0], refs[1], refs[2:]
+    key_ref, refs = refs[0], refs[1:]
     if not first:
         dq_in, refs = refs[0], refs[1:]
     if last:
         dq_out, refs = refs[:parts], refs[parts:]
     else:
         dq_out, refs = refs[0], refs[1:]
-    kv_out, dq, dkv, key_t, docs_t, docs_s = refs
+    kv_out, dkv, key_t, docs_t = refs
     row, me = place[0], place[1]
     width = GROUP * rows
     span = parts * rows
-    for a in range(parts):
-        docs = own[2 * span + a * EXTRA : 2 * span + a * EXTRA + 1, 0:rows].astype(F32)
-        docs_s[a] = jnp.min(docs)
-    dq[...] = jnp.zeros_like(dq)
+
+    def ids(ref, start, stop):
+        return ref[2 * span + start * EXTRA : 2 * span + stop * EXTRA, 0:rows].astype(F32)
+
+    ends = [jnp.max(ids(key_ref, k * parts // 2, (k + 1) * parts // 2)) for k in range(2)]
     dkv[...] = jnp.zeros_like(dkv)
-    for b in range(parts):
-        cut = slice(b * rows, (b + 1) * rows)
-        key_t[:, cut] = key_ref[cut, :].T
-        docs = key_ref[2 * span + b * EXTRA : 2 * span + b * EXTRA + 1, 0:rows].astype(F32)
-        docs_t[cut, :] = jnp.broadcast_to(docs, (rows, rows)).T
-        if (b + 1) % (parts // 2) == 0:
-            docs_s[parts + b // (parts // 2)] = jnp.max(docs)
+
+    @pl.when(row >= offset)
+    def _():
+        for b in range(parts):
+            cut = slice(b * rows, (b + 1) * rows)
+            key_t[:, cut] = key_ref[cut, :].T
+            docs_t[cut, :] = jnp.broadcast_to(ids(key_ref, b, b + 1)[0:1], (rows, rows)).T
+
+    def add_query_grad(s, term=None):
+        total = term if first else dq_in[s]
+        if not first and term is not None:
+            total = total + term
+        if last:
+            dq_out[s][...] = total.astype(BF16)
+        else:
+            dq_out[s] = total
+
     half = span // 2
     for s in range(parts):
         a = me ^ s
         near = offset * span + a * rows
-        low = (near - half + 1 < reach) & (row >= offset) & (docs_s[a] <= docs_s[parts])
-        high = (near - span + 1 < reach) & (row >= offset) & (docs_s[a] <= docs_s[parts + 1])
+        start = jnp.min(queries[s][2 * width + 3 * EXTRA :, 0:rows].astype(F32))
+        low = (near - half + 1 < reach) & (row >= offset) & (start <= ends[0])
+        high = (near - span + 1 < reach) & (row >= offset) & (start <= ends[1])
         if offset == 0:
             high = high & (a * rows + rows > half)
 
         def block(start, stop, s=s, a=a, near=near):
-            docs = own[pl.ds(pl.multiple_of(2 * span + a * EXTRA, EXTRA), EXTRA), :]
-            docs = docs.astype(F32)[0:1, 0:rows]
+            docs = queries[s][2 * width + 3 * EXTRA :, 0:rows].astype(F32)[0:1]
             query = queries[s][0:width, :]
             grad = queries[s][width : 2 * width, :]
-            stats = queries[s][2 * width :, :].astype(F32)
+            stats = queries[s][2 * width : 2 * width + 3 * EXTRA, :].astype(F32)
             stats = stats[0:EXTRA] + stats[EXTRA : 2 * EXTRA] + stats[2 * EXTRA :]
             gap = (
                 near
@@ -206,20 +217,16 @@
             dscore = jnp.concatenate(dscores, 1)
             dkv[start:stop, :] += dot(dscore, query, ((1,), (0,)))
             dkv[span + start : span + stop, :] += dot(prob, grad, ((1,), (0,)))
-            dq[s] += dot(key_t[:, start:stop], dscore, ((1,), (0,)))
+            add_query_grad(s, dot(key_t[:, start:stop], dscore, ((1,), (0,))))
 
         pl.when(low & high)(functools.partial(block, 0, span))
         pl.when(high & ~low)(functools.partial(block, half, span))
         if offset == 0:
             pl.when(low & ~high)(functools.partial(block, 0, half))
+        else:
+            pl.when(~high)(functools.partial(add_query_grad, s))
 
     kv_out[...] = dkv[...].astype(kv_out.dtype)
-    for s in range(parts):
-        total = dq[s] if first else dq[s] + dq_in[s]
-        if last:
-            dq_out[s][...] = total.astype(BF16)
-        else:
-            dq_out[s] = total
 
 
 def add_terms(place, arrived, term, out):
@@ -288,6 +295,10 @@
         pairs = [(t, ((t + steps * parts) % count) ^ s) for t in range(count)]
         return lax.ppermute(value, "tok", pairs)
 
+    def lower(value, offset):
+        pairs = [(t, t - parts) for t in range(offset * parts, count)]
+        return lax.ppermute(value, "tok", pairs)
+
     def exchange(pieces):
         return [pieces[0]] + [move(pieces[s], 0, s) for s in range(1, parts)]
 
@@ -305,8 +316,8 @@
     pieces = exchange(pieces)
     *query_pieces, token = call(
         functools.partial(pack_queries, rows),
-        (place, queries, output_gradient, attention_output, log_sum_norm),
-        [shape((2 * width + 3 * EXTRA, HEAD_SIZE), BF16)] * parts + [TOKEN],
+        (place, queries, output_gradient, attention_output, log_sum_norm, doc_ids.reshape(1, rows)),
+        [shape((2 * width + 4 * EXTRA, HEAD_SIZE), BF16)] * parts + [TOKEN],
         scratch=[
             pltpu.VMEM(queries.shape, BF16),
             pltpu.VMEM(queries.shape, BF16),
@@ -314,7 +325,7 @@
             pltpu.SemaphoreType.DMA((parts, 2, GROUP)),
             pltpu.SemaphoreType.DMA((2,)),
         ],
-        specs=[HBM, HBM, HBM, VMEM],
+        specs=[HBM, HBM, HBM, VMEM, VMEM],
     )
     (own,) = call(
         functools.partial(join, rows),
@@ -331,7 +342,7 @@
     dq, own_pieces, sent = None, None, None
     for k, offset in enumerate(stages):
         first, last = k == 0, k == len(stages) - 1
-        ins = [place, *query_pieces, own, windows[offset]]
+        ins = [place, *query_pieces, windows[offset]]
         if not first:
             ins.append(dq)
         if last:
@@ -358,10 +369,10 @@
             )
             sent = [move(piece, -1, s) for s, piece in enumerate(got)]
         elif sent is None:
-            sent = move(term, -1)
+            sent = lower(term, offset)
         else:
             (term,) = call(add_terms, (place, sent, term), [shape(kv_shape, BF16)])
-            sent = move(term, -1)
+            sent = lower(term, offset)
 
     dq_pieces = exchange(dq)
     query_grad, token = call(

time: 58.1 us -> 61.1 us (1.052)
  starting transfers between devices: 19.4 us -> 21.4 us
  Pallas kernels: 14.5 us -> 15.5 us
    ppermute x19 -> x18, starting transfers between devices: 19.4 us -> 20.7 us  [move(): return lax.ppermute(value, 'tok', pairs)]
    pallas_call x10, Pallas kernels: 14.5 us -> 15.5 us  [call(): pl.pallas_call(kernel, out_shape=outs, in_specs=[SMEM] + specs, out_specs...]
    ppermute x0 -> x1, starting transfers between devices: none -> 0.68 us  [lower(): return lax.ppermute(value, 'tok', pairs)]
    ppermute x19 -> x18, waiting for transfers between devices: 23 us -> 22.9 us  [move(): return lax.ppermute(value, 'tok', pairs)]
  transfers between devices with their start and end apart: 19 -> 19, of which waited for: 9 -> 8; matrix products, arithmetic and copies ran while one was open for 0% -> 0% of each run, Pallas kernels for 17% -> 17%
where the time goes in v4:
time: 61.1 us; the launch traced here: 60.9 us
  waiting for transfers between devices  22.9 us (37%)
  starting transfers between devices  21.4 us (35%)
  Pallas kernels  15.5 us (25%)
  between operations  0.96 us (2%)
    ppermute x18, waiting for transfers between devices, move(): return lax.ppermute(value, 'tok', pairs)  22.9 us
    ppermute x18, starting transfers between devices, move(): return lax.ppermute(value, 'tok', pairs)  20.7 us
    pallas_call x10, Pallas kernels, call(): pl.pallas_call(kernel, out_shape=outs, in_specs=[SMEM] + specs, out_specs...  15.5 us
  transfers between devices with their start and end apart: 19, of which 8 were waited for; matrix products, arithmetic and copies ran while one was open for 0% of the time, Pallas kernels for 17%

profile of v4, /device:TPU:0, one launch (start us, length us, event | category | flops | bytes accessed | tf_op | source)
XLA Modules:
  0.0 60.9 jit_solution(3154834275711406738)
XLA Ops:
  0.7 1.5 %shard_map.95 = (bf16[264,128]{1,0:T(8,128)(2,1)S(1)}, bf16[264,128]{1,0:T(8,128)(2,1)S(1)}, bf16[264,128]{1,0:T(8,128)(2,1)S(1)}, bf16[264,128]{1,0:T(8,128)(2,1)S(1)}) custom-call(s32[2]{0:T(128)S(1)} %pad_add_fusion.place, bf16[128,512]{1,0:T(8,128)(2,1)} %key_ref.1, bf16[128,512]{1,0:T(8,128)(2,1)} %value_ref.1, s32[1,128]{1,0:T(1,128)} %bitcast.3), custom_call_target="tpu_custom_call" | custom-call | bytes 533000 | tf_op jit(solution)/shard_map/pallas_call | solution.py:42
  2.2 0.6 collective-permute-start.3
  2.8 2.6 %collective-permute-start.4 = (bf16[264,128]{1,0:T(8,128)(2,1)S(1)}, bf16[264,128]{1,0:T(8,128)(2,1)S(1)}, u32[]{:S(2)}, u32[]{:S(2)}) collective-permute-start(bf16[264,128]{1,0:T(8,128)(2,1)S(1)} %get-tuple-element.39), channel_id=1, source_target_pairs={{0,2},{1,3},{2,0},{3,1},{4,6},{5,7},{6,4},{7,5},{8,10},{9,11},{10,... | collective-permute-start | bytes 202760 | tf_op jit(solution)/shard_map/ppermute | solution.py:296
  5.4 3.0 %shard_map.94 = (bf16[1056,128]{1,0:T(8,128)(2,1)S(1)}, bf16[1056,128]{1,0:T(8,128)(2,1)S(1)}, bf16[1056,128]{1,0:T(8,128)(2,1)S(1)}, bf16[1056,128]{1,0:T(8,128)(2,1)S(1)}, f32[8,128]{1,0:T(8,128)S(1)}) custom-call(s32[2]{0:T(128)S(1)} %pad_add_fusion.place, bf16[128,2048]{1,0:T(8,128)(2,1)} %query_ref.1, bf16[128,2048]{1,0:T(8,128)(2,1)} %grad_ref.1, ...), custom_call_target="tpu_custom_call" | custom-call | bytes 2667016 | tf_op jit(solution)/shard_map/pallas_call | solution.py:42
  8.4 1.1 %collective-permute-done.5.refs_3_ = bf16[264,128]{1,0:T(8,128)(2,1)S(1)} collective-permute-done((bf16[264,128]{1,0:T(8,128)(2,1)S(1)}, bf16[264,128]{1,0:T(8,128)(2,1)S(1)}, u32[]{:S(2)}, u32[]{:S(2)}) %collective-permute-start.5) | collective-permute-done | bytes 67616 | tf_op jit(solution)/shard_map/ppermute | solution.py:296
  9.5 0.6 shard_map.96.refs_4_
  10.1 1.6 %collective-permute-start.6 = (bf16[1056,128]{1,0:T(8,128)(2,1)S(1)}, bf16[1056,128]{1,0:T(8,128)(2,1)S(1)}, u32[]{:S(2)}, u32[]{:S(2)}) collective-permute-start(bf16[1056,128]{1,0:T(8,128)(2,1)S(1)} %shard_map.96.refs_4_), channel_id=1, source_target_pairs={{0,4},{1,5},{2,6},{3,7},{4,8},{5,9},{6,10},{7,11},{8,12},{9,13},{1... | collective-permute-start | bytes 811016 | tf_op jit(solution)/shard_map/ppermute | solution.py:296
  11.7 1.3 %collective-permute-start.1 = (bf16[1056,128]{1,0:T(8,128)(2,1)S(1)}, bf16[1056,128]{1,0:T(8,128)(2,1)S(1)}, u32[]{:S(2)}, u32[]{:S(2)}) collective-permute-start(bf16[1056,128]{1,0:T(8,128)(2,1)S(1)} %get-tuple-element.35), channel_id=1, source_target_pairs={{0,2},{1,3},{2,0},{3,1},{4,6},{5,7},{6,4},{7,5},{8,10},{9,11},{10,... | collective-permute-start | bytes 811016 | tf_op jit(solution)/shard_map/ppermute | solution.py:296
  13.1 0.5 collective-permute-start.2
  13.6 7.0 %collective-permute-done.6.refs_4_ = bf16[1056,128]{1,0:T(8,128)(2,1)S(1)} collective-permute-done((bf16[1056,128]{1,0:T(8,128)(2,1)S(1)}, bf16[1056,128]{1,0:T(8,128)(2,1)S(1)}, u32[]{:S(2)}, u32[]{:S(2)}) %collective-permute-start.6) | collective-permute-done | bytes 270368 | tf_op jit(solution)/shard_map/ppermute | solution.py:296
  20.5 0.5 collective-permute-done.1.refs_2_
  21.1 4.9 %collective-permute-done.2.refs_3_ = bf16[1056,128]{1,0:T(8,128)(2,1)S(1)} collective-permute-done((bf16[1056,128]{1,0:T(8,128)(2,1)S(1)}, bf16[1056,128]{1,0:T(8,128)(2,1)S(1)}, u32[]{:S(2)}, u32[]{:S(2)}) %collective-permute-start.2) | collective-permute-done | bytes 270368 | tf_op jit(solution)/shard_map/ppermute | solution.py:296
  25.9 3.8 %shard_map.97 = (f32[4,128,512]{2,1,0:T(8,128)S(1)}, f32[1024,128]{1,0:T(8,128)S(1)}) custom-call(s32[2]{0:T(128)S(1)} %pad_add_fusion.place, bf16[1056,128]{1,0:T(8,128)(2,1)S(1)} %get-tuple-element.33.refs_0_, bf16[1056,128]{1,0:T(8,128)(2,1)S(1)} %collective-permute-done.refs_1_, bf16[1056,128]{1,0:T(8,128)(2,1)S(1)} %collective-permute-done.1.refs_2_, ...), custom_call_target="tpu_custom_call" | custom-call | flops 1342177280 | bytes 2924552 | tf_op jit(solution)/shard_map/pallas_call | solution.py:42
  29.8 0.3 collective-permute-done.7.refs_4_
  30.1 1.4 %shard_map.98 = (f32[4,128,512]{2,1,0:T(8,128)S(1)}, bf16[1024,128]{1,0:T(8,128)(2,1)S(1)}) custom-call(s32[2]{0:T(128)S(1)} %pad_add_fusion.place, bf16[1056,128]{1,0:T(8,128)(2,1)S(1)} %get-tuple-element.33.refs_0_, bf16[1056,128]{1,0:T(8,128)(2,1)S(1)} %collective-permute-done.refs_1_, bf16[1056,128]{1,0:T(8,128)(2,1)S(1)} %collective-permute-done.1.refs_2_, ...), custom_call_target="tpu_custom_call" | custom-call | flops 1342177280 | bytes 3710984 | tf_op jit(solution)/shard_map/pallas_call | solution.py:42
  31.5 0.7 %collective-permute-start.14 = (bf16[1024,128]{1,0:T(8,128)(2,1)S(1)}, bf16[1024,128]{1,0:T(8,128)(2,1)S(1)}, u32[]{:S(2)}, u32[]{:S(2)}) collective-permute-start(bf16[1024,128]{1,0:T(8,128)(2,1)S(1)} %get-tuple-element.54), channel_id=1, source_target_pairs={{8,4},{9,5},{10,6},{11,7},{12,8},{13,9},{14,10},{15,11},{24,20},{2... | collective-permute-start | bytes 786440 | tf_op jit(solution)/shard_map/ppermute | solution.py:300
  32.2 1.3 %shard_map.99 = (bf16[128,512]{1,0:T(8,128)(2,1)S(1)}, bf16[128,512]{1,0:T(8,128)(2,1)S(1)}, bf16[128,512]{1,0:T(8,128)(2,1)S(1)}, bf16[128,512]{1,0:T(8,128)(2,1)S(1)}, f32[1024,128]{1,0:T(8,128)S(1)}) custom-call(s32[2]{0:T(128)S(1)} %pad_add_fusion.place, bf16[1056,128]{1,0:T(8,128)(2,1)S(1)} %get-tuple-element.33.refs_0_, ...), custom_call_target="tpu_custom_call" | custom-call | flops 1342177280 | bytes 3448840 | tf_op jit(solution)/shard_map/pallas_call | solution.py:42
  33.5 0.4 collective-permute-start.8
  33.8 1.5 %collective-permute-start.9 = (bf16[128,512]{1,0:T(8,128)(2,1)S(1)}, bf16[128,512]{1,0:T(8,128)(2,1)S(1)}, u32[]{:S(2)}, u32[]{:S(2)}) collective-permute-start(bf16[128,512]{1,0:T(8,128)(2,1)S(1)} %get-tuple-element.46), channel_id=1, source_target_pairs={{0,2},{1,3},{2,0},{3,1},{4,6},{5,7},{6,4},{7,5},{8,10},{9,11},{10,... | collective-permute-start | bytes 393224 | tf_op jit(solution)/shard_map/ppermute | solution.py:296
  35.4 0.6 shard_map.101
  36.0 0.6 %collective-permute-start.11 = (bf16[256,128]{1,0:T(8,128)(2,1)S(1)}, bf16[256,128]{1,0:T(8,128)(2,1)S(1)}, u32[]{:S(2)}, u32[]{:S(2)}) collective-permute-start(bf16[256,128]{1,0:T(8,128)(2,1)S(1)} %get-tuple-element.51), channel_id=1, source_target_pairs={{0,1},{1,0},{2,3},{3,2},{4,5},{5,4},{6,7},{7,6},{8,9},{9,8},{10,11... | collective-permute-start | bytes 196616 | tf_op jit(solution)/shard_map/ppermute | solution.py:296
  36.6 1.5 %collective-permute-start.12 = (bf16[256,128]{1,0:T(8,128)(2,1)S(1)}, bf16[256,128]{1,0:T(8,128)(2,1)S(1)}, u32[]{:S(2)}, u32[]{:S(2)}) collective-permute-start(bf16[256,128]{1,0:T(8,128)(2,1)S(1)} %get-tuple-element.52), channel_id=1, source_target_pairs={{0,2},{1,3},{2,0},{3,1},{4,6},{5,7},{6,4},{7,5},{8,10},{9,11},{10,... | collective-permute-start | bytes 196616 | tf_op jit(solution)/shard_map/ppermute | solution.py:296
  38.1 0.6 shard_map.102
  38.7 0.2 collective-permute-start.13
  39.0 5.4 %collective-permute-done.12.refs_2_ = bf16[256,128]{1,0:T(8,128)(2,1)S(1)} collective-permute-done((bf16[256,128]{1,0:T(8,128)(2,1)S(1)}, bf16[256,128]{1,0:T(8,128)(2,1)S(1)}, u32[]{:S(2)}, u32[]{:S(2)}) %collective-permute-start.12) | collective-permute-done | bytes 65568 | tf_op jit(solution)/shard_map/ppermute | solution.py:296
  44.4 6.3 %collective-permute-start.15 = (bf16[256,128]{1,0:T(8,128)(2,1)S(1)}, bf16[256,128]{1,0:T(8,128)(2,1)S(1)}, u32[]{:S(2)}, u32[]{:S(2)}) collective-permute-start(bf16[256,128]{1,0:T(8,128)(2,1)S(1)} %get-tuple-element.56), channel_id=1, source_target_pairs={{0,12},{1,13},{2,14},{3,15},{4,0},{5,1},{6,2},{7,3},{8,4},{9,5},{1... | collective-permute-start | bytes 196616 | tf_op jit(solution)/shard_map/ppermute | solution.py:296
  50.7 0.5 collective-permute-start.16
  51.2 3.0 %collective-permute-start.17 = (bf16[256,128]{1,0:T(8,128)(2,1)S(1)}, bf16[256,128]{1,0:T(8,128)(2,1)S(1)}, u32[]{:S(2)}, u32[]{:S(2)}) collective-permute-start(bf16[256,128]{1,0:T(8,128)(2,1)S(1)} %get-tuple-element.58), channel_id=1, source_target_pairs={{0,14},{1,15},{2,12},{3,13},{4,2},{5,3},{6,0},{7,1},{8,6},{9,7},{1... | collective-permute-start | bytes 196616 | tf_op jit(solution)/shard_map/ppermute | solution.py:296
  54.2 1.4 %shard_map.100 = (bf16[128,2048]{1,0:T(8,128)(2,1)}, f32[8,128]{1,0:T(8,128)S(1)}) custom-call(s32[2]{0:T(128)S(1)} %pad_add_fusion.place, bf16[128,512]{1,0:T(8,128)(2,1)S(1)} %get-tuple-element.44.refs_0_, bf16[128,512]{1,0:T(8,128)(2,1)S(1)} %collective-permute-done.8.refs_1_, bf16[128,512]{1,0:T(8,128)(2,1)S(1)} %collective-permute-done.9.refs_2_, ...), custom_call_target="tpu_custom_call" | custom-call | bytes 1052680 | tf_op jit(solution)/shard_map/pallas_call | solution.py:42
  55.6 1.0 %collective-permute-done.17.refs_6_ = bf16[256,128]{1,0:T(8,128)(2,1)S(1)} collective-permute-done((bf16[256,128]{1,0:T(8,128)(2,1)S(1)}, bf16[256,128]{1,0:T(8,128)(2,1)S(1)}, u32[]{:S(2)}, u32[]{:S(2)}) %collective-permute-start.17) | collective-permute-done | bytes 65568 | tf_op jit(solution)/shard_map/ppermute | solution.py:296
  56.6 2.8 %collective-permute-done.18.refs_7_ = bf16[256,128]{1,0:T(8,128)(2,1)S(1)} collective-permute-done((bf16[256,128]{1,0:T(8,128)(2,1)S(1)}, bf16[256,128]{1,0:T(8,128)(2,1)S(1)}, u32[]{:S(2)}, u32[]{:S(2)}) %collective-permute-start.18) | collective-permute-done | bytes 65568 | tf_op jit(solution)/shard_map/ppermute | solution.py:296
  59.4 1.3 %shard_map.103 = (bf16[128,512]{1,0:T(8,128)(2,1)}, bf16[128,512]{1,0:T(8,128)(2,1)}) custom-call(s32[2]{0:T(128)S(1)} %pad_add_fusion.place, bf16[256,128]{1,0:T(8,128)(2,1)S(1)} %get-tuple-element.50.refs_0_, bf16[256,128]{1,0:T(8,128)(2,1)S(1)} %collective-permute-done.11.refs_1_, bf16[256,128]{1,0:T(8,128)(2,1)S(1)} %collective-permute-done.12.refs_2_, ...), custom_call_target="tpu_custom_call" | custom-call | bytes 790536 | tf_op jit(solution)/shard_map/pallas_call | solution.py:42
  (21 shorter events, 0.2 us)
Async XLA Ops:
  0.7 4.7 %copy-start = (f32[16,128]{1,0:T(8,128)S(1)}, f32[16,128]{1,0:T(8,128)}, u32[]{:S(2)}) copy-start(f32[16,128]{1,0:T(8,128)} %norm_ref.1) | copy-start | bytes 24580
  2.2 6.2 %collective-permute-start.3 = (bf16[264,128]{1,0:T(8,128)(2,1)S(1)}, bf16[264,128]{1,0:T(8,128)(2,1)S(1)}, u32[]{:S(2)}, u32[]{:S(2)}) collective-permute-start(bf16[264,128]{1,0:T(8,128)(2,1)S(1)} %get-tuple-element.38), channel_id=1, source_target_pairs={{0,1},{1,0},{2,3},{3,2},{4,5},{5,4},{6,7},{7,6},{8,9},{9,8},{10,11... | collective-permute-start | bytes 202760 | tf_op jit(solution)/shard_map/ppermute | solution.py:296
  2.8 2.6 %copy-start.1 = (s32[128]{0:T(128)S(1)}, s32[128]{0:T(128)}, u32[]{:S(2)}) copy-start(s32[128]{0:T(128)} %param.13) | copy-start | bytes 1540
  2.8 5.6 %collective-permute-start.4 = (bf16[264,128]{1,0:T(8,128)(2,1)S(1)}, bf16[264,128]{1,0:T(8,128)(2,1)S(1)}, u32[]{:S(2)}, u32[]{:S(2)}) collective-permute-start(bf16[264,128]{1,0:T(8,128)(2,1)S(1)} %get-tuple-element.39), channel_id=1, source_target_pairs={{0,2},{1,3},{2,0},{3,1},{4,6},{5,7},{6,4},{7,5},{8,10},{9,11},{10,... | collective-permute-start | bytes 202760 | tf_op jit(solution)/shard_map/ppermute | solution.py:296
  5.4 4.1 %collective-permute-start.5 = (bf16[264,128]{1,0:T(8,128)(2,1)S(1)}, bf16[264,128]{1,0:T(8,128)(2,1)S(1)}, u32[]{:S(2)}, u32[]{:S(2)}) collective-permute-start(bf16[264,128]{1,0:T(8,128)(2,1)S(1)} %get-tuple-element.40), channel_id=1, source_target_pairs={{0,3},{1,2},{2,1},{3,0},{4,7},{5,6},{6,5},{7,4},{8,11},{9,10},{10,... | collective-permute-start | bytes 202760 | tf_op jit(solution)/shard_map/ppermute | solution.py:296
  10.1 10.4 %collective-permute-start.6 = (bf16[1056,128]{1,0:T(8,128)(2,1)S(1)}, bf16[1056,128]{1,0:T(8,128)(2,1)S(1)}, u32[]{:S(2)}, u32[]{:S(2)}) collective-permute-start(bf16[1056,128]{1,0:T(8,128)(2,1)S(1)} %shard_map.96.refs_4_), channel_id=1, source_target_pairs={{0,4},{1,5},{2,6},{3,7},{4,8},{5,9},{6,10},{7,11},{8,12},{9,13},{1... | collective-permute-start | bytes 811016 | tf_op jit(solution)/shard_map/ppermute | solution.py:296
  11.7 8.8 %collective-permute-start = (bf16[1056,128]{1,0:T(8,128)(2,1)S(1)}, bf16[1056,128]{1,0:T(8,128)(2,1)S(1)}, u32[]{:S(2)}, u32[]{:S(2)}) collective-permute-start(bf16[1056,128]{1,0:T(8,128)(2,1)S(1)} %get-tuple-element.34), channel_id=1, source_target_pairs={{0,1},{1,0},{2,3},{3,2},{4,5},{5,4},{6,7},{7,6},{8,9},{9,8},{10,11... | collective-permute-start | bytes 811016 | tf_op jit(solution)/shard_map/ppermute | solution.py:296
  11.7 9.4 %collective-permute-start.1 = (bf16[1056,128]{1,0:T(8,128)(2,1)S(1)}, bf16[1056,128]{1,0:T(8,128)(2,1)S(1)}, u32[]{:S(2)}, u32[]{:S(2)}) collective-permute-start(bf16[1056,128]{1,0:T(8,128)(2,1)S(1)} %get-tuple-element.35), channel_id=1, source_target_pairs={{0,2},{1,3},{2,0},{3,1},{4,6},{5,7},{6,4},{7,5},{8,10},{9,11},{10,... | collective-permute-start | bytes 811016 | tf_op jit(solution)/shard_map/ppermute | solution.py:296
  13.1 12.9 %collective-permute-start.2 = (bf16[1056,128]{1,0:T(8,128)(2,1)S(1)}, bf16[1056,128]{1,0:T(8,128)(2,1)S(1)}, u32[]{:S(2)}, u32[]{:S(2)}) collective-permute-start(bf16[1056,128]{1,0:T(8,128)(2,1)S(1)} %get-tuple-element.36), channel_id=1, source_target_pairs={{0,3},{1,2},{2,1},{3,0},{4,7},{5,6},{6,5},{7,4},{8,11},{9,10},{10,... | collective-permute-start | bytes 811016 | tf_op jit(solution)/shard_map/ppermute | solution.py:296
  20.5 9.5 %collective-permute-start.7 = (bf16[1056,128]{1,0:T(8,128)(2,1)S(1)}, bf16[1056,128]{1,0:T(8,128)(2,1)S(1)}, u32[]{:S(2)}, u32[]{:S(2)}) collective-permute-start(bf16[1056,128]{1,0:T(8,128)(2,1)S(1)} %collective-permute-done.6.refs_4_), channel_id=1, source_target_pairs={{0,4},{1,5},{2,6},{3,7},{4,8},{5,9},{6,10},{7,11},{8,12},{9,13},{1... | collective-permute-start | bytes 811016 | tf_op jit(solution)/shard_map/ppermute | solution.py:296
  31.5 5.1 %collective-permute-start.14 = (bf16[1024,128]{1,0:T(8,128)(2,1)S(1)}, bf16[1024,128]{1,0:T(8,128)(2,1)S(1)}, u32[]{:S(2)}, u32[]{:S(2)}) collective-permute-start(bf16[1024,128]{1,0:T(8,128)(2,1)S(1)} %get-tuple-element.54), channel_id=1, source_target_pairs={{8,4},{9,5},{10,6},{11,7},{12,8},{13,9},{14,10},{15,11},{24,20},{2... | collective-permute-start | bytes 786440 | tf_op jit(solution)/shard_map/ppermute | solution.py:300
  33.5 17.2 %collective-permute-start.8 = (bf16[128,512]{1,0:T(8,128)(2,1)S(1)}, bf16[128,512]{1,0:T(8,128)(2,1)S(1)}, u32[]{:S(2)}, u32[]{:S(2)}) collective-permute-start(bf16[128,512]{1,0:T(8,128)(2,1)S(1)} %get-tuple-element.45), channel_id=1, source_target_pairs={{0,1},{1,0},{2,3},{3,2},{4,5},{5,4},{6,7},{7,6},{8,9},{9,8},{10,11... | collective-permute-start | bytes 393224 | tf_op jit(solution)/shard_map/ppermute | solution.py:296
  33.8 17.3 %collective-permute-start.9 = (bf16[128,512]{1,0:T(8,128)(2,1)S(1)}, bf16[128,512]{1,0:T(8,128)(2,1)S(1)}, u32[]{:S(2)}, u32[]{:S(2)}) collective-permute-start(bf16[128,512]{1,0:T(8,128)(2,1)S(1)} %get-tuple-element.46), channel_id=1, source_target_pairs={{0,2},{1,3},{2,0},{3,1},{4,6},{5,7},{6,4},{7,5},{8,10},{9,11},{10,... | collective-permute-start | bytes 393224 | tf_op jit(solution)/shard_map/ppermute | solution.py:296
  35.3 18.8 %collective-permute-start.10 = (bf16[128,512]{1,0:T(8,128)(2,1)S(1)}, bf16[128,512]{1,0:T(8,128)(2,1)S(1)}, u32[]{:S(2)}, u32[]{:S(2)}) collective-permute-start(bf16[128,512]{1,0:T(8,128)(2,1)S(1)} %get-tuple-element.47), channel_id=1, source_target_pairs={{0,3},{1,2},{2,1},{3,0},{4,7},{5,6},{6,5},{7,4},{8,11},{9,10},{10,... | collective-permute-start | bytes 393224 | tf_op jit(solution)/shard_map/ppermute | solution.py:296
  36.0 2.7 %collective-permute-start.11 = (bf16[256,128]{1,0:T(8,128)(2,1)S(1)}, bf16[256,128]{1,0:T(8,128)(2,1)S(1)}, u32[]{:S(2)}, u32[]{:S(2)}) collective-permute-start(bf16[256,128]{1,0:T(8,128)(2,1)S(1)} %get-tuple-element.51), channel_id=1, source_target_pairs={{0,1},{1,0},{2,3},{3,2},{4,5},{5,4},{6,7},{7,6},{8,9},{9,8},{10,11... | collective-permute-start | bytes 196616 | tf_op jit(solution)/shard_map/ppermute | solution.py:296
  36.6 7.7 %collective-permute-start.12 = (bf16[256,128]{1,0:T(8,128)(2,1)S(1)}, bf16[256,128]{1,0:T(8,128)(2,1)S(1)}, u32[]{:S(2)}, u32[]{:S(2)}) collective-permute-start(bf16[256,128]{1,0:T(8,128)(2,1)S(1)} %get-tuple-element.52), channel_id=1, source_target_pairs={{0,2},{1,3},{2,0},{3,1},{4,6},{5,7},{6,4},{7,5},{8,10},{9,11},{10,... | collective-permute-start | bytes 196616 | tf_op jit(solution)/shard_map/ppermute | solution.py:296
  38.7 16.9 %collective-permute-start.13 = (bf16[256,128]{1,0:T(8,128)(2,1)S(1)}, bf16[256,128]{1,0:T(8,128)(2,1)S(1)}, u32[]{:S(2)}, u32[]{:S(2)}) collective-permute-start(bf16[256,128]{1,0:T(8,128)(2,1)S(1)} %get-tuple-element.53), channel_id=1, source_target_pairs={{0,3},{1,2},{2,1},{3,0},{4,7},{5,6},{6,5},{7,4},{8,11},{9,10},{10,... | collective-permute-start | bytes 196616 | tf_op jit(solution)/shard_map/ppermute | solution.py:296
  44.4 11.3 %collective-permute-start.15 = (bf16[256,128]{1,0:T(8,128)(2,1)S(1)}, bf16[256,128]{1,0:T(8,128)(2,1)S(1)}, u32[]{:S(2)}, u32[]{:S(2)}) collective-permute-start(bf16[256,128]{1,0:T(8,128)(2,1)S(1)} %get-tuple-element.56), channel_id=1, source_target_pairs={{0,12},{1,13},{2,14},{3,15},{4,0},{5,1},{6,2},{7,3},{8,4},{9,5},{1... | collective-permute-start | bytes 196616 | tf_op jit(solution)/shard_map/ppermute | solution.py:296
  50.7 4.9 %collective-permute-start.16 = (bf16[256,128]{1,0:T(8,128)(2,1)S(1)}, bf16[256,128]{1,0:T(8,128)(2,1)S(1)}, u32[]{:S(2)}, u32[]{:S(2)}) collective-permute-start(bf16[256,128]{1,0:T(8,128)(2,1)S(1)} %get-tuple-element.57), channel_id=1, source_target_pairs={{0,13},{1,12},{2,15},{3,14},{4,1},{5,0},{6,3},{7,2},{8,5},{9,4},{1... | collective-permute-start | bytes 196616 | tf_op jit(solution)/shard_map/ppermute | solution.py:296
  51.2 5.5 %collective-permute-start.17 = (bf16[256,128]{1,0:T(8,128)(2,1)S(1)}, bf16[256,128]{1,0:T(8,128)(2,1)S(1)}, u32[]{:S(2)}, u32[]{:S(2)}) collective-permute-start(bf16[256,128]{1,0:T(8,128)(2,1)S(1)} %get-tuple-element.58), channel_id=1, source_target_pairs={{0,14},{1,15},{2,12},{3,13},{4,2},{5,3},{6,0},{7,1},{8,6},{9,7},{1... | collective-permute-start | bytes 196616 | tf_op jit(solution)/shard_map/ppermute | solution.py:296
  54.2 5.3 %collective-permute-start.18 = (bf16[256,128]{1,0:T(8,128)(2,1)S(1)}, bf16[256,128]{1,0:T(8,128)(2,1)S(1)}, u32[]{:S(2)}, u32[]{:S(2)}) collective-permute-start(bf16[256,128]{1,0:T(8,128)(2,1)S(1)} %get-tuple-element.59), channel_id=1, source_target_pairs={{0,15},{1,14},{2,13},{3,12},{4,3},{5,2},{6,1},{7,0},{8,7},{9,6},{1... | collective-permute-start | bytes 196616 | tf_op jit(solution)/shard_map/ppermute | solution.py:296

commit v5 on v3

--- a/solution.py
+++ b/solution.py
@@ -54,8 +54,8 @@
     return pl.ds(pl.multiple_of(g * HEAD_SIZE, HEAD_SIZE), HEAD_SIZE)
 
 
-def pack_keys(rows, place, key_ref, value_ref, doc_ref, *rest):
-    outs, (ids, doc_sem, sems) = rest[:-3], rest[-3:]
+def pack_keys(rows, place, key_ref, value_ref, doc_ref, grad_ref, output_ref, *rest):
+    outs, (grads, outputs, ids, doc_sem, sems, more_sems) = rest[:-6], rest[-6:]
     first = pltpu.make_async_copy(doc_ref, ids, doc_sem)
     first.start()
     copies = []
@@ -64,6 +64,8 @@
         for k, source in enumerate((key_ref, value_ref)):
             target = out.at[k * rows : (k + 1) * rows, :]
             copies.append(pltpu.make_async_copy(source.at[:, cut], target, sems.at[s, k]))
+    copies.append(pltpu.make_async_copy(grad_ref, grads, more_sems.at[0]))
+    copies.append(pltpu.make_async_copy(output_ref, outputs, more_sems.at[1]))
     for copy in copies:
         copy.start()
     first.wait()
@@ -74,24 +76,20 @@
         copy.wait()
 
 
-def pack_queries(rows, place, query_ref, grad_ref, output_ref, norm_ref, *rest):
-    outs, (token, grads, outputs, stats, sems, more_sems) = rest[:-6], rest[-6:]
-    first = pltpu.make_async_copy(grad_ref, grads, more_sems.at[0])
-    second = pltpu.make_async_copy(output_ref, outputs, more_sems.at[1])
-    first.start()
-    second.start()
+def pack_queries(rows, place, query_ref, grads, outputs, norm_ref, *rest):
+    outs, (token, stats, sems) = rest[:-3], rest[-3:]
     copies = []
     for s, out in enumerate(outs):
         for h in range(GROUP):
             cut = head_columns((place[1] ^ s) * GROUP + h)
-            for k, source in enumerate((query_ref, grad_ref)):
-                at = (k * GROUP + h) * rows
-                target = out.at[at : at + rows, :]
-                copies.append(pltpu.make_async_copy(source.at[:, cut], target, sems.at[s, k, h]))
+            target = out.at[h * rows : (h + 1) * rows, :]
+            copies.append(pltpu.make_async_copy(query_ref.at[:, cut], target, sems.at[s, h]))
     for copy in copies:
         copy.start()
-    first.wait()
-    second.wait()
+    for s, out in enumerate(outs):
+        for h in range(GROUP):
+            at = (GROUP + h) * rows
+            out[at : at + rows, :] = grads[:, head_columns((place[1] ^ s) * GROUP + h)]
     lane = lax.broadcasted_iota(jnp.int32, (rows, HEAD_SIZE), 1)
     columns = jnp.zeros((rows, HEAD_SIZE), F32)
     for h in range(QUERY_HEADS):
@@ -152,74 +150,91 @@
     row, me = place[0], place[1]
     width = GROUP * rows
     span = parts * rows
-    for a in range(parts):
-        docs = own[2 * span + a * EXTRA : 2 * span + a * EXTRA + 1, 0:rows].astype(F32)
-        docs_s[a] = jnp.min(docs)
-    dq[...] = jnp.zeros_like(dq)
-    dkv[...] = jnp.zeros_like(dkv)
-    for b in range(parts):
-        cut = slice(b * rows, (b + 1) * rows)
-        key_t[:, cut] = key_ref[cut, :].T
-        docs = key_ref[2 * span + b * EXTRA : 2 * span + b * EXTRA + 1, 0:rows].astype(F32)
-        docs_t[cut, :] = jnp.broadcast_to(docs, (rows, rows)).T
-        if (b + 1) % (parts // 2) == 0:
-            docs_s[parts + b // (parts // 2)] = jnp.max(docs)
-    half = span // 2
-    for s in range(parts):
-        a = me ^ s
-        near = offset * span + a * rows
-        low = (near - half + 1 < reach) & (row >= offset) & (docs_s[a] <= docs_s[parts])
-        high = (near - span + 1 < reach) & (row >= offset) & (docs_s[a] <= docs_s[parts + 1])
-        if offset == 0:
-            high = high & (a * rows + rows > half)
-
-        def block(start, stop, s=s, a=a, near=near):
-            docs = own[pl.ds(pl.multiple_of(2 * span + a * EXTRA, EXTRA), EXTRA), :]
-            docs = docs.astype(F32)[0:1, 0:rows]
-            query = queries[s][0:width, :]
-            grad = queries[s][width : 2 * width, :]
-            stats = queries[s][2 * width :, :].astype(F32)
-            stats = stats[0:EXTRA] + stats[EXTRA : 2 * EXTRA] + stats[2 * EXTRA :]
-            gap = (
-                near
-                - start
-                + lax.broadcasted_iota(jnp.int32, (stop - start, rows), 1)
-                - lax.broadcasted_iota(jnp.int32, (stop - start, rows), 0)
-            )
-            mask = docs_t[start:stop, :] == docs
+
+    def work():
+        for a in range(parts):
+            docs = own[2 * span + a * EXTRA : 2 * span + a * EXTRA + 1, 0:rows].astype(F32)
+            docs_s[a] = jnp.min(docs)
+        dq[...] = jnp.zeros_like(dq)
+        dkv[...] = jnp.zeros_like(dkv)
+        for b in range(parts):
+            cut = slice(b * rows, (b + 1) * rows)
+            key_t[:, cut] = key_ref[cut, :].T
+            docs = key_ref[2 * span + b * EXTRA : 2 * span + b * EXTRA + 1, 0:rows].astype(F32)
+            docs_t[cut, :] = jnp.broadcast_to(docs, (rows, rows)).T
+            if (b + 1) % (parts // 2) == 0:
+                docs_s[parts + b // (parts // 2)] = jnp.max(docs)
+        half = span // 2
+        for s in range(parts):
+            a = me ^ s
+            near = offset * span + a * rows
+            low = (near - half + 1 < reach) & (docs_s[a] <= docs_s[parts])
+            high = (near - span + 1 < reach) & (docs_s[a] <= docs_s[parts + 1])
             if offset == 0:
-                mask = mask & (gap >= 0)
-            if (offset + 1) * span > WINDOW:
-                mask = mask & (gap < WINDOW)
-            scores = dot(key_ref[start:stop, :], query, ((1,), (1,)))
-            dprob = dot(key_ref[span + start : span + stop, :], grad, ((1,), (1,)))
-            probs, dscores = [], []
-            for h in range(GROUP):
-                cut = slice(h * rows, (h + 1) * rows)
-                norm = stats[h : h + 1, :] * LOG2E
-                delta = stats[GROUP + h : GROUP + h + 1, :]
-                prob = jnp.exp2(scores[:, cut] * (SCALE * LOG2E) - norm)
-                prob = jnp.where(mask, prob, 0.0)
-                probs.append(prob.astype(BF16))
-                dscores.append((prob * (dprob[:, cut] - delta) * SCALE).astype(BF16))
-            prob = jnp.concatenate(probs, 1)
-            dscore = jnp.concatenate(dscores, 1)
-            dkv[start:stop, :] += dot(dscore, query, ((1,), (0,)))
-            dkv[span + start : span + stop, :] += dot(prob, grad, ((1,), (0,)))
-            dq[s] += dot(key_t[:, start:stop], dscore, ((1,), (0,)))
-
-        pl.when(low & high)(functools.partial(block, 0, span))
-        pl.when(high & ~low)(functools.partial(block, half, span))
-        if offset == 0:
-            pl.when(low & ~high)(functools.partial(block, 0, half))
-
-    kv_out[...] = dkv[...].astype(kv_out.dtype)
-    for s in range(parts):
-        total = dq[s] if first else dq[s] + dq_in[s]
-        if last:
-            dq_out[s][...] = total.astype(BF16)
-        else:
-            dq_out[s] = total
+                high = high & (a * rows + rows > half)
+
+            def block(start, stop, s=s, a=a, near=near):
+                docs = own[pl.ds(pl.multiple_of(2 * span + a * EXTRA, EXTRA), EXTRA), :]
+                docs = docs.astype(F32)[0:1, 0:rows]
+                query = queries[s][0:width, :]
+                grad = queries[s][width : 2 * width, :]
+                stats = queries[s][2 * width :, :].astype(F32)
+                stats = stats[0:EXTRA] + stats[EXTRA : 2 * EXTRA] + stats[2 * EXTRA :]
+                gap = (
+                    near
+                    - start
+                    + lax.broadcasted_iota(jnp.int32, (stop - start, rows), 1)
+                    - lax.broadcasted_iota(jnp.int32, (stop - start, rows), 0)
+                )
+                mask = docs_t[start:stop, :] == docs
+                if offset == 0:
+                    mask = mask & (gap >= 0)
+                if (offset + 1) * span > WINDOW:
+                    mask = mask & (gap < WINDOW)
+                scores = dot(key_ref[start:stop, :], query, ((1,), (1,)))
+                dprob = dot(key_ref[span + start : span + stop, :], grad, ((1,), (1,)))
+                probs, dscores = [], []
+                for h in range(GROUP):
+                    cut = slice(h * rows, (h + 1) * rows)
+                    norm = stats[h : h + 1, :] * LOG2E
+                    delta = stats[GROUP + h : GROUP + h + 1, :]
+                    prob = jnp.exp2(scores[:, cut] * (SCALE * LOG2E) - norm)
+                    prob = jnp.where(mask, prob, 0.0)
+                    probs.append(prob.astype(BF16))
+                    dscores.append((prob * (dprob[:, cut] - delta) * SCALE).astype(BF16))
+                prob = jnp.concatenate(probs, 1)
+                dscore = jnp.concatenate(dscores, 1)
+                dkv[start:stop, :] += dot(dscore, query, ((1,), (0,)))
+                dkv[span + start : span + stop, :] += dot(prob, grad, ((1,), (0,)))
+                dq[s] += dot(key_t[:, start:stop], dscore, ((1,), (0,)))
+
+            pl.when(low & high)(functools.partial(block, 0, span))
+            pl.when(high & ~low)(functools.partial(block, half, span))
+            if offset == 0:
+                pl.when(low & ~high)(functools.partial(block, 0, half))
+
+        kv_out[...] = dkv[...].astype(kv_out.dtype)
+        for s in range(parts):
+            total = dq[s] if first else dq[s] + dq_in[s]
+            if last:
+                dq_out[s][...] = total.astype(BF16)
+            else:
+                dq_out[s] = total
+
+    if first:
+        work()
+        return
+
+    @pl.when(row < offset)
+    def _():
+        kv_out[...] = jnp.zeros_like(kv_out)
+        for s in range(parts):
+            if last:
+                dq_out[s][...] = dq_in[s].astype(BF16)
+            else:
+                dq_out[s] = dq_in[s]
+
+    pl.when(row >= offset)(work)
 
 
 def add_terms(place, arrived, term, out):
@@ -291,30 +306,28 @@
     def exchange(pieces):
         return [pieces[0]] + [move(pieces[s], 0, s) for s in range(1, parts)]
 
-    pieces = call(
+    *pieces, grads, outputs = call(
         functools.partial(pack_keys, rows),
-        (place, key_matrix, value_matrix, doc_ids.reshape(1, rows)),
-        [shape((2 * rows + EXTRA, HEAD_SIZE), BF16)] * parts,
+        (place, key_matrix, value_matrix, doc_ids.reshape(1, rows), output_gradient, attention_output),
+        [shape((2 * rows + EXTRA, HEAD_SIZE), BF16)] * parts + [shape(queries.shape, BF16)] * 2,
         scratch=[
             pltpu.VMEM((1, rows), jnp.int32),
             pltpu.SemaphoreType.DMA(()),
             pltpu.SemaphoreType.DMA((parts, 2)),
+            pltpu.SemaphoreType.DMA((2,)),
         ],
-        specs=[HBM, HBM, HBM],
+        specs=[HBM] * 5,
     )
     pieces = exchange(pieces)
     *query_pieces, token = call(
         functools.partial(pack_queries, rows),
-        (place, queries, output_gradient, attention_output, log_sum_norm),
+        (place, queries, grads, outputs, log_sum_norm),
         [shape((2 * width + 3 * EXTRA, HEAD_SIZE), BF16)] * parts + [TOKEN],
         scratch=[
-            pltpu.VMEM(queries.shape, BF16),
-            pltpu.VMEM(queries.shape, BF16),
             pltpu.VMEM((parts, 2 * GROUP, rows), F32),
-            pltpu.SemaphoreType.DMA((parts, 2, GROUP)),
-            pltpu.SemaphoreType.DMA((2,)),
+            pltpu.SemaphoreType.DMA((parts, GROUP)),
         ],
-        specs=[HBM, HBM, HBM, VMEM],
+        specs=[HBM, VMEM, VMEM, VMEM],
     )
     (own,) = call(
         functools.partial(join, rows),

time: 58.1 us -> 58.5 us (level)
  Pallas kernels: 14.5 us -> 13.4 us
  waiting for transfers between devices: 23 us -> 24 us
    pallas_call x10, Pallas kernels: 14.5 us -> 13.4 us  [call(): pl.pallas_call(kernel, out_shape=outs, in_specs=[SMEM] + specs, out_specs...]
    ppermute x19, waiting for transfers between devices: 23 us -> 24 us  [move(): return lax.ppermute(value, 'tok', pairs)]
  transfers between devices with their start and end apart: 19 -> 19, of which waited for: 9 -> 10; matrix products, arithmetic and copies ran while one was open for 0% -> 0% of each run, Pallas kernels for 17% -> 15%
where the time goes in v5:
time: 58.5 us; the launch traced here: 58.2 us
  waiting for transfers between devices  24 us (41%)
  starting transfers between devices  19.8 us (34%)
  Pallas kernels  13.4 us (23%)
  between operations  0.96 us (2%)
    ppermute x19, waiting for transfers between devices, move(): return lax.ppermute(value, 'tok', pairs)  24 us
    ppermute x19, starting transfers between devices, move(): return lax.ppermute(value, 'tok', pairs)  19.8 us
    pallas_call x10, Pallas kernels, call(): pl.pallas_call(kernel, out_shape=outs, in_specs=[SMEM] + specs, out_specs...  13.4 us
  transfers between devices with their start and end apart: 19, of which 10 were waited for; matrix products, arithmetic and copies ran while one was open for 0% of the time, Pallas kernels for 15%

profile of v5, /device:TPU:0, one launch (start us, length us, event | category | flops | bytes accessed | tf_op | source)
XLA Modules:
  0.0 58.2 jit_solution(3445876219131883952)
XLA Ops:
  0.7 2.0 %shard_map.94 = (bf16[264,128]{1,0:T(8,128)(2,1)S(1)}, bf16[264,128]{1,0:T(8,128)(2,1)S(1)}, bf16[264,128]{1,0:T(8,128)(2,1)S(1)}, bf16[264,128]{1,0:T(8,128)(2,...) custom-call(s32[2]{0:T(128)S(1)} %pad_add_fusion.place, bf16[128,512]{1,0:T(8,128)(2,1)} %key_ref.1, ...), custom_call_target="tpu_custom_call" | custom-call | bytes 2630152 | tf_op jit(solution)/shard_map/pallas_call | solution.py:42
  2.7 0.6 collective-permute-start.3
  3.3 2.6 %collective-permute-start.4 = (bf16[264,128]{1,0:T(8,128)(2,1)S(1)}, bf16[264,128]{1,0:T(8,128)(2,1)S(1)}, u32[]{:S(2)}, u32[]{:S(2)}) collective-permute-start(bf16[264,128]{1,0:T(8,128)(2,1)S(1)} %get-tuple-element.43), channel_id=1, source_target_pairs={{0,2},{1,3},{2,0},{3,1},{4,6},{5,7},{6,4},{7,5},{8,10},{9,11},{10,... | collective-permute-start | bytes 202760 | tf_op jit(solution)/shard_map/ppermute | solution.py:304
  5.9 2.0 %shard_map.95 = (bf16[1048,128]{1,0:T(8,128)(2,1)S(1)}, bf16[1048,128]{1,0:T(8,128)(2,1)S(1)}, bf16[1048,128]{1,0:T(8,128)(2,1)S(1)}, bf16[1048,128]{1,0:T(8,128)(2,1)S(1)}, f32[8,128]{1,0:T(8,128)S(1)}) custom-call(s32[2]{0:T(128)S(1)} %pad_add_fusion.place, bf16[128,2048]{1,0:T(8,128)(2,1)} %query_ref.1, bf16[128,2048]{1,0:T(8,128)(2,1)S(1)} %get-tuple-element.35.grads, ...), custom_call_target="tpu_custom_call" | custom-call | bytes 2658312 | tf_op jit(solution)/shard_map/pallas_call | solution.py:42
  7.9 0.7 %collective-permute-done.4.refs_2_ = bf16[264,128]{1,0:T(8,128)(2,1)S(1)} collective-permute-done((bf16[264,128]{1,0:T(8,128)(2,1)S(1)}, bf16[264,128]{1,0:T(8,128)(2,1)S(1)}, u32[]{:S(2)}, u32[]{:S(2)}) %collective-permute-start.4) | collective-permute-done | bytes 67616 | tf_op jit(solution)/shard_map/ppermute | solution.py:304
  8.6 1.4 %collective-permute-done.5.refs_3_ = bf16[264,128]{1,0:T(8,128)(2,1)S(1)} collective-permute-done((bf16[264,128]{1,0:T(8,128)(2,1)S(1)}, bf16[264,128]{1,0:T(8,128)(2,1)S(1)}, u32[]{:S(2)}, u32[]{:S(2)}) %collective-permute-start.5) | collective-permute-done | bytes 67616 | tf_op jit(solution)/shard_map/ppermute | solution.py:304
  10.0 0.6 shard_map.96.refs_4_.refs_5_
  10.6 1.6 %collective-permute-start.6 = (bf16[1056,128]{1,0:T(8,128)(2,1)S(1)}, bf16[1056,128]{1,0:T(8,128)(2,1)S(1)}, u32[]{:S(2)}, u32[]{:S(2)}) collective-permute-start(bf16[1056,128]{1,0:T(8,128)(2,1)S(1)} %shard_map.96.refs_4_.refs_5_), channel_id=1, source_target_pairs={{0,4},{1,5},{2,6},{3,7},{4,8},{5,9},{6,10},{7,11},{8,12},{9,13},{1... | collective-permute-start | bytes 811016 | tf_op jit(solution)/shard_map/ppermute | solution.py:304
  12.2 1.4 %collective-permute-start.1 = (bf16[1048,128]{1,0:T(8,128)(2,1)S(1)}, bf16[1048,128]{1,0:T(8,128)(2,1)S(1)}, u32[]{:S(2)}, u32[]{:S(2)}) collective-permute-start(bf16[1048,128]{1,0:T(8,128)(2,1)S(1)} %get-tuple-element.39), channel_id=1, source_target_pairs={{0,2},{1,3},{2,0},{3,1},{4,6},{5,7},{6,4},{7,5},{8,10},{9,11},{10,... | collective-permute-start | bytes 804872 | tf_op jit(solution)/shard_map/ppermute | solution.py:304
  13.5 0.5 collective-permute-start.2
  14.0 7.0 %collective-permute-done.6.refs_5_ = bf16[1056,128]{1,0:T(8,128)(2,1)S(1)} collective-permute-done((bf16[1056,128]{1,0:T(8,128)(2,1)S(1)}, bf16[1056,128]{1,0:T(8,128)(2,1)S(1)}, u32[]{:S(2)}, u32[]{:S(2)}) %collective-permute-start.6) | collective-permute-done | bytes 270368 | tf_op jit(solution)/shard_map/ppermute | solution.py:304
  21.0 0.5 collective-permute-done.1.refs_2_
  21.5 4.8 %collective-permute-done.2.refs_3_ = bf16[1048,128]{1,0:T(8,128)(2,1)S(1)} collective-permute-done((bf16[1048,128]{1,0:T(8,128)(2,1)S(1)}, bf16[1048,128]{1,0:T(8,128)(2,1)S(1)}, u32[]{:S(2)}, u32[]{:S(2)}) %collective-permute-start.2) | collective-permute-done | bytes 268320 | tf_op jit(solution)/shard_map/ppermute | solution.py:304
  26.3 3.4 %shard_map.97 = (f32[4,128,512]{2,1,0:T(8,128)S(1)}, f32[1024,128]{1,0:T(8,128)S(1)}) custom-call(s32[2]{0:T(128)S(1)} %pad_add_fusion.place, bf16[1048,128]{1,0:T(8,128)(2,1)S(1)} %get-tuple-element.37.refs_0_, bf16[1048,128]{1,0:T(8,128)(2,1)S(1)} %collective-permute-done.refs_1_, bf16[1048,128]{1,0:T(8,128)(2,1)S(1)} %collective-permute-done.1.refs_2_, ...), custom_call_target="tpu_custom_call" | custom-call | flops 1342177280 | bytes 3186696 | tf_op jit(solution)/shard_map/pallas_call | solution.py:42
  29.8 0.8 %collective-permute-done.7.refs_5_ = bf16[1056,128]{1,0:T(8,128)(2,1)S(1)} collective-permute-done((bf16[1056,128]{1,0:T(8,128)(2,1)S(1)}, bf16[1056,128]{1,0:T(8,128)(2,1)S(1)}, u32[]{:S(2)}, u32[]{:S(2)}) %collective-permute-start.7) | collective-permute-done | bytes 270368 | tf_op jit(solution)/shard_map/ppermute | solution.py:304
  30.6 0.8 %shard_map.98 = (f32[4,128,512]{2,1,0:T(8,128)S(1)}, bf16[1024,128]{1,0:T(8,128)(2,1)S(1)}) custom-call(s32[2]{0:T(128)S(1)} %pad_add_fusion.place, bf16[1048,128]{1,0:T(8,128)(2,1)S(1)} %get-tuple-element.37.refs_0_, bf16[1048,128]{1,0:T(8,128)(2,1)S(1)} %collective-permute-done.refs_1_, bf16[1048,128]{1,0:T(8,128)(2,1)S(1)} %collective-permute-done.1.refs_2_, ...), custom_call_target="tpu_custom_call" | custom-call | flops 1342177280 | bytes 3973128 | tf_op jit(solution)/shard_map/pallas_call | solution.py:42
  31.4 3.0 %collective-permute-start.14 = (bf16[1024,128]{1,0:T(8,128)(2,1)S(1)}, bf16[1024,128]{1,0:T(8,128)(2,1)S(1)}, u32[]{:S(2)}, u32[]{:S(2)}) collective-permute-start(bf16[1024,128]{1,0:T(8,128)(2,1)S(1)} %get-tuple-element.58), channel_id=1, source_target_pairs={{0,12},{1,13},{2,14},{3,15},{4,0},{5,1},{6,2},{7,3},{8,4},{9,5},{1... | collective-permute-start | bytes 786440 | tf_op jit(solution)/shard_map/ppermute | solution.py:304
  34.4 0.6 %shard_map.99 = (bf16[128,512]{1,0:T(8,128)(2,1)S(1)}, bf16[128,512]{1,0:T(8,128)(2,1)S(1)}, bf16[128,512]{1,0:T(8,128)(2,1)S(1)}, bf16[128,512]{1,0:T(8,128)(2,1)S(1)}, f32[1024,128]{1,0:T(8,128)S(1)}) custom-call(s32[2]{0:T(128)S(1)} %pad_add_fusion.place, bf16[1048,128]{1,0:T(8,128)(2,1)S(1)} %get-tuple-element.37.refs_0_, ...), custom_call_target="tpu_custom_call" | custom-call | flops 1342177280 | bytes 3710984 | tf_op jit(solution)/shard_map/pallas_call | solution.py:42
  35.0 0.4 collective-permute-start.8
  35.4 1.3 %collective-permute-start.9 = (bf16[128,512]{1,0:T(8,128)(2,1)S(1)}, bf16[128,512]{1,0:T(8,128)(2,1)S(1)}, u32[]{:S(2)}, u32[]{:S(2)}) collective-permute-start(bf16[128,512]{1,0:T(8,128)(2,1)S(1)} %get-tuple-element.50), channel_id=1, source_target_pairs={{0,2},{1,3},{2,0},{3,1},{4,6},{5,7},{6,4},{7,5},{8,10},{9,11},{10,... | collective-permute-start | bytes 393224 | tf_op jit(solution)/shard_map/ppermute | solution.py:304
  36.9 0.6 shard_map.101
  37.5 0.6 %collective-permute-start.11 = (bf16[256,128]{1,0:T(8,128)(2,1)S(1)}, bf16[256,128]{1,0:T(8,128)(2,1)S(1)}, u32[]{:S(2)}, u32[]{:S(2)}) collective-permute-start(bf16[256,128]{1,0:T(8,128)(2,1)S(1)} %get-tuple-element.55), channel_id=1, source_target_pairs={{0,1},{1,0},{2,3},{3,2},{4,5},{5,4},{6,7},{7,6},{8,9},{9,8},{10,11... | collective-permute-start | bytes 196616 | tf_op jit(solution)/shard_map/ppermute | solution.py:304
  38.2 2.5 %collective-permute-done.14.refs_0_ = bf16[1024,128]{1,0:T(8,128)(2,1)S(1)} collective-permute-done((bf16[1024,128]{1,0:T(8,128)(2,1)S(1)}, bf16[1024,128]{1,0:T(8,128)(2,1)S(1)}, u32[]{:S(2)}, u32[]{:S(2)}) %collective-permute-start.14) | collective-permute-done | bytes 262176 | tf_op jit(solution)/shard_map/ppermute | solution.py:304
  40.7 1.3 %collective-permute-start.12 = (bf16[256,128]{1,0:T(8,128)(2,1)S(1)}, bf16[256,128]{1,0:T(8,128)(2,1)S(1)}, u32[]{:S(2)}, u32[]{:S(2)}) collective-permute-start(bf16[256,128]{1,0:T(8,128)(2,1)S(1)} %get-tuple-element.56), channel_id=1, source_target_pairs={{0,2},{1,3},{2,0},{3,1},{4,6},{5,7},{6,4},{7,5},{8,10},{9,11},{10,... | collective-permute-start | bytes 196616 | tf_op jit(solution)/shard_map/ppermute | solution.py:304
  42.0 0.6 %shard_map.102 = (bf16[256,128]{1,0:T(8,128)(2,1)S(1)}, bf16[256,128]{1,0:T(8,128)(2,1)S(1)}, bf16[256,128]{1,0:T(8,128)(2,1)S(1)}, bf16[256,128]{1,0:T(8,128)(2,1)S(1)}) custom-call(s32[2]{0:T(128)S(1)} %pad_add_fusion.place, bf16[1024,128]{1,0:T(8,128)(2,1)S(1)} %collective-permute-done.14.refs_0_, f32[1024,128]{1,0:T(8,128)S(1)} %get-tuple-element.59.refs_1_), custom_call_target="tpu_custom_call" | custom-call | bytes 1048584 | tf_op jit(solution)/shard_map/pallas_call | solution.py:42
  42.7 2.6 %collective-permute-done.12.refs_2_ = bf16[256,128]{1,0:T(8,128)(2,1)S(1)} collective-permute-done((bf16[256,128]{1,0:T(8,128)(2,1)S(1)}, bf16[256,128]{1,0:T(8,128)(2,1)S(1)}, u32[]{:S(2)}, u32[]{:S(2)}) %collective-permute-start.12) | collective-permute-done | bytes 65568 | tf_op jit(solution)/shard_map/ppermute | solution.py:304
  45.2 4.0 %collective-permute-start.15 = (bf16[256,128]{1,0:T(8,128)(2,1)S(1)}, bf16[256,128]{1,0:T(8,128)(2,1)S(1)}, u32[]{:S(2)}, u32[]{:S(2)}) collective-permute-start(bf16[256,128]{1,0:T(8,128)(2,1)S(1)} %get-tuple-element.60), channel_id=1, source_target_pairs={{0,12},{1,13},{2,14},{3,15},{4,0},{5,1},{6,2},{7,3},{8,4},{9,5},{1... | collective-permute-start | bytes 196616 | tf_op jit(solution)/shard_map/ppermute | solution.py:304
  49.2 2.2 %collective-permute-start.17 = (bf16[256,128]{1,0:T(8,128)(2,1)S(1)}, bf16[256,128]{1,0:T(8,128)(2,1)S(1)}, u32[]{:S(2)}, u32[]{:S(2)}) collective-permute-start(bf16[256,128]{1,0:T(8,128)(2,1)S(1)} %get-tuple-element.62), channel_id=1, source_target_pairs={{0,14},{1,15},{2,12},{3,13},{4,2},{5,3},{6,0},{7,1},{8,6},{9,7},{1... | collective-permute-start | bytes 196616 | tf_op jit(solution)/shard_map/ppermute | solution.py:304
  51.5 1.4 %shard_map.100 = (bf16[128,2048]{1,0:T(8,128)(2,1)}, f32[8,128]{1,0:T(8,128)S(1)}) custom-call(s32[2]{0:T(128)S(1)} %pad_add_fusion.place, bf16[128,512]{1,0:T(8,128)(2,1)S(1)} %get-tuple-element.48.refs_0_, bf16[128,512]{1,0:T(8,128)(2,1)S(1)} %collective-permute-done.8.refs_1_, bf16[128,512]{1,0:T(8,128)(2,1)S(1)} %collective-permute-done.9.refs_2_, ...), custom_call_target="tpu_custom_call" | custom-call | bytes 1052680 | tf_op jit(solution)/shard_map/pallas_call | solution.py:42
  53.0 1.6 %collective-permute-done.17.refs_6_ = bf16[256,128]{1,0:T(8,128)(2,1)S(1)} collective-permute-done((bf16[256,128]{1,0:T(8,128)(2,1)S(1)}, bf16[256,128]{1,0:T(8,128)(2,1)S(1)}, u32[]{:S(2)}, u32[]{:S(2)}) %collective-permute-start.17) | collective-permute-done | bytes 65568 | tf_op jit(solution)/shard_map/ppermute | solution.py:304
  54.6 2.1 %collective-permute-done.18.refs_7_ = bf16[256,128]{1,0:T(8,128)(2,1)S(1)} collective-permute-done((bf16[256,128]{1,0:T(8,128)(2,1)S(1)}, bf16[256,128]{1,0:T(8,128)(2,1)S(1)}, u32[]{:S(2)}, u32[]{:S(2)}) %collective-permute-start.18) | collective-permute-done | bytes 65568 | tf_op jit(solution)/shard_map/ppermute | solution.py:304
  56.7 1.3 %shard_map.103 = (bf16[128,512]{1,0:T(8,128)(2,1)}, bf16[128,512]{1,0:T(8,128)(2,1)}) custom-call(s32[2]{0:T(128)S(1)} %pad_add_fusion.place, bf16[256,128]{1,0:T(8,128)(2,1)S(1)} %get-tuple-element.54.refs_0_, bf16[256,128]{1,0:T(8,128)(2,1)S(1)} %collective-permute-done.11.refs_1_, bf16[256,128]{1,0:T(8,128)(2,1)S(1)} %collective-permute-done.12.refs_2_, ...), custom_call_target="tpu_custom_call" | custom-call | bytes 790536 | tf_op jit(solution)/shard_map/pallas_call | solution.py:42
  (19 shorter events, 0.5 us)
Async XLA Ops:
  2.7 3.2 %copy-start = (f32[16,128]{1,0:T(8,128)S(1)}, f32[16,128]{1,0:T(8,128)}, u32[]{:S(2)}) copy-start(f32[16,128]{1,0:T(8,128)} %norm_ref.1) | copy-start | bytes 24580
  2.7 5.2 %collective-permute-start.3 = (bf16[264,128]{1,0:T(8,128)(2,1)S(1)}, bf16[264,128]{1,0:T(8,128)(2,1)S(1)}, u32[]{:S(2)}, u32[]{:S(2)}) collective-permute-start(bf16[264,128]{1,0:T(8,128)(2,1)S(1)} %get-tuple-element.42), channel_id=1, source_target_pairs={{0,1},{1,0},{2,3},{3,2},{4,5},{5,4},{6,7},{7,6},{8,9},{9,8},{10,11... | collective-permute-start | bytes 202760 | tf_op jit(solution)/shard_map/ppermute | solution.py:304
  3.3 5.3 %collective-permute-start.4 = (bf16[264,128]{1,0:T(8,128)(2,1)S(1)}, bf16[264,128]{1,0:T(8,128)(2,1)S(1)}, u32[]{:S(2)}, u32[]{:S(2)}) collective-permute-start(bf16[264,128]{1,0:T(8,128)(2,1)S(1)} %get-tuple-element.43), channel_id=1, source_target_pairs={{0,2},{1,3},{2,0},{3,1},{4,6},{5,7},{6,4},{7,5},{8,10},{9,11},{10,... | collective-permute-start | bytes 202760 | tf_op jit(solution)/shard_map/ppermute | solution.py:304
  5.9 4.1 %collective-permute-start.5 = (bf16[264,128]{1,0:T(8,128)(2,1)S(1)}, bf16[264,128]{1,0:T(8,128)(2,1)S(1)}, u32[]{:S(2)}, u32[]{:S(2)}) collective-permute-start(bf16[264,128]{1,0:T(8,128)(2,1)S(1)} %get-tuple-element.44), channel_id=1, source_target_pairs={{0,3},{1,2},{2,1},{3,0},{4,7},{5,6},{6,5},{7,4},{8,11},{9,10},{10,... | collective-permute-start | bytes 202760 | tf_op jit(solution)/shard_map/ppermute | solution.py:304
  10.6 10.5 %collective-permute-start.6 = (bf16[1056,128]{1,0:T(8,128)(2,1)S(1)}, bf16[1056,128]{1,0:T(8,128)(2,1)S(1)}, u32[]{:S(2)}, u32[]{:S(2)}) collective-permute-start(bf16[1056,128]{1,0:T(8,128)(2,1)S(1)} %shard_map.96.refs_4_.refs_5_), channel_id=1, source_target_pairs={{0,4},{1,5},{2,6},{3,7},{4,8},{5,9},{6,10},{7,11},{8,12},{9,13},{1... | collective-permute-start | bytes 811016 | tf_op jit(solution)/shard_map/ppermute | solution.py:304
  12.2 8.8 %collective-permute-start = (bf16[1048,128]{1,0:T(8,128)(2,1)S(1)}, bf16[1048,128]{1,0:T(8,128)(2,1)S(1)}, u32[]{:S(2)}, u32[]{:S(2)}) collective-permute-start(bf16[1048,128]{1,0:T(8,128)(2,1)S(1)} %get-tuple-element.38), channel_id=1, source_target_pairs={{0,1},{1,0},{2,3},{3,2},{4,5},{5,4},{6,7},{7,6},{8,9},{9,8},{10,11... | collective-permute-start | bytes 804872 | tf_op jit(solution)/shard_map/ppermute | solution.py:304
  12.2 9.3 %collective-permute-start.1 = (bf16[1048,128]{1,0:T(8,128)(2,1)S(1)}, bf16[1048,128]{1,0:T(8,128)(2,1)S(1)}, u32[]{:S(2)}, u32[]{:S(2)}) collective-permute-start(bf16[1048,128]{1,0:T(8,128)(2,1)S(1)} %get-tuple-element.39), channel_id=1, source_target_pairs={{0,2},{1,3},{2,0},{3,1},{4,6},{5,7},{6,4},{7,5},{8,10},{9,11},{10,... | collective-permute-start | bytes 804872 | tf_op jit(solution)/shard_map/ppermute | solution.py:304
  13.5 12.8 %collective-permute-start.2 = (bf16[1048,128]{1,0:T(8,128)(2,1)S(1)}, bf16[1048,128]{1,0:T(8,128)(2,1)S(1)}, u32[]{:S(2)}, u32[]{:S(2)}) collective-permute-start(bf16[1048,128]{1,0:T(8,128)(2,1)S(1)} %get-tuple-element.40), channel_id=1, source_target_pairs={{0,3},{1,2},{2,1},{3,0},{4,7},{5,6},{6,5},{7,4},{8,11},{9,10},{10,... | collective-permute-start | bytes 804872 | tf_op jit(solution)/shard_map/ppermute | solution.py:304
  21.0 9.5 %collective-permute-start.7 = (bf16[1056,128]{1,0:T(8,128)(2,1)S(1)}, bf16[1056,128]{1,0:T(8,128)(2,1)S(1)}, u32[]{:S(2)}, u32[]{:S(2)}) collective-permute-start(bf16[1056,128]{1,0:T(8,128)(2,1)S(1)} %collective-permute-done.6.refs_5_), channel_id=1, source_target_pairs={{0,4},{1,5},{2,6},{3,7},{4,8},{5,9},{6,10},{7,11},{8,12},{9,13},{1... | collective-permute-start | bytes 811016 | tf_op jit(solution)/shard_map/ppermute | solution.py:304
  31.4 9.3 %collective-permute-start.14 = (bf16[1024,128]{1,0:T(8,128)(2,1)S(1)}, bf16[1024,128]{1,0:T(8,128)(2,1)S(1)}, u32[]{:S(2)}, u32[]{:S(2)}) collective-permute-start(bf16[1024,128]{1,0:T(8,128)(2,1)S(1)} %get-tuple-element.58), channel_id=1, source_target_pairs={{0,12},{1,13},{2,14},{3,15},{4,0},{5,1},{6,2},{7,3},{8,4},{9,5},{1... | collective-permute-start | bytes 786440 | tf_op jit(solution)/shard_map/ppermute | solution.py:304
  35.0 14.2 %collective-permute-start.8 = (bf16[128,512]{1,0:T(8,128)(2,1)S(1)}, bf16[128,512]{1,0:T(8,128)(2,1)S(1)}, u32[]{:S(2)}, u32[]{:S(2)}) collective-permute-start(bf16[128,512]{1,0:T(8,128)(2,1)S(1)} %get-tuple-element.49), channel_id=1, source_target_pairs={{0,1},{1,0},{2,3},{3,2},{4,5},{5,4},{6,7},{7,6},{8,9},{9,8},{10,11... | collective-permute-start | bytes 393224 | tf_op jit(solution)/shard_map/ppermute | solution.py:304
  35.4 13.9 %collective-permute-start.9 = (bf16[128,512]{1,0:T(8,128)(2,1)S(1)}, bf16[128,512]{1,0:T(8,128)(2,1)S(1)}, u32[]{:S(2)}, u32[]{:S(2)}) collective-permute-start(bf16[128,512]{1,0:T(8,128)(2,1)S(1)} %get-tuple-element.50), channel_id=1, source_target_pairs={{0,2},{1,3},{2,0},{3,1},{4,6},{5,7},{6,4},{7,5},{8,10},{9,11},{10,... | collective-permute-start | bytes 393224 | tf_op jit(solution)/shard_map/ppermute | solution.py:304
  36.7 14.8 %collective-permute-start.10 = (bf16[128,512]{1,0:T(8,128)(2,1)S(1)}, bf16[128,512]{1,0:T(8,128)(2,1)S(1)}, u32[]{:S(2)}, u32[]{:S(2)}) collective-permute-start(bf16[128,512]{1,0:T(8,128)(2,1)S(1)} %get-tuple-element.51), channel_id=1, source_target_pairs={{0,3},{1,2},{2,1},{3,0},{4,7},{5,6},{6,5},{7,4},{8,11},{9,10},{10,... | collective-permute-start | bytes 393224 | tf_op jit(solution)/shard_map/ppermute | solution.py:304
  37.5 5.0 %collective-permute-start.11 = (bf16[256,128]{1,0:T(8,128)(2,1)S(1)}, bf16[256,128]{1,0:T(8,128)(2,1)S(1)}, u32[]{:S(2)}, u32[]{:S(2)}) collective-permute-start(bf16[256,128]{1,0:T(8,128)(2,1)S(1)} %get-tuple-element.55), channel_id=1, source_target_pairs={{0,1},{1,0},{2,3},{3,2},{4,5},{5,4},{6,7},{7,6},{8,9},{9,8},{10,11... | collective-permute-start | bytes 196616 | tf_op jit(solution)/shard_map/ppermute | solution.py:304
  40.7 4.5 %collective-permute-start.12 = (bf16[256,128]{1,0:T(8,128)(2,1)S(1)}, bf16[256,128]{1,0:T(8,128)(2,1)S(1)}, u32[]{:S(2)}, u32[]{:S(2)}) collective-permute-start(bf16[256,128]{1,0:T(8,128)(2,1)S(1)} %get-tuple-element.56), channel_id=1, source_target_pairs={{0,2},{1,3},{2,0},{3,1},{4,6},{5,7},{6,4},{7,5},{8,10},{9,11},{10,... | collective-permute-start | bytes 196616 | tf_op jit(solution)/shard_map/ppermute | solution.py:304
  42.6 10.4 %collective-permute-start.13 = (bf16[256,128]{1,0:T(8,128)(2,1)S(1)}, bf16[256,128]{1,0:T(8,128)(2,1)S(1)}, u32[]{:S(2)}, u32[]{:S(2)}) collective-permute-start(bf16[256,128]{1,0:T(8,128)(2,1)S(1)} %get-tuple-element.57), channel_id=1, source_target_pairs={{0,3},{1,2},{2,1},{3,0},{4,7},{5,6},{6,5},{7,4},{8,11},{9,10},{10,... | collective-permute-start | bytes 196616 | tf_op jit(solution)/shard_map/ppermute | solution.py:304
  45.2 7.7 %collective-permute-start.15 = (bf16[256,128]{1,0:T(8,128)(2,1)S(1)}, bf16[256,128]{1,0:T(8,128)(2,1)S(1)}, u32[]{:S(2)}, u32[]{:S(2)}) collective-permute-start(bf16[256,128]{1,0:T(8,128)(2,1)S(1)} %get-tuple-element.60), channel_id=1, source_target_pairs={{0,12},{1,13},{2,14},{3,15},{4,0},{5,1},{6,2},{7,3},{8,4},{9,5},{1... | collective-permute-start | bytes 196616 | tf_op jit(solution)/shard_map/ppermute | solution.py:304
  49.2 3.7 %collective-permute-start.16 = (bf16[256,128]{1,0:T(8,128)(2,1)S(1)}, bf16[256,128]{1,0:T(8,128)(2,1)S(1)}, u32[]{:S(2)}, u32[]{:S(2)}) collective-permute-start(bf16[256,128]{1,0:T(8,128)(2,1)S(1)} %get-tuple-element.61), channel_id=1, source_target_pairs={{0,13},{1,12},{2,15},{3,14},{4,1},{5,0},{6,3},{7,2},{8,5},{9,4},{1... | collective-permute-start | bytes 196616 | tf_op jit(solution)/shard_map/ppermute | solution.py:304
  49.2 5.4 %collective-permute-start.17 = (bf16[256,128]{1,0:T(8,128)(2,1)S(1)}, bf16[256,128]{1,0:T(8,128)(2,1)S(1)}, u32[]{:S(2)}, u32[]{:S(2)}) collective-permute-start(bf16[256,128]{1,0:T(8,128)(2,1)S(1)} %get-tuple-element.62), channel_id=1, source_target_pairs={{0,14},{1,15},{2,12},{3,13},{4,2},{5,3},{6,0},{7,1},{8,6},{9,7},{1... | collective-permute-start | bytes 196616 | tf_op jit(solution)/shard_map/ppermute | solution.py:304
  51.5 5.3 %collective-permute-start.18 = (bf16[256,128]{1,0:T(8,128)(2,1)S(1)}, bf16[256,128]{1,0:T(8,128)(2,1)S(1)}, u32[]{:S(2)}, u32[]{:S(2)}) collective-permute-start(bf16[256,128]{1,0:T(8,128)(2,1)S(1)} %get-tuple-element.63), channel_id=1, source_target_pairs={{0,15},{1,14},{2,13},{3,12},{4,3},{5,2},{6,1},{7,0},{8,7},{9,6},{1... | collective-permute-start | bytes 196616 | tf_op jit(solution)/shard_map/ppermute | solution.py:304

commit v6 on v5

--- a/solution.py
+++ b/solution.py
@@ -299,9 +299,17 @@
     width = GROUP * rows
     shape = jax.ShapeDtypeStruct
 
-    def move(value, steps, s=0):
-        pairs = [(t, ((t + steps * parts) % count) ^ s) for t in range(count)]
-        return lax.ppermute(value, "tok", pairs)
+    def move(value, steps, s=0, low=0):
+        def target(t):
+            row, me = divmod(t, parts)
+            if row < low:
+                return t ^ 1
+            if low <= row + steps < count // parts:
+                return ((row + steps) * parts + me) ^ s
+            row = low + (row - low + steps) % (count // parts - low)
+            return row * parts + me
+
+        return lax.ppermute(value, "tok", [(t, target(t)) for t in range(count)])
 
     def exchange(pieces):
         return [pieces[0]] + [move(pieces[s], 0, s) for s in range(1, parts)]
@@ -336,8 +344,8 @@
     )
     query_pieces = exchange(query_pieces)
     windows = [own]
-    for _ in range(behind):
-        windows.append(move(windows[-1], 1))
+    for k in range(behind):
+        windows.append(move(windows[-1], 1, low=k))
 
     kv_shape = (2 * span, HEAD_SIZE)
     stages = [0] + list(range(behind, 0, -1))
@@ -371,10 +379,10 @@
             )
             sent = [move(piece, -1, s) for s, piece in enumerate(got)]
         elif sent is None:
-            sent = move(term, -1)
+            sent = move(term, -1, low=offset - 1)
         else:
             (term,) = call(add_terms, (place, sent, term), [shape(kv_shape, BF16)])
-            sent = move(term, -1)
+            sent = move(term, -1, low=offset - 1)
 
     dq_pieces = exchange(dq)
     query_grad, token = call(

time: 58.5 us -> 57.8 us (0.988)
  waiting for transfers between devices: 24 us -> 23.1 us
    ppermute x19, waiting for transfers between devices: 24 us -> 23.1 us  [move(): return lax.ppermute(value, 'tok', [(t, target(t)) for t in range(count)])]
  transfers between devices with their start and end apart: 19 -> 19, of which waited for: 10 -> 8; matrix products, arithmetic and copies ran while one was open for 0% -> 0% of each run, Pallas kernels for 15% -> 15%
where the time goes in v6:
time: 57.8 us; the launch traced here: 57.5 us
  waiting for transfers between devices  23.1 us (40%)
  starting transfers between devices  20 us (35%)
  Pallas kernels  13.4 us (23%)
  between operations  0.95 us (2%)
    ppermute x19, waiting for transfers between devices, move(): return lax.ppermute(value, 'tok', [(t, target(t)) for t in range(count)])  23.1 us
    ppermute x19, starting transfers between devices, move(): return lax.ppermute(value, 'tok', [(t, target(t)) for t in range(count)])  20 us
    pallas_call x10, Pallas kernels, call(): pl.pallas_call(kernel, out_shape=outs, in_specs=[SMEM] + specs, out_specs...  13.4 us
  transfers between devices with their start and end apart: 19, of which 8 were waited for; matrix products, arithmetic and copies ran while one was open for 0% of the time, Pallas kernels for 15%

profile of v6, /device:TPU:0, one launch (start us, length us, event | category | flops | bytes accessed | tf_op | source)
XLA Modules:
  0.0 57.5 jit_solution(9714896210283181868)
XLA Ops:
  0.7 2.0 %shard_map.94 = (bf16[264,128]{1,0:T(8,128)(2,1)S(1)}, bf16[264,128]{1,0:T(8,128)(2,1)S(1)}, bf16[264,128]{1,0:T(8,128)(2,1)S(1)}, bf16[264,128]{1,0:T(8,128)(2,...) custom-call(s32[2]{0:T(128)S(1)} %pad_add_fusion.place, bf16[128,512]{1,0:T(8,128)(2,1)} %key_ref.1, ...), custom_call_target="tpu_custom_call" | custom-call | bytes 2630152 | tf_op jit(solution)/shard_map/pallas_call | solution.py:42
  2.7 0.6 collective-permute-start.3
  3.3 2.6 %collective-permute-start.4 = (bf16[264,128]{1,0:T(8,128)(2,1)S(1)}, bf16[264,128]{1,0:T(8,128)(2,1)S(1)}, u32[]{:S(2)}, u32[]{:S(2)}) collective-permute-start(bf16[264,128]{1,0:T(8,128)(2,1)S(1)} %get-tuple-element.43), channel_id=1, source_target_pairs={{0,2},{1,3},{2,0},{3,1},{4,6},{5,7},{6,4},{7,5},{8,10},{9,11},{10,... | collective-permute-start | bytes 202760 | tf_op jit(solution)/shard_map/ppermute | solution.py:312
  5.9 2.0 %shard_map.95 = (bf16[1048,128]{1,0:T(8,128)(2,1)S(1)}, bf16[1048,128]{1,0:T(8,128)(2,1)S(1)}, bf16[1048,128]{1,0:T(8,128)(2,1)S(1)}, bf16[1048,128]{1,0:T(8,128)(2,1)S(1)}, f32[8,128]{1,0:T(8,128)S(1)}) custom-call(s32[2]{0:T(128)S(1)} %pad_add_fusion.place, bf16[128,2048]{1,0:T(8,128)(2,1)} %query_ref.1, bf16[128,2048]{1,0:T(8,128)(2,1)S(1)} %get-tuple-element.35.grads, ...), custom_call_target="tpu_custom_call" | custom-call | bytes 2658312 | tf_op jit(solution)/shard_map/pallas_call | solution.py:42
  7.9 0.7 %collective-permute-done.4.refs_2_ = bf16[264,128]{1,0:T(8,128)(2,1)S(1)} collective-permute-done((bf16[264,128]{1,0:T(8,128)(2,1)S(1)}, bf16[264,128]{1,0:T(8,128)(2,1)S(1)}, u32[]{:S(2)}, u32[]{:S(2)}) %collective-permute-start.4) | collective-permute-done | bytes 67616 | tf_op jit(solution)/shard_map/ppermute | solution.py:312
  8.6 1.4 %collective-permute-done.5.refs_3_ = bf16[264,128]{1,0:T(8,128)(2,1)S(1)} collective-permute-done((bf16[264,128]{1,0:T(8,128)(2,1)S(1)}, bf16[264,128]{1,0:T(8,128)(2,1)S(1)}, u32[]{:S(2)}, u32[]{:S(2)}) %collective-permute-start.5) | collective-permute-done | bytes 67616 | tf_op jit(solution)/shard_map/ppermute | solution.py:312
  10.0 0.6 shard_map.96.refs_4_.refs_5_
  10.6 1.6 %collective-permute-start.6 = (bf16[1056,128]{1,0:T(8,128)(2,1)S(1)}, bf16[1056,128]{1,0:T(8,128)(2,1)S(1)}, u32[]{:S(2)}, u32[]{:S(2)}) collective-permute-start(bf16[1056,128]{1,0:T(8,128)(2,1)S(1)} %shard_map.96.refs_4_.refs_5_), channel_id=1, source_target_pairs={{0,4},{1,5},{2,6},{3,7},{4,8},{5,9},{6,10},{7,11},{8,12},{9,13},{1... | collective-permute-start | bytes 811016 | tf_op jit(solution)/shard_map/ppermute | solution.py:312
  12.2 1.4 %collective-permute-start.1 = (bf16[1048,128]{1,0:T(8,128)(2,1)S(1)}, bf16[1048,128]{1,0:T(8,128)(2,1)S(1)}, u32[]{:S(2)}, u32[]{:S(2)}) collective-permute-start(bf16[1048,128]{1,0:T(8,128)(2,1)S(1)} %get-tuple-element.39), channel_id=1, source_target_pairs={{0,2},{1,3},{2,0},{3,1},{4,6},{5,7},{6,4},{7,5},{8,10},{9,11},{10,... | collective-permute-start | bytes 804872 | tf_op jit(solution)/shard_map/ppermute | solution.py:312
  13.5 0.5 collective-permute-start.2
  14.0 7.0 %collective-permute-done.6.refs_5_ = bf16[1056,128]{1,0:T(8,128)(2,1)S(1)} collective-permute-done((bf16[1056,128]{1,0:T(8,128)(2,1)S(1)}, bf16[1056,128]{1,0:T(8,128)(2,1)S(1)}, u32[]{:S(2)}, u32[]{:S(2)}) %collective-permute-start.6) | collective-permute-done | bytes 270368 | tf_op jit(solution)/shard_map/ppermute | solution.py:312
  21.0 0.5 collective-permute-done.1.refs_2_
  21.5 4.8 %collective-permute-done.2.refs_3_ = bf16[1048,128]{1,0:T(8,128)(2,1)S(1)} collective-permute-done((bf16[1048,128]{1,0:T(8,128)(2,1)S(1)}, bf16[1048,128]{1,0:T(8,128)(2,1)S(1)}, u32[]{:S(2)}, u32[]{:S(2)}) %collective-permute-start.2) | collective-permute-done | bytes 268320 | tf_op jit(solution)/shard_map/ppermute | solution.py:312
  26.3 3.4 %shard_map.97 = (f32[4,128,512]{2,1,0:T(8,128)S(1)}, f32[1024,128]{1,0:T(8,128)S(1)}) custom-call(s32[2]{0:T(128)S(1)} %pad_add_fusion.place, bf16[1048,128]{1,0:T(8,128)(2,1)S(1)} %get-tuple-element.37.refs_0_, bf16[1048,128]{1,0:T(8,128)(2,1)S(1)} %collective-permute-done.refs_1_, bf16[1048,128]{1,0:T(8,128)(2,1)S(1)} %collective-permute-done.1.refs_2_, ...), custom_call_target="tpu_custom_call" | custom-call | flops 1342177280 | bytes 3186696 | tf_op jit(solution)/shard_map/pallas_call | solution.py:42
  29.8 0.8 %shard_map.98 = (f32[4,128,512]{2,1,0:T(8,128)S(1)}, bf16[1024,128]{1,0:T(8,128)(2,1)S(1)}) custom-call(s32[2]{0:T(128)S(1)} %pad_add_fusion.place, bf16[1048,128]{1,0:T(8,128)(2,1)S(1)} %get-tuple-element.37.refs_0_, bf16[1048,128]{1,0:T(8,128)(2,1)S(1)} %collective-permute-done.refs_1_, bf16[1048,128]{1,0:T(8,128)(2,1)S(1)} %collective-permute-done.1.refs_2_, ...), custom_call_target="tpu_custom_call" | custom-call | flops 1342177280 | bytes 3973128 | tf_op jit(solution)/shard_map/pallas_call | solution.py:42
  30.6 0.3 collective-permute-start.14
  30.9 0.6 %shard_map.99 = (bf16[128,512]{1,0:T(8,128)(2,1)S(1)}, bf16[128,512]{1,0:T(8,128)(2,1)S(1)}, bf16[128,512]{1,0:T(8,128)(2,1)S(1)}, bf16[128,512]{1,0:T(8,128)(2,1)S(1)}, f32[1024,128]{1,0:T(8,128)S(1)}) custom-call(s32[2]{0:T(128)S(1)} %pad_add_fusion.place, bf16[1048,128]{1,0:T(8,128)(2,1)S(1)} %get-tuple-element.37.refs_0_, ...), custom_call_target="tpu_custom_call" | custom-call | flops 1342177280 | bytes 3710984 | tf_op jit(solution)/shard_map/pallas_call | solution.py:42
  31.6 0.3 collective-permute-start.8
  31.9 1.2 %collective-permute-start.9 = (bf16[128,512]{1,0:T(8,128)(2,1)S(1)}, bf16[128,512]{1,0:T(8,128)(2,1)S(1)}, u32[]{:S(2)}, u32[]{:S(2)}) collective-permute-start(bf16[128,512]{1,0:T(8,128)(2,1)S(1)} %get-tuple-element.50), channel_id=1, source_target_pairs={{0,2},{1,3},{2,0},{3,1},{4,6},{5,7},{6,4},{7,5},{8,10},{9,11},{10,... | collective-permute-start | bytes 393224 | tf_op jit(solution)/shard_map/ppermute | solution.py:312
  33.1 0.4 collective-permute-start.10
  33.5 0.6 shard_map.101
  34.1 0.6 collective-permute-start.11
  34.7 1.2 %collective-permute-start.12 = (bf16[256,128]{1,0:T(8,128)(2,1)S(1)}, bf16[256,128]{1,0:T(8,128)(2,1)S(1)}, u32[]{:S(2)}, u32[]{:S(2)}) collective-permute-start(bf16[256,128]{1,0:T(8,128)(2,1)S(1)} %get-tuple-element.56), channel_id=1, source_target_pairs={{0,2},{1,3},{2,0},{3,1},{4,6},{5,7},{6,4},{7,5},{8,10},{9,11},{10,... | collective-permute-start | bytes 196616 | tf_op jit(solution)/shard_map/ppermute | solution.py:312
  35.9 0.6 %shard_map.102 = (bf16[256,128]{1,0:T(8,128)(2,1)S(1)}, bf16[256,128]{1,0:T(8,128)(2,1)S(1)}, bf16[256,128]{1,0:T(8,128)(2,1)S(1)}, bf16[256,128]{1,0:T(8,128)(2,1)S(1)}) custom-call(s32[2]{0:T(128)S(1)} %pad_add_fusion.place, bf16[1024,128]{1,0:T(8,128)(2,1)S(1)} %collective-permute-done.14.refs_0_, f32[1024,128]{1,0:T(8,128)S(1)} %get-tuple-element.59.refs_1_), custom_call_target="tpu_custom_call" | custom-call | bytes 1048584 | tf_op jit(solution)/shard_map/pallas_call | solution.py:42
  36.5 0.3 collective-permute-start.13
  36.8 5.7 %collective-permute-done.12.refs_2_ = bf16[256,128]{1,0:T(8,128)(2,1)S(1)} collective-permute-done((bf16[256,128]{1,0:T(8,128)(2,1)S(1)}, bf16[256,128]{1,0:T(8,128)(2,1)S(1)}, u32[]{:S(2)}, u32[]{:S(2)}) %collective-permute-start.12) | collective-permute-done | bytes 65568 | tf_op jit(solution)/shard_map/ppermute | solution.py:312
  42.5 5.9 %collective-permute-start.15 = (bf16[256,128]{1,0:T(8,128)(2,1)S(1)}, bf16[256,128]{1,0:T(8,128)(2,1)S(1)}, u32[]{:S(2)}, u32[]{:S(2)}) collective-permute-start(bf16[256,128]{1,0:T(8,128)(2,1)S(1)} %get-tuple-element.60), channel_id=1, source_target_pairs={{0,12},{1,13},{2,14},{3,15},{4,0},{5,1},{6,2},{7,3},{8,4},{9,5},{1... | collective-permute-start | bytes 196616 | tf_op jit(solution)/shard_map/ppermute | solution.py:312
  48.3 2.4 %collective-permute-start.16 = (bf16[256,128]{1,0:T(8,128)(2,1)S(1)}, bf16[256,128]{1,0:T(8,128)(2,1)S(1)}, u32[]{:S(2)}, u32[]{:S(2)}) collective-permute-start(bf16[256,128]{1,0:T(8,128)(2,1)S(1)} %get-tuple-element.61), channel_id=1, source_target_pairs={{0,12},{1,13},{2,14},{3,15},{4,1},{5,0},{6,3},{7,2},{8,5},{9,4},{1... | collective-permute-start | bytes 196616 | tf_op jit(solution)/shard_map/ppermute | solution.py:312
  50.8 0.7 %collective-permute-start.18 = (bf16[256,128]{1,0:T(8,128)(2,1)S(1)}, bf16[256,128]{1,0:T(8,128)(2,1)S(1)}, u32[]{:S(2)}, u32[]{:S(2)}) collective-permute-start(bf16[256,128]{1,0:T(8,128)(2,1)S(1)} %get-tuple-element.63), channel_id=1, source_target_pairs={{0,12},{1,13},{2,14},{3,15},{4,3},{5,2},{6,1},{7,0},{8,7},{9,6},{1... | collective-permute-start | bytes 196616 | tf_op jit(solution)/shard_map/ppermute | solution.py:312
  51.5 1.4 %shard_map.100 = (bf16[128,2048]{1,0:T(8,128)(2,1)}, f32[8,128]{1,0:T(8,128)S(1)}) custom-call(s32[2]{0:T(128)S(1)} %pad_add_fusion.place, bf16[128,512]{1,0:T(8,128)(2,1)S(1)} %get-tuple-element.48.refs_0_, bf16[128,512]{1,0:T(8,128)(2,1)S(1)} %collective-permute-done.8.refs_1_, bf16[128,512]{1,0:T(8,128)(2,1)S(1)} %collective-permute-done.9.refs_2_, ...), custom_call_target="tpu_custom_call" | custom-call | bytes 1052680 | tf_op jit(solution)/shard_map/pallas_call | solution.py:42
  53.0 3.0 %collective-permute-done.17.refs_6_ = bf16[256,128]{1,0:T(8,128)(2,1)S(1)} collective-permute-done((bf16[256,128]{1,0:T(8,128)(2,1)S(1)}, bf16[256,128]{1,0:T(8,128)(2,1)S(1)}, u32[]{:S(2)}, u32[]{:S(2)}) %collective-permute-start.17) | collective-permute-done | bytes 65568 | tf_op jit(solution)/shard_map/ppermute | solution.py:312
  56.1 1.3 %shard_map.103 = (bf16[128,512]{1,0:T(8,128)(2,1)}, bf16[128,512]{1,0:T(8,128)(2,1)}) custom-call(s32[2]{0:T(128)S(1)} %pad_add_fusion.place, bf16[256,128]{1,0:T(8,128)(2,1)S(1)} %get-tuple-element.54.refs_0_, bf16[256,128]{1,0:T(8,128)(2,1)S(1)} %collective-permute-done.11.refs_1_, bf16[256,128]{1,0:T(8,128)(2,1)S(1)} %collective-permute-done.12.refs_2_, ...), custom_call_target="tpu_custom_call" | custom-call | bytes 790536 | tf_op jit(solution)/shard_map/pallas_call | solution.py:42
  (19 shorter events, 0.3 us)
Async XLA Ops:
  2.7 3.2 %copy-start = (f32[16,128]{1,0:T(8,128)S(1)}, f32[16,128]{1,0:T(8,128)}, u32[]{:S(2)}) copy-start(f32[16,128]{1,0:T(8,128)} %norm_ref.1) | copy-start | bytes 24580
  2.7 5.2 %collective-permute-start.3 = (bf16[264,128]{1,0:T(8,128)(2,1)S(1)}, bf16[264,128]{1,0:T(8,128)(2,1)S(1)}, u32[]{:S(2)}, u32[]{:S(2)}) collective-permute-start(bf16[264,128]{1,0:T(8,128)(2,1)S(1)} %get-tuple-element.42), channel_id=1, source_target_pairs={{0,1},{1,0},{2,3},{3,2},{4,5},{5,4},{6,7},{7,6},{8,9},{9,8},{10,11... | collective-permute-start | bytes 202760 | tf_op jit(solution)/shard_map/ppermute | solution.py:312
  3.3 5.3 %collective-permute-start.4 = (bf16[264,128]{1,0:T(8,128)(2,1)S(1)}, bf16[264,128]{1,0:T(8,128)(2,1)S(1)}, u32[]{:S(2)}, u32[]{:S(2)}) collective-permute-start(bf16[264,128]{1,0:T(8,128)(2,1)S(1)} %get-tuple-element.43), channel_id=1, source_target_pairs={{0,2},{1,3},{2,0},{3,1},{4,6},{5,7},{6,4},{7,5},{8,10},{9,11},{10,... | collective-permute-start | bytes 202760 | tf_op jit(solution)/shard_map/ppermute | solution.py:312
  5.9 4.1 %collective-permute-start.5 = (bf16[264,128]{1,0:T(8,128)(2,1)S(1)}, bf16[264,128]{1,0:T(8,128)(2,1)S(1)}, u32[]{:S(2)}, u32[]{:S(2)}) collective-permute-start(bf16[264,128]{1,0:T(8,128)(2,1)S(1)} %get-tuple-element.44), channel_id=1, source_target_pairs={{0,3},{1,2},{2,1},{3,0},{4,7},{5,6},{6,5},{7,4},{8,11},{9,10},{10,... | collective-permute-start | bytes 202760 | tf_op jit(solution)/shard_map/ppermute | solution.py:312
  10.6 10.5 %collective-permute-start.6 = (bf16[1056,128]{1,0:T(8,128)(2,1)S(1)}, bf16[1056,128]{1,0:T(8,128)(2,1)S(1)}, u32[]{:S(2)}, u32[]{:S(2)}) collective-permute-start(bf16[1056,128]{1,0:T(8,128)(2,1)S(1)} %shard_map.96.refs_4_.refs_5_), channel_id=1, source_target_pairs={{0,4},{1,5},{2,6},{3,7},{4,8},{5,9},{6,10},{7,11},{8,12},{9,13},{1... | collective-permute-start | bytes 811016 | tf_op jit(solution)/shard_map/ppermute | solution.py:312
  12.2 8.8 %collective-permute-start = (bf16[1048,128]{1,0:T(8,128)(2,1)S(1)}, bf16[1048,128]{1,0:T(8,128)(2,1)S(1)}, u32[]{:S(2)}, u32[]{:S(2)}) collective-permute-start(bf16[1048,128]{1,0:T(8,128)(2,1)S(1)} %get-tuple-element.38), channel_id=1, source_target_pairs={{0,1},{1,0},{2,3},{3,2},{4,5},{5,4},{6,7},{7,6},{8,9},{9,8},{10,11... | collective-permute-start | bytes 804872 | tf_op jit(solution)/shard_map/ppermute | solution.py:312
  12.2 9.3 %collective-permute-start.1 = (bf16[1048,128]{1,0:T(8,128)(2,1)S(1)}, bf16[1048,128]{1,0:T(8,128)(2,1)S(1)}, u32[]{:S(2)}, u32[]{:S(2)}) collective-permute-start(bf16[1048,128]{1,0:T(8,128)(2,1)S(1)} %get-tuple-element.39), channel_id=1, source_target_pairs={{0,2},{1,3},{2,0},{3,1},{4,6},{5,7},{6,4},{7,5},{8,10},{9,11},{10,... | collective-permute-start | bytes 804872 | tf_op jit(solution)/shard_map/ppermute | solution.py:312
  13.5 12.8 %collective-permute-start.2 = (bf16[1048,128]{1,0:T(8,128)(2,1)S(1)}, bf16[1048,128]{1,0:T(8,128)(2,1)S(1)}, u32[]{:S(2)}, u32[]{:S(2)}) collective-permute-start(bf16[1048,128]{1,0:T(8,128)(2,1)S(1)} %get-tuple-element.40), channel_id=1, source_target_pairs={{0,3},{1,2},{2,1},{3,0},{4,7},{5,6},{6,5},{7,4},{8,11},{9,10},{10,... | collective-permute-start | bytes 804872 | tf_op jit(solution)/shard_map/ppermute | solution.py:312
  21.0 8.7 %collective-permute-start.7 = (bf16[1056,128]{1,0:T(8,128)(2,1)S(1)}, bf16[1056,128]{1,0:T(8,128)(2,1)S(1)}, u32[]{:S(2)}, u32[]{:S(2)}) collective-permute-start(bf16[1056,128]{1,0:T(8,128)(2,1)S(1)} %collective-permute-done.6.refs_5_), channel_id=1, source_target_pairs={{0,1},{1,0},{2,3},{3,2},{4,8},{5,9},{6,10},{7,11},{8,12},{9,13},{1... | collective-permute-start | bytes 811016 | tf_op jit(solution)/shard_map/ppermute | solution.py:312
  30.6 4.0 %collective-permute-start.14 = (bf16[1024,128]{1,0:T(8,128)(2,1)S(1)}, bf16[1024,128]{1,0:T(8,128)(2,1)S(1)}, u32[]{:S(2)}, u32[]{:S(2)}) collective-permute-start(bf16[1024,128]{1,0:T(8,128)(2,1)S(1)} %get-tuple-element.58), channel_id=1, source_target_pairs={{0,1},{1,0},{2,3},{3,2},{4,12},{5,13},{6,14},{7,15},{8,4},{9,5},{1... | collective-permute-start | bytes 786440 | tf_op jit(solution)/shard_map/ppermute | solution.py:312
  31.6 16.8 %collective-permute-start.8 = (bf16[128,512]{1,0:T(8,128)(2,1)S(1)}, bf16[128,512]{1,0:T(8,128)(2,1)S(1)}, u32[]{:S(2)}, u32[]{:S(2)}) collective-permute-start(bf16[128,512]{1,0:T(8,128)(2,1)S(1)} %get-tuple-element.49), channel_id=1, source_target_pairs={{0,1},{1,0},{2,3},{3,2},{4,5},{5,4},{6,7},{7,6},{8,9},{9,8},{10,11... | collective-permute-start | bytes 393224 | tf_op jit(solution)/shard_map/ppermute | solution.py:312
  31.9 18.8 %collective-permute-start.9 = (bf16[128,512]{1,0:T(8,128)(2,1)S(1)}, bf16[128,512]{1,0:T(8,128)(2,1)S(1)}, u32[]{:S(2)}, u32[]{:S(2)}) collective-permute-start(bf16[128,512]{1,0:T(8,128)(2,1)S(1)} %get-tuple-element.50), channel_id=1, source_target_pairs={{0,2},{1,3},{2,0},{3,1},{4,6},{5,7},{6,4},{7,5},{8,10},{9,11},{10,... | collective-permute-start | bytes 393224 | tf_op jit(solution)/shard_map/ppermute | solution.py:312
  33.1 17.7 %collective-permute-start.10 = (bf16[128,512]{1,0:T(8,128)(2,1)S(1)}, bf16[128,512]{1,0:T(8,128)(2,1)S(1)}, u32[]{:S(2)}, u32[]{:S(2)}) collective-permute-start(bf16[128,512]{1,0:T(8,128)(2,1)S(1)} %get-tuple-element.51), channel_id=1, source_target_pairs={{0,3},{1,2},{2,1},{3,0},{4,7},{5,6},{6,5},{7,4},{8,11},{9,10},{10,... | collective-permute-start | bytes 393224 | tf_op jit(solution)/shard_map/ppermute | solution.py:312
  34.1 2.4 %collective-permute-start.11 = (bf16[256,128]{1,0:T(8,128)(2,1)S(1)}, bf16[256,128]{1,0:T(8,128)(2,1)S(1)}, u32[]{:S(2)}, u32[]{:S(2)}) collective-permute-start(bf16[256,128]{1,0:T(8,128)(2,1)S(1)} %get-tuple-element.55), channel_id=1, source_target_pairs={{0,1},{1,0},{2,3},{3,2},{4,5},{5,4},{6,7},{7,6},{8,9},{9,8},{10,11... | collective-permute-start | bytes 196616 | tf_op jit(solution)/shard_map/ppermute | solution.py:312
  34.7 7.8 %collective-permute-start.12 = (bf16[256,128]{1,0:T(8,128)(2,1)S(1)}, bf16[256,128]{1,0:T(8,128)(2,1)S(1)}, u32[]{:S(2)}, u32[]{:S(2)}) collective-permute-start(bf16[256,128]{1,0:T(8,128)(2,1)S(1)} %get-tuple-element.56), channel_id=1, source_target_pairs={{0,2},{1,3},{2,0},{3,1},{4,6},{5,7},{6,4},{7,5},{8,10},{9,11},{10,... | collective-permute-start | bytes 196616 | tf_op jit(solution)/shard_map/ppermute | solution.py:312
  36.5 16.5 %collective-permute-start.13 = (bf16[256,128]{1,0:T(8,128)(2,1)S(1)}, bf16[256,128]{1,0:T(8,128)(2,1)S(1)}, u32[]{:S(2)}, u32[]{:S(2)}) collective-permute-start(bf16[256,128]{1,0:T(8,128)(2,1)S(1)} %get-tuple-element.57), channel_id=1, source_target_pairs={{0,3},{1,2},{2,1},{3,0},{4,7},{5,6},{6,5},{7,4},{8,11},{9,10},{10,... | collective-permute-start | bytes 196616 | tf_op jit(solution)/shard_map/ppermute | solution.py:312
  42.5 10.5 %collective-permute-start.15 = (bf16[256,128]{1,0:T(8,128)(2,1)S(1)}, bf16[256,128]{1,0:T(8,128)(2,1)S(1)}, u32[]{:S(2)}, u32[]{:S(2)}) collective-permute-start(bf16[256,128]{1,0:T(8,128)(2,1)S(1)} %get-tuple-element.60), channel_id=1, source_target_pairs={{0,12},{1,13},{2,14},{3,15},{4,0},{5,1},{6,2},{7,3},{8,4},{9,5},{1... | collective-permute-start | bytes 196616 | tf_op jit(solution)/shard_map/ppermute | solution.py:312
  48.3 4.7 %collective-permute-start.16 = (bf16[256,128]{1,0:T(8,128)(2,1)S(1)}, bf16[256,128]{1,0:T(8,128)(2,1)S(1)}, u32[]{:S(2)}, u32[]{:S(2)}) collective-permute-start(bf16[256,128]{1,0:T(8,128)(2,1)S(1)} %get-tuple-element.61), channel_id=1, source_target_pairs={{0,12},{1,13},{2,14},{3,15},{4,1},{5,0},{6,3},{7,2},{8,5},{9,4},{1... | collective-permute-start | bytes 196616 | tf_op jit(solution)/shard_map/ppermute | solution.py:312
  50.7 5.4 %collective-permute-start.17 = (bf16[256,128]{1,0:T(8,128)(2,1)S(1)}, bf16[256,128]{1,0:T(8,128)(2,1)S(1)}, u32[]{:S(2)}, u32[]{:S(2)}) collective-permute-start(bf16[256,128]{1,0:T(8,128)(2,1)S(1)} %get-tuple-element.62), channel_id=1, source_target_pairs={{0,12},{1,13},{2,14},{3,15},{4,2},{5,3},{6,0},{7,1},{8,6},{9,7},{1... | collective-permute-start | bytes 196616 | tf_op jit(solution)/shard_map/ppermute | solution.py:312
  50.8 5.3 %collective-permute-start.18 = (bf16[256,128]{1,0:T(8,128)(2,1)S(1)}, bf16[256,128]{1,0:T(8,128)(2,1)S(1)}, u32[]{:S(2)}, u32[]{:S(2)}) collective-permute-start(bf16[256,128]{1,0:T(8,128)(2,1)S(1)} %get-tuple-element.63), channel_id=1, source_target_pairs={{0,12},{1,13},{2,14},{3,15},{4,3},{5,2},{6,1},{7,0},{8,7},{9,6},{1... | collective-permute-start | bytes 196616 | tf_op jit(solution)/shard_map/ppermute | solution.py:312

commit v7 on v6

--- a/solution.py
+++ b/solution.py
@@ -241,14 +241,16 @@
     out[...] = (arrived[...].astype(F32) + term[...]).astype(BF16)
 
 
-def cut_terms(rows, count, place, *refs):
-    parts = KEY_VALUE_HEADS
-    terms, outs = refs[:count], refs[-parts:]
-    for s, out in enumerate(outs):
-        for k in range(2):
-            at = pl.multiple_of((k * parts + (place[1] ^ s)) * rows, rows)
-            total = sum(term[pl.ds(at, rows), :].astype(F32) for term in terms)
-            out[k * rows : (k + 1) * rows, :] = total.astype(BF16)
+def cut_terms(rows, count, groups, place, *refs):
+    parts = KEY_VALUE_HEADS
+    terms, outs = refs[:count], refs[-len(groups) :]
+    for group, out in zip(groups, outs):
+        for n, s in enumerate(group):
+            for k in range(2):
+                at = pl.multiple_of((k * parts + (place[1] ^ s)) * rows, rows)
+                total = sum(term[pl.ds(at, rows), :].astype(F32) for term in terms)
+                start = (2 * n + k) * rows
+                out[start : start + rows, :] = total.astype(BF16)
 
 
 def spread_queries(rows, place, *refs):
@@ -274,7 +276,7 @@
     for s in range(parts):
         term = pieces[s][...].astype(F32)
         for k in range(1, sources):
-            term = term + pieces[k * parts + s][...].astype(F32)
+            term = term + pieces[k * parts + s][0 : 2 * rows, :].astype(F32)
         total[s] = term.astype(BF16)
         for k, out in enumerate((key_out, value_out)):
             source = total.at[s, k * rows : (k + 1) * rows, :]
@@ -370,14 +372,22 @@
         dq, term = (got[:parts] if last else got[0]), got[-1]
         piece_shapes = [shape((2 * rows, HEAD_SIZE), BF16)] * parts
         if offset == 0:
-            own_pieces = call(functools.partial(cut_terms, rows, 1), (place, term), piece_shapes)
+            own_pieces = call(
+                functools.partial(cut_terms, rows, 1, [[s] for s in range(parts)]),
+                (place, term),
+                piece_shapes,
+            )
             own_pieces = exchange(own_pieces)
         elif offset == 1:
             terms = (term,) if sent is None else (sent, term)
+            groups = ((2, 3), (0,), (1,))
             got = call(
-                functools.partial(cut_terms, rows, len(terms)), (place, *terms), piece_shapes
+                functools.partial(cut_terms, rows, len(terms), groups),
+                (place, *terms),
+                [shape((2 * rows * len(group), HEAD_SIZE), BF16) for group in groups],
             )
-            sent = [move(piece, -1, s) for s, piece in enumerate(got)]
+            far, straight, beside = [move(piece, -1, group[0]) for piece, group in zip(got, groups)]
+            sent = [straight, beside, far, move(far[2 * rows :], 0, 1)]
         elif sent is None:
             sent = move(term, -1, low=offset - 1)
         else:

time: 57.8 us -> 58.9 us (1.019)
  starting transfers between devices: 20 us -> 27.6 us
  waiting for transfers between devices: 23.1 us -> 16.7 us
    ppermute x19, starting transfers between devices: 20 us -> 27.6 us  [move(): return lax.ppermute(value, 'tok', [(t, target(t)) for t in range(count)])]
    ppermute x19, waiting for transfers between devices: 23.1 us -> 16.7 us  [move(): return lax.ppermute(value, 'tok', [(t, target(t)) for t in range(count)])]
  transfers between devices with their start and end apart: 19 -> 19, of which waited for: 8 -> 8; matrix products, arithmetic and copies ran while one was open for 0% -> 0% of each run, Pallas kernels for 15% -> 14%
where the time goes in v7:
time: 58.9 us; the launch traced here: 58.7 us
  starting transfers between devices  27.6 us (47%)
  waiting for transfers between devices  16.7 us (28%)
  Pallas kernels  13.4 us (23%)
  between operations  0.94 us (2%)
    ppermute x19, starting transfers between devices, move(): return lax.ppermute(value, 'tok', [(t, target(t)) for t in range(count)])  27.6 us
    ppermute x19, waiting for transfers between devices, move(): return lax.ppermute(value, 'tok', [(t, target(t)) for t in range(count)])  16.7 us
    pallas_call x10, Pallas kernels, call(): pl.pallas_call(kernel, out_shape=outs, in_specs=[SMEM] + specs, out_specs...  13.4 us
  transfers between devices with their start and end apart: 19, of which 8 were waited for; matrix products, arithmetic and copies ran while one was open for 0% of the time, Pallas kernels for 14%

profile of v7, /device:TPU:0, one launch (start us, length us, event | category | flops | bytes accessed | tf_op | source)
XLA Modules:
  0.0 58.7 jit_solution(5012096239917803757)
XLA Ops:
  0.7 2.0 %shard_map.94 = (bf16[264,128]{1,0:T(8,128)(2,1)S(1)}, bf16[264,128]{1,0:T(8,128)(2,1)S(1)}, bf16[264,128]{1,0:T(8,128)(2,1)S(1)}, bf16[264,128]{1,0:T(8,128)(2,...) custom-call(s32[2]{0:T(128)S(1)} %pad_add_fusion.place, bf16[128,512]{1,0:T(8,128)(2,1)} %key_ref.1, ...), custom_call_target="tpu_custom_call" | custom-call | bytes 2630152 | tf_op jit(solution)/shard_map/pallas_call | solution.py:42
  2.7 0.6 collective-permute-start.3
  3.3 2.6 %collective-permute-start.4 = (bf16[264,128]{1,0:T(8,128)(2,1)S(1)}, bf16[264,128]{1,0:T(8,128)(2,1)S(1)}, u32[]{:S(2)}, u32[]{:S(2)}) collective-permute-start(bf16[264,128]{1,0:T(8,128)(2,1)S(1)} %get-tuple-element.42), channel_id=1, source_target_pairs={{0,2},{1,3},{2,0},{3,1},{4,6},{5,7},{6,4},{7,5},{8,10},{9,11},{10,... | collective-permute-start | bytes 202760 | tf_op jit(solution)/shard_map/ppermute | solution.py:314
  5.9 2.0 %shard_map.95 = (bf16[1048,128]{1,0:T(8,128)(2,1)S(1)}, bf16[1048,128]{1,0:T(8,128)(2,1)S(1)}, bf16[1048,128]{1,0:T(8,128)(2,1)S(1)}, bf16[1048,128]{1,0:T(8,128)(2,1)S(1)}, f32[8,128]{1,0:T(8,128)S(1)}) custom-call(s32[2]{0:T(128)S(1)} %pad_add_fusion.place, bf16[128,2048]{1,0:T(8,128)(2,1)} %query_ref.1, bf16[128,2048]{1,0:T(8,128)(2,1)S(1)} %get-tuple-element.34.grads, ...), custom_call_target="tpu_custom_call" | custom-call | bytes 2658312 | tf_op jit(solution)/shard_map/pallas_call | solution.py:42
  7.9 0.7 %collective-permute-done.4.refs_2_ = bf16[264,128]{1,0:T(8,128)(2,1)S(1)} collective-permute-done((bf16[264,128]{1,0:T(8,128)(2,1)S(1)}, bf16[264,128]{1,0:T(8,128)(2,1)S(1)}, u32[]{:S(2)}, u32[]{:S(2)}) %collective-permute-start.4) | collective-permute-done | bytes 67616 | tf_op jit(solution)/shard_map/ppermute | solution.py:314
  8.6 1.4 %collective-permute-done.5.refs_3_ = bf16[264,128]{1,0:T(8,128)(2,1)S(1)} collective-permute-done((bf16[264,128]{1,0:T(8,128)(2,1)S(1)}, bf16[264,128]{1,0:T(8,128)(2,1)S(1)}, u32[]{:S(2)}, u32[]{:S(2)}) %collective-permute-start.5) | collective-permute-done | bytes 67616 | tf_op jit(solution)/shard_map/ppermute | solution.py:314
  10.0 0.6 shard_map.96.refs_4_.refs_5_
  10.6 1.6 %collective-permute-start.6 = (bf16[1056,128]{1,0:T(8,128)(2,1)S(1)}, bf16[1056,128]{1,0:T(8,128)(2,1)S(1)}, u32[]{:S(2)}, u32[]{:S(2)}) collective-permute-start(bf16[1056,128]{1,0:T(8,128)(2,1)S(1)} %shard_map.96.refs_4_.refs_5_), channel_id=1, source_target_pairs={{0,4},{1,5},{2,6},{3,7},{4,8},{5,9},{6,10},{7,11},{8,12},{9,13},{1... | collective-permute-start | bytes 811016 | tf_op jit(solution)/shard_map/ppermute | solution.py:314
  12.2 1.4 %collective-permute-start.1 = (bf16[1048,128]{1,0:T(8,128)(2,1)S(1)}, bf16[1048,128]{1,0:T(8,128)(2,1)S(1)}, u32[]{:S(2)}, u32[]{:S(2)}) collective-permute-start(bf16[1048,128]{1,0:T(8,128)(2,1)S(1)} %get-tuple-element.38), channel_id=1, source_target_pairs={{0,2},{1,3},{2,0},{3,1},{4,6},{5,7},{6,4},{7,5},{8,10},{9,11},{10,... | collective-permute-start | bytes 804872 | tf_op jit(solution)/shard_map/ppermute | solution.py:314
  13.5 0.5 collective-permute-start.2
  14.0 7.0 %collective-permute-done.6.refs_5_ = bf16[1056,128]{1,0:T(8,128)(2,1)S(1)} collective-permute-done((bf16[1056,128]{1,0:T(8,128)(2,1)S(1)}, bf16[1056,128]{1,0:T(8,128)(2,1)S(1)}, u32[]{:S(2)}, u32[]{:S(2)}) %collective-permute-start.6) | collective-permute-done | bytes 270368 | tf_op jit(solution)/shard_map/ppermute | solution.py:314
  21.0 0.5 collective-permute-done.1.refs_2_
  21.5 4.8 %collective-permute-done.2.refs_3_ = bf16[1048,128]{1,0:T(8,128)(2,1)S(1)} collective-permute-done((bf16[1048,128]{1,0:T(8,128)(2,1)S(1)}, bf16[1048,128]{1,0:T(8,128)(2,1)S(1)}, u32[]{:S(2)}, u32[]{:S(2)}) %collective-permute-start.2) | collective-permute-done | bytes 268320 | tf_op jit(solution)/shard_map/ppermute | solution.py:314
  26.3 3.4 %shard_map.97 = (f32[4,128,512]{2,1,0:T(8,128)S(1)}, f32[1024,128]{1,0:T(8,128)S(1)}) custom-call(s32[2]{0:T(128)S(1)} %pad_add_fusion.place, bf16[1048,128]{1,0:T(8,128)(2,1)S(1)} %get-tuple-element.36.refs_0_, bf16[1048,128]{1,0:T(8,128)(2,1)S(1)} %collective-permute-done.refs_1_, bf16[1048,128]{1,0:T(8,128)(2,1)S(1)} %collective-permute-done.1.refs_2_, ...), custom_call_target="tpu_custom_call" | custom-call | flops 1342177280 | bytes 3186696 | tf_op jit(solution)/shard_map/pallas_call | solution.py:42
  29.8 0.8 %shard_map.98 = (f32[4,128,512]{2,1,0:T(8,128)S(1)}, bf16[1024,128]{1,0:T(8,128)(2,1)S(1)}) custom-call(s32[2]{0:T(128)S(1)} %pad_add_fusion.place, bf16[1048,128]{1,0:T(8,128)(2,1)S(1)} %get-tuple-element.36.refs_0_, bf16[1048,128]{1,0:T(8,128)(2,1)S(1)} %collective-permute-done.refs_1_, bf16[1048,128]{1,0:T(8,128)(2,1)S(1)} %collective-permute-done.1.refs_2_, ...), custom_call_target="tpu_custom_call" | custom-call | flops 1342177280 | bytes 3973128 | tf_op jit(solution)/shard_map/pallas_call | solution.py:42
  30.6 0.3 collective-permute-start.14
  30.9 0.6 %shard_map.99 = (bf16[128,512]{1,0:T(8,128)(2,1)S(1)}, bf16[128,512]{1,0:T(8,128)(2,1)S(1)}, bf16[128,512]{1,0:T(8,128)(2,1)S(1)}, bf16[128,512]{1,0:T(8,128)(2,1)S(1)}, f32[1024,128]{1,0:T(8,128)S(1)}) custom-call(s32[2]{0:T(128)S(1)} %pad_add_fusion.place, bf16[1048,128]{1,0:T(8,128)(2,1)S(1)} %get-tuple-element.36.refs_0_, ...), custom_call_target="tpu_custom_call" | custom-call | flops 1342177280 | bytes 3710984 | tf_op jit(solution)/shard_map/pallas_call | solution.py:42
  31.6 0.6 %collective-permute-done.14.refs_0_ = bf16[1024,128]{1,0:T(8,128)(2,1)S(1)} collective-permute-done((bf16[1024,128]{1,0:T(8,128)(2,1)S(1)}, bf16[1024,128]{1,0:T(8,128)(2,1)S(1)}, u32[]{:S(2)}, u32[]{:S(2)}) %collective-permute-start.14) | collective-permute-done | bytes 262176 | tf_op jit(solution)/shard_map/ppermute | solution.py:314
  32.2 0.6 %shard_map.102 = (bf16[512,128]{1,0:T(8,128)(2,1)S(1)}, bf16[256,128]{1,0:T(8,128)(2,1)S(1)}, bf16[256,128]{1,0:T(8,128)(2,1)S(1)}) custom-call(s32[2]{0:T(128)S(1)} %pad_add_fusion.place, bf16[1024,128]{1,0:T(8,128)(2,1)S(1)} %collective-permute-done.14.refs_0_, f32[1024,128]{1,0:T(8,128)S(1)} %get-tuple-element.58.refs_1_), custom_call_target="tpu_custom_call" | custom-call | bytes 1048584 | tf_op jit(solution)/shard_map/pallas_call | solution.py:42
  32.8 11.9 %collective-permute-start.17 = (bf16[512,128]{1,0:T(8,128)(2,1)S(1)}, bf16[512,128]{1,0:T(8,128)(2,1)S(1)}, u32[]{:S(2)}, u32[]{:S(2)}) collective-permute-start(bf16[512,128]{1,0:T(8,128)(2,1)S(1)} %get-tuple-element.61), channel_id=1, source_target_pairs={{0,12},{1,13},{2,14},{3,15},{4,2},{5,3},{6,0},{7,1},{8,6},{9,7},{1... | collective-permute-start | bytes 393224 | tf_op jit(solution)/shard_map/ppermute | solution.py:314
  44.7 1.3 %collective-permute-start.9 = (bf16[128,512]{1,0:T(8,128)(2,1)S(1)}, bf16[128,512]{1,0:T(8,128)(2,1)S(1)}, u32[]{:S(2)}, u32[]{:S(2)}) collective-permute-start(bf16[128,512]{1,0:T(8,128)(2,1)S(1)} %get-tuple-element.49), channel_id=1, source_target_pairs={{0,2},{1,3},{2,0},{3,1},{4,6},{5,7},{6,4},{7,5},{8,10},{9,11},{10,... | collective-permute-start | bytes 393224 | tf_op jit(solution)/shard_map/ppermute | solution.py:314
  46.0 0.6 collective-permute-start.10
  46.6 0.6 shard_map.101
  47.2 0.3 collective-permute-start.11
  47.5 1.3 %collective-permute-start.12 = (bf16[256,128]{1,0:T(8,128)(2,1)S(1)}, bf16[256,128]{1,0:T(8,128)(2,1)S(1)}, u32[]{:S(2)}, u32[]{:S(2)}) collective-permute-start(bf16[256,128]{1,0:T(8,128)(2,1)S(1)} %get-tuple-element.55), channel_id=1, source_target_pairs={{0,2},{1,3},{2,0},{3,1},{4,6},{5,7},{6,4},{7,5},{8,10},{9,11},{10,... | collective-permute-start | bytes 196616 | tf_op jit(solution)/shard_map/ppermute | solution.py:314
  48.9 0.8 %collective-permute-start.13 = (bf16[256,128]{1,0:T(8,128)(2,1)S(1)}, bf16[256,128]{1,0:T(8,128)(2,1)S(1)}, u32[]{:S(2)}, u32[]{:S(2)}) collective-permute-start(bf16[256,128]{1,0:T(8,128)(2,1)S(1)} %get-tuple-element.56), channel_id=1, source_target_pairs={{0,3},{1,2},{2,1},{3,0},{4,7},{5,6},{6,5},{7,4},{8,11},{9,10},{10,... | collective-permute-start | bytes 196616 | tf_op jit(solution)/shard_map/ppermute | solution.py:314
  49.7 3.6 %collective-permute-start.15 = (bf16[256,128]{1,0:T(8,128)(2,1)S(1)}, bf16[256,128]{1,0:T(8,128)(2,1)S(1)}, u32[]{:S(2)}, u32[]{:S(2)}) collective-permute-start(bf16[256,128]{1,0:T(8,128)(2,1)S(1)} %get-tuple-element.59), channel_id=1, source_target_pairs={{0,12},{1,13},{2,14},{3,15},{4,0},{5,1},{6,2},{7,3},{8,4},{9,5},{1... | collective-permute-start | bytes 196616 | tf_op jit(solution)/shard_map/ppermute | solution.py:314
  53.4 0.7 %collective-permute-start.18 = (bf16[256,128]{1,0:T(8,128)(2,1)S(1)}, bf16[256,128]{1,0:T(8,128)(2,1)S(1)}, u32[]{:S(2)}, u32[]{:S(2)}) collective-permute-start(bf16[256,128]{1,0:T(8,128)(2,1)S(1)} %slice.4), channel_id=1, source_target_pairs={{0,1},{1,0},{2,3},{3,2},{4,5},{5,4},{6,7},{7,6},{8,9},{9,8},{10,11... | collective-permute-start | bytes 196616 | tf_op jit(solution)/shard_map/ppermute | solution.py:314
  54.0 1.4 %shard_map.100 = (bf16[128,2048]{1,0:T(8,128)(2,1)}, f32[8,128]{1,0:T(8,128)S(1)}) custom-call(s32[2]{0:T(128)S(1)} %pad_add_fusion.place, bf16[128,512]{1,0:T(8,128)(2,1)S(1)} %get-tuple-element.47.refs_0_, bf16[128,512]{1,0:T(8,128)(2,1)S(1)} %collective-permute-done.8.refs_1_, bf16[128,512]{1,0:T(8,128)(2,1)S(1)} %collective-permute-done.9.refs_2_, ...), custom_call_target="tpu_custom_call" | custom-call | bytes 1052680 | tf_op jit(solution)/shard_map/pallas_call | solution.py:42
  55.5 0.3 collective-permute-done.13.refs_3_
  55.8 1.4 %collective-permute-done.16.refs_5_ = bf16[256,128]{1,0:T(8,128)(2,1)S(1)} collective-permute-done((bf16[256,128]{1,0:T(8,128)(2,1)S(1)}, bf16[256,128]{1,0:T(8,128)(2,1)S(1)}, u32[]{:S(2)}, u32[]{:S(2)}) %collective-permute-start.16) | collective-permute-done | bytes 65568 | tf_op jit(solution)/shard_map/ppermute | solution.py:314
  57.2 1.3 %shard_map.103 = (bf16[128,512]{1,0:T(8,128)(2,1)}, bf16[128,512]{1,0:T(8,128)(2,1)}) custom-call(s32[2]{0:T(128)S(1)} %pad_add_fusion.place, bf16[256,128]{1,0:T(8,128)(2,1)S(1)} %get-tuple-element.53.refs_0_, bf16[256,128]{1,0:T(8,128)(2,1)S(1)} %collective-permute-done.11.refs_1_, bf16[256,128]{1,0:T(8,128)(2,1)S(1)} %collective-permute-done.12.refs_2_, ...), custom_call_target="tpu_custom_call" | custom-call | bytes 856072 | tf_op jit(solution)/shard_map/pallas_call | solution.py:42
  (20 shorter events, 0.2 us)
Async XLA Ops:
  2.7 3.2 %copy-start = (f32[16,128]{1,0:T(8,128)S(1)}, f32[16,128]{1,0:T(8,128)}, u32[]{:S(2)}) copy-start(f32[16,128]{1,0:T(8,128)} %norm_ref.1) | copy-start | bytes 24580
  2.7 5.2 %collective-permute-start.3 = (bf16[264,128]{1,0:T(8,128)(2,1)S(1)}, bf16[264,128]{1,0:T(8,128)(2,1)S(1)}, u32[]{:S(2)}, u32[]{:S(2)}) collective-permute-start(bf16[264,128]{1,0:T(8,128)(2,1)S(1)} %get-tuple-element.41), channel_id=1, source_target_pairs={{0,1},{1,0},{2,3},{3,2},{4,5},{5,4},{6,7},{7,6},{8,9},{9,8},{10,11... | collective-permute-start | bytes 202760 | tf_op jit(solution)/shard_map/ppermute | solution.py:314
  3.3 5.3 %collective-permute-start.4 = (bf16[264,128]{1,0:T(8,128)(2,1)S(1)}, bf16[264,128]{1,0:T(8,128)(2,1)S(1)}, u32[]{:S(2)}, u32[]{:S(2)}) collective-permute-start(bf16[264,128]{1,0:T(8,128)(2,1)S(1)} %get-tuple-element.42), channel_id=1, source_target_pairs={{0,2},{1,3},{2,0},{3,1},{4,6},{5,7},{6,4},{7,5},{8,10},{9,11},{10,... | collective-permute-start | bytes 202760 | tf_op jit(solution)/shard_map/ppermute | solution.py:314
  5.9 4.1 %collective-permute-start.5 = (bf16[264,128]{1,0:T(8,128)(2,1)S(1)}, bf16[264,128]{1,0:T(8,128)(2,1)S(1)}, u32[]{:S(2)}, u32[]{:S(2)}) collective-permute-start(bf16[264,128]{1,0:T(8,128)(2,1)S(1)} %get-tuple-element.43), channel_id=1, source_target_pairs={{0,3},{1,2},{2,1},{3,0},{4,7},{5,6},{6,5},{7,4},{8,11},{9,10},{10,... | collective-permute-start | bytes 202760 | tf_op jit(solution)/shard_map/ppermute | solution.py:314
  10.6 10.5 %collective-permute-start.6 = (bf16[1056,128]{1,0:T(8,128)(2,1)S(1)}, bf16[1056,128]{1,0:T(8,128)(2,1)S(1)}, u32[]{:S(2)}, u32[]{:S(2)}) collective-permute-start(bf16[1056,128]{1,0:T(8,128)(2,1)S(1)} %shard_map.96.refs_4_.refs_5_), channel_id=1, source_target_pairs={{0,4},{1,5},{2,6},{3,7},{4,8},{5,9},{6,10},{7,11},{8,12},{9,13},{1... | collective-permute-start | bytes 811016 | tf_op jit(solution)/shard_map/ppermute | solution.py:314
  12.2 8.8 %collective-permute-start = (bf16[1048,128]{1,0:T(8,128)(2,1)S(1)}, bf16[1048,128]{1,0:T(8,128)(2,1)S(1)}, u32[]{:S(2)}, u32[]{:S(2)}) collective-permute-start(bf16[1048,128]{1,0:T(8,128)(2,1)S(1)} %get-tuple-element.37), channel_id=1, source_target_pairs={{0,1},{1,0},{2,3},{3,2},{4,5},{5,4},{6,7},{7,6},{8,9},{9,8},{10,11... | collective-permute-start | bytes 804872 | tf_op jit(solution)/shard_map/ppermute | solution.py:314
  12.2 9.3 %collective-permute-start.1 = (bf16[1048,128]{1,0:T(8,128)(2,1)S(1)}, bf16[1048,128]{1,0:T(8,128)(2,1)S(1)}, u32[]{:S(2)}, u32[]{:S(2)}) collective-permute-start(bf16[1048,128]{1,0:T(8,128)(2,1)S(1)} %get-tuple-element.38), channel_id=1, source_target_pairs={{0,2},{1,3},{2,0},{3,1},{4,6},{5,7},{6,4},{7,5},{8,10},{9,11},{10,... | collective-permute-start | bytes 804872 | tf_op jit(solution)/shard_map/ppermute | solution.py:314
  13.5 12.8 %collective-permute-start.2 = (bf16[1048,128]{1,0:T(8,128)(2,1)S(1)}, bf16[1048,128]{1,0:T(8,128)(2,1)S(1)}, u32[]{:S(2)}, u32[]{:S(2)}) collective-permute-start(bf16[1048,128]{1,0:T(8,128)(2,1)S(1)} %get-tuple-element.39), channel_id=1, source_target_pairs={{0,3},{1,2},{2,1},{3,0},{4,7},{5,6},{6,5},{7,4},{8,11},{9,10},{10,... | collective-permute-start | bytes 804872 | tf_op jit(solution)/shard_map/ppermute | solution.py:314
  21.0 8.7 %collective-permute-start.7 = (bf16[1056,128]{1,0:T(8,128)(2,1)S(1)}, bf16[1056,128]{1,0:T(8,128)(2,1)S(1)}, u32[]{:S(2)}, u32[]{:S(2)}) collective-permute-start(bf16[1056,128]{1,0:T(8,128)(2,1)S(1)} %collective-permute-done.6.refs_5_), channel_id=1, source_target_pairs={{0,1},{1,0},{2,3},{3,2},{4,8},{5,9},{6,10},{7,11},{8,12},{9,13},{1... | collective-permute-start | bytes 811016 | tf_op jit(solution)/shard_map/ppermute | solution.py:314
  30.6 1.6 %collective-permute-start.14 = (bf16[1024,128]{1,0:T(8,128)(2,1)S(1)}, bf16[1024,128]{1,0:T(8,128)(2,1)S(1)}, u32[]{:S(2)}, u32[]{:S(2)}) collective-permute-start(bf16[1024,128]{1,0:T(8,128)(2,1)S(1)} %get-tuple-element.57), channel_id=1, source_target_pairs={{0,1},{1,0},{2,3},{3,2},{4,12},{5,13},{6,14},{7,15},{8,4},{9,5},{1... | collective-permute-start | bytes 786440 | tf_op jit(solution)/shard_map/ppermute | solution.py:314
  32.8 14.7 %collective-permute-start.17 = (bf16[512,128]{1,0:T(8,128)(2,1)S(1)}, bf16[512,128]{1,0:T(8,128)(2,1)S(1)}, u32[]{:S(2)}, u32[]{:S(2)}) collective-permute-start(bf16[512,128]{1,0:T(8,128)(2,1)S(1)} %get-tuple-element.61), channel_id=1, source_target_pairs={{0,12},{1,13},{2,14},{3,15},{4,2},{5,3},{6,0},{7,1},{8,6},{9,7},{1... | collective-permute-start | bytes 393224 | tf_op jit(solution)/shard_map/ppermute | solution.py:314
  44.7 4.9 %collective-permute-start.8 = (bf16[128,512]{1,0:T(8,128)(2,1)S(1)}, bf16[128,512]{1,0:T(8,128)(2,1)S(1)}, u32[]{:S(2)}, u32[]{:S(2)}) collective-permute-start(bf16[128,512]{1,0:T(8,128)(2,1)S(1)} %get-tuple-element.48), channel_id=1, source_target_pairs={{0,1},{1,0},{2,3},{3,2},{4,5},{5,4},{6,7},{7,6},{8,9},{9,8},{10,11... | collective-permute-start | bytes 393224 | tf_op jit(solution)/shard_map/ppermute | solution.py:314
  44.7 8.6 %collective-permute-start.9 = (bf16[128,512]{1,0:T(8,128)(2,1)S(1)}, bf16[128,512]{1,0:T(8,128)(2,1)S(1)}, u32[]{:S(2)}, u32[]{:S(2)}) collective-permute-start(bf16[128,512]{1,0:T(8,128)(2,1)S(1)} %get-tuple-element.49), channel_id=1, source_target_pairs={{0,2},{1,3},{2,0},{3,1},{4,6},{5,7},{6,4},{7,5},{8,10},{9,11},{10,... | collective-permute-start | bytes 393224 | tf_op jit(solution)/shard_map/ppermute | solution.py:314
  46.0 7.4 %collective-permute-start.10 = (bf16[128,512]{1,0:T(8,128)(2,1)S(1)}, bf16[128,512]{1,0:T(8,128)(2,1)S(1)}, u32[]{:S(2)}, u32[]{:S(2)}) collective-permute-start(bf16[128,512]{1,0:T(8,128)(2,1)S(1)} %get-tuple-element.50), channel_id=1, source_target_pairs={{0,3},{1,2},{2,1},{3,0},{4,7},{5,6},{6,5},{7,4},{8,11},{9,10},{10,... | collective-permute-start | bytes 393224 | tf_op jit(solution)/shard_map/ppermute | solution.py:314
  47.2 1.7 %collective-permute-start.11 = (bf16[256,128]{1,0:T(8,128)(2,1)S(1)}, bf16[256,128]{1,0:T(8,128)(2,1)S(1)}, u32[]{:S(2)}, u32[]{:S(2)}) collective-permute-start(bf16[256,128]{1,0:T(8,128)(2,1)S(1)} %get-tuple-element.54), channel_id=1, source_target_pairs={{0,1},{1,0},{2,3},{3,2},{4,5},{5,4},{6,7},{7,6},{8,9},{9,8},{10,11... | collective-permute-start | bytes 196616 | tf_op jit(solution)/shard_map/ppermute | solution.py:314
  47.5 8.0 %collective-permute-start.12 = (bf16[256,128]{1,0:T(8,128)(2,1)S(1)}, bf16[256,128]{1,0:T(8,128)(2,1)S(1)}, u32[]{:S(2)}, u32[]{:S(2)}) collective-permute-start(bf16[256,128]{1,0:T(8,128)(2,1)S(1)} %get-tuple-element.55), channel_id=1, source_target_pairs={{0,2},{1,3},{2,0},{3,1},{4,6},{5,7},{6,4},{7,5},{8,10},{9,11},{10,... | collective-permute-start | bytes 196616 | tf_op jit(solution)/shard_map/ppermute | solution.py:314
  48.9 6.9 %collective-permute-start.13 = (bf16[256,128]{1,0:T(8,128)(2,1)S(1)}, bf16[256,128]{1,0:T(8,128)(2,1)S(1)}, u32[]{:S(2)}, u32[]{:S(2)}) collective-permute-start(bf16[256,128]{1,0:T(8,128)(2,1)S(1)} %get-tuple-element.56), channel_id=1, source_target_pairs={{0,3},{1,2},{2,1},{3,0},{4,7},{5,6},{6,5},{7,4},{8,11},{9,10},{10,... | collective-permute-start | bytes 196616 | tf_op jit(solution)/shard_map/ppermute | solution.py:314
  49.7 6.1 %collective-permute-start.15 = (bf16[256,128]{1,0:T(8,128)(2,1)S(1)}, bf16[256,128]{1,0:T(8,128)(2,1)S(1)}, u32[]{:S(2)}, u32[]{:S(2)}) collective-permute-start(bf16[256,128]{1,0:T(8,128)(2,1)S(1)} %get-tuple-element.59), channel_id=1, source_target_pairs={{0,12},{1,13},{2,14},{3,15},{4,0},{5,1},{6,2},{7,3},{8,4},{9,5},{1... | collective-permute-start | bytes 196616 | tf_op jit(solution)/shard_map/ppermute | solution.py:314
  53.3 3.9 %collective-permute-start.16 = (bf16[256,128]{1,0:T(8,128)(2,1)S(1)}, bf16[256,128]{1,0:T(8,128)(2,1)S(1)}, u32[]{:S(2)}, u32[]{:S(2)}) collective-permute-start(bf16[256,128]{1,0:T(8,128)(2,1)S(1)} %get-tuple-element.60), channel_id=1, source_target_pairs={{0,12},{1,13},{2,14},{3,15},{4,1},{5,0},{6,3},{7,2},{8,5},{9,4},{1... | collective-permute-start | bytes 196616 | tf_op jit(solution)/shard_map/ppermute | solution.py:314
  53.4 3.8 %collective-permute-start.18 = (bf16[256,128]{1,0:T(8,128)(2,1)S(1)}, bf16[256,128]{1,0:T(8,128)(2,1)S(1)}, u32[]{:S(2)}, u32[]{:S(2)}) collective-permute-start(bf16[256,128]{1,0:T(8,128)(2,1)S(1)} %slice.4), channel_id=1, source_target_pairs={{0,1},{1,0},{2,3},{3,2},{4,5},{5,4},{6,7},{7,6},{8,9},{9,8},{10,11... | collective-permute-start | bytes 196616 | tf_op jit(solution)/shard_map/ppermute | solution.py:314

commit v8 on v7

--- a/solution.py
+++ b/solution.py
@@ -146,7 +146,7 @@
         dq_out, refs = refs[:parts], refs[parts:]
     else:
         dq_out, refs = refs[0], refs[1:]
-    kv_out, dq, dkv, key_t, docs_t, docs_s = refs
+    (*kv_out, dq, dkv, key_t, docs_t, docs_s) = refs
     row, me = place[0], place[1]
     width = GROUP * rows
     span = parts * rows
@@ -213,7 +213,8 @@
             if offset == 0:
                 pl.when(low & ~high)(functools.partial(block, 0, half))
 
-        kv_out[...] = dkv[...].astype(kv_out.dtype)
+        for k, out in enumerate(kv_out):
+            out[...] = dkv[k * span : (k + 1) * span, :].astype(out.dtype)
         for s in range(parts):
             total = dq[s] if first else dq[s] + dq_in[s]
             if last:
@@ -227,7 +228,8 @@
 
     @pl.when(row < offset)
     def _():
-        kv_out[...] = jnp.zeros_like(kv_out)
+        for out in kv_out:
+            out[...] = jnp.zeros_like(out)
         for s in range(parts):
             if last:
                 dq_out[s][...] = dq_in[s].astype(BF16)
@@ -241,16 +243,20 @@
     out[...] = (arrived[...].astype(F32) + term[...]).astype(BF16)
 
 
+def cut_own(rows, place, key_ref, value_ref, *outs):
+    for s, out in enumerate(outs):
+        at = pl.multiple_of((place[1] ^ s) * rows, rows)
+        for k, term in enumerate((key_ref, value_ref)):
+            out[k * rows : (k + 1) * rows, :] = term[pl.ds(at, rows), :].astype(BF16)
+
+
 def cut_terms(rows, count, groups, place, *refs):
-    parts = KEY_VALUE_HEADS
     terms, outs = refs[:count], refs[-len(groups) :]
     for group, out in zip(groups, outs):
         for n, s in enumerate(group):
-            for k in range(2):
-                at = pl.multiple_of((k * parts + (place[1] ^ s)) * rows, rows)
-                total = sum(term[pl.ds(at, rows), :].astype(F32) for term in terms)
-                start = (2 * n + k) * rows
-                out[start : start + rows, :] = total.astype(BF16)
+            at = pl.multiple_of((place[1] ^ s) * rows, rows)
+            total = sum(term[pl.ds(at, rows), :].astype(F32) for term in terms)
+            out[n * rows : (n + 1) * rows, :] = total.astype(BF16)
 
 
 def spread_queries(rows, place, *refs):
@@ -269,19 +275,19 @@
         copy.wait()
 
 
-def spread_keys(rows, sources, place, *refs):
+def spread_keys(rows, moved, place, *refs):
     parts = KEY_VALUE_HEADS
     pieces, (key_out, value_out, total, sems) = refs[:-5], refs[-4:]
     copies = []
     for s in range(parts):
-        term = pieces[s][...].astype(F32)
-        for k in range(1, sources):
-            term = term + pieces[k * parts + s][0 : 2 * rows, :].astype(F32)
-        total[s] = term.astype(BF16)
         for k, out in enumerate((key_out, value_out)):
-            source = total.at[s, k * rows : (k + 1) * rows, :]
+            cut = slice(k * rows, (k + 1) * rows)
+            term = pieces[s][cut, :].astype(F32)
+            if moved:
+                term = term + pieces[(k + 1) * parts + s][0:rows, :].astype(F32)
+            total[s, cut, :] = term.astype(BF16)
             target = out.at[:, head_columns(place[1] ^ s)]
-            copies.append(pltpu.make_async_copy(source, target, sems.at[s, k]))
+            copies.append(pltpu.make_async_copy(total.at[s, cut, :], target, sems.at[s, k]))
             copies[-1].start()
     for copy in copies:
         copy.wait()
@@ -349,7 +355,7 @@
     for k in range(behind):
         windows.append(move(windows[-1], 1, low=k))
 
-    kv_shape = (2 * span, HEAD_SIZE)
+    kv_shape = (span, HEAD_SIZE)
     stages = [0] + list(range(behind, 0, -1))
     dq, own_pieces, sent = None, None, None
     for k, offset in enumerate(stages):
@@ -361,7 +367,7 @@
             outs = [shape((HEAD_SIZE, width), BF16)] * parts
         else:
             outs = [shape((parts, HEAD_SIZE, width), F32)]
-        outs = outs + [shape(kv_shape, BF16 if offset == behind > 0 else F32)]
+        outs = outs + [shape(kv_shape, BF16 if offset == behind > 0 else F32)] * 2
         got = call(
             functools.partial(attend, rows, offset, reach, first, last),
             ins,
@@ -369,30 +375,34 @@
             scratch=attend_scratch(rows),
             flops=10 * span * span * GROUP * HEAD_SIZE,
         )
-        dq, term = (got[:parts] if last else got[0]), got[-1]
-        piece_shapes = [shape((2 * rows, HEAD_SIZE), BF16)] * parts
+        dq, terms = (got[:parts] if last else got[0]), got[-2:]
         if offset == 0:
             own_pieces = call(
-                functools.partial(cut_terms, rows, 1, [[s] for s in range(parts)]),
-                (place, term),
-                piece_shapes,
+                functools.partial(cut_own, rows),
+                (place, *terms),
+                [shape((2 * rows, HEAD_SIZE), BF16)] * parts,
             )
             own_pieces = exchange(own_pieces)
-        elif offset == 1:
-            terms = (term,) if sent is None else (sent, term)
+            continue
+        if sent is not None:
+            terms = [(arrived, term) for arrived, term in zip(sent, terms)]
+        else:
+            terms = [(term,) for term in terms]
+        sent = []
+        for k, pair in enumerate(terms):
+            if offset > 1:
+                if len(pair) > 1:
+                    pair = call(add_terms, (place, *pair), [shape(kv_shape, BF16)])
+                sent.append(move(pair[0], -1, low=offset - 1))
+                continue
             groups = ((2, 3), (0,), (1,))
-            got = call(
-                functools.partial(cut_terms, rows, len(terms), groups),
-                (place, *terms),
-                [shape((2 * rows * len(group), HEAD_SIZE), BF16) for group in groups],
+            cut = call(
+                functools.partial(cut_terms, rows, len(pair), groups),
+                (place, *pair),
+                [shape((rows * len(group), HEAD_SIZE), BF16) for group in groups],
             )
-            far, straight, beside = [move(piece, -1, group[0]) for piece, group in zip(got, groups)]
-            sent = [straight, beside, far, move(far[2 * rows :], 0, 1)]
-        elif sent is None:
-            sent = move(term, -1, low=offset - 1)
-        else:
-            (term,) = call(add_terms, (place, sent, term), [shape(kv_shape, BF16)])
-            sent = move(term, -1, low=offset - 1)
+            far, straight, beside = [move(piece, -1, group[0]) for piece, group in zip(cut, groups)]
+            sent += [straight, beside, far, move(far[rows:], 0, 1)]
 
     dq_pieces = exchange(dq)
     query_grad, token = call(
@@ -407,7 +417,7 @@
     )
     pieces = own_pieces + (sent or [])
     key_grad, value_grad = call(
-        functools.partial(spread_keys, rows, len(pieces) // parts),
+        functools.partial(spread_keys, rows, sent is not None),
         (place, *pieces, token),
         [shape((rows, parts * HEAD_SIZE), BF16)] * 2,
         scratch=[

time: 58.9 us -> 62.4 us (1.059)
  starting transfers between devices: 27.6 us -> 29.7 us
  waiting for transfers between devices: 16.7 us -> 17.5 us
    ppermute x19 -> x24, starting transfers between devices: 27.6 us -> 29.7 us  [move(): return lax.ppermute(value, 'tok', [(t, target(t)) for t in range(count)])]
    ppermute x19 -> x24, waiting for transfers between devices: 16.7 us -> 17.5 us  [move(): return lax.ppermute(value, 'tok', [(t, target(t)) for t in range(count)])]
    pallas_call x10 -> x11, Pallas kernels: 13.4 us -> 13.9 us  [call(): pl.pallas_call(kernel, out_shape=outs, in_specs=[SMEM] + specs, out_specs...]
  transfers between devices with their start and end apart: 19 -> 24, of which waited for: 8 -> 7; matrix products, arithmetic and copies ran while one was open for 0% -> 0% of each run, Pallas kernels for 14% -> 15%
where the time goes in v8:
time: 62.4 us; the launch traced here: 62.2 us
  starting transfers between devices  29.7 us (48%)
  waiting for transfers between devices  17.5 us (28%)
  Pallas kernels  13.9 us (22%)
  between operations  0.97 us (2%)
    ppermute x24, starting transfers between devices, move(): return lax.ppermute(value, 'tok', [(t, target(t)) for t in range(count)])  29.7 us
    ppermute x24, waiting for transfers between devices, move(): return lax.ppermute(value, 'tok', [(t, target(t)) for t in range(count)])  17.5 us
    pallas_call x11, Pallas kernels, call(): pl.pallas_call(kernel, out_shape=outs, in_specs=[SMEM] + specs, out_specs...  13.9 us
  transfers between devices with their start and end apart: 24, of which 7 were waited for; matrix products, arithmetic and copies ran while one was open for 0% of the time, Pallas kernels for 15%

profile of v8, /device:TPU:0, one launch (start us, length us, event | category | flops | bytes accessed | tf_op | source)
XLA Modules:
  0.0 62.2 jit_solution(7563608705429590531)
XLA Ops:
  0.7 2.0 %shard_map.94 = (bf16[264,128]{1,0:T(8,128)(2,1)S(1)}, bf16[264,128]{1,0:T(8,128)(2,1)S(1)}, bf16[264,128]{1,0:T(8,128)(2,1)S(1)}, bf16[264,128]{1,0:T(8,128)(2,...) custom-call(s32[2]{0:T(128)S(1)} %pad_add_fusion.place, bf16[128,512]{1,0:T(8,128)(2,1)} %key_ref.1, ...), custom_call_target="tpu_custom_call" | custom-call | bytes 2630152 | tf_op jit(solution)/shard_map/pallas_call | solution.py:42
  2.7 0.6 collective-permute-start.3
  3.3 2.6 %collective-permute-start.4 = (bf16[264,128]{1,0:T(8,128)(2,1)S(1)}, bf16[264,128]{1,0:T(8,128)(2,1)S(1)}, u32[]{:S(2)}, u32[]{:S(2)}) collective-permute-start(bf16[264,128]{1,0:T(8,128)(2,1)S(1)} %get-tuple-element.48), channel_id=1, source_target_pairs={{0,2},{1,3},{2,0},{3,1},{4,6},{5,7},{6,4},{7,5},{8,10},{9,11},{10,... | collective-permute-start | bytes 202760 | tf_op jit(solution)/shard_map/ppermute | solution.py:320
  5.9 2.0 %shard_map.95 = (bf16[1048,128]{1,0:T(8,128)(2,1)S(1)}, bf16[1048,128]{1,0:T(8,128)(2,1)S(1)}, bf16[1048,128]{1,0:T(8,128)(2,1)S(1)}, bf16[1048,128]{1,0:T(8,128)(2,1)S(1)}, f32[8,128]{1,0:T(8,128)S(1)}) custom-call(s32[2]{0:T(128)S(1)} %pad_add_fusion.place, bf16[128,2048]{1,0:T(8,128)(2,1)} %query_ref.1, bf16[128,2048]{1,0:T(8,128)(2,1)S(1)} %get-tuple-element.40.grads, ...), custom_call_target="tpu_custom_call" | custom-call | bytes 2658312 | tf_op jit(solution)/shard_map/pallas_call | solution.py:42
  7.9 0.7 %collective-permute-done.4.refs_2_ = bf16[264,128]{1,0:T(8,128)(2,1)S(1)} collective-permute-done((bf16[264,128]{1,0:T(8,128)(2,1)S(1)}, bf16[264,128]{1,0:T(8,128)(2,1)S(1)}, u32[]{:S(2)}, u32[]{:S(2)}) %collective-permute-start.4) | collective-permute-done | bytes 67616 | tf_op jit(solution)/shard_map/ppermute | solution.py:320
  8.6 1.4 %collective-permute-done.5.refs_3_ = bf16[264,128]{1,0:T(8,128)(2,1)S(1)} collective-permute-done((bf16[264,128]{1,0:T(8,128)(2,1)S(1)}, bf16[264,128]{1,0:T(8,128)(2,1)S(1)}, u32[]{:S(2)}, u32[]{:S(2)}) %collective-permute-start.5) | collective-permute-done | bytes 67616 | tf_op jit(solution)/shard_map/ppermute | solution.py:320
  10.0 0.6 shard_map.96.refs_4_.refs_5_
  10.6 1.6 %collective-permute-start.6 = (bf16[1056,128]{1,0:T(8,128)(2,1)S(1)}, bf16[1056,128]{1,0:T(8,128)(2,1)S(1)}, u32[]{:S(2)}, u32[]{:S(2)}) collective-permute-start(bf16[1056,128]{1,0:T(8,128)(2,1)S(1)} %shard_map.96.refs_4_.refs_5_), channel_id=1, source_target_pairs={{0,4},{1,5},{2,6},{3,7},{4,8},{5,9},{6,10},{7,11},{8,12},{9,13},{1... | collective-permute-start | bytes 811016 | tf_op jit(solution)/shard_map/ppermute | solution.py:320
  12.2 1.4 %collective-permute-start.1 = (bf16[1048,128]{1,0:T(8,128)(2,1)S(1)}, bf16[1048,128]{1,0:T(8,128)(2,1)S(1)}, u32[]{:S(2)}, u32[]{:S(2)}) collective-permute-start(bf16[1048,128]{1,0:T(8,128)(2,1)S(1)} %get-tuple-element.44), channel_id=1, source_target_pairs={{0,2},{1,3},{2,0},{3,1},{4,6},{5,7},{6,4},{7,5},{8,10},{9,11},{10,... | collective-permute-start | bytes 804872 | tf_op jit(solution)/shard_map/ppermute | solution.py:320
  13.5 0.5 collective-permute-start.2
  14.0 7.0 %collective-permute-done.6.refs_5_ = bf16[1056,128]{1,0:T(8,128)(2,1)S(1)} collective-permute-done((bf16[1056,128]{1,0:T(8,128)(2,1)S(1)}, bf16[1056,128]{1,0:T(8,128)(2,1)S(1)}, u32[]{:S(2)}, u32[]{:S(2)}) %collective-permute-start.6) | collective-permute-done | bytes 270368 | tf_op jit(solution)/shard_map/ppermute | solution.py:320
  21.5 4.8 %collective-permute-done.2.refs_3_ = bf16[1048,128]{1,0:T(8,128)(2,1)S(1)} collective-permute-done((bf16[1048,128]{1,0:T(8,128)(2,1)S(1)}, bf16[1048,128]{1,0:T(8,128)(2,1)S(1)}, u32[]{:S(2)}, u32[]{:S(2)}) %collective-permute-start.2) | collective-permute-done | bytes 268320 | tf_op jit(solution)/shard_map/ppermute | solution.py:320
  26.3 3.4 %shard_map.97 = (f32[4,128,512]{2,1,0:T(8,128)S(1)}, f32[512,128]{1,0:T(8,128)S(1)}, f32[512,128]{1,0:T(8,128)S(1)}) custom-call(s32[2]{0:T(128)S(1)} %pad_add_fusion.place, bf16[1048,128]{1,0:T(8,128)(2,1)S(1)} %get-tuple-element.42.refs_0_, bf16[1048,128]{1,0:T(8,128)(2,1)S(1)} %collective-permute-done.refs_1_, ...), custom_call_target="tpu_custom_call" | custom-call | flops 1342177280 | bytes 3186696 | tf_op jit(solution)/shard_map/pallas_call | solution.py:42
  29.8 0.8 %shard_map.98 = (f32[4,128,512]{2,1,0:T(8,128)S(1)}, bf16[512,128]{1,0:T(8,128)(2,1)S(1)}, bf16[512,128]{1,0:T(8,128)(2,1)S(1)}) custom-call(s32[2]{0:T(128)S(1)} %pad_add_fusion.place, bf16[1048,128]{1,0:T(8,128)(2,1)S(1)} %get-tuple-element.42.refs_0_, bf16[1048,128]{1,0:T(8,128)(2,1)S(1)} %collective-permute-done.refs_1_, ...), custom_call_target="tpu_custom_call" | custom-call | flops 1342177280 | bytes 3973128 | tf_op jit(solution)/shard_map/pallas_call | solution.py:42
  31.2 0.6 shard_map.101
  32.1 1.3 %collective-permute-start.12 = (bf16[256,128]{1,0:T(8,128)(2,1)S(1)}, bf16[256,128]{1,0:T(8,128)(2,1)S(1)}, u32[]{:S(2)}, u32[]{:S(2)}) collective-permute-start(bf16[256,128]{1,0:T(8,128)(2,1)S(1)} %get-tuple-element.62), channel_id=1, source_target_pairs={{0,2},{1,3},{2,0},{3,1},{4,6},{5,7},{6,4},{7,5},{8,10},{9,11},{10,... | collective-permute-start | bytes 196616 | tf_op jit(solution)/shard_map/ppermute | solution.py:320
  33.4 0.6 %shard_map.99 = (bf16[128,512]{1,0:T(8,128)(2,1)S(1)}, bf16[128,512]{1,0:T(8,128)(2,1)S(1)}, bf16[128,512]{1,0:T(8,128)(2,1)S(1)}, bf16[128,512]{1,0:T(8,128)(2,...) custom-call(s32[2]{0:T(128)S(1)} %pad_add_fusion.place, bf16[1048,128]{1,0:T(8,128)(2,1)S(1)} %get-tuple-element.42.refs_0_, ...), custom_call_target="tpu_custom_call" | custom-call | flops 1342177280 | bytes 3710984 | tf_op jit(solution)/shard_map/pallas_call | solution.py:42
  34.0 0.6 shard_map.102
  34.6 7.6 %collective-permute-start.17 = (bf16[256,128]{1,0:T(8,128)(2,1)S(1)}, bf16[256,128]{1,0:T(8,128)(2,1)S(1)}, u32[]{:S(2)}, u32[]{:S(2)}) collective-permute-start(bf16[256,128]{1,0:T(8,128)(2,1)S(1)} %get-tuple-element.68), channel_id=1, source_target_pairs={{0,12},{1,13},{2,14},{3,15},{4,2},{5,3},{6,0},{7,1},{8,6},{9,7},{1... | collective-permute-start | bytes 196616 | tf_op jit(solution)/shard_map/ppermute | solution.py:320
  42.2 1.1 %collective-permute-start.9 = (bf16[128,512]{1,0:T(8,128)(2,1)S(1)}, bf16[128,512]{1,0:T(8,128)(2,1)S(1)}, u32[]{:S(2)}, u32[]{:S(2)}) collective-permute-start(bf16[128,512]{1,0:T(8,128)(2,1)S(1)} %get-tuple-element.55), channel_id=1, source_target_pairs={{0,2},{1,3},{2,0},{3,1},{4,6},{5,7},{6,4},{7,5},{8,10},{9,11},{10,... | collective-permute-start | bytes 393224 | tf_op jit(solution)/shard_map/ppermute | solution.py:320
  43.3 0.8 %collective-permute-start.10 = (bf16[128,512]{1,0:T(8,128)(2,1)S(1)}, bf16[128,512]{1,0:T(8,128)(2,1)S(1)}, u32[]{:S(2)}, u32[]{:S(2)}) collective-permute-start(bf16[128,512]{1,0:T(8,128)(2,1)S(1)} %get-tuple-element.56), channel_id=1, source_target_pairs={{0,3},{1,2},{2,1},{3,0},{4,7},{5,6},{6,5},{7,4},{8,11},{9,10},{10,... | collective-permute-start | bytes 393224 | tf_op jit(solution)/shard_map/ppermute | solution.py:320
  44.1 0.6 shard_map.103
  44.7 2.8 %collective-permute-start.22 = (bf16[256,128]{1,0:T(8,128)(2,1)S(1)}, bf16[256,128]{1,0:T(8,128)(2,1)S(1)}, u32[]{:S(2)}, u32[]{:S(2)}) collective-permute-start(bf16[256,128]{1,0:T(8,128)(2,1)S(1)} %get-tuple-element.73), channel_id=1, source_target_pairs={{0,12},{1,13},{2,14},{3,15},{4,2},{5,3},{6,0},{7,1},{8,6},{9,7},{1... | collective-permute-start | bytes 196616 | tf_op jit(solution)/shard_map/ppermute | solution.py:320
  47.5 0.8 %collective-permute-start.13 = (bf16[256,128]{1,0:T(8,128)(2,1)S(1)}, bf16[256,128]{1,0:T(8,128)(2,1)S(1)}, u32[]{:S(2)}, u32[]{:S(2)}) collective-permute-start(bf16[256,128]{1,0:T(8,128)(2,1)S(1)} %get-tuple-element.63), channel_id=1, source_target_pairs={{0,3},{1,2},{2,1},{3,0},{4,7},{5,6},{6,5},{7,4},{8,11},{9,10},{10,... | collective-permute-start | bytes 196616 | tf_op jit(solution)/shard_map/ppermute | solution.py:320
  48.3 1.7 %collective-permute-done.22.refs_10_ = bf16[256,128]{1,0:T(8,128)(2,1)S(1)} collective-permute-done((bf16[256,128]{1,0:T(8,128)(2,1)S(1)}, bf16[256,128]{1,0:T(8,128)(2,1)S(1)}, u32[]{:S(2)}, u32[]{:S(2)}) %collective-permute-start.22) | collective-permute-done | bytes 65568 | tf_op jit(solution)/shard_map/ppermute | solution.py:320
  50.0 3.5 %collective-permute-start.15 = (bf16[128,128]{1,0:T(8,128)(2,1)S(1)}, bf16[128,128]{1,0:T(8,128)(2,1)S(1)}, u32[]{:S(2)}, u32[]{:S(2)}) collective-permute-start(bf16[128,128]{1,0:T(8,128)(2,1)S(1)} %get-tuple-element.66), channel_id=1, source_target_pairs={{0,12},{1,13},{2,14},{3,15},{4,0},{5,1},{6,2},{7,3},{8,4},{9,5},{1... | collective-permute-start | bytes 98312 | tf_op jit(solution)/shard_map/ppermute | solution.py:320
  53.5 1.1 %collective-permute-start.16 = (bf16[128,128]{1,0:T(8,128)(2,1)S(1)}, bf16[128,128]{1,0:T(8,128)(2,1)S(1)}, u32[]{:S(2)}, u32[]{:S(2)}) collective-permute-start(bf16[128,128]{1,0:T(8,128)(2,1)S(1)} %get-tuple-element.67), channel_id=1, source_target_pairs={{0,12},{1,13},{2,14},{3,15},{4,1},{5,0},{6,3},{7,2},{8,5},{9,4},{1... | collective-permute-start | bytes 98312 | tf_op jit(solution)/shard_map/ppermute | solution.py:320
  54.6 2.6 %collective-permute-start.20 = (bf16[128,128]{1,0:T(8,128)(2,1)S(1)}, bf16[128,128]{1,0:T(8,128)(2,1)S(1)}, u32[]{:S(2)}, u32[]{:S(2)}) collective-permute-start(bf16[128,128]{1,0:T(8,128)(2,1)S(1)} %get-tuple-element.71), channel_id=1, source_target_pairs={{0,12},{1,13},{2,14},{3,15},{4,0},{5,1},{6,2},{7,3},{8,4},{9,5},{1... | collective-permute-start | bytes 98312 | tf_op jit(solution)/shard_map/ppermute | solution.py:320
  57.3 0.5 collective-permute-start.23
  57.9 1.4 %shard_map.100 = (bf16[128,2048]{1,0:T(8,128)(2,1)}, f32[8,128]{1,0:T(8,128)S(1)}) custom-call(s32[2]{0:T(128)S(1)} %pad_add_fusion.place, bf16[128,512]{1,0:T(8,128)(2,1)S(1)} %get-tuple-element.53.refs_0_, bf16[128,512]{1,0:T(8,128)(2,1)S(1)} %collective-permute-done.8.refs_1_, bf16[128,512]{1,0:T(8,128)(2,1)S(1)} %collective-permute-done.9.refs_2_, ...), custom_call_target="tpu_custom_call" | custom-call | bytes 1052680 | tf_op jit(solution)/shard_map/pallas_call | solution.py:42
  59.3 1.4 %collective-permute-done.21.refs_9_ = bf16[128,128]{1,0:T(8,128)(2,1)S(1)} collective-permute-done((bf16[128,128]{1,0:T(8,128)(2,1)S(1)}, bf16[128,128]{1,0:T(8,128)(2,1)S(1)}, u32[]{:S(2)}, u32[]{:S(2)}) %collective-permute-start.21) | collective-permute-done | bytes 32800 | tf_op jit(solution)/shard_map/ppermute | solution.py:320
  60.7 1.3 %shard_map.104 = (bf16[128,512]{1,0:T(8,128)(2,1)}, bf16[128,512]{1,0:T(8,128)(2,1)}) custom-call(s32[2]{0:T(128)S(1)} %pad_add_fusion.place, bf16[256,128]{1,0:T(8,128)(2,1)S(1)} %get-tuple-element.60.refs_0_, bf16[256,128]{1,0:T(8,128)(2,1)S(1)} %collective-permute-done.11.refs_1_, bf16[256,128]{1,0:T(8,128)(2,1)S(1)} %collective-permute-done.12.refs_2_, ...), custom_call_target="tpu_custom_call" | custom-call | bytes 856072 | tf_op jit(solution)/shard_map/pallas_call | solution.py:42
  (32 shorter events, 1.7 us)
Async XLA Ops:
  2.7 3.2 %copy-start = (f32[16,128]{1,0:T(8,128)S(1)}, f32[16,128]{1,0:T(8,128)}, u32[]{:S(2)}) copy-start(f32[16,128]{1,0:T(8,128)} %norm_ref.1) | copy-start | bytes 24580
  2.7 5.2 %collective-permute-start.3 = (bf16[264,128]{1,0:T(8,128)(2,1)S(1)}, bf16[264,128]{1,0:T(8,128)(2,1)S(1)}, u32[]{:S(2)}, u32[]{:S(2)}) collective-permute-start(bf16[264,128]{1,0:T(8,128)(2,1)S(1)} %get-tuple-element.47), channel_id=1, source_target_pairs={{0,1},{1,0},{2,3},{3,2},{4,5},{5,4},{6,7},{7,6},{8,9},{9,8},{10,11... | collective-permute-start | bytes 202760 | tf_op jit(solution)/shard_map/ppermute | solution.py:320
  3.3 5.3 %collective-permute-start.4 = (bf16[264,128]{1,0:T(8,128)(2,1)S(1)}, bf16[264,128]{1,0:T(8,128)(2,1)S(1)}, u32[]{:S(2)}, u32[]{:S(2)}) collective-permute-start(bf16[264,128]{1,0:T(8,128)(2,1)S(1)} %get-tuple-element.48), channel_id=1, source_target_pairs={{0,2},{1,3},{2,0},{3,1},{4,6},{5,7},{6,4},{7,5},{8,10},{9,11},{10,... | collective-permute-start | bytes 202760 | tf_op jit(solution)/shard_map/ppermute | solution.py:320
  5.9 4.1 %collective-permute-start.5 = (bf16[264,128]{1,0:T(8,128)(2,1)S(1)}, bf16[264,128]{1,0:T(8,128)(2,1)S(1)}, u32[]{:S(2)}, u32[]{:S(2)}) collective-permute-start(bf16[264,128]{1,0:T(8,128)(2,1)S(1)} %get-tuple-element.49), channel_id=1, source_target_pairs={{0,3},{1,2},{2,1},{3,0},{4,7},{5,6},{6,5},{7,4},{8,11},{9,10},{10,... | collective-permute-start | bytes 202760 | tf_op jit(solution)/shard_map/ppermute | solution.py:320
  10.6 10.5 %collective-permute-start.6 = (bf16[1056,128]{1,0:T(8,128)(2,1)S(1)}, bf16[1056,128]{1,0:T(8,128)(2,1)S(1)}, u32[]{:S(2)}, u32[]{:S(2)}) collective-permute-start(bf16[1056,128]{1,0:T(8,128)(2,1)S(1)} %shard_map.96.refs_4_.refs_5_), channel_id=1, source_target_pairs={{0,4},{1,5},{2,6},{3,7},{4,8},{5,9},{6,10},{7,11},{8,12},{9,13},{1... | collective-permute-start | bytes 811016 | tf_op jit(solution)/shard_map/ppermute | solution.py:320
  12.2 8.8 %collective-permute-start = (bf16[1048,128]{1,0:T(8,128)(2,1)S(1)}, bf16[1048,128]{1,0:T(8,128)(2,1)S(1)}, u32[]{:S(2)}, u32[]{:S(2)}) collective-permute-start(bf16[1048,128]{1,0:T(8,128)(2,1)S(1)} %get-tuple-element.43), channel_id=1, source_target_pairs={{0,1},{1,0},{2,3},{3,2},{4,5},{5,4},{6,7},{7,6},{8,9},{9,8},{10,11... | collective-permute-start | bytes 804872 | tf_op jit(solution)/shard_map/ppermute | solution.py:320
  12.2 9.3 %collective-permute-start.1 = (bf16[1048,128]{1,0:T(8,128)(2,1)S(1)}, bf16[1048,128]{1,0:T(8,128)(2,1)S(1)}, u32[]{:S(2)}, u32[]{:S(2)}) collective-permute-start(bf16[1048,128]{1,0:T(8,128)(2,1)S(1)} %get-tuple-element.44), channel_id=1, source_target_pairs={{0,2},{1,3},{2,0},{3,1},{4,6},{5,7},{6,4},{7,5},{8,10},{9,11},{10,... | collective-permute-start | bytes 804872 | tf_op jit(solution)/shard_map/ppermute | solution.py:320
  13.5 12.8 %collective-permute-start.2 = (bf16[1048,128]{1,0:T(8,128)(2,1)S(1)}, bf16[1048,128]{1,0:T(8,128)(2,1)S(1)}, u32[]{:S(2)}, u32[]{:S(2)}) collective-permute-start(bf16[1048,128]{1,0:T(8,128)(2,1)S(1)} %get-tuple-element.45), channel_id=1, source_target_pairs={{0,3},{1,2},{2,1},{3,0},{4,7},{5,6},{6,5},{7,4},{8,11},{9,10},{10,... | collective-permute-start | bytes 804872 | tf_op jit(solution)/shard_map/ppermute | solution.py:320
  21.0 8.7 %collective-permute-start.7 = (bf16[1056,128]{1,0:T(8,128)(2,1)S(1)}, bf16[1056,128]{1,0:T(8,128)(2,1)S(1)}, u32[]{:S(2)}, u32[]{:S(2)}) collective-permute-start(bf16[1056,128]{1,0:T(8,128)(2,1)S(1)} %collective-permute-done.6.refs_5_), channel_id=1, source_target_pairs={{0,1},{1,0},{2,3},{3,2},{4,8},{5,9},{6,10},{7,11},{8,12},{9,13},{1... | collective-permute-start | bytes 811016 | tf_op jit(solution)/shard_map/ppermute | solution.py:320
  30.6 3.4 %collective-permute-start.14 = (bf16[512,128]{1,0:T(8,128)(2,1)S(1)}, bf16[512,128]{1,0:T(8,128)(2,1)S(1)}, u32[]{:S(2)}, u32[]{:S(2)}) collective-permute-start(bf16[512,128]{1,0:T(8,128)(2,1)S(1)} %get-tuple-element.64), channel_id=1, source_target_pairs={{0,1},{1,0},{2,3},{3,2},{4,12},{5,13},{6,14},{7,15},{8,4},{9,5},{1... | collective-permute-start | bytes 393224 | tf_op jit(solution)/shard_map/ppermute | solution.py:320
  30.9 12.4 %collective-permute-start.19 = (bf16[512,128]{1,0:T(8,128)(2,1)S(1)}, bf16[512,128]{1,0:T(8,128)(2,1)S(1)}, u32[]{:S(2)}, u32[]{:S(2)}) collective-permute-start(bf16[512,128]{1,0:T(8,128)(2,1)S(1)} %get-tuple-element.69), channel_id=1, source_target_pairs={{0,1},{1,0},{2,3},{3,2},{4,12},{5,13},{6,14},{7,15},{8,4},{9,5},{1... | collective-permute-start | bytes 393224 | tf_op jit(solution)/shard_map/ppermute | solution.py:320
  31.7 10.5 %collective-permute-start.11 = (bf16[256,128]{1,0:T(8,128)(2,1)S(1)}, bf16[256,128]{1,0:T(8,128)(2,1)S(1)}, u32[]{:S(2)}, u32[]{:S(2)}) collective-permute-start(bf16[256,128]{1,0:T(8,128)(2,1)S(1)} %get-tuple-element.61), channel_id=1, source_target_pairs={{0,1},{1,0},{2,3},{3,2},{4,5},{5,4},{6,7},{7,6},{8,9},{9,8},{10,11... | collective-permute-start | bytes 196616 | tf_op jit(solution)/shard_map/ppermute | solution.py:320
  32.1 12.6 %collective-permute-start.12 = (bf16[256,128]{1,0:T(8,128)(2,1)S(1)}, bf16[256,128]{1,0:T(8,128)(2,1)S(1)}, u32[]{:S(2)}, u32[]{:S(2)}) collective-permute-start(bf16[256,128]{1,0:T(8,128)(2,1)S(1)} %get-tuple-element.62), channel_id=1, source_target_pairs={{0,2},{1,3},{2,0},{3,1},{4,6},{5,7},{6,4},{7,5},{8,10},{9,11},{10,... | collective-permute-start | bytes 196616 | tf_op jit(solution)/shard_map/ppermute | solution.py:320
  34.6 12.9 %collective-permute-start.17 = (bf16[256,128]{1,0:T(8,128)(2,1)S(1)}, bf16[256,128]{1,0:T(8,128)(2,1)S(1)}, u32[]{:S(2)}, u32[]{:S(2)}) collective-permute-start(bf16[256,128]{1,0:T(8,128)(2,1)S(1)} %get-tuple-element.68), channel_id=1, source_target_pairs={{0,12},{1,13},{2,14},{3,15},{4,2},{5,3},{6,0},{7,1},{8,6},{9,7},{1... | collective-permute-start | bytes 196616 | tf_op jit(solution)/shard_map/ppermute | solution.py:320
  42.2 12.4 %collective-permute-start.8 = (bf16[128,512]{1,0:T(8,128)(2,1)S(1)}, bf16[128,512]{1,0:T(8,128)(2,1)S(1)}, u32[]{:S(2)}, u32[]{:S(2)}) collective-permute-start(bf16[128,512]{1,0:T(8,128)(2,1)S(1)} %get-tuple-element.54), channel_id=1, source_target_pairs={{0,1},{1,0},{2,3},{3,2},{4,5},{5,4},{6,7},{7,6},{8,9},{9,8},{10,11... | collective-permute-start | bytes 393224 | tf_op jit(solution)/shard_map/ppermute | solution.py:320
  42.2 14.9 %collective-permute-start.9 = (bf16[128,512]{1,0:T(8,128)(2,1)S(1)}, bf16[128,512]{1,0:T(8,128)(2,1)S(1)}, u32[]{:S(2)}, u32[]{:S(2)}) collective-permute-start(bf16[128,512]{1,0:T(8,128)(2,1)S(1)} %get-tuple-element.55), channel_id=1, source_target_pairs={{0,2},{1,3},{2,0},{3,1},{4,6},{5,7},{6,4},{7,5},{8,10},{9,11},{10,... | collective-permute-start | bytes 393224 | tf_op jit(solution)/shard_map/ppermute | solution.py:320
  43.3 14.0 %collective-permute-start.10 = (bf16[128,512]{1,0:T(8,128)(2,1)S(1)}, bf16[128,512]{1,0:T(8,128)(2,1)S(1)}, u32[]{:S(2)}, u32[]{:S(2)}) collective-permute-start(bf16[128,512]{1,0:T(8,128)(2,1)S(1)} %get-tuple-element.56), channel_id=1, source_target_pairs={{0,3},{1,2},{2,1},{3,0},{4,7},{5,6},{6,5},{7,4},{8,11},{9,10},{10,... | collective-permute-start | bytes 393224 | tf_op jit(solution)/shard_map/ppermute | solution.py:320
  44.7 5.3 %collective-permute-start.22 = (bf16[256,128]{1,0:T(8,128)(2,1)S(1)}, bf16[256,128]{1,0:T(8,128)(2,1)S(1)}, u32[]{:S(2)}, u32[]{:S(2)}) collective-permute-start(bf16[256,128]{1,0:T(8,128)(2,1)S(1)} %get-tuple-element.73), channel_id=1, source_target_pairs={{0,12},{1,13},{2,14},{3,15},{4,2},{5,3},{6,0},{7,1},{8,6},{9,7},{1... | collective-permute-start | bytes 196616 | tf_op jit(solution)/shard_map/ppermute | solution.py:320
  47.5 6.1 %collective-permute-start.13 = (bf16[256,128]{1,0:T(8,128)(2,1)S(1)}, bf16[256,128]{1,0:T(8,128)(2,1)S(1)}, u32[]{:S(2)}, u32[]{:S(2)}) collective-permute-start(bf16[256,128]{1,0:T(8,128)(2,1)S(1)} %get-tuple-element.63), channel_id=1, source_target_pairs={{0,3},{1,2},{2,1},{3,0},{4,7},{5,6},{6,5},{7,4},{8,11},{9,10},{10,... | collective-permute-start | bytes 196616 | tf_op jit(solution)/shard_map/ppermute | solution.py:320
  50.0 7.3 %collective-permute-start.15 = (bf16[128,128]{1,0:T(8,128)(2,1)S(1)}, bf16[128,128]{1,0:T(8,128)(2,1)S(1)}, u32[]{:S(2)}, u32[]{:S(2)}) collective-permute-start(bf16[128,128]{1,0:T(8,128)(2,1)S(1)} %get-tuple-element.66), channel_id=1, source_target_pairs={{0,12},{1,13},{2,14},{3,15},{4,0},{5,1},{6,2},{7,3},{8,4},{9,5},{1... | collective-permute-start | bytes 98312 | tf_op jit(solution)/shard_map/ppermute | solution.py:320
  53.5 5.8 %collective-permute-start.16 = (bf16[128,128]{1,0:T(8,128)(2,1)S(1)}, bf16[128,128]{1,0:T(8,128)(2,1)S(1)}, u32[]{:S(2)}, u32[]{:S(2)}) collective-permute-start(bf16[128,128]{1,0:T(8,128)(2,1)S(1)} %get-tuple-element.67), channel_id=1, source_target_pairs={{0,12},{1,13},{2,14},{3,15},{4,1},{5,0},{6,3},{7,2},{8,5},{9,4},{1... | collective-permute-start | bytes 98312 | tf_op jit(solution)/shard_map/ppermute | solution.py:320
  54.6 4.7 %collective-permute-start.20 = (bf16[128,128]{1,0:T(8,128)(2,1)S(1)}, bf16[128,128]{1,0:T(8,128)(2,1)S(1)}, u32[]{:S(2)}, u32[]{:S(2)}) collective-permute-start(bf16[128,128]{1,0:T(8,128)(2,1)S(1)} %get-tuple-element.71), channel_id=1, source_target_pairs={{0,12},{1,13},{2,14},{3,15},{4,0},{5,1},{6,2},{7,3},{8,4},{9,5},{1... | collective-permute-start | bytes 98312 | tf_op jit(solution)/shard_map/ppermute | solution.py:320
  57.2 3.5 %collective-permute-start.21 = (bf16[128,128]{1,0:T(8,128)(2,1)S(1)}, bf16[128,128]{1,0:T(8,128)(2,1)S(1)}, u32[]{:S(2)}, u32[]{:S(2)}) collective-permute-start(bf16[128,128]{1,0:T(8,128)(2,1)S(1)} %get-tuple-element.72), channel_id=1, source_target_pairs={{0,12},{1,13},{2,14},{3,15},{4,1},{5,0},{6,3},{7,2},{8,5},{9,4},{1... | collective-permute-start | bytes 98312 | tf_op jit(solution)/shard_map/ppermute | solution.py:320
  57.3 3.4 %collective-permute-start.18 = (bf16[128,128]{1,0:T(8,128)(2,1)S(1)}, bf16[128,128]{1,0:T(8,128)(2,1)S(1)}, u32[]{:S(2)}, u32[]{:S(2)}) collective-permute-start(bf16[128,128]{1,0:T(8,128)(2,1)S(1)} %slice.8), channel_id=1, source_target_pairs={{0,1},{1,0},{2,3},{3,2},{4,5},{5,4},{6,7},{7,6},{8,9},{9,8},{10,11... | collective-permute-start | bytes 98312 | tf_op jit(solution)/shard_map/ppermute | solution.py:320
  57.3 3.4 %collective-permute-start.23 = (bf16[128,128]{1,0:T(8,128)(2,1)S(1)}, bf16[128,128]{1,0:T(8,128)(2,1)S(1)}, u32[]{:S(2)}, u32[]{:S(2)}) collective-permute-start(bf16[128,128]{1,0:T(8,128)(2,1)S(1)} %slice.9), channel_id=1, source_target_pairs={{0,1},{1,0},{2,3},{3,2},{4,5},{5,4},{6,7},{7,6},{8,9},{9,8},{10,11... | collective-permute-start | bytes 98312 | tf_op jit(solution)/shard_map/ppermute | solution.py:320

commit v9 on v7

--- a/solution.py
+++ b/solution.py
@@ -142,6 +142,8 @@
     own, key_ref, refs = refs[0], refs[1], refs[2:]
     if not first:
         dq_in, refs = refs[0], refs[1:]
+    if last and not first:
+        own_terms, refs = refs[0], refs[1:]
     if last:
         dq_out, refs = refs[:parts], refs[parts:]
     else:
@@ -217,9 +219,19 @@
         for s in range(parts):
             total = dq[s] if first else dq[s] + dq_in[s]
             if last:
-                dq_out[s][...] = total.astype(BF16)
+                close(s, total)
             else:
                 dq_out[s] = total
+
+    def close(s, total):
+        out, a = dq_out[s], me ^ s
+        for h in range(GROUP):
+            at = slice(h * HEAD_SIZE, (h + 1) * HEAD_SIZE)
+            out[at, :] = total[:, h * rows : (h + 1) * rows].astype(BF16)
+        for k in range(2):
+            at = GROUP * HEAD_SIZE + k * rows
+            term = (kv_out if first else own_terms)[pl.ds(pl.multiple_of(k * span + a * rows, rows), rows), :]
+            out[at : at + rows, :] = term.astype(BF16)
 
     if first:
         work()
@@ -230,7 +242,7 @@
         kv_out[...] = jnp.zeros_like(kv_out)
         for s in range(parts):
             if last:
-                dq_out[s][...] = dq_in[s].astype(BF16)
+                close(s, dq_in[s])
             else:
                 dq_out[s] = dq_in[s]
 
@@ -253,14 +265,14 @@
                 out[start : start + rows, :] = total.astype(BF16)
 
 
-def spread_queries(rows, place, *refs):
+def spread_queries(place, *refs):
     pieces, (out, token, turned, sems) = refs[:-4], refs[-4:]
     width = GROUP * HEAD_SIZE
     copies = []
     for s, piece in enumerate(pieces):
         for h in range(GROUP):
             cut = slice(h * HEAD_SIZE, (h + 1) * HEAD_SIZE)
-            turned[s, :, cut] = piece[:, h * rows : (h + 1) * rows].T
+            turned[s, :, cut] = piece[cut, :].T
         cut = pl.ds(pl.multiple_of((place[1] ^ s) * width, width), width)
         copies.append(pltpu.make_async_copy(turned.at[s], out.at[:, cut], sems.at[s]))
         copies[-1].start()
@@ -274,7 +286,7 @@
     pieces, (key_out, value_out, total, sems) = refs[:-5], refs[-4:]
     copies = []
     for s in range(parts):
-        term = pieces[s][...].astype(F32)
+        term = pieces[s][GROUP * HEAD_SIZE :, :].astype(F32)
         for k in range(1, sources):
             term = term + pieces[k * parts + s][0 : 2 * rows, :].astype(F32)
         total[s] = term.astype(BF16)
@@ -351,14 +363,16 @@
 
     kv_shape = (2 * span, HEAD_SIZE)
     stages = [0] + list(range(behind, 0, -1))
-    dq, own_pieces, sent = None, None, None
+    dq, own_terms, sent = None, None, None
     for k, offset in enumerate(stages):
         first, last = k == 0, k == len(stages) - 1
         ins = [place, *query_pieces, own, windows[offset]]
         if not first:
             ins.append(dq)
+        if last and not first:
+            ins.append(own_terms)
         if last:
-            outs = [shape((HEAD_SIZE, width), BF16)] * parts
+            outs = [shape((GROUP * HEAD_SIZE + 2 * rows, rows), BF16)] * parts
         else:
             outs = [shape((parts, HEAD_SIZE, width), F32)]
         outs = outs + [shape(kv_shape, BF16 if offset == behind > 0 else F32)]
@@ -370,14 +384,8 @@
             flops=10 * span * span * GROUP * HEAD_SIZE,
         )
         dq, term = (got[:parts] if last else got[0]), got[-1]
-        piece_shapes = [shape((2 * rows, HEAD_SIZE), BF16)] * parts
         if offset == 0:
-            own_pieces = call(
-                functools.partial(cut_terms, rows, 1, [[s] for s in range(parts)]),
-                (place, term),
-                piece_shapes,
-            )
-            own_pieces = exchange(own_pieces)
+            own_terms = term
         elif offset == 1:
             terms = (term,) if sent is None else (sent, term)
             groups = ((2, 3), (0,), (1,))
@@ -396,7 +404,7 @@
 
     dq_pieces = exchange(dq)
     query_grad, token = call(
-        functools.partial(spread_queries, rows),
+        spread_queries,
         (place, *dq_pieces),
         [shape((rows, parts * GROUP * HEAD_SIZE), BF16), TOKEN],
         scratch=[
@@ -405,7 +413,7 @@
         ],
         out_specs=[HBM, VMEM],
     )
-    pieces = own_pieces + (sent or [])
+    pieces = dq_pieces + (sent or [])
     key_grad, value_grad = call(
         functools.partial(spread_keys, rows, len(pieces) // parts),
         (place, *pieces, token),

time: 58.9 us -> 55.9 us (0.949)
  starting transfers between devices: 27.6 us -> 24.6 us
  Pallas kernels: 13.4 us -> 12.8 us
    ppermute x19 -> x16, starting transfers between devices: 27.6 us -> 24.6 us  [move(): return lax.ppermute(value, 'tok', [(t, target(t)) for t in range(count)])]
    ppermute x19 -> x16, waiting for transfers between devices: 16.7 us -> 17.2 us  [move(): return lax.ppermute(value, 'tok', [(t, target(t)) for t in range(count)])]
    pallas_call x10 -> x9, Pallas kernels: 13.4 us -> 12.8 us  [call(): pl.pallas_call(kernel, out_shape=outs, in_specs=[SMEM] + specs, out_specs...]
  transfers between devices with their start and end apart: 19 -> 16, of which waited for: 8 -> 7; matrix products, arithmetic and copies ran while one was open for 0% -> 0% of each run, Pallas kernels for 14% -> 15%
where the time goes in v9:
time: 55.9 us; the launch traced here: 55.7 us
  starting transfers between devices  24.6 us (44%)
  waiting for transfers between devices  17.2 us (31%)
  Pallas kernels  12.8 us (23%)
  between operations  0.94 us (2%)
    ppermute x16, starting transfers between devices, move(): return lax.ppermute(value, 'tok', [(t, target(t)) for t in range(count)])  24.6 us
    ppermute x16, waiting for transfers between devices, move(): return lax.ppermute(value, 'tok', [(t, target(t)) for t in range(count)])  17.2 us
    pallas_call x9, Pallas kernels, call(): pl.pallas_call(kernel, out_shape=outs, in_specs=[SMEM] + specs, out_specs...  12.8 us
  transfers between devices with their start and end apart: 16, of which 7 were waited for; matrix products, arithmetic and copies ran while one was open for 0% of the time, Pallas kernels for 15%

profile of v9, /device:TPU:0, one launch (start us, length us, event | category | flops | bytes accessed | tf_op | source)
XLA Modules:
  0.0 55.7 jit_solution(16495726649379507228)
XLA Ops:
  0.6 0.1 pad_add_fusion.place
  0.7 2.0 %shard_map.94 = (bf16[264,128]{1,0:T(8,128)(2,1)S(1)}, bf16[264,128]{1,0:T(8,128)(2,1)S(1)}, bf16[264,128]{1,0:T(8,128)(2,1)S(1)}, bf16[264,128]{1,0:T(8,128)(2,...) custom-call(s32[2]{0:T(128)S(1)} %pad_add_fusion.place, bf16[128,512]{1,0:T(8,128)(2,1)} %key_ref.1, ...), custom_call_target="tpu_custom_call" | custom-call | bytes 2630152 | tf_op jit(solution)/shard_map/pallas_call | solution.py:42
  2.7 0.0 copy-start
  2.7 0.6 %collective-permute-start.3 = (bf16[264,128]{1,0:T(8,128)(2,1)S(1)}, bf16[264,128]{1,0:T(8,128)(2,1)S(1)}, u32[]{:S(2)}, u32[]{:S(2)}) collective-permute-start(bf16[264,128]{1,0:T(8,128)(2,1)S(1)} %get-tuple-element.37), channel_id=1, source_target_pairs={{0,1},{1,0},{2,3},{3,2},{4,5},{5,4},{6,7},{7,6},{8,9},{9,8},{10,11... | collective-permute-start | bytes 202760 | tf_op jit(solution)/shard_map/ppermute | solution.py:326
  3.3 2.6 %collective-permute-start.4 = (bf16[264,128]{1,0:T(8,128)(2,1)S(1)}, bf16[264,128]{1,0:T(8,128)(2,1)S(1)}, u32[]{:S(2)}, u32[]{:S(2)}) collective-permute-start(bf16[264,128]{1,0:T(8,128)(2,1)S(1)} %get-tuple-element.38), channel_id=1, source_target_pairs={{0,2},{1,3},{2,0},{3,1},{4,6},{5,7},{6,4},{7,5},{8,10},{9,11},{10,... | collective-permute-start | bytes 202760 | tf_op jit(solution)/shard_map/ppermute | solution.py:326
  5.9 0.0 collective-permute-start.5
  5.9 2.0 %shard_map.95 = (bf16[1048,128]{1,0:T(8,128)(2,1)S(1)}, bf16[1048,128]{1,0:T(8,128)(2,1)S(1)}, bf16[1048,128]{1,0:T(8,128)(2,1)S(1)}, bf16[1048,128]{1,0:T(8,128)(2,1)S(1)}, f32[8,128]{1,0:T(8,128)S(1)}) custom-call(s32[2]{0:T(128)S(1)} %pad_add_fusion.place, bf16[128,2048]{1,0:T(8,128)(2,1)} %query_ref.1, bf16[128,2048]{1,0:T(8,128)(2,1)S(1)} %get-tuple-element.30.grads, ...), custom_call_target="tpu_custom_call" | custom-call | bytes 2658312 | tf_op jit(solution)/shard_map/pallas_call | solution.py:42
  7.9 0.7 %collective-permute-done.4.refs_2_ = bf16[264,128]{1,0:T(8,128)(2,1)S(1)} collective-permute-done((bf16[264,128]{1,0:T(8,128)(2,1)S(1)}, bf16[264,128]{1,0:T(8,128)(2,1)S(1)}, u32[]{:S(2)}, u32[]{:S(2)}) %collective-permute-start.4) | collective-permute-done | bytes 67616 | tf_op jit(solution)/shard_map/ppermute | solution.py:326
  8.6 1.4 %collective-permute-done.5.refs_3_ = bf16[264,128]{1,0:T(8,128)(2,1)S(1)} collective-permute-done((bf16[264,128]{1,0:T(8,128)(2,1)S(1)}, bf16[264,128]{1,0:T(8,128)(2,1)S(1)}, u32[]{:S(2)}, u32[]{:S(2)}) %collective-permute-start.5) | collective-permute-done | bytes 67616 | tf_op jit(solution)/shard_map/ppermute | solution.py:326
  10.0 0.6 %shard_map.96.refs_4_.refs_5_ = bf16[1056,128]{1,0:T(8,128)(2,1)S(1)} custom-call(s32[2]{0:T(128)S(1)} %pad_add_fusion.place, bf16[264,128]{1,0:T(8,128)(2,1)S(1)} %get-tuple-element.36.refs_0_, bf16[264,128]{1,0:T(8,128)(2,1)S(1)} %collective-permute-done.3.refs_1_, bf16[264,128]{1,0:T(8,128)(2,1)S(1)} %collective-permute-done.4.refs_2_, ...), custom_call_target="tpu_custom_call" | custom-call | bytes 544776 | tf_op jit(solution)/shard_map/pallas_call | solution.py:42
  10.6 1.6 %collective-permute-start.6 = (bf16[1056,128]{1,0:T(8,128)(2,1)S(1)}, bf16[1056,128]{1,0:T(8,128)(2,1)S(1)}, u32[]{:S(2)}, u32[]{:S(2)}) collective-permute-start(bf16[1056,128]{1,0:T(8,128)(2,1)S(1)} %shard_map.96.refs_4_.refs_5_), channel_id=1, source_target_pairs={{0,4},{1,5},{2,6},{3,7},{4,8},{5,9},{6,10},{7,11},{8,12},{9,13},{1... | collective-permute-start | bytes 811016 | tf_op jit(solution)/shard_map/ppermute | solution.py:326
  12.2 1.4 %collective-permute-start.1 = (bf16[1048,128]{1,0:T(8,128)(2,1)S(1)}, bf16[1048,128]{1,0:T(8,128)(2,1)S(1)}, u32[]{:S(2)}, u32[]{:S(2)}) collective-permute-start(bf16[1048,128]{1,0:T(8,128)(2,1)S(1)} %get-tuple-element.34), channel_id=1, source_target_pairs={{0,2},{1,3},{2,0},{3,1},{4,6},{5,7},{6,4},{7,5},{8,10},{9,11},{10,... | collective-permute-start | bytes 804872 | tf_op jit(solution)/shard_map/ppermute | solution.py:326
  13.5 0.5 collective-permute-start.2
  14.0 7.0 %collective-permute-done.6.refs_5_ = bf16[1056,128]{1,0:T(8,128)(2,1)S(1)} collective-permute-done((bf16[1056,128]{1,0:T(8,128)(2,1)S(1)}, bf16[1056,128]{1,0:T(8,128)(2,1)S(1)}, u32[]{:S(2)}, u32[]{:S(2)}) %collective-permute-start.6) | collective-permute-done | bytes 270368 | tf_op jit(solution)/shard_map/ppermute | solution.py:326
  21.0 0.5 collective-permute-done.1.refs_2_
  21.5 4.8 %collective-permute-done.2.refs_3_ = bf16[1048,128]{1,0:T(8,128)(2,1)S(1)} collective-permute-done((bf16[1048,128]{1,0:T(8,128)(2,1)S(1)}, bf16[1048,128]{1,0:T(8,128)(2,1)S(1)}, u32[]{:S(2)}, u32[]{:S(2)}) %collective-permute-start.2) | collective-permute-done | bytes 268320 | tf_op jit(solution)/shard_map/ppermute | solution.py:326
  26.3 3.4 %shard_map.97 = (f32[4,128,512]{2,1,0:T(8,128)S(1)}, f32[1024,128]{1,0:T(8,128)S(1)}) custom-call(s32[2]{0:T(128)S(1)} %pad_add_fusion.place, bf16[1048,128]{1,0:T(8,128)(2,1)S(1)} %get-tuple-element.32.refs_0_, bf16[1048,128]{1,0:T(8,128)(2,1)S(1)} %collective-permute-done.refs_1_, bf16[1048,128]{1,0:T(8,128)(2,1)S(1)} %collective-permute-done.1.refs_2_, ...), custom_call_target="tpu_custom_call" | custom-call | flops 1342177280 | bytes 3186696 | tf_op jit(solution)/shard_map/pallas_call | solution.py:42
  29.8 0.8 %shard_map.98 = (f32[4,128,512]{2,1,0:T(8,128)S(1)}, bf16[1024,128]{1,0:T(8,128)(2,1)S(1)}) custom-call(s32[2]{0:T(128)S(1)} %pad_add_fusion.place, bf16[1048,128]{1,0:T(8,128)(2,1)S(1)} %get-tuple-element.32.refs_0_, bf16[1048,128]{1,0:T(8,128)(2,1)S(1)} %collective-permute-done.refs_1_, bf16[1048,128]{1,0:T(8,128)(2,1)S(1)} %collective-permute-done.1.refs_2_, ...), custom_call_target="tpu_custom_call" | custom-call | flops 1342177280 | bytes 3973128 | tf_op jit(solution)/shard_map/pallas_call | solution.py:42
  30.6 0.3 collective-permute-start.11
  30.9 0.7 %shard_map.99 = (bf16[768,128]{1,0:T(8,128)(2,1)S(1)}, bf16[768,128]{1,0:T(8,128)(2,1)S(1)}, bf16[768,128]{1,0:T(8,128)(2,1)S(1)}, bf16[768,128]{1,0:T(8,128)(2,1)S(1)}, f32[1024,128]{1,0:T(8,128)S(1)}) custom-call(s32[2]{0:T(128)S(1)} %pad_add_fusion.place, bf16[1048,128]{1,0:T(8,128)(2,1)S(1)} %get-tuple-element.32.refs_0_, ...), custom_call_target="tpu_custom_call" | custom-call | flops 1342177280 | bytes 4497416 | tf_op jit(solution)/shard_map/pallas_call | solution.py:42
  31.6 0.3 collective-permute-start.8
  31.9 1.2 %collective-permute-start.9 = (bf16[768,128]{1,0:T(8,128)(2,1)S(1)}, bf16[768,128]{1,0:T(8,128)(2,1)S(1)}, u32[]{:S(2)}, u32[]{:S(2)}) collective-permute-start(bf16[768,128]{1,0:T(8,128)(2,1)S(1)} %get-tuple-element.46), channel_id=1, source_target_pairs={{0,2},{1,3},{2,0},{3,1},{4,6},{5,7},{6,4},{7,5},{8,10},{9,11},{10,... | collective-permute-start | bytes 589832 | tf_op jit(solution)/shard_map/ppermute | solution.py:326
  33.1 0.4 collective-permute-start.10
  33.5 0.6 %shard_map.101 = (bf16[512,128]{1,0:T(8,128)(2,1)S(1)}, bf16[256,128]{1,0:T(8,128)(2,1)S(1)}, bf16[256,128]{1,0:T(8,128)(2,1)S(1)}) custom-call(s32[2]{0:T(128)S(1)} %pad_add_fusion.place, bf16[1024,128]{1,0:T(8,128)(2,1)S(1)} %collective-permute-done.11.refs_0_, f32[1024,128]{1,0:T(8,128)S(1)} %get-tuple-element.50.refs_1_), custom_call_target="tpu_custom_call" | custom-call | bytes 1048584 | tf_op jit(solution)/shard_map/pallas_call | solution.py:42
  34.1 10.5 %collective-permute-start.14 = (bf16[512,128]{1,0:T(8,128)(2,1)S(1)}, bf16[512,128]{1,0:T(8,128)(2,1)S(1)}, u32[]{:S(2)}, u32[]{:S(2)}) collective-permute-start(bf16[512,128]{1,0:T(8,128)(2,1)S(1)} %get-tuple-element.53), channel_id=1, source_target_pairs={{0,12},{1,13},{2,14},{3,15},{4,2},{5,3},{6,0},{7,1},{8,6},{9,7},{1... | collective-permute-start | bytes 393224 | tf_op jit(solution)/shard_map/ppermute | solution.py:326
  44.7 0.8 %collective-permute-start.12 = (bf16[256,128]{1,0:T(8,128)(2,1)S(1)}, bf16[256,128]{1,0:T(8,128)(2,1)S(1)}, u32[]{:S(2)}, u32[]{:S(2)}) collective-permute-start(bf16[256,128]{1,0:T(8,128)(2,1)S(1)} %get-tuple-element.51), channel_id=1, source_target_pairs={{0,12},{1,13},{2,14},{3,15},{4,0},{5,1},{6,2},{7,3},{8,4},{9,5},{1... | collective-permute-start | bytes 196616 | tf_op jit(solution)/shard_map/ppermute | solution.py:326
  45.5 2.5 %collective-permute-done.14.refs_6_ = bf16[512,128]{1,0:T(8,128)(2,1)S(1)} collective-permute-done((bf16[512,128]{1,0:T(8,128)(2,1)S(1)}, bf16[512,128]{1,0:T(8,128)(2,1)S(1)}, u32[]{:S(2)}, u32[]{:S(2)}) %collective-permute-start.14) | collective-permute-done | bytes 131104 | tf_op jit(solution)/shard_map/ppermute | solution.py:326
  48.0 4.3 %collective-permute-start.13 = (bf16[256,128]{1,0:T(8,128)(2,1)S(1)}, bf16[256,128]{1,0:T(8,128)(2,1)S(1)}, u32[]{:S(2)}, u32[]{:S(2)}) collective-permute-start(bf16[256,128]{1,0:T(8,128)(2,1)S(1)} %get-tuple-element.52), channel_id=1, source_target_pairs={{0,12},{1,13},{2,14},{3,15},{4,1},{5,0},{6,3},{7,2},{8,5},{9,4},{1... | collective-permute-start | bytes 196616 | tf_op jit(solution)/shard_map/ppermute | solution.py:326
  52.3 0.1 collective-permute-start.15
  52.4 1.4 %shard_map.100 = (bf16[128,2048]{1,0:T(8,128)(2,1)}, f32[8,128]{1,0:T(8,128)S(1)}) custom-call(s32[2]{0:T(128)S(1)} %pad_add_fusion.place, bf16[768,128]{1,0:T(8,128)(2,1)S(1)} %get-tuple-element.44.refs_0_, bf16[768,128]{1,0:T(8,128)(2,1)S(1)} %collective-permute-done.8.refs_1_, bf16[768,128]{1,0:T(8,128)(2,1)S(1)} %collective-permute-done.9.refs_2_, ...), custom_call_target="tpu_custom_call" | custom-call | bytes 1314824 | tf_op jit(solution)/shard_map/pallas_call | solution.py:42
  53.9 0.3 collective-permute-done.13.refs_5_
  54.2 1.3 %shard_map.102 = (bf16[128,512]{1,0:T(8,128)(2,1)}, bf16[128,512]{1,0:T(8,128)(2,1)}) custom-call(s32[2]{0:T(128)S(1)} %pad_add_fusion.place, bf16[768,128]{1,0:T(8,128)(2,1)S(1)} %get-tuple-element.44.refs_0_, bf16[768,128]{1,0:T(8,128)(2,1)S(1)} %collective-permute-done.8.refs_1_, bf16[768,128]{1,0:T(8,128)(2,1)S(1)} %collective-permute-done.9.refs_2_, ...), custom_call_target="tpu_custom_call" | custom-call | bytes 1380360 | tf_op jit(solution)/shard_map/pallas_call | solution.py:42
  (13 shorter events, 0.0 us)
Async XLA Ops:
  2.7 3.2 %copy-start = (f32[16,128]{1,0:T(8,128)S(1)}, f32[16,128]{1,0:T(8,128)}, u32[]{:S(2)}) copy-start(f32[16,128]{1,0:T(8,128)} %norm_ref.1) | copy-start | bytes 24580
  2.7 5.2 %collective-permute-start.3 = (bf16[264,128]{1,0:T(8,128)(2,1)S(1)}, bf16[264,128]{1,0:T(8,128)(2,1)S(1)}, u32[]{:S(2)}, u32[]{:S(2)}) collective-permute-start(bf16[264,128]{1,0:T(8,128)(2,1)S(1)} %get-tuple-element.37), channel_id=1, source_target_pairs={{0,1},{1,0},{2,3},{3,2},{4,5},{5,4},{6,7},{7,6},{8,9},{9,8},{10,11... | collective-permute-start | bytes 202760 | tf_op jit(solution)/shard_map/ppermute | solution.py:326
  3.3 5.3 %collective-permute-start.4 = (bf16[264,128]{1,0:T(8,128)(2,1)S(1)}, bf16[264,128]{1,0:T(8,128)(2,1)S(1)}, u32[]{:S(2)}, u32[]{:S(2)}) collective-permute-start(bf16[264,128]{1,0:T(8,128)(2,1)S(1)} %get-tuple-element.38), channel_id=1, source_target_pairs={{0,2},{1,3},{2,0},{3,1},{4,6},{5,7},{6,4},{7,5},{8,10},{9,11},{10,... | collective-permute-start | bytes 202760 | tf_op jit(solution)/shard_map/ppermute | solution.py:326
  5.9 4.1 %collective-permute-start.5 = (bf16[264,128]{1,0:T(8,128)(2,1)S(1)}, bf16[264,128]{1,0:T(8,128)(2,1)S(1)}, u32[]{:S(2)}, u32[]{:S(2)}) collective-permute-start(bf16[264,128]{1,0:T(8,128)(2,1)S(1)} %get-tuple-element.39), channel_id=1, source_target_pairs={{0,3},{1,2},{2,1},{3,0},{4,7},{5,6},{6,5},{7,4},{8,11},{9,10},{10,... | collective-permute-start | bytes 202760 | tf_op jit(solution)/shard_map/ppermute | solution.py:326
  10.6 10.5 %collective-permute-start.6 = (bf16[1056,128]{1,0:T(8,128)(2,1)S(1)}, bf16[1056,128]{1,0:T(8,128)(2,1)S(1)}, u32[]{:S(2)}, u32[]{:S(2)}) collective-permute-start(bf16[1056,128]{1,0:T(8,128)(2,1)S(1)} %shard_map.96.refs_4_.refs_5_), channel_id=1, source_target_pairs={{0,4},{1,5},{2,6},{3,7},{4,8},{5,9},{6,10},{7,11},{8,12},{9,13},{1... | collective-permute-start | bytes 811016 | tf_op jit(solution)/shard_map/ppermute | solution.py:326
  12.2 8.8 %collective-permute-start = (bf16[1048,128]{1,0:T(8,128)(2,1)S(1)}, bf16[1048,128]{1,0:T(8,128)(2,1)S(1)}, u32[]{:S(2)}, u32[]{:S(2)}) collective-permute-start(bf16[1048,128]{1,0:T(8,128)(2,1)S(1)} %get-tuple-element.33), channel_id=1, source_target_pairs={{0,1},{1,0},{2,3},{3,2},{4,5},{5,4},{6,7},{7,6},{8,9},{9,8},{10,11... | collective-permute-start | bytes 804872 | tf_op jit(solution)/shard_map/ppermute | solution.py:326
  12.2 9.3 %collective-permute-start.1 = (bf16[1048,128]{1,0:T(8,128)(2,1)S(1)}, bf16[1048,128]{1,0:T(8,128)(2,1)S(1)}, u32[]{:S(2)}, u32[]{:S(2)}) collective-permute-start(bf16[1048,128]{1,0:T(8,128)(2,1)S(1)} %get-tuple-element.34), channel_id=1, source_target_pairs={{0,2},{1,3},{2,0},{3,1},{4,6},{5,7},{6,4},{7,5},{8,10},{9,11},{10,... | collective-permute-start | bytes 804872 | tf_op jit(solution)/shard_map/ppermute | solution.py:326
  13.5 12.8 %collective-permute-start.2 = (bf16[1048,128]{1,0:T(8,128)(2,1)S(1)}, bf16[1048,128]{1,0:T(8,128)(2,1)S(1)}, u32[]{:S(2)}, u32[]{:S(2)}) collective-permute-start(bf16[1048,128]{1,0:T(8,128)(2,1)S(1)} %get-tuple-element.35), channel_id=1, source_target_pairs={{0,3},{1,2},{2,1},{3,0},{4,7},{5,6},{6,5},{7,4},{8,11},{9,10},{10,... | collective-permute-start | bytes 804872 | tf_op jit(solution)/shard_map/ppermute | solution.py:326
  21.0 8.7 %collective-permute-start.7 = (bf16[1056,128]{1,0:T(8,128)(2,1)S(1)}, bf16[1056,128]{1,0:T(8,128)(2,1)S(1)}, u32[]{:S(2)}, u32[]{:S(2)}) collective-permute-start(bf16[1056,128]{1,0:T(8,128)(2,1)S(1)} %collective-permute-done.6.refs_5_), channel_id=1, source_target_pairs={{0,1},{1,0},{2,3},{3,2},{4,8},{5,9},{6,10},{7,11},{8,12},{9,13},{1... | collective-permute-start | bytes 811016 | tf_op jit(solution)/shard_map/ppermute | solution.py:326
  30.6 2.9 %collective-permute-start.11 = (bf16[1024,128]{1,0:T(8,128)(2,1)S(1)}, bf16[1024,128]{1,0:T(8,128)(2,1)S(1)}, u32[]{:S(2)}, u32[]{:S(2)}) collective-permute-start(bf16[1024,128]{1,0:T(8,128)(2,1)S(1)} %get-tuple-element.49), channel_id=1, source_target_pairs={{0,1},{1,0},{2,3},{3,2},{4,12},{5,13},{6,14},{7,15},{8,4},{9,5},{1... | collective-permute-start | bytes 786440 | tf_op jit(solution)/shard_map/ppermute | solution.py:326
  31.6 20.7 %collective-permute-start.8 = (bf16[768,128]{1,0:T(8,128)(2,1)S(1)}, bf16[768,128]{1,0:T(8,128)(2,1)S(1)}, u32[]{:S(2)}, u32[]{:S(2)}) collective-permute-start(bf16[768,128]{1,0:T(8,128)(2,1)S(1)} %get-tuple-element.45), channel_id=1, source_target_pairs={{0,1},{1,0},{2,3},{3,2},{4,5},{5,4},{6,7},{7,6},{8,9},{9,8},{10,11... | collective-permute-start | bytes 589832 | tf_op jit(solution)/shard_map/ppermute | solution.py:326
  31.9 20.5 %collective-permute-start.9 = (bf16[768,128]{1,0:T(8,128)(2,1)S(1)}, bf16[768,128]{1,0:T(8,128)(2,1)S(1)}, u32[]{:S(2)}, u32[]{:S(2)}) collective-permute-start(bf16[768,128]{1,0:T(8,128)(2,1)S(1)} %get-tuple-element.46), channel_id=1, source_target_pairs={{0,2},{1,3},{2,0},{3,1},{4,6},{5,7},{6,4},{7,5},{8,10},{9,11},{10,... | collective-permute-start | bytes 589832 | tf_op jit(solution)/shard_map/ppermute | solution.py:326
  33.1 19.3 %collective-permute-start.10 = (bf16[768,128]{1,0:T(8,128)(2,1)S(1)}, bf16[768,128]{1,0:T(8,128)(2,1)S(1)}, u32[]{:S(2)}, u32[]{:S(2)}) collective-permute-start(bf16[768,128]{1,0:T(8,128)(2,1)S(1)} %get-tuple-element.47), channel_id=1, source_target_pairs={{0,3},{1,2},{2,1},{3,0},{4,7},{5,6},{6,5},{7,4},{8,11},{9,10},{10,... | collective-permute-start | bytes 589832 | tf_op jit(solution)/shard_map/ppermute | solution.py:326
  34.1 13.9 %collective-permute-start.14 = (bf16[512,128]{1,0:T(8,128)(2,1)S(1)}, bf16[512,128]{1,0:T(8,128)(2,1)S(1)}, u32[]{:S(2)}, u32[]{:S(2)}) collective-permute-start(bf16[512,128]{1,0:T(8,128)(2,1)S(1)} %get-tuple-element.53), channel_id=1, source_target_pairs={{0,12},{1,13},{2,14},{3,15},{4,2},{5,3},{6,0},{7,1},{8,6},{9,7},{1... | collective-permute-start | bytes 393224 | tf_op jit(solution)/shard_map/ppermute | solution.py:326
  44.7 9.2 %collective-permute-start.12 = (bf16[256,128]{1,0:T(8,128)(2,1)S(1)}, bf16[256,128]{1,0:T(8,128)(2,1)S(1)}, u32[]{:S(2)}, u32[]{:S(2)}) collective-permute-start(bf16[256,128]{1,0:T(8,128)(2,1)S(1)} %get-tuple-element.51), channel_id=1, source_target_pairs={{0,12},{1,13},{2,14},{3,15},{4,0},{5,1},{6,2},{7,3},{8,4},{9,5},{1... | collective-permute-start | bytes 196616 | tf_op jit(solution)/shard_map/ppermute | solution.py:326
  48.0 6.2 %collective-permute-start.13 = (bf16[256,128]{1,0:T(8,128)(2,1)S(1)}, bf16[256,128]{1,0:T(8,128)(2,1)S(1)}, u32[]{:S(2)}, u32[]{:S(2)}) collective-permute-start(bf16[256,128]{1,0:T(8,128)(2,1)S(1)} %get-tuple-element.52), channel_id=1, source_target_pairs={{0,12},{1,13},{2,14},{3,15},{4,1},{5,0},{6,3},{7,2},{8,5},{9,4},{1... | collective-permute-start | bytes 196616 | tf_op jit(solution)/shard_map/ppermute | solution.py:326
  52.3 1.9 %collective-permute-start.15 = (bf16[256,128]{1,0:T(8,128)(2,1)S(1)}, bf16[256,128]{1,0:T(8,128)(2,1)S(1)}, u32[]{:S(2)}, u32[]{:S(2)}) collective-permute-start(bf16[256,128]{1,0:T(8,128)(2,1)S(1)} %slice.4), channel_id=1, source_target_pairs={{0,1},{1,0},{2,3},{3,2},{4,5},{5,4},{6,7},{7,6},{8,9},{9,8},{10,11... | collective-permute-start | bytes 196616 | tf_op jit(solution)/shard_map/ppermute | solution.py:326

commit v10 on v9

--- a/solution.py
+++ b/solution.py
@@ -136,19 +136,21 @@
     ]
 
 
-def attend(rows, offset, reach, first, last, place, *refs):
+def attend(rows, offset, reach, earlier, last, place, *refs):
     parts = KEY_VALUE_HEADS
     queries, refs = refs[:parts], refs[parts:]
     own, key_ref, refs = refs[0], refs[1], refs[2:]
-    if not first:
-        dq_in, refs = refs[0], refs[1:]
+    first = earlier == 0
+    if last:
+        dq_in, refs = refs[:earlier], refs[earlier:]
     if last and not first:
         own_terms, refs = refs[0], refs[1:]
     if last:
         dq_out, refs = refs[:parts], refs[parts:]
     else:
         dq_out, refs = refs[0], refs[1:]
-    kv_out, dq, dkv, key_t, docs_t, docs_s = refs
+    kv_out, dq_sum, dkv, key_t, docs_t, docs_s = refs
+    dq = dq_sum if last else dq_out
     row, me = place[0], place[1]
     width = GROUP * rows
     span = parts * rows
@@ -216,12 +218,9 @@
                 pl.when(low & ~high)(functools.partial(block, 0, half))
 
         kv_out[...] = dkv[...].astype(kv_out.dtype)
-        for s in range(parts):
-            total = dq[s] if first else dq[s] + dq_in[s]
-            if last:
-                close(s, total)
-            else:
-                dq_out[s] = total
+        if last:
+            for s in range(parts):
+                close(s, sum([part[s] for part in dq_in], dq[s]))
 
     def close(s, total):
         out, a = dq_out[s], me ^ s
@@ -240,11 +239,11 @@
     @pl.when(row < offset)
     def _():
         kv_out[...] = jnp.zeros_like(kv_out)
-        for s in range(parts):
-            if last:
-                close(s, dq_in[s])
-            else:
-                dq_out[s] = dq_in[s]
+        if last:
+            for s in range(parts):
+                close(s, sum([part[s] for part in dq_in[1:]], dq_in[0][s]))
+        else:
+            dq_out[...] = jnp.zeros_like(dq_out)
 
     pl.when(row >= offset)(work)
 
@@ -363,27 +362,29 @@
 
     kv_shape = (2 * span, HEAD_SIZE)
     stages = [0] + list(range(behind, 0, -1))
-    dq, own_terms, sent = None, None, None
+    dq_parts, own_terms, sent = [], None, None
     for k, offset in enumerate(stages):
         first, last = k == 0, k == len(stages) - 1
         ins = [place, *query_pieces, own, windows[offset]]
-        if not first:
-            ins.append(dq)
         if last and not first:
-            ins.append(own_terms)
+            ins += [*dq_parts, own_terms]
         if last:
             outs = [shape((GROUP * HEAD_SIZE + 2 * rows, rows), BF16)] * parts
         else:
             outs = [shape((parts, HEAD_SIZE, width), F32)]
         outs = outs + [shape(kv_shape, BF16 if offset == behind > 0 else F32)]
         got = call(
-            functools.partial(attend, rows, offset, reach, first, last),
+            functools.partial(attend, rows, offset, reach, k, last),
             ins,
             outs,
             scratch=attend_scratch(rows),
             flops=10 * span * span * GROUP * HEAD_SIZE,
         )
-        dq, term = (got[:parts] if last else got[0]), got[-1]
+        term = got[-1]
+        if last:
+            dq = got[:parts]
+        else:
+            dq_parts.append(got[0])
         if offset == 0:
             own_terms = term
         elif offset == 1:

time: 55.9 us -> 60.4 us (1.081)
  the two profiles are of different devices: /device:TPU:0 before, /device:TPU:17 now
where the time goes in v10:
time: 60.4 us; the launch traced here: 60.2 us
  waiting for transfers between devices  29.6 us (49%)
  Pallas kernels  17.1 us (28%)
  starting transfers between devices  12.5 us (21%)
  between operations  0.94 us (2%)
    ppermute x16, waiting for transfers between devices, move(): return lax.ppermute(value, 'tok', [(t, target(t)) for t in range(count)])  29.6 us
    pallas_call x9, Pallas kernels, call(): pl.pallas_call(kernel, out_shape=outs, in_specs=[SMEM] + specs, out_specs...  17.1 us
    ppermute x16, starting transfers between devices, move(): return lax.ppermute(value, 'tok', [(t, target(t)) for t in range(count)])  12.5 us
  transfers between devices with their start and end apart: 16, of which 6 were waited for; matrix products, arithmetic and copies ran while one was open for 0% of the time, Pallas kernels for 20%

profile of v10, /device:TPU:17, one launch (start us, length us, event | category | flops | bytes accessed | tf_op | source)
XLA Modules:
  0.0 60.2 jit_solution(6641934227753303300)
XLA Ops:
  0.6 0.1 pad_add_fusion.place
  0.7 2.0 %shard_map.94 = (bf16[264,128]{1,0:T(8,128)(2,1)S(1)}, bf16[264,128]{1,0:T(8,128)(2,1)S(1)}, bf16[264,128]{1,0:T(8,128)(2,1)S(1)}, bf16[264,128]{1,0:T(8,128)(2,...) custom-call(s32[2]{0:T(128)S(1)} %pad_add_fusion.place, bf16[128,512]{1,0:T(8,128)(2,1)} %key_ref.1, ...), custom_call_target="tpu_custom_call" | custom-call | bytes 2630152 | tf_op jit(solution)/shard_map/pallas_call | solution.py:42
  2.7 0.0 copy-start
  2.7 0.7 %collective-permute-start.3 = (bf16[264,128]{1,0:T(8,128)(2,1)S(1)}, bf16[264,128]{1,0:T(8,128)(2,1)S(1)}, u32[]{:S(2)}, u32[]{:S(2)}) collective-permute-start(bf16[264,128]{1,0:T(8,128)(2,1)S(1)} %get-tuple-element.37), channel_id=1, source_target_pairs={{0,1},{1,0},{2,3},{3,2},{4,5},{5,4},{6,7},{7,6},{8,9},{9,8},{10,11... | collective-permute-start | bytes 202760 | tf_op jit(solution)/shard_map/ppermute | solution.py:325
  3.5 1.2 %collective-permute-start.4 = (bf16[264,128]{1,0:T(8,128)(2,1)S(1)}, bf16[264,128]{1,0:T(8,128)(2,1)S(1)}, u32[]{:S(2)}, u32[]{:S(2)}) collective-permute-start(bf16[264,128]{1,0:T(8,128)(2,1)S(1)} %get-tuple-element.38), channel_id=1, source_target_pairs={{0,2},{1,3},{2,0},{3,1},{4,6},{5,7},{6,4},{7,5},{8,10},{9,11},{10,... | collective-permute-start | bytes 202760 | tf_op jit(solution)/shard_map/ppermute | solution.py:325
  4.7 0.5 collective-permute-start.5
  5.2 2.0 %shard_map.95 = (bf16[1048,128]{1,0:T(8,128)(2,1)S(1)}, bf16[1048,128]{1,0:T(8,128)(2,1)S(1)}, bf16[1048,128]{1,0:T(8,128)(2,1)S(1)}, bf16[1048,128]{1,0:T(8,128)(2,1)S(1)}, f32[8,128]{1,0:T(8,128)S(1)}) custom-call(s32[2]{0:T(128)S(1)} %pad_add_fusion.place, bf16[128,2048]{1,0:T(8,128)(2,1)} %query_ref.1, bf16[128,2048]{1,0:T(8,128)(2,1)S(1)} %get-tuple-element.30.grads, ...), custom_call_target="tpu_custom_call" | custom-call | bytes 2658312 | tf_op jit(solution)/shard_map/pallas_call | solution.py:42
  7.2 1.6 %collective-permute-done.5.refs_3_ = bf16[264,128]{1,0:T(8,128)(2,1)S(1)} collective-permute-done((bf16[264,128]{1,0:T(8,128)(2,1)S(1)}, bf16[264,128]{1,0:T(8,128)(2,1)S(1)}, u32[]{:S(2)}, u32[]{:S(2)}) %collective-permute-start.5) | collective-permute-done | bytes 67616 | tf_op jit(solution)/shard_map/ppermute | solution.py:325
  8.8 0.6 shard_map.96.refs_4_.refs_5_
  9.4 1.3 %collective-permute-start.6 = (bf16[1056,128]{1,0:T(8,128)(2,1)S(1)}, bf16[1056,128]{1,0:T(8,128)(2,1)S(1)}, u32[]{:S(2)}, u32[]{:S(2)}) collective-permute-start(bf16[1056,128]{1,0:T(8,128)(2,1)S(1)} %shard_map.96.refs_4_.refs_5_), channel_id=1, source_target_pairs={{0,4},{1,5},{2,6},{3,7},{4,8},{5,9},{6,10},{7,11},{8,12},{9,13},{1... | collective-permute-start | bytes 811016 | tf_op jit(solution)/shard_map/ppermute | solution.py:325
  10.7 6.4 %collective-permute-done.6.refs_5_ = bf16[1056,128]{1,0:T(8,128)(2,1)S(1)} collective-permute-done((bf16[1056,128]{1,0:T(8,128)(2,1)S(1)}, bf16[1056,128]{1,0:T(8,128)(2,1)S(1)}, u32[]{:S(2)}, u32[]{:S(2)}) %collective-permute-start.6) | collective-permute-done | bytes 270368 | tf_op jit(solution)/shard_map/ppermute | solution.py:325
  17.1 1.3 %collective-permute-start.7 = (bf16[1056,128]{1,0:T(8,128)(2,1)S(1)}, bf16[1056,128]{1,0:T(8,128)(2,1)S(1)}, u32[]{:S(2)}, u32[]{:S(2)}) collective-permute-start(bf16[1056,128]{1,0:T(8,128)(2,1)S(1)} %collective-permute-done.6.refs_5_), channel_id=1, source_target_pairs={{0,1},{1,0},{2,3},{3,2},{4,8},{5,9},{6,10},{7,11},{8,12},{9,13},{1... | collective-permute-start | bytes 811016 | tf_op jit(solution)/shard_map/ppermute | solution.py:325
  18.4 1.5 %collective-permute-start = (bf16[1048,128]{1,0:T(8,128)(2,1)S(1)}, bf16[1048,128]{1,0:T(8,128)(2,1)S(1)}, u32[]{:S(2)}, u32[]{:S(2)}) collective-permute-start(bf16[1048,128]{1,0:T(8,128)(2,1)S(1)} %get-tuple-element.33), channel_id=1, source_target_pairs={{0,1},{1,0},{2,3},{3,2},{4,5},{5,4},{6,7},{7,6},{8,9},{9,8},{10,11... | collective-permute-start | bytes 804872 | tf_op jit(solution)/shard_map/ppermute | solution.py:325
  19.9 1.2 %collective-permute-start.1 = (bf16[1048,128]{1,0:T(8,128)(2,1)S(1)}, bf16[1048,128]{1,0:T(8,128)(2,1)S(1)}, u32[]{:S(2)}, u32[]{:S(2)}) collective-permute-start(bf16[1048,128]{1,0:T(8,128)(2,1)S(1)} %get-tuple-element.34), channel_id=1, source_target_pairs={{0,2},{1,3},{2,0},{3,1},{4,6},{5,7},{6,4},{7,5},{8,10},{9,11},{10,... | collective-permute-start | bytes 804872 | tf_op jit(solution)/shard_map/ppermute | solution.py:325
  21.1 0.4 collective-permute-start.2
  21.6 6.4 %collective-permute-done.1.refs_2_ = bf16[1048,128]{1,0:T(8,128)(2,1)S(1)} collective-permute-done((bf16[1048,128]{1,0:T(8,128)(2,1)S(1)}, bf16[1048,128]{1,0:T(8,128)(2,1)S(1)}, u32[]{:S(2)}, u32[]{:S(2)}) %collective-permute-start.1) | collective-permute-done | bytes 268320 | tf_op jit(solution)/shard_map/ppermute | solution.py:325
  27.9 5.9 %collective-permute-done.2.refs_3_ = bf16[1048,128]{1,0:T(8,128)(2,1)S(1)} collective-permute-done((bf16[1048,128]{1,0:T(8,128)(2,1)S(1)}, bf16[1048,128]{1,0:T(8,128)(2,1)S(1)}, u32[]{:S(2)}, u32[]{:S(2)}) %collective-permute-start.2) | collective-permute-done | bytes 268320 | tf_op jit(solution)/shard_map/ppermute | solution.py:325
  33.8 0.8 %shard_map.98 = (f32[4,128,512]{2,1,0:T(8,128)S(1)}, bf16[1024,128]{1,0:T(8,128)(2,1)S(1)}) custom-call(s32[2]{0:T(128)S(1)} %pad_add_fusion.place, bf16[1048,128]{1,0:T(8,128)(2,1)S(1)} %get-tuple-element.32.refs_0_, bf16[1048,128]{1,0:T(8,128)(2,1)S(1)} %collective-permute-done.refs_1_, bf16[1048,128]{1,0:T(8,128)(2,1)S(1)} %collective-permute-done.1.refs_2_, ...), custom_call_target="tpu_custom_call" | custom-call | flops 1342177280 | bytes 2924552 | tf_op jit(solution)/shard_map/pallas_call | solution.py:42
  34.7 0.1 collective-permute-start.11
  34.8 3.8 %shard_map.97 = (f32[4,128,512]{2,1,0:T(8,128)S(1)}, f32[1024,128]{1,0:T(8,128)S(1)}) custom-call(s32[2]{0:T(128)S(1)} %pad_add_fusion.place, bf16[1048,128]{1,0:T(8,128)(2,1)S(1)} %get-tuple-element.32.refs_0_, bf16[1048,128]{1,0:T(8,128)(2,1)S(1)} %collective-permute-done.refs_1_, bf16[1048,128]{1,0:T(8,128)(2,1)S(1)} %collective-permute-done.1.refs_2_, ...), custom_call_target="tpu_custom_call" | custom-call | flops 1342177280 | bytes 3186696 | tf_op jit(solution)/shard_map/pallas_call | solution.py:42
  38.6 4.5 %shard_map.99 = (bf16[768,128]{1,0:T(8,128)(2,1)S(1)}, bf16[768,128]{1,0:T(8,128)(2,1)S(1)}, bf16[768,128]{1,0:T(8,128)(2,1)S(1)}, bf16[768,128]{1,0:T(8,128)(2,1)S(1)}, f32[1024,128]{1,0:T(8,128)S(1)}) custom-call(s32[2]{0:T(128)S(1)} %pad_add_fusion.place, bf16[1048,128]{1,0:T(8,128)(2,1)S(1)} %get-tuple-element.32.refs_0_, ...), custom_call_target="tpu_custom_call" | custom-call | flops 1342177280 | bytes 5545992 | tf_op jit(solution)/shard_map/pallas_call | solution.py:42
  43.1 0.5 collective-permute-start.8
  43.6 1.2 %collective-permute-start.9 = (bf16[768,128]{1,0:T(8,128)(2,1)S(1)}, bf16[768,128]{1,0:T(8,128)(2,1)S(1)}, u32[]{:S(2)}, u32[]{:S(2)}) collective-permute-start(bf16[768,128]{1,0:T(8,128)(2,1)S(1)} %get-tuple-element.46), channel_id=1, source_target_pairs={{0,2},{1,3},{2,0},{3,1},{4,6},{5,7},{6,4},{7,5},{8,10},{9,11},{10,... | collective-permute-start | bytes 589832 | tf_op jit(solution)/shard_map/ppermute | solution.py:325
  44.8 0.5 collective-permute-start.10
  45.3 0.6 %shard_map.101 = (bf16[512,128]{1,0:T(8,128)(2,1)S(1)}, bf16[256,128]{1,0:T(8,128)(2,1)S(1)}, bf16[256,128]{1,0:T(8,128)(2,1)S(1)}) custom-call(s32[2]{0:T(128)S(1)} %pad_add_fusion.place, bf16[1024,128]{1,0:T(8,128)(2,1)S(1)} %collective-permute-done.11.refs_0_, f32[1024,128]{1,0:T(8,128)S(1)} %get-tuple-element.50.refs_1_), custom_call_target="tpu_custom_call" | custom-call | bytes 1048584 | tf_op jit(solution)/shard_map/pallas_call | solution.py:42
  45.9 0.3 collective-permute-start.14
  46.2 5.6 %collective-permute-done.14.refs_6_ = bf16[512,128]{1,0:T(8,128)(2,1)S(1)} collective-permute-done((bf16[512,128]{1,0:T(8,128)(2,1)S(1)}, bf16[512,128]{1,0:T(8,128)(2,1)S(1)}, u32[]{:S(2)}, u32[]{:S(2)}) %collective-permute-start.14) | collective-permute-done | bytes 131104 | tf_op jit(solution)/shard_map/ppermute | solution.py:325
  51.8 1.3 %collective-permute-start.13 = (bf16[256,128]{1,0:T(8,128)(2,1)S(1)}, bf16[256,128]{1,0:T(8,128)(2,1)S(1)}, u32[]{:S(2)}, u32[]{:S(2)}) collective-permute-start(bf16[256,128]{1,0:T(8,128)(2,1)S(1)} %get-tuple-element.52), channel_id=1, source_target_pairs={{0,12},{1,13},{2,14},{3,15},{4,1},{5,0},{6,3},{7,2},{8,5},{9,4},{1... | collective-permute-start | bytes 196616 | tf_op jit(solution)/shard_map/ppermute | solution.py:325
  53.1 0.4 collective-permute-start.15
  53.5 3.7 %collective-permute-done.10.refs_3_ = bf16[768,128]{1,0:T(8,128)(2,1)S(1)} collective-permute-done((bf16[768,128]{1,0:T(8,128)(2,1)S(1)}, bf16[768,128]{1,0:T(8,128)(2,1)S(1)}, u32[]{:S(2)}, u32[]{:S(2)}) %collective-permute-start.10) | collective-permute-done | bytes 196640 | tf_op jit(solution)/shard_map/ppermute | solution.py:325
  57.2 1.4 %shard_map.100 = (bf16[128,2048]{1,0:T(8,128)(2,1)}, f32[8,128]{1,0:T(8,128)S(1)}) custom-call(s32[2]{0:T(128)S(1)} %pad_add_fusion.place, bf16[768,128]{1,0:T(8,128)(2,1)S(1)} %get-tuple-element.44.refs_0_, bf16[768,128]{1,0:T(8,128)(2,1)S(1)} %collective-permute-done.8.refs_1_, bf16[768,128]{1,0:T(8,128)(2,1)S(1)} %collective-permute-done.9.refs_2_, ...), custom_call_target="tpu_custom_call" | custom-call | bytes 1314824 | tf_op jit(solution)/shard_map/pallas_call | solution.py:42
  58.7 1.3 %shard_map.102 = (bf16[128,512]{1,0:T(8,128)(2,1)}, bf16[128,512]{1,0:T(8,128)(2,1)}) custom-call(s32[2]{0:T(128)S(1)} %pad_add_fusion.place, bf16[768,128]{1,0:T(8,128)(2,1)S(1)} %get-tuple-element.44.refs_0_, bf16[768,128]{1,0:T(8,128)(2,1)S(1)} %collective-permute-done.8.refs_1_, bf16[768,128]{1,0:T(8,128)(2,1)S(1)} %collective-permute-done.9.refs_2_, ...), custom_call_target="tpu_custom_call" | custom-call | bytes 1380360 | tf_op jit(solution)/shard_map/pallas_call | solution.py:42
  (13 shorter events, 0.0 us)
Async XLA Ops:
  2.7 2.5 %copy-start = (f32[16,128]{1,0:T(8,128)S(1)}, f32[16,128]{1,0:T(8,128)}, u32[]{:S(2)}) copy-start(f32[16,128]{1,0:T(8,128)} %norm_ref.1) | copy-start | bytes 24580
  2.7 4.5 %collective-permute-start.3 = (bf16[264,128]{1,0:T(8,128)(2,1)S(1)}, bf16[264,128]{1,0:T(8,128)(2,1)S(1)}, u32[]{:S(2)}, u32[]{:S(2)}) collective-permute-start(bf16[264,128]{1,0:T(8,128)(2,1)S(1)} %get-tuple-element.37), channel_id=1, source_target_pairs={{0,1},{1,0},{2,3},{3,2},{4,5},{5,4},{6,7},{7,6},{8,9},{9,8},{10,11... | collective-permute-start | bytes 202760 | tf_op jit(solution)/shard_map/ppermute | solution.py:325
  3.5 3.7 %collective-permute-start.4 = (bf16[264,128]{1,0:T(8,128)(2,1)S(1)}, bf16[264,128]{1,0:T(8,128)(2,1)S(1)}, u32[]{:S(2)}, u32[]{:S(2)}) collective-permute-start(bf16[264,128]{1,0:T(8,128)(2,1)S(1)} %get-tuple-element.38), channel_id=1, source_target_pairs={{0,2},{1,3},{2,0},{3,1},{4,6},{5,7},{6,4},{7,5},{8,10},{9,11},{10,... | collective-permute-start | bytes 202760 | tf_op jit(solution)/shard_map/ppermute | solution.py:325
  4.7 4.1 %collective-permute-start.5 = (bf16[264,128]{1,0:T(8,128)(2,1)S(1)}, bf16[264,128]{1,0:T(8,128)(2,1)S(1)}, u32[]{:S(2)}, u32[]{:S(2)}) collective-permute-start(bf16[264,128]{1,0:T(8,128)(2,1)S(1)} %get-tuple-element.39), channel_id=1, source_target_pairs={{0,3},{1,2},{2,1},{3,0},{4,7},{5,6},{6,5},{7,4},{8,11},{9,10},{10,... | collective-permute-start | bytes 202760 | tf_op jit(solution)/shard_map/ppermute | solution.py:325
  9.4 7.7 %collective-permute-start.6 = (bf16[1056,128]{1,0:T(8,128)(2,1)S(1)}, bf16[1056,128]{1,0:T(8,128)(2,1)S(1)}, u32[]{:S(2)}, u32[]{:S(2)}) collective-permute-start(bf16[1056,128]{1,0:T(8,128)(2,1)S(1)} %shard_map.96.refs_4_.refs_5_), channel_id=1, source_target_pairs={{0,4},{1,5},{2,6},{3,7},{4,8},{5,9},{6,10},{7,11},{8,12},{9,13},{1... | collective-permute-start | bytes 811016 | tf_op jit(solution)/shard_map/ppermute | solution.py:325
  17.1 16.7 %collective-permute-start.7 = (bf16[1056,128]{1,0:T(8,128)(2,1)S(1)}, bf16[1056,128]{1,0:T(8,128)(2,1)S(1)}, u32[]{:S(2)}, u32[]{:S(2)}) collective-permute-start(bf16[1056,128]{1,0:T(8,128)(2,1)S(1)} %collective-permute-done.6.refs_5_), channel_id=1, source_target_pairs={{0,1},{1,0},{2,3},{3,2},{4,8},{5,9},{6,10},{7,11},{8,12},{9,13},{1... | collective-permute-start | bytes 811016 | tf_op jit(solution)/shard_map/ppermute | solution.py:325
  18.4 3.1 %collective-permute-start = (bf16[1048,128]{1,0:T(8,128)(2,1)S(1)}, bf16[1048,128]{1,0:T(8,128)(2,1)S(1)}, u32[]{:S(2)}, u32[]{:S(2)}) collective-permute-start(bf16[1048,128]{1,0:T(8,128)(2,1)S(1)} %get-tuple-element.33), channel_id=1, source_target_pairs={{0,1},{1,0},{2,3},{3,2},{4,5},{5,4},{6,7},{7,6},{8,9},{9,8},{10,11... | collective-permute-start | bytes 804872 | tf_op jit(solution)/shard_map/ppermute | solution.py:325
  19.9 8.0 %collective-permute-start.1 = (bf16[1048,128]{1,0:T(8,128)(2,1)S(1)}, bf16[1048,128]{1,0:T(8,128)(2,1)S(1)}, u32[]{:S(2)}, u32[]{:S(2)}) collective-permute-start(bf16[1048,128]{1,0:T(8,128)(2,1)S(1)} %get-tuple-element.34), channel_id=1, source_target_pairs={{0,2},{1,3},{2,0},{3,1},{4,6},{5,7},{6,4},{7,5},{8,10},{9,11},{10,... | collective-permute-start | bytes 804872 | tf_op jit(solution)/shard_map/ppermute | solution.py:325
  21.1 12.7 %collective-permute-start.2 = (bf16[1048,128]{1,0:T(8,128)(2,1)S(1)}, bf16[1048,128]{1,0:T(8,128)(2,1)S(1)}, u32[]{:S(2)}, u32[]{:S(2)}) collective-permute-start(bf16[1048,128]{1,0:T(8,128)(2,1)S(1)} %get-tuple-element.35), channel_id=1, source_target_pairs={{0,3},{1,2},{2,1},{3,0},{4,7},{5,6},{6,5},{7,4},{8,11},{9,10},{10,... | collective-permute-start | bytes 804872 | tf_op jit(solution)/shard_map/ppermute | solution.py:325
  34.7 10.6 %collective-permute-start.11 = (bf16[1024,128]{1,0:T(8,128)(2,1)S(1)}, bf16[1024,128]{1,0:T(8,128)(2,1)S(1)}, u32[]{:S(2)}, u32[]{:S(2)}) collective-permute-start(bf16[1024,128]{1,0:T(8,128)(2,1)S(1)} %get-tuple-element.49), channel_id=1, source_target_pairs={{0,1},{1,0},{2,3},{3,2},{4,12},{5,13},{6,14},{7,15},{8,4},{9,5},{1... | collective-permute-start | bytes 786440 | tf_op jit(solution)/shard_map/ppermute | solution.py:325
  43.1 10.0 %collective-permute-start.8 = (bf16[768,128]{1,0:T(8,128)(2,1)S(1)}, bf16[768,128]{1,0:T(8,128)(2,1)S(1)}, u32[]{:S(2)}, u32[]{:S(2)}) collective-permute-start(bf16[768,128]{1,0:T(8,128)(2,1)S(1)} %get-tuple-element.45), channel_id=1, source_target_pairs={{0,1},{1,0},{2,3},{3,2},{4,5},{5,4},{6,7},{7,6},{8,9},{9,8},{10,11... | collective-permute-start | bytes 589832 | tf_op jit(solution)/shard_map/ppermute | solution.py:325
  43.6 9.9 %collective-permute-start.9 = (bf16[768,128]{1,0:T(8,128)(2,1)S(1)}, bf16[768,128]{1,0:T(8,128)(2,1)S(1)}, u32[]{:S(2)}, u32[]{:S(2)}) collective-permute-start(bf16[768,128]{1,0:T(8,128)(2,1)S(1)} %get-tuple-element.46), channel_id=1, source_target_pairs={{0,2},{1,3},{2,0},{3,1},{4,6},{5,7},{6,4},{7,5},{8,10},{9,11},{10,... | collective-permute-start | bytes 589832 | tf_op jit(solution)/shard_map/ppermute | solution.py:325
  44.8 12.4 %collective-permute-start.10 = (bf16[768,128]{1,0:T(8,128)(2,1)S(1)}, bf16[768,128]{1,0:T(8,128)(2,1)S(1)}, u32[]{:S(2)}, u32[]{:S(2)}) collective-permute-start(bf16[768,128]{1,0:T(8,128)(2,1)S(1)} %get-tuple-element.47), channel_id=1, source_target_pairs={{0,3},{1,2},{2,1},{3,0},{4,7},{5,6},{6,5},{7,4},{8,11},{9,10},{10,... | collective-permute-start | bytes 589832 | tf_op jit(solution)/shard_map/ppermute | solution.py:325
  45.9 5.9 %collective-permute-start.14 = (bf16[512,128]{1,0:T(8,128)(2,1)S(1)}, bf16[512,128]{1,0:T(8,128)(2,1)S(1)}, u32[]{:S(2)}, u32[]{:S(2)}) collective-permute-start(bf16[512,128]{1,0:T(8,128)(2,1)S(1)} %get-tuple-element.53), channel_id=1, source_target_pairs={{0,12},{1,13},{2,14},{3,15},{4,2},{5,3},{6,0},{7,1},{8,6},{9,7},{1... | collective-permute-start | bytes 393224 | tf_op jit(solution)/shard_map/ppermute | solution.py:325
  46.2 12.5 %collective-permute-start.12 = (bf16[256,128]{1,0:T(8,128)(2,1)S(1)}, bf16[256,128]{1,0:T(8,128)(2,1)S(1)}, u32[]{:S(2)}, u32[]{:S(2)}) collective-permute-start(bf16[256,128]{1,0:T(8,128)(2,1)S(1)} %get-tuple-element.51), channel_id=1, source_target_pairs={{0,12},{1,13},{2,14},{3,15},{4,0},{5,1},{6,2},{7,3},{8,4},{9,5},{1... | collective-permute-start | bytes 196616 | tf_op jit(solution)/shard_map/ppermute | solution.py:325
  51.8 6.9 %collective-permute-start.13 = (bf16[256,128]{1,0:T(8,128)(2,1)S(1)}, bf16[256,128]{1,0:T(8,128)(2,1)S(1)}, u32[]{:S(2)}, u32[]{:S(2)}) collective-permute-start(bf16[256,128]{1,0:T(8,128)(2,1)S(1)} %get-tuple-element.52), channel_id=1, source_target_pairs={{0,12},{1,13},{2,14},{3,15},{4,1},{5,0},{6,3},{7,2},{8,5},{9,4},{1... | collective-permute-start | bytes 196616 | tf_op jit(solution)/shard_map/ppermute | solution.py:325
  53.1 5.6 %collective-permute-start.15 = (bf16[256,128]{1,0:T(8,128)(2,1)S(1)}, bf16[256,128]{1,0:T(8,128)(2,1)S(1)}, u32[]{:S(2)}, u32[]{:S(2)}) collective-permute-start(bf16[256,128]{1,0:T(8,128)(2,1)S(1)} %slice.4), channel_id=1, source_target_pairs={{0,1},{1,0},{2,3},{3,2},{4,5},{5,4},{6,7},{7,6},{8,9},{9,8},{10,11... | collective-permute-start | bytes 196616 | tf_op jit(solution)/shard_map/ppermute | solution.py:325

commit v11 on v10

--- a/solution.py
+++ b/solution.py
@@ -54,8 +54,8 @@
     return pl.ds(pl.multiple_of(g * HEAD_SIZE, HEAD_SIZE), HEAD_SIZE)
 
 
-def pack_keys(rows, place, key_ref, value_ref, doc_ref, grad_ref, output_ref, *rest):
-    outs, (grads, outputs, ids, doc_sem, sems, more_sems) = rest[:-6], rest[-6:]
+def pack_keys(rows, place, key_ref, value_ref, doc_ref, query_ref, grad_ref, output_ref, *rest):
+    outs, (queries, grads, outputs, ids, doc_sem, sems, more_sems) = rest[:-7], rest[-7:]
     first = pltpu.make_async_copy(doc_ref, ids, doc_sem)
     first.start()
     copies = []
@@ -66,6 +66,7 @@
             copies.append(pltpu.make_async_copy(source.at[:, cut], target, sems.at[s, k]))
     copies.append(pltpu.make_async_copy(grad_ref, grads, more_sems.at[0]))
     copies.append(pltpu.make_async_copy(output_ref, outputs, more_sems.at[1]))
+    copies.append(pltpu.make_async_copy(query_ref, queries, more_sems.at[2]))
     for copy in copies:
         copy.start()
     first.wait()
@@ -77,19 +78,13 @@
 
 
 def pack_queries(rows, place, query_ref, grads, outputs, norm_ref, *rest):
-    outs, (token, stats, sems) = rest[:-3], rest[-3:]
-    copies = []
+    outs, (token, stats) = rest[:-2], rest[-2:]
     for s, out in enumerate(outs):
         for h in range(GROUP):
             cut = head_columns((place[1] ^ s) * GROUP + h)
-            target = out.at[h * rows : (h + 1) * rows, :]
-            copies.append(pltpu.make_async_copy(query_ref.at[:, cut], target, sems.at[s, h]))
-    for copy in copies:
-        copy.start()
-    for s, out in enumerate(outs):
-        for h in range(GROUP):
-            at = (GROUP + h) * rows
-            out[at : at + rows, :] = grads[:, head_columns((place[1] ^ s) * GROUP + h)]
+            for k, source in enumerate((query_ref, grads)):
+                at = (k * GROUP + h) * rows
+                out[at : at + rows, :] = source[:, cut]
     lane = lax.broadcasted_iota(jnp.int32, (rows, HEAD_SIZE), 1)
     columns = jnp.zeros((rows, HEAD_SIZE), F32)
     for h in range(QUERY_HEADS):
@@ -107,8 +102,6 @@
             at = 2 * GROUP * rows + part * EXTRA
             out[at : at + EXTRA, 0:rows] = term
             left = left - term.astype(F32)
-    for copy in copies:
-        copy.wait()
     token[...] = jnp.zeros_like(token)
 
 
@@ -327,28 +320,27 @@
     def exchange(pieces):
         return [pieces[0]] + [move(pieces[s], 0, s) for s in range(1, parts)]
 
-    *pieces, grads, outputs = call(
+    *pieces, held, grads, outputs = call(
         functools.partial(pack_keys, rows),
-        (place, key_matrix, value_matrix, doc_ids.reshape(1, rows), output_gradient, attention_output),
-        [shape((2 * rows + EXTRA, HEAD_SIZE), BF16)] * parts + [shape(queries.shape, BF16)] * 2,
+        (place, key_matrix, value_matrix, doc_ids.reshape(1, rows), queries, output_gradient, attention_output),
+        [shape((2 * rows + EXTRA, HEAD_SIZE), BF16)] * parts + [shape(queries.shape, BF16)] * 3,
         scratch=[
             pltpu.VMEM((1, rows), jnp.int32),
             pltpu.SemaphoreType.DMA(()),
             pltpu.SemaphoreType.DMA((parts, 2)),
-            pltpu.SemaphoreType.DMA((2,)),
+            pltpu.SemaphoreType.DMA((3,)),
         ],
-        specs=[HBM] * 5,
+        specs=[HBM] * 6,
     )
     pieces = exchange(pieces)
     *query_pieces, token = call(
         functools.partial(pack_queries, rows),
-        (place, queries, grads, outputs, log_sum_norm),
+        (place, held, grads, outputs, log_sum_norm),
         [shape((2 * width + 3 * EXTRA, HEAD_SIZE), BF16)] * parts + [TOKEN],
         scratch=[
             pltpu.VMEM((parts, 2 * GROUP, rows), F32),
-            pltpu.SemaphoreType.DMA((parts, GROUP)),
         ],
-        specs=[HBM, VMEM, VMEM, VMEM],
+        specs=[VMEM, VMEM, VMEM, VMEM],
     )
     (own,) = call(
         functools.partial(join, rows),

time: 60.4 us -> 60.5 us (level)
  the two profiles are of different devices: /device:TPU:17 before, /device:TPU:0 now
where the time goes in v11:
time: 60.5 us; the launch traced here: 59.4 us
  waiting for transfers between devices  24.8 us (41%)
  starting transfers between devices  21.4 us (35%)
  Pallas kernels  12.2 us (20%)
  between operations  0.94 us (2%)
    ppermute x16, waiting for transfers between devices, move(): return lax.ppermute(value, 'tok', [(t, target(t)) for t in range(count)])  24.8 us
    ppermute x16, starting transfers between devices, move(): return lax.ppermute(value, 'tok', [(t, target(t)) for t in range(count)])  21.4 us
    pallas_call x9, Pallas kernels, call(): pl.pallas_call(kernel, out_shape=outs, in_specs=[SMEM] + specs, out_specs...  12.2 us
  transfers between devices with their start and end apart: 16, of which 7 were waited for; matrix products, arithmetic and copies ran while one was open for 0% of the time, Pallas kernels for 13%

profile of v11, /device:TPU:0, one launch (start us, length us, event | category | flops | bytes accessed | tf_op | source)
XLA Modules:
  0.0 59.4 jit_solution(5439332221285528305)
XLA Ops:
  0.6 0.1 pad_add_fusion.place
  0.7 2.2 %shard_map.94 = (bf16[264,128]{1,0:T(8,128)(2,1)S(1)}, bf16[264,128]{1,0:T(8,128)(2,1)S(1)}, bf16[264,128]{1,0:T(8,128)(2,1)S(1)}, bf16[264,128]{1,0:T(8,128)(2,...) custom-call(s32[2]{0:T(128)S(1)} %pad_add_fusion.place, ...), custom_call_target="tpu_custom_call" | custom-call | bytes 3678728 | tf_op jit(solution)/shard_map/pallas_call | solution.py:42
  2.9 0.0 copy-start
  2.9 0.6 collective-permute-start.3
  3.5 2.6 %collective-permute-start.4 = (bf16[264,128]{1,0:T(8,128)(2,1)S(1)}, bf16[264,128]{1,0:T(8,128)(2,1)S(1)}, u32[]{:S(2)}, u32[]{:S(2)}) collective-permute-start(bf16[264,128]{1,0:T(8,128)(2,1)S(1)} %get-tuple-element.40), channel_id=1, source_target_pairs={{0,2},{1,3},{2,0},{3,1},{4,6},{5,7},{6,4},{7,5},{8,10},{9,11},{10,... | collective-permute-start | bytes 202760 | tf_op jit(solution)/shard_map/ppermute | solution.py:318
  6.0 0.0 collective-permute-start.5
  6.1 1.1 %shard_map.95 = (bf16[1048,128]{1,0:T(8,128)(2,1)S(1)}, bf16[1048,128]{1,0:T(8,128)(2,1)S(1)}, bf16[1048,128]{1,0:T(8,128)(2,1)S(1)}, bf16[1048,128]{1,0:T(8,128)(2,1)S(1)}, f32[8,128]{1,0:T(8,128)S(1)}) custom-call(s32[2]{0:T(128)S(1)} %pad_add_fusion.place, bf16[128,2048]{1,0:T(8,128)(2,1)S(1)} %get-tuple-element.31.query_ref, ...), custom_call_target="tpu_custom_call" | custom-call | bytes 2658312 | tf_op jit(solution)/shard_map/pallas_call | solution.py:42
  7.2 1.6 %collective-permute-done.4.refs_2_ = bf16[264,128]{1,0:T(8,128)(2,1)S(1)} collective-permute-done((bf16[264,128]{1,0:T(8,128)(2,1)S(1)}, bf16[264,128]{1,0:T(8,128)(2,1)S(1)}, u32[]{:S(2)}, u32[]{:S(2)}) %collective-permute-start.4) | collective-permute-done | bytes 67616 | tf_op jit(solution)/shard_map/ppermute | solution.py:318
  8.8 1.4 %collective-permute-done.5.refs_3_ = bf16[264,128]{1,0:T(8,128)(2,1)S(1)} collective-permute-done((bf16[264,128]{1,0:T(8,128)(2,1)S(1)}, bf16[264,128]{1,0:T(8,128)(2,1)S(1)}, u32[]{:S(2)}, u32[]{:S(2)}) %collective-permute-start.5) | collective-permute-done | bytes 67616 | tf_op jit(solution)/shard_map/ppermute | solution.py:318
  10.1 0.6 shard_map.96.refs_4_.refs_5_
  10.7 1.6 %collective-permute-start.6 = (bf16[1056,128]{1,0:T(8,128)(2,1)S(1)}, bf16[1056,128]{1,0:T(8,128)(2,1)S(1)}, u32[]{:S(2)}, u32[]{:S(2)}) collective-permute-start(bf16[1056,128]{1,0:T(8,128)(2,1)S(1)} %shard_map.96.refs_4_.refs_5_), channel_id=1, source_target_pairs={{0,4},{1,5},{2,6},{3,7},{4,8},{5,9},{6,10},{7,11},{8,12},{9,13},{1... | collective-permute-start | bytes 811016 | tf_op jit(solution)/shard_map/ppermute | solution.py:318
  12.3 8.8 %collective-permute-done.6.refs_5_ = bf16[1056,128]{1,0:T(8,128)(2,1)S(1)} collective-permute-done((bf16[1056,128]{1,0:T(8,128)(2,1)S(1)}, bf16[1056,128]{1,0:T(8,128)(2,1)S(1)}, u32[]{:S(2)}, u32[]{:S(2)}) %collective-permute-start.6) | collective-permute-done | bytes 270368 | tf_op jit(solution)/shard_map/ppermute | solution.py:318
  21.2 0.5 collective-permute-start
  21.7 1.5 %collective-permute-start.1 = (bf16[1048,128]{1,0:T(8,128)(2,1)S(1)}, bf16[1048,128]{1,0:T(8,128)(2,1)S(1)}, u32[]{:S(2)}, u32[]{:S(2)}) collective-permute-start(bf16[1048,128]{1,0:T(8,128)(2,1)S(1)} %get-tuple-element.36), channel_id=1, source_target_pairs={{0,2},{1,3},{2,0},{3,1},{4,6},{5,7},{6,4},{7,5},{8,10},{9,11},{10,... | collective-permute-start | bytes 804872 | tf_op jit(solution)/shard_map/ppermute | solution.py:318
  23.2 7.8 %collective-permute-done.1.refs_2_ = bf16[1048,128]{1,0:T(8,128)(2,1)S(1)} collective-permute-done((bf16[1048,128]{1,0:T(8,128)(2,1)S(1)}, bf16[1048,128]{1,0:T(8,128)(2,1)S(1)}, u32[]{:S(2)}, u32[]{:S(2)}) %collective-permute-start.1) | collective-permute-done | bytes 268320 | tf_op jit(solution)/shard_map/ppermute | solution.py:318
  31.0 3.8 %collective-permute-done.2.refs_3_ = bf16[1048,128]{1,0:T(8,128)(2,1)S(1)} collective-permute-done((bf16[1048,128]{1,0:T(8,128)(2,1)S(1)}, bf16[1048,128]{1,0:T(8,128)(2,1)S(1)}, u32[]{:S(2)}, u32[]{:S(2)}) %collective-permute-start.2) | collective-permute-done | bytes 268320 | tf_op jit(solution)/shard_map/ppermute | solution.py:318
  34.8 0.7 %shard_map.98 = (f32[4,128,512]{2,1,0:T(8,128)S(1)}, bf16[1024,128]{1,0:T(8,128)(2,1)S(1)}) custom-call(s32[2]{0:T(128)S(1)} %pad_add_fusion.place, bf16[1048,128]{1,0:T(8,128)(2,1)S(1)} %get-tuple-element.34.refs_0_, bf16[1048,128]{1,0:T(8,128)(2,1)S(1)} %collective-permute-done.refs_1_, bf16[1048,128]{1,0:T(8,128)(2,1)S(1)} %collective-permute-done.1.refs_2_, ...), custom_call_target="tpu_custom_call" | custom-call | flops 1342177280 | bytes 2924552 | tf_op jit(solution)/shard_map/pallas_call | solution.py:42
  35.5 0.8 %collective-permute-start.11 = (bf16[1024,128]{1,0:T(8,128)(2,1)S(1)}, bf16[1024,128]{1,0:T(8,128)(2,1)S(1)}, u32[]{:S(2)}, u32[]{:S(2)}) collective-permute-start(bf16[1024,128]{1,0:T(8,128)(2,1)S(1)} %get-tuple-element.51), channel_id=1, source_target_pairs={{0,1},{1,0},{2,3},{3,2},{4,12},{5,13},{6,14},{7,15},{8,4},{9,5},{1... | collective-permute-start | bytes 786440 | tf_op jit(solution)/shard_map/ppermute | solution.py:318
  36.3 3.5 %shard_map.97 = (f32[4,128,512]{2,1,0:T(8,128)S(1)}, f32[1024,128]{1,0:T(8,128)S(1)}) custom-call(s32[2]{0:T(128)S(1)} %pad_add_fusion.place, bf16[1048,128]{1,0:T(8,128)(2,1)S(1)} %get-tuple-element.34.refs_0_, bf16[1048,128]{1,0:T(8,128)(2,1)S(1)} %collective-permute-done.refs_1_, bf16[1048,128]{1,0:T(8,128)(2,1)S(1)} %collective-permute-done.1.refs_2_, ...), custom_call_target="tpu_custom_call" | custom-call | flops 1342177280 | bytes 3186696 | tf_op jit(solution)/shard_map/pallas_call | solution.py:42
  39.9 0.8 %shard_map.99 = (bf16[768,128]{1,0:T(8,128)(2,1)S(1)}, bf16[768,128]{1,0:T(8,128)(2,1)S(1)}, bf16[768,128]{1,0:T(8,128)(2,1)S(1)}, bf16[768,128]{1,0:T(8,128)(2,1)S(1)}, f32[1024,128]{1,0:T(8,128)S(1)}) custom-call(s32[2]{0:T(128)S(1)} %pad_add_fusion.place, bf16[1048,128]{1,0:T(8,128)(2,1)S(1)} %get-tuple-element.34.refs_0_, ...), custom_call_target="tpu_custom_call" | custom-call | flops 1342177280 | bytes 5545992 | tf_op jit(solution)/shard_map/pallas_call | solution.py:42
  40.6 0.1 collective-permute-start.8
  40.7 1.6 %collective-permute-start.9 = (bf16[768,128]{1,0:T(8,128)(2,1)S(1)}, bf16[768,128]{1,0:T(8,128)(2,1)S(1)}, u32[]{:S(2)}, u32[]{:S(2)}) collective-permute-start(bf16[768,128]{1,0:T(8,128)(2,1)S(1)} %get-tuple-element.48), channel_id=1, source_target_pairs={{0,2},{1,3},{2,0},{3,1},{4,6},{5,7},{6,4},{7,5},{8,10},{9,11},{10,... | collective-permute-start | bytes 589832 | tf_op jit(solution)/shard_map/ppermute | solution.py:318
  42.3 0.3 collective-permute-start.10
  42.6 0.6 %shard_map.101 = (bf16[512,128]{1,0:T(8,128)(2,1)S(1)}, bf16[256,128]{1,0:T(8,128)(2,1)S(1)}, bf16[256,128]{1,0:T(8,128)(2,1)S(1)}) custom-call(s32[2]{0:T(128)S(1)} %pad_add_fusion.place, bf16[1024,128]{1,0:T(8,128)(2,1)S(1)} %collective-permute-done.11.refs_0_, f32[1024,128]{1,0:T(8,128)S(1)} %get-tuple-element.52.refs_1_), custom_call_target="tpu_custom_call" | custom-call | bytes 1048584 | tf_op jit(solution)/shard_map/pallas_call | solution.py:42
  43.2 6.0 %collective-permute-start.14 = (bf16[512,128]{1,0:T(8,128)(2,1)S(1)}, bf16[512,128]{1,0:T(8,128)(2,1)S(1)}, u32[]{:S(2)}, u32[]{:S(2)}) collective-permute-start(bf16[512,128]{1,0:T(8,128)(2,1)S(1)} %get-tuple-element.55), channel_id=1, source_target_pairs={{0,12},{1,13},{2,14},{3,15},{4,2},{5,3},{6,0},{7,1},{8,6},{9,7},{1... | collective-permute-start | bytes 393224 | tf_op jit(solution)/shard_map/ppermute | solution.py:318
  49.2 2.9 %collective-permute-start.12 = (bf16[256,128]{1,0:T(8,128)(2,1)S(1)}, bf16[256,128]{1,0:T(8,128)(2,1)S(1)}, u32[]{:S(2)}, u32[]{:S(2)}) collective-permute-start(bf16[256,128]{1,0:T(8,128)(2,1)S(1)} %get-tuple-element.53), channel_id=1, source_target_pairs={{0,12},{1,13},{2,14},{3,15},{4,0},{5,1},{6,2},{7,3},{8,4},{9,5},{1... | collective-permute-start | bytes 196616 | tf_op jit(solution)/shard_map/ppermute | solution.py:318
  52.1 1.1 %collective-permute-done.14.refs_6_ = bf16[512,128]{1,0:T(8,128)(2,1)S(1)} collective-permute-done((bf16[512,128]{1,0:T(8,128)(2,1)S(1)}, bf16[512,128]{1,0:T(8,128)(2,1)S(1)}, u32[]{:S(2)}, u32[]{:S(2)}) %collective-permute-start.14) | collective-permute-done | bytes 131104 | tf_op jit(solution)/shard_map/ppermute | solution.py:318
  53.1 2.9 %collective-permute-start.13 = (bf16[256,128]{1,0:T(8,128)(2,1)S(1)}, bf16[256,128]{1,0:T(8,128)(2,1)S(1)}, u32[]{:S(2)}, u32[]{:S(2)}) collective-permute-start(bf16[256,128]{1,0:T(8,128)(2,1)S(1)} %get-tuple-element.54), channel_id=1, source_target_pairs={{0,12},{1,13},{2,14},{3,15},{4,1},{5,0},{6,3},{7,2},{8,5},{9,4},{1... | collective-permute-start | bytes 196616 | tf_op jit(solution)/shard_map/ppermute | solution.py:318
  56.0 0.1 collective-permute-start.15
  56.1 1.4 %shard_map.100 = (bf16[128,2048]{1,0:T(8,128)(2,1)}, f32[8,128]{1,0:T(8,128)S(1)}) custom-call(s32[2]{0:T(128)S(1)} %pad_add_fusion.place, bf16[768,128]{1,0:T(8,128)(2,1)S(1)} %get-tuple-element.46.refs_0_, bf16[768,128]{1,0:T(8,128)(2,1)S(1)} %collective-permute-done.8.refs_1_, bf16[768,128]{1,0:T(8,128)(2,1)S(1)} %collective-permute-done.9.refs_2_, ...), custom_call_target="tpu_custom_call" | custom-call | bytes 1314824 | tf_op jit(solution)/shard_map/pallas_call | solution.py:42
  57.6 0.3 collective-permute-done.13.refs_5_
  57.9 1.3 %shard_map.102 = (bf16[128,512]{1,0:T(8,128)(2,1)}, bf16[128,512]{1,0:T(8,128)(2,1)}) custom-call(s32[2]{0:T(128)S(1)} %pad_add_fusion.place, bf16[768,128]{1,0:T(8,128)(2,1)S(1)} %get-tuple-element.46.refs_0_, bf16[768,128]{1,0:T(8,128)(2,1)S(1)} %collective-permute-done.8.refs_1_, bf16[768,128]{1,0:T(8,128)(2,1)S(1)} %collective-permute-done.9.refs_2_, ...), custom_call_target="tpu_custom_call" | custom-call | bytes 1380360 | tf_op jit(solution)/shard_map/pallas_call | solution.py:42
  (13 shorter events, 0.0 us)
Async XLA Ops:
  2.9 3.2 %copy-start = (f32[16,128]{1,0:T(8,128)S(1)}, f32[16,128]{1,0:T(8,128)}, u32[]{:S(2)}) copy-start(f32[16,128]{1,0:T(8,128)} %norm_ref.1) | copy-start | bytes 24580
  2.9 4.3 %collective-permute-start.3 = (bf16[264,128]{1,0:T(8,128)(2,1)S(1)}, bf16[264,128]{1,0:T(8,128)(2,1)S(1)}, u32[]{:S(2)}, u32[]{:S(2)}) collective-permute-start(bf16[264,128]{1,0:T(8,128)(2,1)S(1)} %get-tuple-element.39), channel_id=1, source_target_pairs={{0,1},{1,0},{2,3},{3,2},{4,5},{5,4},{6,7},{7,6},{8,9},{9,8},{10,11... | collective-permute-start | bytes 202760 | tf_op jit(solution)/shard_map/ppermute | solution.py:318
  3.5 5.3 %collective-permute-start.4 = (bf16[264,128]{1,0:T(8,128)(2,1)S(1)}, bf16[264,128]{1,0:T(8,128)(2,1)S(1)}, u32[]{:S(2)}, u32[]{:S(2)}) collective-permute-start(bf16[264,128]{1,0:T(8,128)(2,1)S(1)} %get-tuple-element.40), channel_id=1, source_target_pairs={{0,2},{1,3},{2,0},{3,1},{4,6},{5,7},{6,4},{7,5},{8,10},{9,11},{10,... | collective-permute-start | bytes 202760 | tf_op jit(solution)/shard_map/ppermute | solution.py:318
  6.0 4.1 %collective-permute-start.5 = (bf16[264,128]{1,0:T(8,128)(2,1)S(1)}, bf16[264,128]{1,0:T(8,128)(2,1)S(1)}, u32[]{:S(2)}, u32[]{:S(2)}) collective-permute-start(bf16[264,128]{1,0:T(8,128)(2,1)S(1)} %get-tuple-element.41), channel_id=1, source_target_pairs={{0,3},{1,2},{2,1},{3,0},{4,7},{5,6},{6,5},{7,4},{8,11},{9,10},{10,... | collective-permute-start | bytes 202760 | tf_op jit(solution)/shard_map/ppermute | solution.py:318
  10.7 10.5 %collective-permute-start.6 = (bf16[1056,128]{1,0:T(8,128)(2,1)S(1)}, bf16[1056,128]{1,0:T(8,128)(2,1)S(1)}, u32[]{:S(2)}, u32[]{:S(2)}) collective-permute-start(bf16[1056,128]{1,0:T(8,128)(2,1)S(1)} %shard_map.96.refs_4_.refs_5_), channel_id=1, source_target_pairs={{0,4},{1,5},{2,6},{3,7},{4,8},{5,9},{6,10},{7,11},{8,12},{9,13},{1... | collective-permute-start | bytes 811016 | tf_op jit(solution)/shard_map/ppermute | solution.py:318
  21.2 13.6 %collective-permute-start.7 = (bf16[1056,128]{1,0:T(8,128)(2,1)S(1)}, bf16[1056,128]{1,0:T(8,128)(2,1)S(1)}, u32[]{:S(2)}, u32[]{:S(2)}) collective-permute-start(bf16[1056,128]{1,0:T(8,128)(2,1)S(1)} %collective-permute-done.6.refs_5_), channel_id=1, source_target_pairs={{0,1},{1,0},{2,3},{3,2},{4,8},{5,9},{6,10},{7,11},{8,12},{9,13},{1... | collective-permute-start | bytes 811016 | tf_op jit(solution)/shard_map/ppermute | solution.py:318
  21.2 2.0 %collective-permute-start = (bf16[1048,128]{1,0:T(8,128)(2,1)S(1)}, bf16[1048,128]{1,0:T(8,128)(2,1)S(1)}, u32[]{:S(2)}, u32[]{:S(2)}) collective-permute-start(bf16[1048,128]{1,0:T(8,128)(2,1)S(1)} %get-tuple-element.35), channel_id=1, source_target_pairs={{0,1},{1,0},{2,3},{3,2},{4,5},{5,4},{6,7},{7,6},{8,9},{9,8},{10,11... | collective-permute-start | bytes 804872 | tf_op jit(solution)/shard_map/ppermute | solution.py:318
  21.7 9.3 %collective-permute-start.1 = (bf16[1048,128]{1,0:T(8,128)(2,1)S(1)}, bf16[1048,128]{1,0:T(8,128)(2,1)S(1)}, u32[]{:S(2)}, u32[]{:S(2)}) collective-permute-start(bf16[1048,128]{1,0:T(8,128)(2,1)S(1)} %get-tuple-element.36), channel_id=1, source_target_pairs={{0,2},{1,3},{2,0},{3,1},{4,6},{5,7},{6,4},{7,5},{8,10},{9,11},{10,... | collective-permute-start | bytes 804872 | tf_op jit(solution)/shard_map/ppermute | solution.py:318
  23.2 11.6 %collective-permute-start.2 = (bf16[1048,128]{1,0:T(8,128)(2,1)S(1)}, bf16[1048,128]{1,0:T(8,128)(2,1)S(1)}, u32[]{:S(2)}, u32[]{:S(2)}) collective-permute-start(bf16[1048,128]{1,0:T(8,128)(2,1)S(1)} %get-tuple-element.37), channel_id=1, source_target_pairs={{0,3},{1,2},{2,1},{3,0},{4,7},{5,6},{6,5},{7,4},{8,11},{9,10},{10,... | collective-permute-start | bytes 804872 | tf_op jit(solution)/shard_map/ppermute | solution.py:318
  35.5 7.1 %collective-permute-start.11 = (bf16[1024,128]{1,0:T(8,128)(2,1)S(1)}, bf16[1024,128]{1,0:T(8,128)(2,1)S(1)}, u32[]{:S(2)}, u32[]{:S(2)}) collective-permute-start(bf16[1024,128]{1,0:T(8,128)(2,1)S(1)} %get-tuple-element.51), channel_id=1, source_target_pairs={{0,1},{1,0},{2,3},{3,2},{4,12},{5,13},{6,14},{7,15},{8,4},{9,5},{1... | collective-permute-start | bytes 786440 | tf_op jit(solution)/shard_map/ppermute | solution.py:318
  40.6 15.4 %collective-permute-start.8 = (bf16[768,128]{1,0:T(8,128)(2,1)S(1)}, bf16[768,128]{1,0:T(8,128)(2,1)S(1)}, u32[]{:S(2)}, u32[]{:S(2)}) collective-permute-start(bf16[768,128]{1,0:T(8,128)(2,1)S(1)} %get-tuple-element.47), channel_id=1, source_target_pairs={{0,1},{1,0},{2,3},{3,2},{4,5},{5,4},{6,7},{7,6},{8,9},{9,8},{10,11... | collective-permute-start | bytes 589832 | tf_op jit(solution)/shard_map/ppermute | solution.py:318
  40.7 15.4 %collective-permute-start.9 = (bf16[768,128]{1,0:T(8,128)(2,1)S(1)}, bf16[768,128]{1,0:T(8,128)(2,1)S(1)}, u32[]{:S(2)}, u32[]{:S(2)}) collective-permute-start(bf16[768,128]{1,0:T(8,128)(2,1)S(1)} %get-tuple-element.48), channel_id=1, source_target_pairs={{0,2},{1,3},{2,0},{3,1},{4,6},{5,7},{6,4},{7,5},{8,10},{9,11},{10,... | collective-permute-start | bytes 589832 | tf_op jit(solution)/shard_map/ppermute | solution.py:318
  42.3 13.8 %collective-permute-start.10 = (bf16[768,128]{1,0:T(8,128)(2,1)S(1)}, bf16[768,128]{1,0:T(8,128)(2,1)S(1)}, u32[]{:S(2)}, u32[]{:S(2)}) collective-permute-start(bf16[768,128]{1,0:T(8,128)(2,1)S(1)} %get-tuple-element.49), channel_id=1, source_target_pairs={{0,3},{1,2},{2,1},{3,0},{4,7},{5,6},{6,5},{7,4},{8,11},{9,10},{10,... | collective-permute-start | bytes 589832 | tf_op jit(solution)/shard_map/ppermute | solution.py:318
  43.2 10.0 %collective-permute-start.14 = (bf16[512,128]{1,0:T(8,128)(2,1)S(1)}, bf16[512,128]{1,0:T(8,128)(2,1)S(1)}, u32[]{:S(2)}, u32[]{:S(2)}) collective-permute-start(bf16[512,128]{1,0:T(8,128)(2,1)S(1)} %get-tuple-element.55), channel_id=1, source_target_pairs={{0,12},{1,13},{2,14},{3,15},{4,2},{5,3},{6,0},{7,1},{8,6},{9,7},{1... | collective-permute-start | bytes 393224 | tf_op jit(solution)/shard_map/ppermute | solution.py:318
  49.2 8.4 %collective-permute-start.12 = (bf16[256,128]{1,0:T(8,128)(2,1)S(1)}, bf16[256,128]{1,0:T(8,128)(2,1)S(1)}, u32[]{:S(2)}, u32[]{:S(2)}) collective-permute-start(bf16[256,128]{1,0:T(8,128)(2,1)S(1)} %get-tuple-element.53), channel_id=1, source_target_pairs={{0,12},{1,13},{2,14},{3,15},{4,0},{5,1},{6,2},{7,3},{8,4},{9,5},{1... | collective-permute-start | bytes 196616 | tf_op jit(solution)/shard_map/ppermute | solution.py:318
  53.1 4.8 %collective-permute-start.13 = (bf16[256,128]{1,0:T(8,128)(2,1)S(1)}, bf16[256,128]{1,0:T(8,128)(2,1)S(1)}, u32[]{:S(2)}, u32[]{:S(2)}) collective-permute-start(bf16[256,128]{1,0:T(8,128)(2,1)S(1)} %get-tuple-element.54), channel_id=1, source_target_pairs={{0,12},{1,13},{2,14},{3,15},{4,1},{5,0},{6,3},{7,2},{8,5},{9,4},{1... | collective-permute-start | bytes 196616 | tf_op jit(solution)/shard_map/ppermute | solution.py:318
  56.0 1.9 %collective-permute-start.15 = (bf16[256,128]{1,0:T(8,128)(2,1)S(1)}, bf16[256,128]{1,0:T(8,128)(2,1)S(1)}, u32[]{:S(2)}, u32[]{:S(2)}) collective-permute-start(bf16[256,128]{1,0:T(8,128)(2,1)S(1)} %slice.4), channel_id=1, source_target_pairs={{0,1},{1,0},{2,3},{3,2},{4,5},{5,4},{6,7},{7,6},{8,9},{9,8},{10,11... | collective-permute-start | bytes 196616 | tf_op jit(solution)/shard_map/ppermute | solution.py:318
